TPU v7x, 32 devices: a whole 2x2x4 slice. The times are simulated.
32 devices in a mesh: ctx: 16 (over z, y, x), tp: 2 (over core).
Axes of the slice: x: 2, y: 2, z: 4, core: 2. Of those that a mesh axis runs over, the one named last changes fastest.
Arguments:
- queries: bfloat16 [4096, 2048], P('tp', 'ctx'), may hold values from -6 to 6
- keys_in: bfloat16 [4096, 2048], P('tp', 'ctx'), may hold values from -6 to 6
- values_in: bfloat16 [4096, 2048], P('tp', 'ctx'), may hold values from -6 to 6
- grad_out: bfloat16 [4096, 2048], P('tp', 'ctx'), may hold values from -6 to 6
- residue: float32 [64, 16], replicated, may hold values from -0.07 to 0.07
- decay_rate: float32 [64, 16], replicated, may hold values from 9.765625e-05 to 0.0333333333
Outputs:
- grad_queries: bfloat16 [4096, 2048], P('tp', 'ctx')
- grad_keys: bfloat16 [4096, 2048], P('tp', 'ctx')
- grad_values: bfloat16 [4096, 2048], P('tp', 'ctx')
- grad_residue: float32 [64, 16], replicated
- grad_decay: float32 [64, 16], replicated
All inputs are finite; a program needn't handle non-finite values.
Results may differ from a plain program's by a relative error of at most 0.0085.
Values may be sent and summed in bfloat16 or wider, within the bound.
No kernel may reach another device: no remote copies, remote signals or barrier semaphores. Data moves between devices by JAX's collectives and lax.ppermute only.
A program may use at most 128 MiB of HBM per device.

v0:
```python
import math

import jax
import jax.numpy as jnp
from jax import lax
from jax.sharding import PartitionSpec as P


def dft_tables(size_a, size_b):
    total = size_a * size_b
    rows_a = jnp.arange(size_a, dtype=jnp.int32)
    rows_b = jnp.arange(size_b, dtype=jnp.int32)
    phase_a = (rows_a[:, None] * rows_a[None, :] % size_a).astype(jnp.float32) * (
        2.0 * math.pi / size_a
    )
    phase_b = (rows_b[:, None] * rows_b[None, :] % size_b).astype(jnp.float32) * (
        2.0 * math.pi / size_b
    )
    phase_turn = (rows_a[:, None] * rows_b[None, :] % total).astype(jnp.float32) * (
        2.0 * math.pi / total
    )
    fb_re = jnp.cos(phase_b)
    fb_im = -jnp.sin(phase_b)
    fa_pair = jnp.stack([jnp.cos(phase_a), -jnp.sin(phase_a)], axis=0)
    forward_b = jnp.stack([jnp.stack([fb_re, fb_im], 0), jnp.stack([-fb_im, fb_re], 0)], 0)
    inverse_b = jnp.stack([jnp.stack([fb_re, -fb_im], 0), jnp.stack([fb_im, fb_re], 0)], 0)
    return (fa_pair, forward_b, inverse_b, jnp.cos(phase_turn), -jnp.sin(phase_turn))


def forward_dft(signal, tables):
    fa_pair, forward_b, inverse_b, turn_re, turn_im = tables
    highest = lax.Precision.HIGHEST
    first = jnp.einsum("cab,pak->cpkb", signal, fa_pair, precision=highest)
    first_re = first[:, 0]
    first_im = first[:, 1]
    turned = jnp.stack(
        [
            first_re * turn_re[None] - first_im * turn_im[None],
            first_re * turn_im[None] + first_im * turn_re[None],
        ],
        axis=1,
    )
    return jnp.einsum("cpkb,pqbm->cqkm", turned, forward_b, precision=highest)


def inverse_real(spectrum, tables):
    fa_pair, forward_b, inverse_b, turn_re, turn_im = tables
    highest = lax.Precision.HIGHEST
    middle = jnp.einsum("cpkm,pqbm->cqkb", spectrum, inverse_b, precision=highest)
    middle_re = middle[:, 0]
    middle_im = middle[:, 1]
    back = jnp.stack(
        [
            middle_re * turn_re[None] + middle_im * turn_im[None],
            middle_im * turn_re[None] - middle_re * turn_im[None],
        ],
        axis=1,
    )
    result = jnp.einsum("cpkb,pak->cab", back, fa_pair, precision=highest)
    total = result.shape[1] * result.shape[2]
    return result.reshape(result.shape[0], total) / total


def spectral_work(gated, conv_grad, res_chan, dec_chan):
    chans, length = gated.shape
    total = 2 * length
    size_a = math.isqrt(total)
    while total % size_a != 0:
        size_a -= 1
    size_b = total // size_a
    tables = dft_tables(size_a, size_b)
    highest = lax.Precision.HIGHEST
    positions = jnp.arange(length).astype(jnp.float32)
    basis = jnp.exp(-dec_chan[:, :, None] * positions[None, None, :])
    filt = jnp.einsum("cm,cmt->ct", res_chan, basis, precision=highest)
    fields = jnp.concatenate(
        [gated.astype(jnp.float32), filt, conv_grad.astype(jnp.float32)], axis=0
    )
    padded = jnp.concatenate([fields, jnp.zeros((3 * chans, length), jnp.float32)], axis=1)
    spectra = forward_dft(padded.reshape(3 * chans, size_a, size_b), tables)
    gated_re = spectra[:chans, 0]
    gated_im = spectra[:chans, 1]
    filt_re = spectra[chans : 2 * chans, 0]
    filt_im = spectra[chans : 2 * chans, 1]
    cot_re = spectra[2 * chans :, 0]
    cot_im = spectra[2 * chans :, 1]
    products_re = jnp.concatenate(
        [
            gated_re * filt_re - gated_im * filt_im,
            filt_re * cot_re + filt_im * cot_im,
            gated_re * cot_re + gated_im * cot_im,
        ],
        axis=0,
    )
    products_im = jnp.concatenate(
        [
            gated_re * filt_im + gated_im * filt_re,
            filt_re * cot_im - filt_im * cot_re,
            gated_re * cot_im - gated_im * cot_re,
        ],
        axis=0,
    )
    results = inverse_real(jnp.stack([products_re, products_im], axis=1), tables)[:, :length]
    conv = results[:chans].astype(jnp.bfloat16)
    input_grad = results[chans : 2 * chans].astype(jnp.bfloat16)
    filter_grad = results[2 * chans :]
    res_terms = jnp.einsum("ct,cmt->cm", filter_grad, basis, precision=highest)
    dec_terms = (
        -res_chan
        * dec_chan
        * jnp.einsum("ct,cmt->cm", filter_grad * positions[None, :], basis, precision=highest)
    )
    return (conv, input_grad, res_terms, dec_terms)


def product_bf(first, second):
    return (first.astype(jnp.float32) * second.astype(jnp.float32)).astype(jnp.bfloat16)


def per_device(queries, keys_in, values_in, grad_out, residue, decay_rate):
    chans_tp, tokens_dev = queries.shape
    ctx_count = lax.axis_size("ctx")
    groups_count = residue.shape[0]
    highest = lax.Precision.HIGHEST
    chans_dev = chans_tp // ctx_count
    channel_ids = (
        lax.axis_index("tp") * chans_tp
        + lax.axis_index("ctx") * chans_dev
        + jnp.arange(chans_dev, dtype=jnp.int32)
    )
    onehot = (
        (channel_ids % groups_count)[:, None] == jnp.arange(groups_count, dtype=jnp.int32)[None, :]
    ).astype(jnp.float32)
    res_chan = jnp.dot(onehot, residue, precision=highest)
    dec_chan = jnp.dot(onehot, decay_rate, precision=highest)

    def to_blocks(field):
        return field.reshape(ctx_count, chans_dev, tokens_dev)

    def to_whole(field):
        return field.reshape(chans_dev, ctx_count * tokens_dev)

    def to_return(field):
        return field.reshape(1, chans_dev, ctx_count * tokens_dev)

    moved_query, moved_key, moved_value, moved_grad = (
        lax.all_to_all(to_blocks(queries), "ctx", split_axis=0, concat_axis=2, tiled=True),
        lax.all_to_all(to_blocks(keys_in), "ctx", split_axis=0, concat_axis=2, tiled=True),
        lax.all_to_all(to_blocks(values_in), "ctx", split_axis=0, concat_axis=2, tiled=True),
        lax.all_to_all(to_blocks(grad_out), "ctx", split_axis=0, concat_axis=2, tiled=True),
    )
    whole_query = to_whole(moved_query)
    whole_key = to_whole(moved_key)
    whole_value = to_whole(moved_value)
    whole_grad = to_whole(moved_grad)
    gated = product_bf(whole_key, whole_value)
    conv_grad = product_bf(whole_grad, whole_query)
    conv, input_grad, res_terms, dec_terms = spectral_work(gated, conv_grad, res_chan, dec_chan)
    grad_q_ch = product_bf(whole_grad, conv)
    grad_k_ch = product_bf(input_grad, whole_value)
    grad_v_ch = product_bf(input_grad, whole_key)
    back_q, back_k, back_v = (
        lax.all_to_all(to_return(grad_q_ch), "ctx", split_axis=2, concat_axis=0, tiled=True),
        lax.all_to_all(to_return(grad_k_ch), "ctx", split_axis=2, concat_axis=0, tiled=True),
        lax.all_to_all(to_return(grad_v_ch), "ctx", split_axis=2, concat_axis=0, tiled=True),
    )
    grad_queries = back_q.reshape(chans_tp, tokens_dev)
    grad_keys = back_k.reshape(chans_tp, tokens_dev)
    grad_values = back_v.reshape(chans_tp, tokens_dev)
    res_group = jnp.dot(onehot.T, res_terms, precision=highest)
    dec_group = jnp.dot(onehot.T, dec_terms, precision=highest)
    res_total, dec_total = lax.psum((res_group, dec_group), ("ctx", "tp"))
    whole_length = ctx_count * tokens_dev
    return (
        grad_queries,
        grad_keys,
        grad_values,
        res_total / whole_length,
        dec_total / whole_length,
    )


def solution(mesh):
    in_specs = (P("tp", "ctx"), P("tp", "ctx"), P("tp", "ctx"), P("tp", "ctx"), P(), P())
    out_specs = (P("tp", "ctx"), P("tp", "ctx"), P("tp", "ctx"), P(), P())
    return jax.shard_map(
        per_device, mesh=mesh, in_specs=in_specs, out_specs=out_specs, check_vma=False
    )
```

profile of v0, /device:TPU:0, one launch (start us, length us, event | category | flops | bytes accessed | tf_op | source)
XLA Modules:
  0.0 373.3 jit_solution(8923494113238331859)
XLA Ops:
  0.6 23.4 %all_to_all.81 = bf16[16,128,128]{2,1,0:T(8,128)(2,1)S(1)} all-to-all(bf16[16,128,128]{2,1,0:T(8,128)(2,1)} %bitcast.183), channel_id=1, replica_groups=mesh['ctx'=16,'tp'=2] {'ctx'}, dimensions={0} | all-to-all | bytes 1048576 | tf_op jit(solution)/shard_map/all_to_all | solution.py:148
  29.1 13.3 %all-to-all-done.2 = bf16[16,128,128]{2,1,0:T(8,128)(2,1)S(1)} async-done(((bf16[16,128,128]{2,1,0:T(8,128)(2,1)}), bf16[16,128,128]{2,1,0:T(8,128)(2,1)S(1)}, u32[]{:S(2)}, u32[]{:S(2)}) %all-to-all-start.2) | async-done | bytes 524320 | tf_op jit(solution)/shard_map/all_to_all | solution.py:149
  47.3 5.1 %multiply_reduce_fusion.1 = f32[128,2048]{1,0:T(8,128)S(1)} fusion(f32[128,16]{1,0:T(8,128)S(1)} %copy.93, f32[2048]{0:T(1024)S(1)} %iota_convert_fusion, f32[128,16]{1,0:T(8,128)S(1)} %copy.49), kind=kLoop, calls=%fused_computation.1 | loop fusion | flops 12320768 | bytes 1073152
  54.1 6.6 %all-to-all-done.3 = bf16[16,128,128]{2,1,0:T(8,128)(2,1)S(1)} async-done(((bf16[16,128,128]{2,1,0:T(8,128)(2,1)}), bf16[16,128,128]{2,1,0:T(8,128)(2,1)S(1)}, u32[]{:S(2)}, u32[]{:S(2)}) %all-to-all-start.3) | async-done | bytes 524320 | tf_op jit(solution)/shard_map/all_to_all | solution.py:147
  60.8 4.4 %all-to-all-start = ((bf16[16,128,128]{2,1,0:T(8,128)(2,1)}), bf16[16,128,128]{2,1,0:T(8,128)(2,1)}, u32[]{:S(2)}, u32[]{:S(2)}) async-start(bf16[16,128,128]{2,1,0:T(8,128)(2,1)} %bitcast.1), calls=%async_computation | async-start | bytes 1048576 | tf_op jit(solution)/shard_map/all_to_all | solution.py:150
  70.5 8.6 %all-to-all-done = bf16[16,128,128]{2,1,0:T(8,128)(2,1)} async-done(((bf16[16,128,128]{2,1,0:T(8,128)(2,1)}), bf16[16,128,128]{2,1,0:T(8,128)(2,1)}, u32[]{:S(2)}, u32[]{:S(2)}) %all-to-all-start) | async-done | bytes 524320 | tf_op jit(solution)/shard_map/all_to_all | solution.py:150
  85.3 14.2 %fusion.17 = f32[384,2,64,64]{0,2,3,1:T(8,128)S(1)} fusion(f32[384,64,64]{0,2,1:T(8,128)S(1)} %bitcast.170, f32[1,64,64]{1,2,0:T(8,128)S(1)} %get-tuple-element.32, f32[1,64,64]{1,2,0:T(8,128)S(1)} %get-tuple-element.33), kind=kOutput, calls=%fused_computation.33 | convolution fusion | flops 2415927296 | bytes 18907136 | tf_op jit(solution)/shard_map/cab,pak->cpkb/dot_general | solution.py:33
  103.3 9.6 %pad_maximum_fusion = f32[384,2,64,64]{0,2,3,1:T(8,128)} fusion(f32[384,1,64,64]{0,2,3,1:T(8,128)} %get-tuple-element.10, f32[384,1,64,64]{0,2,3,1:T(8,128)S(1)} %get-tuple-element.9), kind=kLoop, calls=%fused_computation.4 | loop fusion | flops 3145728 | bytes 25165824 | tf_op jit(solution)/shard_map/stack | solution.py:36
  112.9 22.9 %fusion.20 = f32[384,2,64,64]{0,3,2,1:T(8,128)S(1)} fusion(f32[384,2,64,64]{0,2,3,1:T(8,128)} %pad_maximum_fusion, f32[1,2,64,64]{2,3,1,0:T(8,128)S(1)} %get-tuple-element.23, f32[1,2,64,64]{2,3,1,0:T(8,128)S(1)} %get-tuple-element.26), kind=kOutput, calls=%fused_computation.34 | convolution fusion | flops 4831854592 | bytes 25231360 | tf_op jit(solution)/shard_map/cpkb,pqbm->cqkm/dot_general | solution.py:43
  138.5 4.3 %subtract_bitcast_fusion.2 = (f32[128,64,64]{0,2,1:T(8,128)}, f32[128,64,64]{0,2,1:T(8,128)}, f32[128,64,64]{0,2,1:T(8,128)}, f32[128,64,64]{0,2,1:T(8,128)}) fusion(f32[384,2,64,64]{0,3,2,1:T(8,128)S(1)} %fusion.20), kind=kLoop, calls=%fused_computation.41 | loop fusion | flops 6291456 | bytes 20971520 | tf_op jit(solution)/shard_map/sub | solution.py:89
  148.2 13.7 %fusion.23 = f32[2,64,384,64]{2,1,3,0:T(8,128)} fusion(f32[384,1,64,64]{0,3,2,1:T(8,128)S(1)} %maximum_bitcast_fusion.1, f32[384,1,64,64]{0,3,2,1:T(8,128)S(1)} %maximum_bitcast_fusion, f32[1,2,64,64]{2,3,1,0:T(8,128)S(1)} %get-tuple-element.27, f32[1,2,64,64]{2,3,1,0:T(8,128)S(1)} %get-tuple-element.22), kind=kOutput, calls=%fused_computation.35 | convolution fusion | flops 4835000320 | bytes 25231360 | tf_op jit(solution)/shard_map/cpkm,pqbm->cqkb/dot_general | solution.py:49
  161.9 16.4 %copy.121 = f32[2,64,384,64]{2,3,1,0:T(8,128)} copy(f32[2,64,384,64]{2,1,3,0:T(8,128)} %fusion.23) | data formatting | bytes 25165824 | tf_op jit(solution)/shard_map/cpkm,pqbm->cqkb/dot_general | solution.py:49
  178.3 6.0 %multiply_add_fusion = (f32[384,1,64,64]{0,2,3,1:T(8,128)S(1)}, f32[384,1,64,64]{0,2,3,1:T(8,128)S(1)}) fusion(f32[384,2,64,64]{0,2,3,1:T(8,128)} %bitcast.168, f32[64,64]{0,1:T(8,128)S(1)} %get-tuple-element.34, f32[64,64]{0,1:T(8,128)S(1)} %get-tuple-element.35), kind=kLoop, calls=%fused_computation.30 | loop fusion | flops 9437184 | bytes 25198592 | tf_op jit(solution)/shard_map/add | solution.py:54
  184.3 7.4 %fusion.13 = f32[384,64,64]{0,1,2:T(8,128)S(1)} fusion(f32[384,1,64,64]{0,2,3,1:T(8,128)S(1)} %get-tuple-element.8, f32[384,1,64,64]{0,2,3,1:T(8,128)S(1)} %get-tuple-element.7, f32[1,64,64]{1,2,0:T(8,128)S(1)} %get-tuple-element.32, f32[1,64,64]{1,2,0:T(8,128)S(1)} %get-tuple-element.33), kind=kOutput, calls=%fused_computation.23 | convolution fusion | flops 2420645888 | bytes 18907136 | tf_op jit(solution)/shard_map/cpkb,pak->cab/dot_general | solution.py:59
  199.8 8.5 %copy.124 = bf16[1,128,2048]{1,0,2:T(2,128)(2,1)S(1)} copy(bf16[1,128,2048]{1,2,0:T(8,128)(2,1)S(1)} %bitcast.182) | data formatting | bytes 1048576 | tf_op jit(solution)/shard_map/reshape | solution.py:144
  208.9 11.5 %reduce.4 = bf16[2048,128]{1,0:T(8,128)(2,1)S(1)} reduce(bf16[2048,1,128]{2,1,0:T(2,128)(2,1)S(1)} %bitcast.174, bf16[]{:T(256)} %broadcast.254), dimensions={1}, to_apply=%bitcast.167.reduce_sub_computation | reduce | bytes 1048578
  225.3 8.1 %copy.123 = bf16[1,128,2048]{1,0,2:T(2,128)(2,1)S(1)} copy(bf16[1,128,2048]{1,2,0:T(8,128)(2,1)S(1)} %bitcast.181) | data formatting | bytes 1048576 | tf_op jit(solution)/shard_map/reshape | solution.py:144
  233.5 11.5 %reduce.5 = bf16[2048,128]{1,0:T(8,128)(2,1)S(1)} reduce(bf16[2048,1,128]{2,1,0:T(2,128)(2,1)S(1)} %bitcast.176, bf16[]{:T(256)} %broadcast.254), dimensions={1}, to_apply=%bitcast.166.reduce_sub_computation | reduce | bytes 1048578
  245.9 8.3 %copy.122 = bf16[1,128,2048]{1,0,2:T(2,128)(2,1)S(1)} copy(bf16[1,128,2048]{1,2,0:T(8,128)(2,1)S(1)} %bitcast.180) | data formatting | bytes 1048576 | tf_op jit(solution)/shard_map/reshape | solution.py:144
  254.2 11.5 %reduce.6 = bf16[2048,128]{1,0:T(8,128)(2,1)S(1)} reduce(bf16[2048,1,128]{2,1,0:T(2,128)(2,1)S(1)} %bitcast.175, bf16[]{:T(256)} %broadcast.254), dimensions={1}, to_apply=%bitcast.165.reduce_sub_computation | reduce | bytes 1048578
  266.7 7.0 %all-to-all-start.5 = ((bf16[16,2,8192]{2,1,0:T(2,128)(2,1)}), bf16[16,2,8192]{2,1,0:T(2,128)(2,1)S(1)}, u32[]{:S(2)}, u32[]{:S(2)}) async-start(bf16[16,2,8192]{2,1,0:T(2,128)(2,1)} %reshape.265), calls=%async_computation.5 | async-start | bytes 1048576 | tf_op jit(solution)/shard_map/all_to_all | solution.py:164
  280.9 6.4 %all-to-all-done.5 = bf16[16,2,8192]{2,1,0:T(2,128)(2,1)S(1)} async-done(((bf16[16,2,8192]{2,1,0:T(2,128)(2,1)}), bf16[16,2,8192]{2,1,0:T(2,128)(2,1)S(1)}, u32[]{:S(2)}, u32[]{:S(2)}) %all-to-all-start.5) | async-done | bytes 524320 | tf_op jit(solution)/shard_map/all_to_all | solution.py:164
  291.2 34.5 %fusion = f32[128,1,16]{2,1,0:T(1,128)S(1)} fusion(f32[128,2048,1]{1,2,0:T(1,128)S(1)} %copy-done.15, f32[2048]{0:T(1024)S(1)} %iota_convert_fusion, f32[128,16]{1,0:T(8,128)S(1)} %copy-done.17), kind=kOutput, calls=%fused_computation.3 | convolution fusion | flops 54525952 | bytes 1073152 | tf_op jit(solution)/shard_map/ct,cmt->cm/dot_general | solution.py:107
  326.3 40.7 %all-reduce.1 = (f32[64,16]{0,1:T(8,128)S(1)}, f32[64,16]{0,1:T(8,128)S(1)}) all-reduce(f32[64,16]{0,1:T(8,128)S(1)} %fusion.43, f32[64,16]{0,1:T(8,128)S(1)} %fusion.42), channel_id=1, replica_groups=mesh['ctx'=16,'tp'=2] {'ctx','tp'}, use_global_device_ids=true, to_apply=%region_0.1 | all-reduce | flops 2048 | bytes 16384 | tf_op jit(solution)/shard_map/psum | solution.py:172
  (98 shorter events, 67.7 us)
Async XLA Ops:
  0.6 45.7 %copy-start = (f32[64,16]{0,1:T(8,128)S(1)}, f32[64,16]{0,1:T(8,128)}, u32[]{:S(2)}) copy-start(f32[64,16]{0,1:T(8,128)} %param.11) | copy-start | bytes 12292
  24.1 18.4 %all-to-all-start.2 = ((bf16[16,128,128]{2,1,0:T(8,128)(2,1)}), bf16[16,128,128]{2,1,0:T(8,128)(2,1)S(1)}, u32[]{:S(2)}, u32[]{:S(2)}) async-start(bf16[16,128,128]{2,1,0:T(8,128)(2,1)} %bitcast.184), calls=%async_computation.2 | async-start | bytes 1048576 | tf_op jit(solution)/shard_map/all_to_all | solution.py:149
  28.1 37.3 %copy-start.18 = (s32[128]{0:T(128)}, s32[128]{0:T(128)S(1)}, u32[]{:S(2)}) copy-start(s32[128]{0:T(128)S(1)} %and_select_fusion) | copy-start | bytes 1540
  42.5 22.9 %copy-start.13 = (bf16[16,128,128]{2,1,0:T(8,128)(2,1)}, bf16[16,128,128]{2,1,0:T(8,128)(2,1)S(1)}, u32[]{:S(2)}) copy-start(bf16[16,128,128]{2,1,0:T(8,128)(2,1)S(1)} %all-to-all-done.2) | copy-start | bytes 1572868
  42.5 18.3 %all-to-all-start.3 = ((bf16[16,128,128]{2,1,0:T(8,128)(2,1)}), bf16[16,128,128]{2,1,0:T(8,128)(2,1)S(1)}, u32[]{:S(2)}, u32[]{:S(2)}) async-start(bf16[16,128,128]{2,1,0:T(8,128)(2,1)} %bitcast.185), calls=%async_computation.3 | async-start | bytes 1048576 | tf_op jit(solution)/shard_map/all_to_all | solution.py:147
  47.3 18.2 %copy-start.16 = (f32[128,16]{1,0:T(8,128)}, f32[128,16]{1,0:T(8,128)S(1)}, u32[]{:S(2)}) copy-start(f32[128,16]{1,0:T(8,128)S(1)} %copy.49) | copy-start | bytes 24580
  60.8 4.6 %copy-start.14 = (bf16[16,128,128]{2,1,0:T(8,128)(2,1)}, bf16[16,128,128]{2,1,0:T(8,128)(2,1)S(1)}, u32[]{:S(2)}) copy-start(bf16[16,128,128]{2,1,0:T(8,128)(2,1)S(1)} %all-to-all-done.3) | copy-start | bytes 1572868
  60.8 18.4 %all-to-all-start = ((bf16[16,128,128]{2,1,0:T(8,128)(2,1)}), bf16[16,128,128]{2,1,0:T(8,128)(2,1)}, u32[]{:S(2)}, u32[]{:S(2)}) async-start(bf16[16,128,128]{2,1,0:T(8,128)(2,1)} %bitcast.1), calls=%async_computation | async-start | bytes 1048576 | tf_op jit(solution)/shard_map/all_to_all | solution.py:150
  65.8 19.0 %copy-start.3 = (f32[1,128,16,128]{1,3,2,0:T(8,128)}, f32[1,128,16,128]{1,3,2,0:T(8,128)S(1)}, u32[]{:S(2)}) copy-start(f32[1,128,16,128]{1,3,2,0:T(8,128)S(1)} %copy.47) | copy-start | bytes 3145732
  67.7 17.2 %copy-start.5 = (f32[1,128,16,128]{1,3,2,0:T(8,128)}, f32[1,128,16,128]{1,3,2,0:T(8,128)S(1)}, u32[]{:S(2)}) copy-start(f32[1,128,16,128]{1,3,2,0:T(8,128)S(1)} %copy.48) | copy-start | bytes 3145732
  142.8 3.7 copy-start.9
  142.8 4.1 %copy-start.10 = (f32[128,64,64]{0,2,1:T(8,128)S(1)}, f32[128,64,64]{0,2,1:T(8,128)}, u32[]{:S(2)}) copy-start(f32[128,64,64]{0,2,1:T(8,128)} %get-tuple-element.12) | copy-start | bytes 6291460
  142.8 4.7 %copy-start.11 = (f32[128,64,64]{0,2,1:T(8,128)S(1)}, f32[128,64,64]{0,2,1:T(8,128)}, u32[]{:S(2)}) copy-start(f32[128,64,64]{0,2,1:T(8,128)} %get-tuple-element.13) | copy-start | bytes 6291460
  195.4 4.4 %copy-start.2 = (f32[384,64,64]{0,2,1:T(8,128)}, f32[384,64,64]{0,2,1:T(8,128)S(1)}, u32[]{:S(2)}) copy-start(f32[384,64,64]{0,2,1:T(8,128)S(1)} %copy.59) | copy-start | bytes 18874372
  195.4 3.1 copy-start.6
  195.4 4.1 %copy-start.8 = (f32[1,128,16,128]{1,3,2,0:T(8,128)S(1)}, f32[1,128,16,128]{1,3,2,0:T(8,128)}, u32[]{:S(2)}) copy-start(f32[1,128,16,128]{1,3,2,0:T(8,128)} %copy-done.7) | copy-start | bytes 3145732
  221.3 45.4 %all-to-all-start.4 = ((bf16[16,2,8192]{2,1,0:T(2,128)(2,1)}), bf16[16,2,8192]{2,1,0:T(2,128)(2,1)S(1)}, u32[]{:S(2)}, u32[]{:S(2)}) async-start(bf16[16,2,8192]{2,1,0:T(2,128)(2,1)} %reshape.263), calls=%async_computation.4 | async-start | bytes 1048576 | tf_op jit(solution)/shard_map/all_to_all | solution.py:163
  245.9 31.7 %copy-start.17 = (f32[128,16]{1,0:T(8,128)S(1)}, f32[128,16]{1,0:T(8,128)}, u32[]{:S(2)}) copy-start(f32[128,16]{1,0:T(8,128)} %copy-done.16) | copy-start | bytes 24580
  266.7 20.6 %all-to-all-start.5 = ((bf16[16,2,8192]{2,1,0:T(2,128)(2,1)}), bf16[16,2,8192]{2,1,0:T(2,128)(2,1)S(1)}, u32[]{:S(2)}, u32[]{:S(2)}) async-start(bf16[16,2,8192]{2,1,0:T(2,128)(2,1)} %reshape.265), calls=%async_computation.5 | async-start | bytes 1048576 | tf_op jit(solution)/shard_map/all_to_all | solution.py:164
  277.6 13.6 %copy-start.15 = (f32[128,2048,1]{1,2,0:T(1,128)S(1)}, f32[128,2048,1]{1,2,0:T(1,128)}, u32[]{:S(2)}) copy-start(f32[128,2048,1]{1,2,0:T(1,128)} %copy.77) | copy-start | bytes 3145732
  287.3 84.2 %all-to-all-start.6 = ((bf16[16,2,8192]{2,1,0:T(2,128)(2,1)}), bf16[16,2,8192]{2,1,0:T(2,128)(2,1)S(1)}, u32[]{:S(2)}, u32[]{:S(2)}) async-start(bf16[16,2,8192]{2,1,0:T(2,128)(2,1)} %reshape.267), calls=%async_computation.6 | async-start | bytes 1048576 | tf_op jit(solution)/shard_map/all_to_all | solution.py:165
  291.2 34.6 %copy-start.19 = (s32[128]{0:T(128)S(1)}, s32[128]{0:T(128)}, u32[]{:S(2)}) copy-start(s32[128]{0:T(128)} %copy-done.18) | copy-start | bytes 1540
  291.2 34.6 %copy-start.20 = (f32[128,16]{0,1:T(8,128)S(1)}, f32[128,16]{0,1:T(8,128)}, u32[]{:S(2)}) copy-start(f32[128,16]{0,1:T(8,128)} %get-tuple-element.29) | copy-start | bytes 24580
  367.6 5.5 %copy-start.1 = (f32[64,16]{0,1:T(8,128)S(1)}, f32[64,16]{0,1:T(8,128)}, u32[]{:S(2)}) copy-start(f32[64,16]{0,1:T(8,128)} %param.11) | copy-start | bytes 12292
  (3 other events, 6.5 us)
where the time goes:
time: 377 us; the launch traced here: 373 us
  matrix products  95 us (25%)
  other arithmetic  85.7 us (23%)
  local copies, waits for them, and re-layouts  65 us (17%)
  blocking collectives  64.1 us (17%)
  waiting for transfers between devices  35 us (9%)
  starting transfers between devices  27.1 us (7%)
    unnamed x5, other arithmetic  43 us
    psum x1, blocking collectives, per_device(): res_total, dec_total = lax.psum((res_group, dec_group), ('ctx', 'tp'))  40.7 us
    dot_general x1, matrix products, spectral_work(): res_terms = jnp.einsum('ct,cmt->cm', filter_grad, basis, precision=highest)  34.5 us
    reshape x3, local copies, waits for them, and re-layouts, to_return(): return field.reshape(1, chans_dev, ctx_count * tokens_dev)  25 us
    all_to_all x1, blocking collectives, per_device(): lax.all_to_all(to_blocks(keys_in), 'ctx', split_axis=0, concat_axis=2, ti...  23.4 us
    dot_general x1, matrix products, forward_dft(): return jnp.einsum('cpkb,pqbm->cqkm', turned, forward_b, precision=highest)  22.9 us
    dot_general x1, local copies, waits for them, and re-layouts, inverse_real(): jnp.einsum('cpkm,pqbm->cqkb', spectrum, inverse_b, precision=highest)  16.4 us
    dot_general x1, matrix products, forward_dft(): first = jnp.einsum('cab,pak->cpkb', signal, fa_pair, precision=highest)  14.2 us
  transfers between devices with their start and end apart: 6, of which 4 were waited for; matrix products, arithmetic and copies ran while one was open for 27% of the time, Pallas kernels for 0%

commit v1 on v0

v1 whole, which is shorter than its diff:
```python
import functools
import math

import jax
import jax.numpy as jnp
from jax import lax
from jax.experimental import pallas as pl
from jax.experimental.pallas import tpu as pltpu
from jax.sharding import PartitionSpec as P

F32 = jnp.float32
BF16 = jnp.bfloat16
PLANE = 4
NT = (((1,), (1,)), ((), ()))
NN = (((1,), (0,)), ((), ()))
TN = (((0,), (0,)), ((), ()))


def dot(a, b, dims):
    return lax.dot_general(a, b, dims, preferred_element_type=F32)


def product(a, b):
    return (a.astype(F32) * b.astype(F32)).astype(BF16)


def column(block, row):
    modes = block.shape[1]
    eye = lax.broadcasted_iota(jnp.int32, (modes, modes), 0) == lax.broadcasted_iota(
        jnp.int32, (modes, modes), 1
    )
    wide = jnp.broadcast_to(block[row : row + 1, :], (modes, modes))
    return jnp.sum(jnp.where(eye, wide, 0.0), axis=1, keepdims=True)


def lane_iota(shape):
    return lax.broadcasted_iota(jnp.int32, shape, len(shape) - 1)


def states_kernel(place, k_ref, v_ref, g_ref, q_ref, dec_ref, gx_ref, cx_ref, *rest):
    outs, gs, cs = rest[:PLANE], rest[PLANE], rest[PLANE + 1]
    step = pl.program_id(0)
    rows, groups, length = k_ref.shape
    modes = dec_ref.shape[1]
    flat = rows * groups
    gs[...] = product(k_ref[...], v_ref[...]).astype(F32).reshape(flat, length)
    cs[...] = product(g_ref[...], q_ref[...]).astype(F32).reshape(flat, length)
    dec = dec_ref[...]
    ahead = lane_iota((modes, length)).astype(F32)
    behind = float(length) - ahead
    zero = jnp.zeros((modes, length), BF16)
    results = []
    for pair in range(groups // 2):
        left, right = [], []
        for side in range(2):
            group = 2 * pair + side
            rate = column(dec, group)
            fwd = jnp.exp(-rate * behind)
            bwd = jnp.exp(-rate * ahead)
            x = gs[pl.ds(group, rows, stride=groups), :].astype(BF16)
            c = cs[pl.ds(group, rows, stride=groups), :].astype(BF16)
            gx_ref[group] = x
            cx_ref[group] = c
            wx = [zero] * 8
            wx[side] = fwd.astype(BF16)
            wx[4 + side] = (behind * fwd).astype(BF16)
            wc = [zero] * 8
            wc[2 + side] = bwd.astype(BF16)
            wc[6 + side] = (ahead * bwd).astype(BF16)
            left += [x, c]
            right += [jnp.concatenate(wx, axis=0), jnp.concatenate(wc, axis=0)]
        results.append(
            dot(jnp.concatenate(left, axis=1), jnp.concatenate(right, axis=1), NT).astype(BF16)
        )
    for index in range(PLANE):

        @pl.when(step == index)
        def _():
            for pair in range(groups // 2):
                outs[index][pair] = results[pair]


def local_kernel(gx_ref, cx_ref, dec_ref, res_ref, conv_ref, ig_ref, sums_ref):
    groups, rows, length = gx_ref.shape
    modes = dec_ref.shape[1]
    dec, res = dec_ref[...], res_ref[...]
    ahead = lane_iota((modes, length)).astype(F32)
    later = lane_iota((length, length)) >= lax.broadcasted_iota(jnp.int32, (length, length), 0)
    column_of = lane_iota((length, length)) + lax.broadcasted_iota(jnp.int32, (length, length), 0)
    paired = column_of < length
    mirror = jnp.where(column_of == length - 1, 1.0, 0.0).astype(BF16)
    reverse = dot(cx_ref[...].reshape(groups * rows, length), mirror, NN).astype(BF16)
    sub = lax.broadcasted_iota(jnp.int32, (modes, length), 0)
    lane = lane_iota((modes, length))
    lag = float(length - 1) - ahead
    for pair in range(groups // 2):
        total = jnp.zeros((modes, length), F32)
        for side in range(2):
            group = 2 * pair + side
            rate = column(dec, group)
            basis = jnp.exp(-rate * ahead)
            taps = jnp.sum(column(res, group) * basis, axis=0, keepdims=True)
            toep = pltpu.roll(
                jnp.broadcast_to(taps, (length, length)), 0, 1, stride=1, stride_axis=0
            )
            toep = jnp.where(later, toep, 0.0).astype(BF16)
            x, c = gx_ref[group], cx_ref[group]
            conv_ref[0, pl.ds(group, rows, stride=groups), :] = dot(x, toep, NN)
            ig_ref[0, pl.ds(group, rows, stride=groups), :] = dot(c, toep, NT)
            mirrored = reverse[group * rows : (group + 1) * rows]
            prods = jnp.where(paired, dot(x, mirrored, TN), 0.0)
            prods = pltpu.roll(prods, 0, 1, stride=1, stride_axis=0)
            corr = jnp.sum(prods, axis=0, keepdims=True) * jnp.exp(-rate * lag)
            plain = jnp.sum(corr, axis=1, keepdims=True)
            moment = jnp.sum(corr * lag, axis=1, keepdims=True)
            total += jnp.where(lane == sub + side * modes, plain, 0.0)
            total += jnp.where(lane == sub + (2 + side) * modes, moment, 0.0)
        sums_ref[pair : pair + 1, :] = jnp.sum(total, axis=0, keepdims=True)


def split_pair(x, half):
    head = x.astype(BF16).astype(F32)
    tail = (x - head).astype(BF16).astype(F32)
    low = lane_iota(x.shape) < half
    return jnp.where(low, head, pltpu.roll(jnp.where(low, tail, 0.0), half, x.ndim - 1)).astype(BF16)


def join_pair(x, half):
    x = x.astype(F32)
    low = lane_iota(x.shape) < half
    return jnp.where(low, x + pltpu.roll(x, half, x.ndim - 1), 0.0)


def in_order(arrays, place):
    arrays, bit = list(arrays), 1
    while bit < len(arrays):
        swap = (place & bit) != 0
        new = list(arrays)
        for i in range(len(arrays)):
            new[i] = jnp.where(swap, arrays[i ^ bit], arrays[i])
        arrays, bit = new, 2 * bit
    return arrays


def advance(state, decay, gap, half, axis):
    lane = lane_iota(state.shape)
    shifted = pltpu.roll(state, half, axis)
    return decay * (state + jnp.where(lane >= half, gap * shifted, 0.0))


def pair_terms(state, x, modes):
    lanes = x.shape[-1]
    axis = x.ndim - 1
    plain = jnp.sum(state * pltpu.roll(x, lanes - 2 * modes, axis), axis=1)
    first = jnp.sum(state * pltpu.roll(x, lanes - 6 * modes, axis), axis=1)
    second = jnp.sum(state * pltpu.roll(x, 2 * modes, axis), axis=1)
    lane = lane_iota(plain.shape)
    second = pltpu.roll(second, lanes - 2 * modes, 1)
    first = pltpu.roll(first, 2 * modes, 1)
    return jnp.where(
        lane < 2 * modes, plain, jnp.where(lane < 4 * modes, first + second, 0.0)
    )


def scan_blocks(blocks, start, rate, gap, modes):
    half = 4 * modes
    axis = blocks[0].ndim - 1
    lane = lane_iota(blocks[0].shape)
    forward = (lane % half) < 2 * modes
    decay = jnp.exp(-rate * gap)
    state, states = start, []
    for i in range(len(blocks)):
        states.append(state)
        block = jnp.where(forward, blocks[i], blocks[len(blocks) - 1 - i])
        state = advance(state, decay, gap, half, axis) + block
    return states, state


def all_pair_terms(states, blocks, modes):
    lane = lane_iota(blocks[0].shape)
    total = None
    for i in range(len(blocks)):
        term = pair_terms(states[i], blocks[i], modes)
        total = term if total is None else total + term
    return total


def plane_kernel(length, place, rate_ref, *refs):
    *msgs, sums_ref, out_ref, acc = refs
    pairs, rows, lanes = msgs[0].shape
    modes = lanes // 8
    blocks = in_order([m[...].astype(F32) for m in msgs], place[0])
    rate = rate_ref[...].reshape(pairs, 1, lanes)
    states, last = scan_blocks(blocks, jnp.zeros_like(blocks[0]), rate, float(length), modes)
    out_ref[: pairs * rows] = last.astype(BF16).reshape(pairs * rows, lanes)
    acc[...] = sums_ref[...]
    acc[pl.ds(pl.multiple_of(place[0] * pairs, pairs), pairs), :] += all_pair_terms(
        states, blocks, modes
    )
    out_ref[pairs * rows :] = split_pair(acc[...], lanes // 2)


def line_kernel(length, place, rate_ref, *refs):
    count = (len(refs) - 2 * PLANE - 1)
    msgs, lines = refs[:PLANE], refs[PLANE : PLANE + count]
    outs, acc = refs[PLANE + count : -1], refs[-1]
    pairs, rows, lanes = msgs[0].shape
    modes = lanes // 8
    flat = pairs * rows
    rate = rate_ref[...].reshape(pairs, 1, lanes)
    planes = in_order(
        [r[:flat].astype(F32).reshape(pairs, rows, lanes) for r in lines], place[1]
    )
    gap = float(PLANE * length)
    states, _ = scan_blocks(planes, jnp.zeros_like(planes[0]), rate, gap, modes)
    lane = lane_iota(planes[0].shape)
    forward = (lane % (4 * modes)) < 2 * modes
    incoming = jnp.zeros_like(planes[0])
    for i in range(count):
        here = jnp.where(forward, i, count - 1 - i) == place[1]
        incoming = incoming + jnp.where(here, states[i], 0.0)
    total = join_pair(lines[0][flat:], lanes // 2)
    for r in lines[1:]:
        total = total + join_pair(r[flat:], lanes // 2)
    acc[...] = total
    acc[pl.ds(pl.multiple_of(place[0] * pairs, pairs), pairs), :] += all_pair_terms(
        states, planes, modes
    )
    sums = split_pair(acc[...], lanes // 2)
    blocks = in_order([m[...].astype(F32) for m in msgs], place[0])
    states, _ = scan_blocks(blocks, incoming, rate, float(length), modes)
    found = [
        jnp.where(forward, states[i], states[PLANE - 1 - i]) for i in range(PLANE)
    ]
    found = in_order(found, place[0])
    low = lane[: pairs // 2] < 4 * modes
    for i in range(PLANE):
        packed = jnp.where(
            low, found[i][: pairs // 2], pltpu.roll(found[i][pairs // 2 :], 4 * modes, 2)
        )
        outs[i][: flat // 2] = packed.astype(BF16).reshape(flat // 2, lanes)
        outs[i][flat // 2 :] = sums


def outputs_kernel(
    place, k_ref, v_ref, g_ref, conv_ref, ig_ref, dec_ref, res_ref, *refs
):
    incoming, outs, cs, gs = refs[:PLANE], refs[PLANE : PLANE + 3], refs[-2], refs[-1]
    step = pl.program_id(0)
    rows, groups, length = k_ref.shape
    modes = dec_ref.shape[1]
    pairs = groups // 2
    flat = pairs * rows // 2
    dec, res = dec_ref[...], res_ref[...]
    ahead = lane_iota((modes, length)).astype(F32)
    behind = float(length) - ahead
    state = incoming[0][:flat]
    for i in range(1, PLANE):
        state = jnp.where(step == i, incoming[i][:flat], state)
    zero = jnp.zeros((modes, length), BF16)
    for group in range(groups):
        pair, side = group // 2, group % 2
        rate, weight = column(dec, group), column(res, group)
        base = (4 if pair >= pairs // 2 else 0) + side
        left, right = [zero] * 8, [zero] * 8
        left[base] = (weight * jnp.exp(-rate * ahead)).astype(BF16)
        right[base + 2] = (weight * jnp.exp(-rate * behind)).astype(BF16)
        quad = pair % (pairs // 2)
        s = state[quad * rows : (quad + 1) * rows]
        both = dot(
            s,
            jnp.concatenate(
                [jnp.concatenate(left, axis=0), jnp.concatenate(right, axis=0)], axis=1
            ),
            NN,
        )
        cs[pl.ds(group, rows, stride=groups), :] = both[:, :length]
        gs[pl.ds(group, rows, stride=groups), :] = both[:, length:]
    shape = (rows, groups, length)
    conv = (cs[...] + conv_ref[0]).astype(BF16).reshape(shape)
    ig = (gs[...] + ig_ref[0]).astype(BF16).reshape(shape)
    outs[0][...] = product(g_ref[...], conv)
    outs[1][...] = product(ig, v_ref[...])
    outs[2][...] = product(ig, k_ref[...])


def per_device(queries, keys_in, values_in, grad_out, residue, decay_rate):
    chans, length = queries.shape
    groups, modes = residue.shape
    count = lax.axis_size("ctx")
    tp = lax.axis_size("tp")
    depth = count // PLANE
    rows = chans // groups
    part = groups // PLANE
    pairs = part // 2
    lanes = 8 * modes
    me = lax.axis_index("ctx").astype(jnp.int32)
    place = jnp.stack([me % PLANE, me // PLANE])

    def cube(x):
        return x.reshape(rows, groups, length)

    query, key, value, grad = cube(queries), cube(keys_in), cube(values_in), cube(grad_out)
    rates = jnp.tile(decay_rate.reshape(groups // 2, 2 * modes), (1, 4))

    turn = pl.BlockSpec((rows, part, length), lambda i, s: (0, s[0] ^ i, 0))
    small = pl.BlockSpec((part, modes), lambda i, s: (s[0] ^ i, 0))
    deep = pl.BlockSpec((part, rows, length), lambda i, s: (s[0] ^ i, 0, 0))
    whole = pl.BlockSpec((pairs, rows, lanes), lambda i, s: (0, 0, 0))
    gx, cx, *own = pl.pallas_call(
        states_kernel,
        grid_spec=pltpu.PrefetchScalarGridSpec(
            num_scalar_prefetch=1,
            grid=(PLANE,),
            in_specs=[turn] * 4 + [small],
            out_specs=[deep] * 2 + [whole] * PLANE,
            scratch_shapes=[pltpu.VMEM((rows * part, length), F32)] * 2,
        ),
        out_shape=[jax.ShapeDtypeStruct((groups, rows, length), BF16)] * 2
        + [jax.ShapeDtypeStruct((pairs, rows, lanes), BF16)] * PLANE,
        cost_estimate=pl.CostEstimate(flops=10**9, bytes_accessed=3 * 10**6, transcendentals=0),
        name="states",
    )(place, key, value, grad, query, decay_rate)

    def swap(x, bits):
        return lax.ppermute(x, "ctx", [(i, i ^ bits) for i in range(count)])

    near = [own[0]] + [swap(own[i], i) for i in range(1, PLANE)]

    tall = pl.BlockSpec((part, rows, length), lambda i: (i, 0, 0))
    table = pl.BlockSpec((part, modes), lambda i: (i, 0))
    slab = pl.BlockSpec((1, rows * part, length), lambda i: (i, 0, 0))
    conv, ig, sums = pl.pallas_call(
        local_kernel,
        grid=(PLANE,),
        in_specs=[tall] * 2 + [table] * 2,
        out_specs=[slab] * 2 + [pl.BlockSpec((pairs, lanes), lambda i: (i, 0))],
        out_shape=[jax.ShapeDtypeStruct((PLANE, rows * part, length), F32)] * 2
        + [jax.ShapeDtypeStruct((groups // 2, lanes), F32)],
        cost_estimate=pl.CostEstimate(flops=10**9, bytes_accessed=4 * 10**6, transcendentals=0),
        name="local",
    )(gx, cx, decay_rate, residue)

    flat = pairs * rows
    here = pl.BlockSpec((pairs, lanes), lambda i, s: (s[0], 0))

    def full(*shape):
        return pl.BlockSpec(shape, lambda i, s: (0,) * len(shape))

    plane = pl.pallas_call(
        functools.partial(plane_kernel, length),
        grid_spec=pltpu.PrefetchScalarGridSpec(
            num_scalar_prefetch=1,
            grid=(1,),
            in_specs=[here] + [full(pairs, rows, lanes)] * PLANE + [full(groups // 2, lanes)],
            out_specs=full(flat + groups // 2, lanes),
            scratch_shapes=[pltpu.VMEM((groups // 2, lanes), F32)],
        ),
        out_shape=jax.ShapeDtypeStruct((flat + groups // 2, lanes), BF16),
        name="plane",
    )(place, rates, *near, sums)

    line = [plane] + [swap(plane, PLANE * i) for i in range(1, depth)]
    back = pl.pallas_call(
        functools.partial(line_kernel, length),
        grid_spec=pltpu.PrefetchScalarGridSpec(
            num_scalar_prefetch=1,
            grid=(1,),
            in_specs=[here]
            + [full(pairs, rows, lanes)] * PLANE
            + [full(flat + groups // 2, lanes)] * depth,
            out_specs=[full(flat // 2 + groups // 2, lanes)] * PLANE,
            scratch_shapes=[pltpu.VMEM((groups // 2, lanes), F32)],
        ),
        out_shape=[jax.ShapeDtypeStruct((flat // 2 + groups // 2, lanes), BF16)] * PLANE,
        name="line",
    )(place, rates, *near, *line)
    back = [back[0]] + [swap(back[i], i) for i in range(1, PLANE)]

    total = sum(
        b[flat // 2 :, : lanes // 2].astype(F32) + b[flat // 2 :, lanes // 2 :].astype(F32)
        for b in back
    )
    bit = 1
    while bit < tp:
        total = total + lax.ppermute(total, "tp", [(i, i ^ bit) for i in range(tp)])
        bit *= 2

    turned = pl.BlockSpec((1, rows * part, length), lambda i, s: (s[0] ^ i, 0, 0))
    outs = pl.pallas_call(
        outputs_kernel,
        grid_spec=pltpu.PrefetchScalarGridSpec(
            num_scalar_prefetch=1,
            grid=(PLANE,),
            in_specs=[turn] * 3
            + [turned] * 2
            + [small] * 2
            + [full(flat // 2 + groups // 2, lanes)] * PLANE,
            out_specs=[turn] * 3,
            scratch_shapes=[pltpu.VMEM((rows * part, length), F32)] * 2,
        ),
        out_shape=[jax.ShapeDtypeStruct((rows, groups, length), BF16)] * 3,
        cost_estimate=pl.CostEstimate(flops=10**9, bytes_accessed=5 * 10**6, transcendentals=0),
        name="outputs",
    )(place, key, value, grad, conv, ig, decay_rate, residue, *back)
    tokens = count * length
    plain = total[:, : 2 * modes].reshape(groups, modes)
    moment = total[:, 2 * modes :].reshape(groups, modes)
    return (
        outs[0].reshape(chans, length),
        outs[1].reshape(chans, length),
        outs[2].reshape(chans, length),
        plain / tokens,
        -(residue * decay_rate) * moment / tokens,
    )


def solution(mesh):
    in_specs = (P("tp", "ctx"), P("tp", "ctx"), P("tp", "ctx"), P("tp", "ctx"), P(), P())
    out_specs = (P("tp", "ctx"), P("tp", "ctx"), P("tp", "ctx"), P(), P())
    return jax.shard_map(
        per_device, mesh=mesh, in_specs=in_specs, out_specs=out_specs, check_vma=False
    )
```

time: 377 us -> 64.3 us (0.17)
  matrix products: 95 us -> 0 us
  other arithmetic: 85.7 us -> 1.53 us
  blocking collectives: 64.1 us -> 0 us
  local copies, waits for them, and re-layouts: 65 us -> 7.46 us
  Pallas kernels: 0 us -> 31.6 us
  waiting for transfers between devices: 35 us -> 9.7 us
  starting transfers between devices: 27.1 us -> 12.5 us
    dot_general x9 -> x0, matrix products: 95 us -> none  [the longest x1 34.5 us: spectral_work(): res_terms = jnp.einsum('ct,cmt->cm', filter_grad, basis, precision=highest)]
    unnamed x5 -> x0, other arithmetic: 43 us -> none
    psum x1 -> x0, blocking collectives: 40.7 us -> none  [per_device(): res_total, dec_total = lax.psum((res_group, dec_group), ('ctx', 'tp'))]
    all_to_all x6 -> x0, waiting for transfers between devices: 35 us -> none  [the longest x1 13.3 us: per_device(): lax.all_to_all(to_blocks(values_in), 'ctx', split_axis=0, concat_axis=2,...]
    pallas_call x0 -> x5, Pallas kernels: none -> 31.6 us  [the longest x1 13.7 us: per_device(): pl.pallas_call(local_kernel, grid=(PLANE,), in_specs=[tall] * 2 + [table]...]
    all_to_all x6 -> x0, starting transfers between devices: 27.1 us -> none  [the longest x1 7 us: per_device(): lax.all_to_all(to_return(grad_k_ch), 'ctx', split_axis=2, concat_axis=0,...]
    reshape x3 -> x1, local copies, waits for them, and re-layouts: 25 us -> 0.07 us  [per_device(): moment = total[:, 2 * modes:].reshape(groups, modes)]
    all_to_all x1 -> x0, blocking collectives: 23.4 us -> none  [per_device(): lax.all_to_all(to_blocks(keys_in), 'ctx', split_axis=0, concat_axis=2, ti...]
  transfers between devices with their start and end apart: 6 -> 10, of which waited for: 4 -> 6; matrix products, arithmetic and copies ran while one was open for 27% -> 2% of each run, Pallas kernels for 0% -> 31%
where the time goes in v1:
time: 64.3 us; the launch traced here: 63.6 us
  Pallas kernels  31.6 us (49%)
  starting transfers between devices  12.5 us (19%)
  waiting for transfers between devices  9.7 us (15%)
  local copies, waits for them, and re-layouts  7.46 us (12%)
  other arithmetic  1.53 us (2%)
  between operations  0.79 us (1%)
    pallas_call x1, Pallas kernels, per_device(): pl.pallas_call(local_kernel, grid=(PLANE,), in_specs=[tall] * 2 + [table]...  13.7 us
    ppermute x9, starting transfers between devices, swap(): return lax.ppermute(x, 'ctx', [(i, i ^ bits) for i in range(count)])  12.4 us
    ppermute x9, waiting for transfers between devices, swap(): return lax.ppermute(x, 'ctx', [(i, i ^ bits) for i in range(count)])  9.7 us
    unnamed x32, local copies, waits for them, and re-layouts  6.53 us
    pallas_call x1, Pallas kernels, per_device(): pl.pallas_call(outputs_kernel, grid_spec=pltpu.PrefetchScalarGridSpec(num...  6.04 us
    pallas_call x1, Pallas kernels, per_device(): pl.pallas_call(states_kernel, grid_spec=pltpu.PrefetchScalarGridSpec(num_...  5.72 us
    pallas_call x1, Pallas kernels, per_device(): pl.pallas_call(functools.partial(line_kernel, length), grid_spec=pltpu.Pr...  3.36 us
    pallas_call x1, Pallas kernels, per_device(): pl.pallas_call(functools.partial(plane_kernel, length), grid_spec=pltpu.P...  2.79 us
  transfers between devices with their start and end apart: 10, of which 6 were waited for; matrix products, arithmetic and copies ran while one was open for 2% of the time, Pallas kernels for 31%

profile of v1, /device:TPU:0, one launch (start us, length us, event | category | flops | bytes accessed | tf_op | source)
XLA Modules:
  0.0 63.6 jit_solution(10769244979142808846)
XLA Ops:
  0.7 0.7 %copy-done.12 = f32[64,16]{0,1:T(8,128)S(1)} copy-done((f32[64,16]{0,1:T(8,128)S(1)}, f32[64,16]{0,1:T(8,128)}, u32[]{:S(2)}) %copy-start.12) | copy-done | bytes 4120
  1.3 0.7 %copy.18.dec_ref = f32[64,16]{1,0:T(8,128)} copy(f32[64,16]{0,1:T(8,128)S(1)} %copy-done.12) | data formatting | bytes 8192 | tf_op args[5]
  2.6 5.7 %states.1 = (bf16[64,32,128]{2,1,0:T(8,128)(2,1)}, bf16[64,32,128]{2,1,0:T(8,128)(2,1)}, bf16[8,32,128]{2,1,0:T(8,128)(2,1)}, bf16[8,32,128]{2,1,0:T(8,128)(2,1)...) custom-call(s32[2]{0:T(128)} %pad_add_fusion.place, bf16[32,64,128]{2,1,0:T(8,128)(2,1)} %bitcast.9, ...), custom_call_target="tpu_custom_call" | custom-call | flops 1000000000 | bytes 3000000 | tf_op jit(solution)/shard_map/states/pallas_call | solution.py:310
  8.3 3.0 %collective-permute-start = (bf16[8,32,128]{2,1,0:T(8,128)(2,1)}, bf16[8,32,128]{2,1,0:T(8,128)(2,1)S(1)}, u32[]{:S(2)}, u32[]{:S(2)}) collective-permute-start(bf16[8,32,128]{2,1,0:T(8,128)(2,1)} %get-tuple-element.26), channel_id=1, source_target_pairs={{0,2},{2,0},{4,6},{6,4},{8,10},{10,8},{12,14},{14,12},{16,18},{18,... | collective-permute-start | bytes 196616 | tf_op jit(solution)/shard_map/ppermute | solution.py:326
  11.4 1.5 %collective-permute-start.1 = (bf16[8,32,128]{2,1,0:T(8,128)(2,1)}, bf16[8,32,128]{2,1,0:T(8,128)(2,1)S(1)}, u32[]{:S(2)}, u32[]{:S(2)}) collective-permute-start(bf16[8,32,128]{2,1,0:T(8,128)(2,1)} %get-tuple-element.27), channel_id=1, source_target_pairs={{0,4},{2,6},{4,0},{6,2},{8,12},{10,14},{12,8},{14,10},{16,20},{18,... | collective-permute-start | bytes 196616 | tf_op jit(solution)/shard_map/ppermute | solution.py:326
  13.6 0.7 %copy.20.res_ref = f32[64,16]{1,0:T(8,128)} copy(f32[64,16]{0,1:T(8,128)S(1)} %copy-done.13) | data formatting | bytes 8192 | tf_op args[4]
  14.3 0.7 %tile.12.rate_ref = f32[32,128]{1,0:T(8,128)} reshape(f32[32,4,32]{2,1,0:T(4,128)S(1)} %tile.11) | data formatting | bytes 32768 | tf_op jit(solution)/shard_map/tile | solution.py:304
  15.0 13.7 %local.1 = (f32[4,512,128]{2,1,0:T(8,128)}, f32[4,512,128]{2,1,0:T(8,128)}, f32[32,128]{1,0:T(8,128)}) custom-call(bf16[64,32,128]{2,1,0:T(8,128)(2,1)} %get-tuple-element.21.gx_ref, bf16[64,32,128]{2,1,0:T(8,128)(2,1)} %get-tuple-element.22.cx_ref, f32[64,16]{1,0:T(8,128)} %copy.18.dec_ref, f32[64,16]{1,0:T(8,128)} %copy.20.res_ref), custom_call_target="tpu_custom_call" | custom-call | flops 1000000000 | bytes 4000000 | tf_op jit(solution)/shard_map/local/pallas_call | solution.py:333
  29.4 2.8 %plane.1.refs_4_ = bf16[288,128]{1,0:T(8,128)(2,1)} custom-call(s32[2]{0:T(128)} %pad_add_fusion.place, f32[32,128]{1,0:T(8,128)} %tile.12.rate_ref, bf16[8,32,128]{2,1,0:T(8,128)(2,1)} %get-tuple-element.25.refs_0_, bf16[8,32,128]{2,1,0:T(8,128)(2,1)} %copy-done.3, bf16[8,32,128]{2,1,0:T(8,128)(2,1)} %copy-done.4, bf16[8,32,128]{2,1,0:T(8,128)(2,1)} %copy-done.5, ...), custom_call_target="tpu_custom_call" | custom-call | tf_op jit(solution)/shard_map/plane/pallas_call | solution.py:350
  32.2 3.6 %collective-permute-start.5 = (bf16[288,128]{1,0:T(8,128)(2,1)}, bf16[288,128]{1,0:T(8,128)(2,1)S(1)}, u32[]{:S(2)}, u32[]{:S(2)}) collective-permute-start(bf16[288,128]{1,0:T(8,128)(2,1)} %plane.1.refs_4_), channel_id=1, source_target_pairs={{0,24},{2,26},{4,28},{6,30},{8,16},{10,18},{12,20},{14,22},{16,8},... | collective-permute-start | bytes 221192 | tf_op jit(solution)/shard_map/ppermute | solution.py:326
  35.8 0.8 %collective-permute-start.3 = (bf16[288,128]{1,0:T(8,128)(2,1)}, bf16[288,128]{1,0:T(8,128)(2,1)S(1)}, u32[]{:S(2)}, u32[]{:S(2)}) collective-permute-start(bf16[288,128]{1,0:T(8,128)(2,1)} %plane.1.refs_4_), channel_id=1, source_target_pairs={{0,8},{2,10},{4,12},{6,14},{8,0},{10,2},{12,4},{14,6},{16,24},{18,... | collective-permute-start | bytes 221192 | tf_op jit(solution)/shard_map/ppermute | solution.py:326
  36.6 2.6 %collective-permute-done.5.refs_7_ = bf16[288,128]{1,0:T(8,128)(2,1)S(1)} collective-permute-done((bf16[288,128]{1,0:T(8,128)(2,1)}, bf16[288,128]{1,0:T(8,128)(2,1)S(1)}, u32[]{:S(2)}, u32[]{:S(2)}) %collective-permute-start.5) | collective-permute-done | bytes 73760 | tf_op jit(solution)/shard_map/ppermute | solution.py:326
  39.2 2.5 %collective-permute-done.4.refs_6_ = bf16[288,128]{1,0:T(8,128)(2,1)S(1)} collective-permute-done((bf16[288,128]{1,0:T(8,128)(2,1)}, bf16[288,128]{1,0:T(8,128)(2,1)S(1)}, u32[]{:S(2)}, u32[]{:S(2)}) %collective-permute-start.4) | collective-permute-done | bytes 73760 | tf_op jit(solution)/shard_map/ppermute | solution.py:326
  42.3 0.6 copy-done.11
  43.0 3.4 %line.1 = (bf16[160,128]{1,0:T(8,128)(2,1)}, bf16[160,128]{1,0:T(8,128)(2,1)}, bf16[160,128]{1,0:T(8,128)(2,1)}, bf16[160,128]{1,0:T(8,128)(2,1)}) custom-call(s32[2]{0:T(128)} %pad_add_fusion.place, f32[32,128]{1,0:T(8,128)} %tile.12.rate_ref, bf16[8,32,128]{2,1,0:T(8,128)(2,1)} %get-tuple-element.25.refs_0_, bf16[8,32,128]{2,1,0:T(8,128)(2,1)} %copy-done.3, ...), custom_call_target="tpu_custom_call" | custom-call | tf_op jit(solution)/shard_map/line/pallas_call | solution.py:364
  46.3 1.3 %collective-permute-start.6 = (bf16[160,128]{1,0:T(8,128)(2,1)}, bf16[160,128]{1,0:T(8,128)(2,1)S(1)}, u32[]{:S(2)}, u32[]{:S(2)}) collective-permute-start(bf16[160,128]{1,0:T(8,128)(2,1)} %get-tuple-element.31), channel_id=1, source_target_pairs={{0,2},{2,0},{4,6},{6,4},{8,10},{10,8},{12,14},{14,12},{16,18},{18,... | collective-permute-start | bytes 122888 | tf_op jit(solution)/shard_map/ppermute | solution.py:326
  47.7 1.5 %collective-permute-start.7 = (bf16[160,128]{1,0:T(8,128)(2,1)}, bf16[160,128]{1,0:T(8,128)(2,1)S(1)}, u32[]{:S(2)}, u32[]{:S(2)}) collective-permute-start(bf16[160,128]{1,0:T(8,128)(2,1)} %get-tuple-element.32), channel_id=1, source_target_pairs={{0,4},{2,6},{4,0},{6,2},{8,12},{10,14},{12,8},{14,10},{16,20},{18,... | collective-permute-start | bytes 122888 | tf_op jit(solution)/shard_map/ppermute | solution.py:326
  49.8 0.7 %collective-permute-done.6.refs_1_ = bf16[160,128]{1,0:T(8,128)(2,1)S(1)} collective-permute-done((bf16[160,128]{1,0:T(8,128)(2,1)}, bf16[160,128]{1,0:T(8,128)(2,1)S(1)}, u32[]{:S(2)}, u32[]{:S(2)}) %collective-permute-start.6) | collective-permute-done | bytes 40992 | tf_op jit(solution)/shard_map/ppermute | solution.py:326
  50.5 1.4 %collective-permute-done.7.refs_2_ = bf16[160,128]{1,0:T(8,128)(2,1)S(1)} collective-permute-done((bf16[160,128]{1,0:T(8,128)(2,1)}, bf16[160,128]{1,0:T(8,128)(2,1)S(1)}, u32[]{:S(2)}, u32[]{:S(2)}) %collective-permute-start.7) | collective-permute-done | bytes 40992 | tf_op jit(solution)/shard_map/ppermute | solution.py:326
  51.9 2.4 %collective-permute-done.8.refs_3_ = bf16[160,128]{1,0:T(8,128)(2,1)S(1)} collective-permute-done((bf16[160,128]{1,0:T(8,128)(2,1)}, bf16[160,128]{1,0:T(8,128)(2,1)S(1)}, u32[]{:S(2)}, u32[]{:S(2)}) %collective-permute-start.8) | collective-permute-done | bytes 40992 | tf_op jit(solution)/shard_map/ppermute | solution.py:326
  54.3 0.9 %add_add_fusion = f32[32,64]{1,0:T(8,128)S(1)} fusion(bf16[160,128]{1,0:T(8,128)(2,1)S(1)} %collective-permute-done.8.refs_3_, bf16[160,128]{1,0:T(8,128)(2,1)S(1)} %collective-permute-done.7.refs_2_, bf16[160,128]{1,0:T(8,128)(2,1)S(1)} %collective-permute-done.6.refs_1_, bf16[160,128]{1,0:T(8,128)(2,1)} %get-tuple-element.30.refs_0_), kind=kLoop, calls=%fused_computation.2 | loop fusion | flops 30720 | bytes 40960 | tf_op jit(solution)/shard_map/add | solution.py:380
  55.3 6.0 %outputs.1 = (bf16[32,64,128]{2,1,0:T(8,128)(2,1)}, bf16[32,64,128]{2,1,0:T(8,128)(2,1)}, bf16[32,64,128]{2,1,0:T(8,128)(2,1)}) custom-call(s32[2]{0:T(128)} %pad_add_fusion.place, bf16[32,64,128]{2,1,0:T(8,128)(2,1)} %bitcast.10, bf16[32,64,128]{2,1,0:T(8,128)(2,1)} %bitcast.12, bf16[32,64,128]{2,1,0:T(8,128)(2,1)} %bitcast.14, ...), custom_call_target="tpu_custom_call" | custom-call | flops 1000000000 | bytes 5000000 | tf_op jit(solution)/shard_map/outputs/pallas_call | solution.py:390
  62.2 0.7 %copy.27 = f32[64,16]{0,1:T(8,128)} copy(f32[64,16]{1,0:T(8,128)S(1)} %multiply_multiply_fusion) | data formatting | bytes 8192
  62.9 0.7 %copy.26 = f32[64,16]{0,1:T(8,128)} copy(f32[64,16]{1,0:T(8,128)S(1)} %div.20) | data formatting | bytes 8192
  (43 shorter events, 4.2 us)
Async XLA Ops:
  0.6 0.7 %copy-start.12 = (f32[64,16]{0,1:T(8,128)S(1)}, f32[64,16]{0,1:T(8,128)}, u32[]{:S(2)}) copy-start(f32[64,16]{0,1:T(8,128)} %param.11) | copy-start | bytes 12292
  2.6 10.3 %copy-start = (f32[64,16]{1,0:T(8,128)S(1)}, f32[64,16]{1,0:T(8,128)}, u32[]{:S(2)}) copy-start(f32[64,16]{1,0:T(8,128)} %copy.18.dec_ref) | copy-start | bytes 12292
  8.3 20.4 %collective-permute-start = (bf16[8,32,128]{2,1,0:T(8,128)(2,1)}, bf16[8,32,128]{2,1,0:T(8,128)(2,1)S(1)}, u32[]{:S(2)}, u32[]{:S(2)}) collective-permute-start(bf16[8,32,128]{2,1,0:T(8,128)(2,1)} %get-tuple-element.26), channel_id=1, source_target_pairs={{0,2},{2,0},{4,6},{6,4},{8,10},{10,8},{12,14},{14,12},{16,18},{18,... | collective-permute-start | bytes 196616 | tf_op jit(solution)/shard_map/ppermute | solution.py:326
  11.4 17.3 %collective-permute-start.1 = (bf16[8,32,128]{2,1,0:T(8,128)(2,1)}, bf16[8,32,128]{2,1,0:T(8,128)(2,1)S(1)}, u32[]{:S(2)}, u32[]{:S(2)}) collective-permute-start(bf16[8,32,128]{2,1,0:T(8,128)(2,1)} %get-tuple-element.27), channel_id=1, source_target_pairs={{0,4},{2,6},{4,0},{6,2},{8,12},{10,14},{12,8},{14,10},{16,20},{18,... | collective-permute-start | bytes 196616 | tf_op jit(solution)/shard_map/ppermute | solution.py:326
  12.9 0.7 %copy-start.13 = (f32[64,16]{0,1:T(8,128)S(1)}, f32[64,16]{0,1:T(8,128)}, u32[]{:S(2)}) copy-start(f32[64,16]{0,1:T(8,128)} %param.10) | copy-start | bytes 12292
  12.9 15.8 %collective-permute-start.2 = (bf16[8,32,128]{2,1,0:T(8,128)(2,1)}, bf16[8,32,128]{2,1,0:T(8,128)(2,1)S(1)}, u32[]{:S(2)}, u32[]{:S(2)}) collective-permute-start(bf16[8,32,128]{2,1,0:T(8,128)(2,1)} %get-tuple-element.28), channel_id=1, source_target_pairs={{0,6},{2,4},{4,2},{6,0},{8,14},{10,12},{12,10},{14,8},{16,22},{18,... | collective-permute-start | bytes 196616 | tf_op jit(solution)/shard_map/ppermute | solution.py:326
  28.7 0.6 copy-start.3
  28.7 0.6 copy-start.4
  28.7 0.6 %copy-start.5 = (bf16[8,32,128]{2,1,0:T(8,128)(2,1)}, bf16[8,32,128]{2,1,0:T(8,128)(2,1)S(1)}, u32[]{:S(2)}) copy-start(bf16[8,32,128]{2,1,0:T(8,128)(2,1)S(1)} %collective-permute-done.2.refs_3_) | copy-start | bytes 196612
  32.2 7.0 %collective-permute-start.5 = (bf16[288,128]{1,0:T(8,128)(2,1)}, bf16[288,128]{1,0:T(8,128)(2,1)S(1)}, u32[]{:S(2)}, u32[]{:S(2)}) collective-permute-start(bf16[288,128]{1,0:T(8,128)(2,1)} %plane.1.refs_4_), channel_id=1, source_target_pairs={{0,24},{2,26},{4,28},{6,30},{8,16},{10,18},{12,20},{14,22},{16,8},... | collective-permute-start | bytes 221192 | tf_op jit(solution)/shard_map/ppermute | solution.py:326
  35.8 5.9 %collective-permute-start.4 = (bf16[288,128]{1,0:T(8,128)(2,1)}, bf16[288,128]{1,0:T(8,128)(2,1)S(1)}, u32[]{:S(2)}, u32[]{:S(2)}) collective-permute-start(bf16[288,128]{1,0:T(8,128)(2,1)} %plane.1.refs_4_), channel_id=1, source_target_pairs={{0,16},{2,18},{4,20},{6,22},{8,24},{10,26},{12,28},{14,30},{16,0},... | collective-permute-start | bytes 221192 | tf_op jit(solution)/shard_map/ppermute | solution.py:326
  35.8 6.0 %collective-permute-start.3 = (bf16[288,128]{1,0:T(8,128)(2,1)}, bf16[288,128]{1,0:T(8,128)(2,1)S(1)}, u32[]{:S(2)}, u32[]{:S(2)}) collective-permute-start(bf16[288,128]{1,0:T(8,128)(2,1)} %plane.1.refs_4_), channel_id=1, source_target_pairs={{0,8},{2,10},{4,12},{6,14},{8,0},{10,2},{12,4},{14,6},{16,24},{18,... | collective-permute-start | bytes 221192 | tf_op jit(solution)/shard_map/ppermute | solution.py:326
  39.2 2.6 %copy-start.9 = (bf16[288,128]{1,0:T(8,128)(2,1)}, bf16[288,128]{1,0:T(8,128)(2,1)S(1)}, u32[]{:S(2)}) copy-start(bf16[288,128]{1,0:T(8,128)(2,1)S(1)} %collective-permute-done.5.refs_7_) | copy-start | bytes 221188
  41.7 0.6 copy-start.10
  42.3 0.6 copy-start.11
  46.3 4.2 %collective-permute-start.6 = (bf16[160,128]{1,0:T(8,128)(2,1)}, bf16[160,128]{1,0:T(8,128)(2,1)S(1)}, u32[]{:S(2)}, u32[]{:S(2)}) collective-permute-start(bf16[160,128]{1,0:T(8,128)(2,1)} %get-tuple-element.31), channel_id=1, source_target_pairs={{0,2},{2,0},{4,6},{6,4},{8,10},{10,8},{12,14},{14,12},{16,18},{18,... | collective-permute-start | bytes 122888 | tf_op jit(solution)/shard_map/ppermute | solution.py:326
  47.7 4.2 %collective-permute-start.7 = (bf16[160,128]{1,0:T(8,128)(2,1)}, bf16[160,128]{1,0:T(8,128)(2,1)S(1)}, u32[]{:S(2)}, u32[]{:S(2)}) collective-permute-start(bf16[160,128]{1,0:T(8,128)(2,1)} %get-tuple-element.32), channel_id=1, source_target_pairs={{0,4},{2,6},{4,0},{6,2},{8,12},{10,14},{12,8},{14,10},{16,20},{18,... | collective-permute-start | bytes 122888 | tf_op jit(solution)/shard_map/ppermute | solution.py:326
  49.2 5.1 %collective-permute-start.8 = (bf16[160,128]{1,0:T(8,128)(2,1)}, bf16[160,128]{1,0:T(8,128)(2,1)S(1)}, u32[]{:S(2)}, u32[]{:S(2)}) collective-permute-start(bf16[160,128]{1,0:T(8,128)(2,1)} %get-tuple-element.33), channel_id=1, source_target_pairs={{0,6},{2,4},{4,2},{6,0},{8,14},{10,12},{12,10},{14,8},{16,22},{18,... | collective-permute-start | bytes 122888 | tf_op jit(solution)/shard_map/ppermute | solution.py:326
  50.5 4.6 %copy-start.6 = (bf16[160,128]{1,0:T(8,128)(2,1)}, bf16[160,128]{1,0:T(8,128)(2,1)S(1)}, u32[]{:S(2)}) copy-start(bf16[160,128]{1,0:T(8,128)(2,1)S(1)} %collective-permute-done.6.refs_1_) | copy-start | bytes 122884
  51.9 3.3 %copy-start.7 = (bf16[160,128]{1,0:T(8,128)(2,1)}, bf16[160,128]{1,0:T(8,128)(2,1)S(1)}, u32[]{:S(2)}) copy-start(bf16[160,128]{1,0:T(8,128)(2,1)S(1)} %collective-permute-done.7.refs_2_) | copy-start | bytes 122884
  54.3 1.0 %copy-start.8 = (bf16[160,128]{1,0:T(8,128)(2,1)}, bf16[160,128]{1,0:T(8,128)(2,1)S(1)}, u32[]{:S(2)}) copy-start(bf16[160,128]{1,0:T(8,128)(2,1)S(1)} %collective-permute-done.8.refs_3_) | copy-start | bytes 122884
  55.2 6.1 %collective-permute-start.9 = (f32[32,64]{1,0:T(8,128)S(1)}, f32[32,64]{1,0:T(8,128)S(1)}, u32[]{:S(2)}, u32[]{:S(2)}) collective-permute-start(f32[32,64]{1,0:T(8,128)S(1)} %add_add_fusion), channel_id=1, source_target_pairs={{0,1},{1,0},{2,3},{3,2},{4,5},{5,4},{6,7},{7,6},{8,9},{9,8},{10,11... | collective-permute-start | bytes 24584 | tf_op jit(solution)/shard_map/ppermute | solution.py:386
  61.3 0.8 %copy-start.2 = (f32[64,16]{1,0:T(8,128)S(1)}, f32[64,16]{1,0:T(8,128)}, u32[]{:S(2)}) copy-start(f32[64,16]{1,0:T(8,128)} %copy.20.res_ref) | copy-start | bytes 12292
  61.4 0.8 %copy-start.1 = (f32[64,16]{1,0:T(8,128)S(1)}, f32[64,16]{1,0:T(8,128)}, u32[]{:S(2)}) copy-start(f32[64,16]{1,0:T(8,128)} %copy.18.dec_ref) | copy-start | bytes 12292

commit v2 on v1

v2 whole, which is shorter than its diff:
```python
import functools
import math

import jax
import jax.numpy as jnp
from jax import lax
from jax.experimental import pallas as pl
from jax.experimental.pallas import tpu as pltpu
from jax.sharding import PartitionSpec as P

F32 = jnp.float32
BF16 = jnp.bfloat16
PLANE = 4
NT = (((1,), (1,)), ((), ()))
NN = (((1,), (0,)), ((), ()))
TN = (((0,), (0,)), ((), ()))


def dot(a, b, dims):
    return lax.dot_general(a, b, dims, preferred_element_type=F32)


def product(a, b):
    return (a.astype(F32) * b.astype(F32)).astype(BF16)


def column(table, group):
    return jnp.sum(jnp.where(lane_iota(table.shape) == group, table, 0.0), axis=1, keepdims=True)


def mirror_of(length):
    total = lane_iota((length, length)) + lax.broadcasted_iota(jnp.int32, (length, length), 0)
    return jnp.where(total == length - 1, 1.0, 0.0).astype(BF16)


def places():
    me = lax.axis_index("ctx")
    return lax.rem(me, PLANE), lax.div(me, PLANE)


def lane_iota(shape):
    return lax.broadcasted_iota(jnp.int32, shape, len(shape) - 1)


def states_kernel(k_hbm, v_hbm, g_hbm, q_hbm, dec_ref, gx_ref, cx_ref, rate_ref, *rest):
    outs, (bufs, sems, wx_ref, wc_ref, gs, cs) = rest[:PLANE], rest[PLANE:]
    place, _ = places()
    _, rows, part, length = bufs.shape[1:]
    modes, groups = dec_ref.shape
    pairs = part // 2
    flat = rows * part
    sources = (k_hbm, v_hbm, g_hbm, q_hbm)

    def copy(which, quarter):
        return pltpu.make_async_copy(
            sources[which].at[:, pl.ds(quarter * part, part), :],
            bufs.at[which, quarter],
            sems.at[which, quarter],
        )

    for quarter in range(PLANE):
        for which in range(4):
            copy(which, quarter).start()
    dec = dec_ref[...]
    ahead = lane_iota((modes, length)).astype(F32)
    behind = float(length) - ahead
    wide = (modes, 8 * modes)
    target = lane_iota(wide) % (2 * modes) - lax.broadcasted_iota(jnp.int32, wide, 0)

    def weights(index, _):
        rates = jnp.zeros(wide, F32)
        for side in range(2):
            group = 2 * index + side
            rate = column(dec, group)
            fwd = jnp.exp(-rate * behind)
            bwd = jnp.exp(-rate * (behind - 1.0))
            wx_ref[group, 0] = fwd.astype(BF16)
            wx_ref[group, 1] = (behind * fwd).astype(BF16)
            wc_ref[group, 0] = bwd.astype(BF16)
            wc_ref[group, 1] = ((behind - 1.0) * bwd).astype(BF16)
            rates += jnp.where(target == side * modes, rate, 0.0)
        rate_ref[pl.ds(index, 1), :] = jnp.sum(rates, axis=0, keepdims=True)
        return 0

    lax.fori_loop(0, groups // 2, weights, 0, unroll=8)
    mirror = mirror_of(length)
    zero = jnp.zeros((modes, length), BF16)

    def quarter_step(quarter, _):
        for which in range(4):
            copy(which, quarter).wait()
        gs[...] = product(bufs[0, quarter], bufs[1, quarter]).astype(F32).reshape(flat, length)
        cs[...] = dot(
            product(bufs[2, quarter], bufs[3, quarter]).reshape(flat, length), mirror, NN
        )
        results = []
        for pair in range(pairs):
            left, right = [], []
            for side in range(2):
                local = 2 * pair + side
                group = quarter * part + local
                x = gs[pl.ds(local, rows, stride=part), :].astype(BF16)
                c = cs[pl.ds(local, rows, stride=part), :].astype(BF16)
                gx_ref[group] = x
                cx_ref[group] = c
                wx, wc = [zero] * 8, [zero] * 8
                wx[side], wx[4 + side] = wx_ref[group, 0], wx_ref[group, 1]
                wc[2 + side], wc[6 + side] = wc_ref[group, 0], wc_ref[group, 1]
                left += [x, c]
                right += [jnp.concatenate(wx, axis=0), jnp.concatenate(wc, axis=0)]
            results.append(
                dot(jnp.concatenate(left, axis=1), jnp.concatenate(right, axis=1), NT).astype(BF16)
            )
        for index in range(PLANE):

            @pl.when((place ^ quarter) == index)
            def _():
                for pair in range(pairs):
                    outs[index][pair] = results[pair]

        return 0

    lax.fori_loop(0, PLANE, quarter_step, 0)


def sums_kernel(gx_ref, cx_ref, dec_ref, sums_ref, corr_ref):
    groups, rows, length = gx_ref.shape
    modes = dec_ref.shape[0]
    part = groups // PLANE
    paired = (
        lane_iota((length, length)) + lax.broadcasted_iota(jnp.int32, (length, length), 0) < length
    )

    def correlate(quarter, _):
        for local in range(part):
            group = quarter * part + local
            prods = jnp.where(paired, dot(gx_ref[group], cx_ref[group], TN), 0.0)
            prods = pltpu.roll(prods, 0, 1, stride=1, stride_axis=0)
            corr_ref[pl.ds(group, 1), :] = jnp.sum(prods, axis=0, keepdims=True)
        return 0

    lax.fori_loop(0, PLANE, correlate, 0)
    dec = dec_ref[...]
    lag = float(length - 1) - lane_iota((modes, length)).astype(F32)
    lane = lane_iota((modes, sums_ref.shape[1]))

    def contract(quarter, carry):
        plain, moment = carry
        for local in range(part):
            group = quarter * part + local
            terms = jnp.exp(-column(dec, group) * lag) * corr_ref[pl.ds(group, 1), :]
            plain = jnp.where(lane == group, jnp.sum(terms, axis=1, keepdims=True), plain)
            moment = jnp.where(lane == group, jnp.sum(terms * lag, axis=1, keepdims=True), moment)
        return plain, moment

    zero = jnp.zeros(lane.shape, F32)
    plain, moment = lax.fori_loop(0, PLANE, contract, (zero, zero))
    sums_ref[:modes] = plain
    sums_ref[modes:] = moment


def local_kernel(gx_ref, cx_ref, dec_ref, res_ref, conv_ref, ig_ref, wl_ref, wr_ref, toep_ref):
    groups, rows, length = gx_ref.shape
    modes = dec_ref.shape[0]
    part = groups // PLANE
    dec, res = dec_ref[...], res_ref[...]
    ahead = lane_iota((modes, length)).astype(F32)
    later = lane_iota((length, length)) >= lax.broadcasted_iota(jnp.int32, (length, length), 0)

    def quarter_step(quarter, _):
        for local in range(part):
            group = quarter * part + local
            rate = column(dec, group)
            taps = column(res, group) * jnp.exp(-rate * ahead)
            wl_ref[group] = taps.astype(BF16)
            wr_ref[group] = (taps * jnp.exp(-rate)).astype(BF16)
            taps = jnp.sum(taps, axis=0, keepdims=True)
            toep = pltpu.roll(
                jnp.broadcast_to(taps, (length, length)), 0, 1, stride=1, stride_axis=0
            )
            toep_ref[local] = jnp.where(later, toep, 0.0).astype(BF16)
        for local in range(part):
            group = quarter * part + local
            both = dot(
                jnp.concatenate([gx_ref[group], cx_ref[group]], axis=0), toep_ref[local], NN
            )
            conv_ref[quarter, pl.ds(local, rows, stride=part), :] = both[:rows]
            ig_ref[quarter, pl.ds(local, rows, stride=part), :] = both[rows:]
        return 0

    lax.fori_loop(0, PLANE, quarter_step, 0)


def split_pair(x, half):
    head = x.astype(BF16).astype(F32)
    tail = (x - head).astype(BF16).astype(F32)
    low = lane_iota(x.shape) < half
    return jnp.where(low, head, pltpu.roll(jnp.where(low, tail, 0.0), half, x.ndim - 1)).astype(BF16)


def join_pair(x, half):
    x = x.astype(F32)
    low = lane_iota(x.shape) < half
    return jnp.where(low, x + pltpu.roll(x, half, x.ndim - 1), 0.0)


def in_order(arrays, place):
    arrays, bit = list(arrays), 1
    while bit < len(arrays):
        swap = (place & bit) != 0
        new = list(arrays)
        for i in range(len(arrays)):
            new[i] = jnp.where(swap, arrays[i ^ bit], arrays[i])
        arrays, bit = new, 2 * bit
    return arrays


def advance(state, decay, gap, half, axis):
    lane = lane_iota(state.shape)
    shifted = pltpu.roll(state, half, axis)
    return decay * (state + jnp.where(lane >= half, gap * shifted, 0.0))


def pair_terms(state, x, modes):
    lanes = x.shape[-1]
    axis = x.ndim - 1
    plain = jnp.sum(state * pltpu.roll(x, lanes - 2 * modes, axis), axis=1)
    first = jnp.sum(state * pltpu.roll(x, lanes - 6 * modes, axis), axis=1)
    second = jnp.sum(state * pltpu.roll(x, 2 * modes, axis), axis=1)
    lane = lane_iota(plain.shape)
    second = pltpu.roll(second, lanes - 2 * modes, 1)
    first = pltpu.roll(first, 2 * modes, 1)
    return jnp.where(
        lane < 2 * modes, plain, jnp.where(lane < 4 * modes, first + second, 0.0)
    )


def scan_blocks(blocks, start, rate, gap, modes):
    half = 4 * modes
    axis = blocks[0].ndim - 1
    lane = lane_iota(blocks[0].shape)
    forward = (lane % half) < 2 * modes
    decay = jnp.exp(-rate * gap)
    state, states = start, []
    for i in range(len(blocks)):
        states.append(state)
        block = jnp.where(forward, blocks[i], blocks[len(blocks) - 1 - i])
        state = advance(state, decay, gap, half, axis) + block
    return states, state


def all_pair_terms(states, blocks, modes):
    lane = lane_iota(blocks[0].shape)
    total = None
    for i in range(len(blocks)):
        term = pair_terms(states[i], blocks[i], modes)
        total = term if total is None else total + term
    return total


def spread(terms, place, acc, modes):
    pairs = terms.shape[0]
    shape = (pairs, acc.shape[1])
    group = lane_iota(shape) - 2 * pairs * place
    row = lax.broadcasted_iota(jnp.int32, shape, 0)
    for side in range(2):
        chosen = jnp.where(group == 2 * row + side, 1.0, 0.0)
        turned = lax.dot_general(
            terms, chosen, TN, precision=lax.Precision.HIGHEST, preferred_element_type=F32
        )
        acc[:modes] += turned[side * modes : (side + 1) * modes]
        acc[modes:] += turned[(2 + side) * modes : (3 + side) * modes]


def plane_kernel(length, rate_ref, *refs):
    *msgs, sums_ref, out_ref, acc = refs
    place, _ = places()
    pairs, rows, lanes = msgs[0].shape
    modes = lanes // 8
    flat = pairs * rows
    blocks = in_order([m[...].astype(F32) for m in msgs], place)
    rate = rate_ref[pl.ds(pl.multiple_of(place * pairs, pairs), pairs), :].reshape(pairs, 1, lanes)
    states, last = scan_blocks(blocks, jnp.zeros_like(blocks[0]), rate, float(length), modes)
    out_ref[:flat] = last.astype(BF16).reshape(flat, lanes)
    acc[...] = sums_ref[...]
    spread(all_pair_terms(states, blocks, modes), place, acc, modes)
    out_ref[flat:] = split_pair(acc[...], lanes // 2)


def line_kernel(length, rate_ref, *refs):
    count = len(refs) - 2 * PLANE - 1
    msgs, lines = refs[:PLANE], refs[PLANE : PLANE + count]
    outs, acc = refs[PLANE + count : -1], refs[-1]
    place, level = places()
    pairs, rows, lanes = msgs[0].shape
    modes = lanes // 8
    flat = pairs * rows
    rate = rate_ref[pl.ds(pl.multiple_of(place * pairs, pairs), pairs), :].reshape(pairs, 1, lanes)
    planes = in_order([r[:flat].astype(F32).reshape(pairs, rows, lanes) for r in lines], level)
    gap = float(PLANE * length)
    states, _ = scan_blocks(planes, jnp.zeros_like(planes[0]), rate, gap, modes)
    lane = lane_iota(planes[0].shape)
    forward = (lane % (4 * modes)) < 2 * modes
    incoming = jnp.zeros_like(planes[0])
    for i in range(count):
        here = jnp.where(forward, i, count - 1 - i) == level
        incoming = incoming + jnp.where(here, states[i], 0.0)
    total = join_pair(lines[0][flat:], lanes // 2)
    for r in lines[1:]:
        total = total + join_pair(r[flat:], lanes // 2)
    acc[...] = total
    spread(all_pair_terms(states, planes, modes), place, acc, modes)
    sums = split_pair(acc[...], lanes // 2)
    blocks = in_order([m[...].astype(F32) for m in msgs], place)
    states, _ = scan_blocks(blocks, incoming, rate, float(length), modes)
    found = [jnp.where(forward, states[i], states[PLANE - 1 - i]) for i in range(PLANE)]
    found = in_order(found, place)
    low = lane[: pairs // 2] < 4 * modes
    for i in range(PLANE):
        packed = jnp.where(
            low, found[i][: pairs // 2], pltpu.roll(found[i][pairs // 2 :], 4 * modes, 2)
        )
        outs[i][: flat // 2] = packed.astype(BF16).reshape(flat // 2, lanes)
        outs[i][flat // 2 :] = sums


def outputs_kernel(k_hbm, v_hbm, g_hbm, conv_ref, ig_ref, wl_ref, wr_ref, *refs):
    incoming, results = refs[:PLANE], refs[PLANE : PLANE + 3]
    bufs, sems, outs, out_sems, cs, gs = refs[PLANE + 3 :]
    place, _ = places()
    _, rows, part, length = bufs.shape[1:]
    modes = wl_ref.shape[1]
    pairs = part // 2
    flat = pairs * rows // 2
    sources = (k_hbm, v_hbm, g_hbm)

    def copy(which, quarter):
        return pltpu.make_async_copy(
            sources[which].at[:, pl.ds(quarter * part, part), :],
            bufs.at[which, quarter],
            sems.at[which, quarter],
        )

    def store(which, quarter):
        return pltpu.make_async_copy(
            outs.at[which, quarter],
            results[which].at[:, pl.ds(quarter * part, part), :],
            out_sems.at[which, quarter],
        )

    for quarter in range(PLANE):
        for which in range(3):
            copy(which, quarter).start()
    mirror = mirror_of(length)
    zero = jnp.zeros((modes, length), BF16)

    def quarter_step(quarter, _):
        index = place ^ quarter
        state = incoming[0][:flat]
        for i in range(1, PLANE):
            state = jnp.where(index == i, incoming[i][:flat], state)
        for local in range(part):
            group = quarter * part + local
            pair, side = local // 2, local % 2
            base = (4 if pair >= pairs // 2 else 0) + side
            left, right = [zero] * 8, [zero] * 8
            left[base], right[base + 2] = wl_ref[group], wr_ref[group]
            quad = pair % (pairs // 2)
            both = dot(
                state[quad * rows : (quad + 1) * rows],
                jnp.concatenate(
                    [jnp.concatenate(left, axis=0), jnp.concatenate(right, axis=0)], axis=1
                ),
                NN,
            )
            cs[pl.ds(local, rows, stride=part), :] = both[:, :length]
            gs[pl.ds(local, rows, stride=part), :] = both[:, length:]
        shape = (rows, part, length)
        for which in range(3):
            copy(which, quarter).wait()
        conv = (cs[...] + conv_ref[quarter]).astype(BF16).reshape(shape)
        ig = (gs[...] + ig_ref[quarter]).astype(BF16)
        ig = dot(ig, mirror, NN).reshape(shape)
        outs[0, quarter] = product(bufs[2, quarter], conv)
        outs[1, quarter] = product(ig, bufs[1, quarter])
        outs[2, quarter] = product(ig, bufs[0, quarter])
        for which in range(3):
            store(which, quarter).start()
        return 0

    lax.fori_loop(0, PLANE, quarter_step, 0)
    for quarter in range(PLANE):
        for which in range(3):
            store(which, quarter).wait()


def per_device(queries, keys_in, values_in, grad_out, residue, decay_rate):
    chans, length = queries.shape
    groups, modes = residue.shape
    count = lax.axis_size("ctx")
    tp = lax.axis_size("tp")
    depth = count // PLANE
    rows = chans // groups
    part = groups // PLANE
    pairs = part // 2
    lanes = 8 * modes

    def cube(x):
        return x.reshape(rows, groups, length)

    query, key, value, grad = cube(queries), cube(keys_in), cube(values_in), cube(grad_out)
    decay, resid = decay_rate.T, residue.T
    vmem = pl.BlockSpec(memory_space=pltpu.VMEM)
    anywhere = pl.BlockSpec(memory_space=pl.ANY)

    def shaped(shape, dtype):
        return jax.ShapeDtypeStruct(shape, dtype)

    def call(kernel, name, in_specs, out_specs, out_shape, scratch, flops, size):
        return pl.pallas_call(
            kernel,
            in_specs=in_specs,
            out_specs=out_specs,
            out_shape=out_shape,
            scratch_shapes=scratch,
            cost_estimate=pl.CostEstimate(flops=flops, bytes_accessed=size, transcendentals=0),
            compiler_params=pltpu.CompilerParams(vmem_limit_bytes=16 * 2**20),
            name=name,
        )

    grouped = shaped((groups, rows, length), BF16)
    block = shaped((pairs, rows, lanes), BF16)
    plane_f32 = pltpu.VMEM((rows * part, length), F32)
    weight = pltpu.VMEM((groups, 2, modes, length), BF16)
    gx, cx, rates, *own = call(
        states_kernel,
        "states",
        [anywhere] * 4 + [vmem],
        [vmem] * (3 + PLANE),
        [grouped] * 2 + [shaped((groups // 2, lanes), F32)] + [block] * PLANE,
        [
            pltpu.VMEM((4, PLANE, rows, part, length), BF16),
            pltpu.SemaphoreType.DMA((4, PLANE)),
            weight,
            weight,
            plane_f32,
            plane_f32,
        ],
        10**9,
        4 * 10**6,
    )(key, value, grad, query, decay)

    def swap(x, bits):
        return lax.ppermute(x, "ctx", [(i, i ^ bits) for i in range(count)])

    near = [own[0]] + [swap(own[i], i) for i in range(1, PLANE)]
    sums = call(
        sums_kernel,
        "sums",
        [vmem] * 3,
        vmem,
        shaped((2 * modes, lanes), F32),
        [pltpu.VMEM((groups, length), F32)],
        10**9,
        4 * 10**6,
    )(gx, cx, decay)
    flat = pairs * rows
    plane = call(
        functools.partial(plane_kernel, length),
        "plane",
        [vmem] * (2 + PLANE),
        vmem,
        shaped((flat + 2 * modes, lanes), BF16),
        [pltpu.VMEM((2 * modes, lanes), F32)],
        10**7,
        10**6,
    )(rates, *near, sums)
    line = [plane] + [swap(plane, PLANE * i) for i in range(1, depth)]
    natural = shaped((PLANE, rows * part, length), F32)
    table = shaped((groups, modes, length), BF16)
    conv, ig, wl, wr = call(
        local_kernel,
        "local",
        [vmem] * 4,
        [vmem] * 4,
        [natural] * 2 + [table] * 2,
        [pltpu.VMEM((part, length, length), BF16)],
        10**9,
        4 * 10**6,
    )(gx, cx, decay, resid)
    back = call(
        functools.partial(line_kernel, length),
        "line",
        [vmem] * (1 + PLANE + depth),
        [vmem] * PLANE,
        [shaped((flat // 2 + 2 * modes, lanes), BF16)] * PLANE,
        [pltpu.VMEM((2 * modes, lanes), F32)],
        10**7,
        10**6,
    )(rates, *near, *line)
    back = [back[0]] + [swap(back[i], i) for i in range(1, PLANE)]

    total = sum(
        b[flat // 2 :, : lanes // 2].astype(F32) + b[flat // 2 :, lanes // 2 :].astype(F32)
        for b in back
    )
    bit = 1
    while bit < tp:
        total = total + lax.ppermute(total, "tp", [(i, i ^ bit) for i in range(tp)])
        bit *= 2

    outs = call(
        outputs_kernel,
        "outputs",
        [anywhere] * 3 + [vmem] * (4 + PLANE),
        [anywhere] * 3,
        [shaped((rows, groups, length), BF16)] * 3,
        [
            pltpu.VMEM((3, PLANE, rows, part, length), BF16),
            pltpu.SemaphoreType.DMA((3, PLANE)),
            pltpu.VMEM((3, PLANE, rows, part, length), BF16),
            pltpu.SemaphoreType.DMA((3, PLANE)),
            plane_f32,
            plane_f32,
        ],
        10**9,
        5 * 10**6,
    )(key, value, grad, conv, ig, wl, wr, *back)
    tokens = count * length
    plain, moment = total[:modes, :groups], total[modes:, :groups]
    return (
        outs[0].reshape(chans, length),
        outs[1].reshape(chans, length),
        outs[2].reshape(chans, length),
        (plain / tokens).T,
        (-(resid * decay) * moment / tokens).T,
    )


def solution(mesh):
    in_specs = (P("tp", "ctx"), P("tp", "ctx"), P("tp", "ctx"), P("tp", "ctx"), P(), P())
    out_specs = (P("tp", "ctx"), P("tp", "ctx"), P("tp", "ctx"), P(), P())
    return jax.shard_map(
        per_device, mesh=mesh, in_specs=in_specs, out_specs=out_specs, check_vma=False
    )
```

time: 64.3 us -> 44 us (0.68)
  Pallas kernels: 31.6 us -> 16.8 us
  local copies, waits for them, and re-layouts: 7.46 us -> 4.87 us
  waiting for transfers between devices: 9.7 us -> 7.93 us
  other arithmetic: 1.53 us -> 0.7 us
    pallas_call x5 -> x6, Pallas kernels: 31.6 us -> 16.8 us  [the longest x1 5.31 us: per_device(): call(local_kernel, 'local', [vmem] * 4, [vmem] * 4, [natural] * 2 + [tabl...]
    ppermute x9, waiting for transfers between devices: 9.7 us -> 7.93 us  [swap(): return lax.ppermute(x, 'ctx', [(i, i ^ bits) for i in range(count)])]
    unnamed x32 -> x18, local copies, waits for them, and re-layouts: 6.53 us -> 4.87 us
    another operation x3 -> x0, local copies, waits for them, and re-layouts: 0.78 us -> none  [per_device(): rates = jnp.tile(decay_rate.reshape(groups // 2, 2 * modes), (1, 4))]
    add x1, other arithmetic: 0.85 us -> 0.08 us  [per_device(): sum((b[flat // 2:, :lanes // 2].astype(F32) + b[flat // 2:, lanes // 2:]....]
  transfers between devices with their start and end apart: 10 -> 10, of which waited for: 6 -> 3; matrix products, arithmetic and copies ran while one was open for 2% -> 0% of each run, Pallas kernels for 31% -> 27%
where the time goes in v2:
time: 44 us; the launch traced here: 43.7 us
  Pallas kernels  16.8 us (38%)
  starting transfers between devices  12.5 us (28%)
  waiting for transfers between devices  7.93 us (18%)
  local copies, waits for them, and re-layouts  4.87 us (11%)
  between operations  0.78 us (2%)
  other arithmetic  0.7 us (2%)
    ppermute x9, starting transfers between devices, swap(): return lax.ppermute(x, 'ctx', [(i, i ^ bits) for i in range(count)])  12.5 us
    ppermute x9, waiting for transfers between devices, swap(): return lax.ppermute(x, 'ctx', [(i, i ^ bits) for i in range(count)])  7.93 us
    pallas_call x1, Pallas kernels, per_device(): call(local_kernel, 'local', [vmem] * 4, [vmem] * 4, [natural] * 2 + [tabl...  5.31 us
    unnamed x18, local copies, waits for them, and re-layouts  4.87 us
    pallas_call x1, Pallas kernels, per_device(): call(states_kernel, 'states', [anywhere] * 4 + [vmem], [vmem] * (3 + PLAN...  3.43 us
    pallas_call x1, Pallas kernels, per_device(): call(outputs_kernel, 'outputs', [anywhere] * 3 + [vmem] * (4 + PLANE), [a...  3.38 us
    pallas_call x1, Pallas kernels, per_device(): call(sums_kernel, 'sums', [vmem] * 3, vmem, shaped((2 * modes, lanes), F3...  3.12 us
  transfers between devices with their start and end apart: 10, of which 3 were waited for; matrix products, arithmetic and copies ran while one was open for 0% of the time, Pallas kernels for 27%

profile of v2, /device:TPU:0, one launch (start us, length us, event | category | flops | bytes accessed | tf_op | source)
XLA Modules:
  0.0 43.7 jit_solution(15030431223853030715)
XLA Ops:
  0.6 0.7 %copy-done.6 = f32[64,16]{0,1:T(8,128)S(1)} copy-done((f32[64,16]{0,1:T(8,128)S(1)}, f32[64,16]{0,1:T(8,128)}, u32[]{:S(2)}) %copy-start.6) | copy-done | bytes 4120
  1.3 1.0 %copy-done = bf16[2048,128]{1,0:T(8,128)(2,1)S(1)} copy-done((bf16[2048,128]{1,0:T(8,128)(2,1)S(1)}, bf16[2048,128]{1,0:T(8,128)(2,1)}, u32[]{:S(2)}) %copy-start) | copy-done | bytes 524312
  2.4 1.0 %copy-done.2 = bf16[2048,128]{1,0:T(8,128)(2,1)S(1)} copy-done((bf16[2048,128]{1,0:T(8,128)(2,1)S(1)}, bf16[2048,128]{1,0:T(8,128)(2,1)}, u32[]{:S(2)}) %copy-start.2) | copy-done | bytes 524312
  3.4 1.0 %copy-done.4 = bf16[2048,128]{1,0:T(8,128)(2,1)S(1)} copy-done((bf16[2048,128]{1,0:T(8,128)(2,1)S(1)}, bf16[2048,128]{1,0:T(8,128)(2,1)}, u32[]{:S(2)}) %copy-start.4) | copy-done | bytes 524312
  4.5 1.0 %copy-done.8 = bf16[2048,128]{1,0:T(8,128)(2,1)S(1)} copy-done((bf16[2048,128]{1,0:T(8,128)(2,1)S(1)}, bf16[2048,128]{1,0:T(8,128)(2,1)}, u32[]{:S(2)}) %copy-start.8) | copy-done | bytes 524312
  5.5 3.4 %states.1 = (bf16[64,32,128]{2,1,0:T(8,128)(2,1)S(1)}, bf16[64,32,128]{2,1,0:T(8,128)(2,1)S(1)}, f32[32,128]{1,0:T(8,128)S(1)}, bf16[8,32,128]{2,1,0:T(8,128)(2,...) custom-call(bf16[32,64,128]{2,1,0:T(8,128)(2,1)S(1)} %bitcast.15, ...), custom_call_target="tpu_custom_call" | custom-call | flops 1000000000 | bytes 4000000 | tf_op jit(solution)/shard_map/states/pallas_call | solution.py:435
  8.9 3.0 %collective-permute-start = (bf16[8,32,128]{2,1,0:T(8,128)(2,1)S(1)}, bf16[8,32,128]{2,1,0:T(8,128)(2,1)S(1)}, u32[]{:S(2)}, u32[]{:S(2)}) collective-permute-start(bf16[8,32,128]{2,1,0:T(8,128)(2,1)S(1)} %get-tuple-element.31), channel_id=1, source_target_pairs={{0,2},{2,0},{4,6},{6,4},{8,10},{10,8},{12,14},{14,12},{16,18},{18,... | collective-permute-start | bytes 196616 | tf_op jit(solution)/shard_map/ppermute | solution.py:454
  12.0 1.5 %collective-permute-start.1 = (bf16[8,32,128]{2,1,0:T(8,128)(2,1)S(1)}, bf16[8,32,128]{2,1,0:T(8,128)(2,1)S(1)}, u32[]{:S(2)}, u32[]{:S(2)}) collective-permute-start(bf16[8,32,128]{2,1,0:T(8,128)(2,1)S(1)} %get-tuple-element.32), channel_id=1, source_target_pairs={{0,4},{2,6},{4,0},{6,2},{8,12},{10,14},{12,8},{14,10},{16,20},{18,... | collective-permute-start | bytes 196616 | tf_op jit(solution)/shard_map/ppermute | solution.py:454
  13.5 3.1 %sums.1.refs_4_ = f32[32,128]{1,0:T(8,128)S(1)} custom-call(bf16[64,32,128]{2,1,0:T(8,128)(2,1)S(1)} %get-tuple-element.23.gx_ref, bf16[64,32,128]{2,1,0:T(8,128)(2,1)S(1)} %get-tuple-element.24.cx_ref, f32[16,64]{1,0:T(8,128)S(1)} %bitcast.22), custom_call_target="tpu_custom_call" | custom-call | flops 1000000000 | bytes 4000000 | tf_op jit(solution)/shard_map/sums/pallas_call | solution.py:457
  16.7 2.0 %collective-permute-done.2.refs_3_ = bf16[8,32,128]{2,1,0:T(8,128)(2,1)S(1)} collective-permute-done((bf16[8,32,128]{2,1,0:T(8,128)(2,1)S(1)}, bf16[8,32,128]{2,1,0:T(8,128)(2,1)S(1)}, u32[]{:S(2)}, u32[]{:S(2)}) %collective-permute-start.2) | collective-permute-done | bytes 65568 | tf_op jit(solution)/shard_map/ppermute | solution.py:454
  18.7 0.8 %plane.1.refs_4_ = bf16[288,128]{1,0:T(8,128)(2,1)S(1)} custom-call(f32[32,128]{1,0:T(8,128)S(1)} %get-tuple-element.29.rate_ref, bf16[8,32,128]{2,1,0:T(8,128)(2,1)S(1)} %get-tuple-element.30.refs_0_, bf16[8,32,128]{2,1,0:T(8,128)(2,1)S(1)} %collective-permute-done.refs_1_, bf16[8,32,128]{2,1,0:T(8,128)(2,1)S(1)} %collective-permute-done.1.refs_2_, ...), custom_call_target="tpu_custom_call" | custom-call | flops 10000000 | bytes 1000000 | tf_op jit(solution)/shard_map/plane/pallas_call | solution.py:468
  19.4 1.6 %collective-permute-start.3 = (bf16[288,128]{1,0:T(8,128)(2,1)S(1)}, bf16[288,128]{1,0:T(8,128)(2,1)S(1)}, u32[]{:S(2)}, u32[]{:S(2)}) collective-permute-start(bf16[288,128]{1,0:T(8,128)(2,1)S(1)} %plane.1.refs_4_), channel_id=1, source_target_pairs={{0,8},{2,10},{4,12},{6,14},{8,0},{10,2},{12,4},{14,6},{16,24},{18,... | collective-permute-start | bytes 221192 | tf_op jit(solution)/shard_map/ppermute | solution.py:454
  21.0 2.6 %collective-permute-start.4 = (bf16[288,128]{1,0:T(8,128)(2,1)S(1)}, bf16[288,128]{1,0:T(8,128)(2,1)S(1)}, u32[]{:S(2)}, u32[]{:S(2)}) collective-permute-start(bf16[288,128]{1,0:T(8,128)(2,1)S(1)} %plane.1.refs_4_), channel_id=1, source_target_pairs={{0,16},{2,18},{4,20},{6,22},{8,24},{10,26},{12,28},{14,30},{16,0},... | collective-permute-start | bytes 221192 | tf_op jit(solution)/shard_map/ppermute | solution.py:454
  23.6 0.2 collective-permute-start.5
  23.9 4.0 %collective-permute-done.4.refs_6_ = bf16[288,128]{1,0:T(8,128)(2,1)S(1)} collective-permute-done((bf16[288,128]{1,0:T(8,128)(2,1)S(1)}, bf16[288,128]{1,0:T(8,128)(2,1)S(1)}, u32[]{:S(2)}, u32[]{:S(2)}) %collective-permute-start.4) | collective-permute-done | bytes 73760 | tf_op jit(solution)/shard_map/ppermute | solution.py:454
  27.8 1.9 %collective-permute-done.5.refs_7_ = bf16[288,128]{1,0:T(8,128)(2,1)S(1)} collective-permute-done((bf16[288,128]{1,0:T(8,128)(2,1)S(1)}, bf16[288,128]{1,0:T(8,128)(2,1)S(1)}, u32[]{:S(2)}, u32[]{:S(2)}) %collective-permute-start.5) | collective-permute-done | bytes 73760 | tf_op jit(solution)/shard_map/ppermute | solution.py:454
  29.7 0.9 %line.1 = (bf16[160,128]{1,0:T(8,128)(2,1)S(1)}, bf16[160,128]{1,0:T(8,128)(2,1)S(1)}, bf16[160,128]{1,0:T(8,128)(2,1)S(1)}, bf16[160,128]{1,0:T(8,128)(2,1)S(1)}) custom-call(f32[32,128]{1,0:T(8,128)S(1)} %get-tuple-element.29.rate_ref, bf16[8,32,128]{2,1,0:T(8,128)(2,1)S(1)} %get-tuple-element.30.refs_0_, ...), custom_call_target="tpu_custom_call" | custom-call | flops 10000000 | bytes 1000000 | tf_op jit(solution)/shard_map/line/pallas_call | solution.py:491
  30.6 0.6 %collective-permute-start.6 = (bf16[160,128]{1,0:T(8,128)(2,1)S(1)}, bf16[160,128]{1,0:T(8,128)(2,1)S(1)}, u32[]{:S(2)}, u32[]{:S(2)}) collective-permute-start(bf16[160,128]{1,0:T(8,128)(2,1)S(1)} %get-tuple-element.35), channel_id=1, source_target_pairs={{0,2},{2,0},{4,6},{6,4},{8,10},{10,8},{12,14},{14,12},{16,18},{18,... | collective-permute-start | bytes 122888 | tf_op jit(solution)/shard_map/ppermute | solution.py:454
  31.2 1.0 %collective-permute-start.7 = (bf16[160,128]{1,0:T(8,128)(2,1)S(1)}, bf16[160,128]{1,0:T(8,128)(2,1)S(1)}, u32[]{:S(2)}, u32[]{:S(2)}) collective-permute-start(bf16[160,128]{1,0:T(8,128)(2,1)S(1)} %get-tuple-element.36), channel_id=1, source_target_pairs={{0,4},{2,6},{4,0},{6,2},{8,12},{10,14},{12,8},{14,10},{16,20},{18,... | collective-permute-start | bytes 122888 | tf_op jit(solution)/shard_map/ppermute | solution.py:454
  32.2 2.0 %collective-permute-start.8 = (bf16[160,128]{1,0:T(8,128)(2,1)S(1)}, bf16[160,128]{1,0:T(8,128)(2,1)S(1)}, u32[]{:S(2)}, u32[]{:S(2)}) collective-permute-start(bf16[160,128]{1,0:T(8,128)(2,1)S(1)} %get-tuple-element.37), channel_id=1, source_target_pairs={{0,6},{2,4},{4,2},{6,0},{8,14},{10,12},{12,10},{14,8},{16,22},{18,... | collective-permute-start | bytes 122888 | tf_op jit(solution)/shard_map/ppermute | solution.py:454
  34.2 5.3 %local.1 = (f32[4,512,128]{2,1,0:T(8,128)S(1)}, f32[4,512,128]{2,1,0:T(8,128)S(1)}, bf16[64,16,128]{2,1,0:T(8,128)(2,1)S(1)}, bf16[64,16,128]{2,1,0:T(8,128)(2,1)S(1)}) custom-call(bf16[64,32,128]{2,1,0:T(8,128)(2,1)S(1)} %get-tuple-element.23.gx_ref, bf16[64,32,128]{2,1,0:T(8,128)(2,1)S(1)} %get-tuple-element.24.cx_ref, f32[16,64]{1,0:T(8,128)S(1)} %bitcast.23, ...), custom_call_target="tpu_custom_call" | custom-call | flops 1000000000 | bytes 4000000 | tf_op jit(solution)/shard_map/local/pallas_call | solution.py:481
  39.5 0.1 add_add_fusion
  39.6 3.4 %outputs.1 = (bf16[32,64,128]{2,1,0:T(8,128)(2,1)}, bf16[32,64,128]{2,1,0:T(8,128)(2,1)}, bf16[32,64,128]{2,1,0:T(8,128)(2,1)}) custom-call(bf16[32,64,128]{2,1,0:T(8,128)(2,1)S(1)} %bitcast.16, bf16[32,64,128]{2,1,0:T(8,128)(2,1)S(1)} %bitcast.18, bf16[32,64,128]{2,1,0:T(8,128)(2,1)S(1)} %bitcast.20, f32[4,512,128]{2,1,0:T(8,128)S(1)} %get-tuple-element.25.conv_ref, ...), custom_call_target="tpu_custom_call" | custom-call | flops 1000000000 | bytes 5000000 | tf_op jit(solution)/shard_map/outputs/pallas_call | solution.py:512
  43.1 0.6 %fusion.1 = (f32[64,16]{0,1:T(8,128)}, f32[64,16]{0,1:T(8,128)}) fusion(f32[32,64]{1,0:T(8,128)S(1)} %add.31, f32[64,16]{0,1:T(8,128)S(1)} %copy-done.7, f32[64,16]{0,1:T(8,128)S(1)} %copy-done.6), kind=kLoop, calls=%fused_computation.3 | loop fusion | flops 5120 | bytes 24576 | tf_op jit(solution)/shard_map/transpose | solution.py:536
  (23 shorter events, 0.1 us)
Async XLA Ops:
  0.6 0.7 %copy-start.6 = (f32[64,16]{0,1:T(8,128)S(1)}, f32[64,16]{0,1:T(8,128)}, u32[]{:S(2)}) copy-start(f32[64,16]{0,1:T(8,128)} %param.11) | copy-start | bytes 12292
  1.3 1.0 %copy-start = (bf16[2048,128]{1,0:T(8,128)(2,1)S(1)}, bf16[2048,128]{1,0:T(8,128)(2,1)}, u32[]{:S(2)}) copy-start(bf16[2048,128]{1,0:T(8,128)(2,1)} %param.7) | copy-start | bytes 1572868
  2.4 1.0 %copy-start.2 = (bf16[2048,128]{1,0:T(8,128)(2,1)S(1)}, bf16[2048,128]{1,0:T(8,128)(2,1)}, u32[]{:S(2)}) copy-start(bf16[2048,128]{1,0:T(8,128)(2,1)} %param.8) | copy-start | bytes 1572868
  3.4 1.0 %copy-start.4 = (bf16[2048,128]{1,0:T(8,128)(2,1)S(1)}, bf16[2048,128]{1,0:T(8,128)(2,1)}, u32[]{:S(2)}) copy-start(bf16[2048,128]{1,0:T(8,128)(2,1)} %param.9) | copy-start | bytes 1572868
  4.5 1.0 %copy-start.8 = (bf16[2048,128]{1,0:T(8,128)(2,1)S(1)}, bf16[2048,128]{1,0:T(8,128)(2,1)}, u32[]{:S(2)}) copy-start(bf16[2048,128]{1,0:T(8,128)(2,1)} %param.6) | copy-start | bytes 1572868
  8.9 7.7 %collective-permute-start = (bf16[8,32,128]{2,1,0:T(8,128)(2,1)S(1)}, bf16[8,32,128]{2,1,0:T(8,128)(2,1)S(1)}, u32[]{:S(2)}, u32[]{:S(2)}) collective-permute-start(bf16[8,32,128]{2,1,0:T(8,128)(2,1)S(1)} %get-tuple-element.31), channel_id=1, source_target_pairs={{0,2},{2,0},{4,6},{6,4},{8,10},{10,8},{12,14},{14,12},{16,18},{18,... | collective-permute-start | bytes 196616 | tf_op jit(solution)/shard_map/ppermute | solution.py:454
  12.0 4.7 %collective-permute-start.1 = (bf16[8,32,128]{2,1,0:T(8,128)(2,1)S(1)}, bf16[8,32,128]{2,1,0:T(8,128)(2,1)S(1)}, u32[]{:S(2)}, u32[]{:S(2)}) collective-permute-start(bf16[8,32,128]{2,1,0:T(8,128)(2,1)S(1)} %get-tuple-element.32), channel_id=1, source_target_pairs={{0,4},{2,6},{4,0},{6,2},{8,12},{10,14},{12,8},{14,10},{16,20},{18,... | collective-permute-start | bytes 196616 | tf_op jit(solution)/shard_map/ppermute | solution.py:454
  13.5 5.2 %collective-permute-start.2 = (bf16[8,32,128]{2,1,0:T(8,128)(2,1)S(1)}, bf16[8,32,128]{2,1,0:T(8,128)(2,1)S(1)}, u32[]{:S(2)}, u32[]{:S(2)}) collective-permute-start(bf16[8,32,128]{2,1,0:T(8,128)(2,1)S(1)} %get-tuple-element.33), channel_id=1, source_target_pairs={{0,6},{2,4},{4,2},{6,0},{8,14},{10,12},{12,10},{14,8},{16,22},{18,... | collective-permute-start | bytes 196616 | tf_op jit(solution)/shard_map/ppermute | solution.py:454
  19.4 14.7 %copy-start.7 = (f32[64,16]{0,1:T(8,128)S(1)}, f32[64,16]{0,1:T(8,128)}, u32[]{:S(2)}) copy-start(f32[64,16]{0,1:T(8,128)} %param.10) | copy-start | bytes 12292
  19.4 4.5 %collective-permute-start.3 = (bf16[288,128]{1,0:T(8,128)(2,1)S(1)}, bf16[288,128]{1,0:T(8,128)(2,1)S(1)}, u32[]{:S(2)}, u32[]{:S(2)}) collective-permute-start(bf16[288,128]{1,0:T(8,128)(2,1)S(1)} %plane.1.refs_4_), channel_id=1, source_target_pairs={{0,8},{2,10},{4,12},{6,14},{8,0},{10,2},{12,4},{14,6},{16,24},{18,... | collective-permute-start | bytes 221192 | tf_op jit(solution)/shard_map/ppermute | solution.py:454
  21.0 6.8 %collective-permute-start.4 = (bf16[288,128]{1,0:T(8,128)(2,1)S(1)}, bf16[288,128]{1,0:T(8,128)(2,1)S(1)}, u32[]{:S(2)}, u32[]{:S(2)}) collective-permute-start(bf16[288,128]{1,0:T(8,128)(2,1)S(1)} %plane.1.refs_4_), channel_id=1, source_target_pairs={{0,16},{2,18},{4,20},{6,22},{8,24},{10,26},{12,28},{14,30},{16,0},... | collective-permute-start | bytes 221192 | tf_op jit(solution)/shard_map/ppermute | solution.py:454
  23.6 6.2 %collective-permute-start.5 = (bf16[288,128]{1,0:T(8,128)(2,1)S(1)}, bf16[288,128]{1,0:T(8,128)(2,1)S(1)}, u32[]{:S(2)}, u32[]{:S(2)}) collective-permute-start(bf16[288,128]{1,0:T(8,128)(2,1)S(1)} %plane.1.refs_4_), channel_id=1, source_target_pairs={{0,24},{2,26},{4,28},{6,30},{8,16},{10,18},{12,20},{14,22},{16,8},... | collective-permute-start | bytes 221192 | tf_op jit(solution)/shard_map/ppermute | solution.py:454
  30.6 8.9 %collective-permute-start.6 = (bf16[160,128]{1,0:T(8,128)(2,1)S(1)}, bf16[160,128]{1,0:T(8,128)(2,1)S(1)}, u32[]{:S(2)}, u32[]{:S(2)}) collective-permute-start(bf16[160,128]{1,0:T(8,128)(2,1)S(1)} %get-tuple-element.35), channel_id=1, source_target_pairs={{0,2},{2,0},{4,6},{6,4},{8,10},{10,8},{12,14},{14,12},{16,18},{18,... | collective-permute-start | bytes 122888 | tf_op jit(solution)/shard_map/ppermute | solution.py:454
  31.2 8.3 %collective-permute-start.7 = (bf16[160,128]{1,0:T(8,128)(2,1)S(1)}, bf16[160,128]{1,0:T(8,128)(2,1)S(1)}, u32[]{:S(2)}, u32[]{:S(2)}) collective-permute-start(bf16[160,128]{1,0:T(8,128)(2,1)S(1)} %get-tuple-element.36), channel_id=1, source_target_pairs={{0,4},{2,6},{4,0},{6,2},{8,12},{10,14},{12,8},{14,10},{16,20},{18,... | collective-permute-start | bytes 122888 | tf_op jit(solution)/shard_map/ppermute | solution.py:454
  32.2 7.3 %collective-permute-start.8 = (bf16[160,128]{1,0:T(8,128)(2,1)S(1)}, bf16[160,128]{1,0:T(8,128)(2,1)S(1)}, u32[]{:S(2)}, u32[]{:S(2)}) collective-permute-start(bf16[160,128]{1,0:T(8,128)(2,1)S(1)} %get-tuple-element.37), channel_id=1, source_target_pairs={{0,6},{2,4},{4,2},{6,0},{8,14},{10,12},{12,10},{14,8},{16,22},{18,... | collective-permute-start | bytes 122888 | tf_op jit(solution)/shard_map/ppermute | solution.py:454
  34.2 5.5 %copy-start.1 = (bf16[2048,128]{1,0:T(8,128)(2,1)S(1)}, bf16[2048,128]{1,0:T(8,128)(2,1)}, u32[]{:S(2)}) copy-start(bf16[2048,128]{1,0:T(8,128)(2,1)} %param.7) | copy-start | bytes 1572868
  34.2 5.5 %copy-start.3 = (bf16[2048,128]{1,0:T(8,128)(2,1)S(1)}, bf16[2048,128]{1,0:T(8,128)(2,1)}, u32[]{:S(2)}) copy-start(bf16[2048,128]{1,0:T(8,128)(2,1)} %param.8) | copy-start | bytes 1572868
  34.2 5.5 %copy-start.5 = (bf16[2048,128]{1,0:T(8,128)(2,1)S(1)}, bf16[2048,128]{1,0:T(8,128)(2,1)}, u32[]{:S(2)}) copy-start(bf16[2048,128]{1,0:T(8,128)(2,1)} %param.9) | copy-start | bytes 1572868
  39.6 3.4 %collective-permute-start.9 = (f32[32,64]{1,0:T(8,128)S(1)}, f32[32,64]{1,0:T(8,128)S(1)}, u32[]{:S(2)}, u32[]{:S(2)}) collective-permute-start(f32[32,64]{1,0:T(8,128)S(1)} %add_add_fusion), channel_id=1, source_target_pairs={{0,1},{1,0},{2,3},{3,2},{4,5},{5,4},{6,7},{7,6},{8,9},{9,8},{10,11... | collective-permute-start | bytes 24584 | tf_op jit(solution)/shard_map/ppermute | solution.py:509

commit v3 on v2

--- a/solution.py
+++ b/solution.py
@@ -42,8 +42,8 @@
     return lax.broadcasted_iota(jnp.int32, shape, len(shape) - 1)
 
 
-def states_kernel(k_hbm, v_hbm, g_hbm, q_hbm, dec_ref, gx_ref, cx_ref, rate_ref, *rest):
-    outs, (bufs, sems, wx_ref, wc_ref, gs, cs) = rest[:PLANE], rest[PLANE:]
+def states_kernel(dec_hbm, k_hbm, v_hbm, g_hbm, q_hbm, gx_ref, cx_ref, rate_ref, *rest):
+    outs, (dec_ref, dec_sem, bufs, sems, wx_ref, wc_ref, gs, cs) = rest[:PLANE], rest[PLANE:]
     place, _ = places()
     _, rows, part, length = bufs.shape[1:]
     modes, groups = dec_ref.shape
@@ -58,9 +58,12 @@
             sems.at[which, quarter],
         )
 
+    rates_in = pltpu.make_async_copy(dec_hbm, dec_ref, dec_sem)
+    rates_in.start()
     for quarter in range(PLANE):
         for which in range(4):
             copy(which, quarter).start()
+    rates_in.wait()
     dec = dec_ref[...]
     ahead = lane_iota((modes, length)).astype(F32)
     behind = float(length) - ahead
@@ -159,7 +162,7 @@
     sums_ref[modes:] = moment
 
 
-def local_kernel(gx_ref, cx_ref, dec_ref, res_ref, conv_ref, ig_ref, wl_ref, wr_ref, toep_ref):
+def local_kernel(gx_ref, cx_ref, dec_ref, res_ref, after_ref, conv_ref, ig_ref, wl_ref, wr_ref, toep_ref):
     groups, rows, length = gx_ref.shape
     modes = dec_ref.shape[0]
     part = groups // PLANE
@@ -287,7 +290,7 @@
     out_ref[flat:] = split_pair(acc[...], lanes // 2)
 
 
-def line_kernel(length, rate_ref, *refs):
+def line_kernel(length, rate_ref, after_ref, *refs):
     count = len(refs) - 2 * PLANE - 1
     msgs, lines = refs[:PLANE], refs[PLANE : PLANE + count]
     outs, acc = refs[PLANE + count : -1], refs[-1]
@@ -324,23 +327,14 @@
         outs[i][flat // 2 :] = sums
 
 
-def outputs_kernel(k_hbm, v_hbm, g_hbm, conv_ref, ig_ref, wl_ref, wr_ref, *refs):
+def outputs_kernel(k_ref, v_ref, g_ref, conv_ref, ig_ref, wl_ref, wr_ref, *refs):
     incoming, results = refs[:PLANE], refs[PLANE : PLANE + 3]
-    bufs, sems, outs, out_sems, cs, gs = refs[PLANE + 3 :]
+    outs, out_sems, cs, gs = refs[PLANE + 3 :]
     place, _ = places()
-    _, rows, part, length = bufs.shape[1:]
+    _, rows, part, length = outs.shape[1:]
     modes = wl_ref.shape[1]
     pairs = part // 2
     flat = pairs * rows // 2
-    sources = (k_hbm, v_hbm, g_hbm)
-
-    def copy(which, quarter):
-        return pltpu.make_async_copy(
-            sources[which].at[:, pl.ds(quarter * part, part), :],
-            bufs.at[which, quarter],
-            sems.at[which, quarter],
-        )
-
     def store(which, quarter):
         return pltpu.make_async_copy(
             outs.at[which, quarter],
@@ -348,9 +342,6 @@
             out_sems.at[which, quarter],
         )
 
-    for quarter in range(PLANE):
-        for which in range(3):
-            copy(which, quarter).start()
     mirror = mirror_of(length)
     zero = jnp.zeros((modes, length), BF16)
 
@@ -376,14 +367,13 @@
             cs[pl.ds(local, rows, stride=part), :] = both[:, :length]
             gs[pl.ds(local, rows, stride=part), :] = both[:, length:]
         shape = (rows, part, length)
-        for which in range(3):
-            copy(which, quarter).wait()
+        own = pl.ds(pl.multiple_of(quarter * part, part), part)
         conv = (cs[...] + conv_ref[quarter]).astype(BF16).reshape(shape)
         ig = (gs[...] + ig_ref[quarter]).astype(BF16)
         ig = dot(ig, mirror, NN).reshape(shape)
-        outs[0, quarter] = product(bufs[2, quarter], conv)
-        outs[1, quarter] = product(ig, bufs[1, quarter])
-        outs[2, quarter] = product(ig, bufs[0, quarter])
+        outs[0, quarter] = product(g_ref[:, own, :], conv)
+        outs[1, quarter] = product(ig, v_ref[:, own, :])
+        outs[2, quarter] = product(ig, k_ref[:, own, :])
         for which in range(3):
             store(which, quarter).start()
         return 0
@@ -411,7 +401,7 @@
     query, key, value, grad = cube(queries), cube(keys_in), cube(values_in), cube(grad_out)
     decay, resid = decay_rate.T, residue.T
     vmem = pl.BlockSpec(memory_space=pltpu.VMEM)
-    anywhere = pl.BlockSpec(memory_space=pl.ANY)
+    anywhere = pl.BlockSpec(memory_space=pltpu.HBM)
 
     def shaped(shape, dtype):
         return jax.ShapeDtypeStruct(shape, dtype)
@@ -435,10 +425,12 @@
     gx, cx, rates, *own = call(
         states_kernel,
         "states",
-        [anywhere] * 4 + [vmem],
+        [anywhere] * 5,
         [vmem] * (3 + PLANE),
         [grouped] * 2 + [shaped((groups // 2, lanes), F32)] + [block] * PLANE,
         [
+            pltpu.VMEM((modes, groups), F32),
+            pltpu.SemaphoreType.DMA,
             pltpu.VMEM((4, PLANE, rows, part, length), BF16),
             pltpu.SemaphoreType.DMA((4, PLANE)),
             weight,
@@ -448,7 +440,7 @@
         ],
         10**9,
         4 * 10**6,
-    )(key, value, grad, query, decay)
+    )(*(pltpu.with_memory_space_constraint(x, pltpu.HBM) for x in (decay, key, value, grad, query)))
 
     def swap(x, bits):
         return lax.ppermute(x, "ctx", [(i, i ^ bits) for i in range(count)])
@@ -481,23 +473,23 @@
     conv, ig, wl, wr = call(
         local_kernel,
         "local",
-        [vmem] * 4,
+        [vmem] * 5,
         [vmem] * 4,
         [natural] * 2 + [table] * 2,
         [pltpu.VMEM((part, length, length), BF16)],
         10**9,
         4 * 10**6,
-    )(gx, cx, decay, resid)
+    )(gx, cx, decay, resid, plane)
     back = call(
         functools.partial(line_kernel, length),
         "line",
-        [vmem] * (1 + PLANE + depth),
+        [vmem] * (2 + PLANE + depth),
         [vmem] * PLANE,
         [shaped((flat // 2 + 2 * modes, lanes), BF16)] * PLANE,
         [pltpu.VMEM((2 * modes, lanes), F32)],
         10**7,
         10**6,
-    )(rates, *near, *line)
+    )(rates, wl, *near, *line)
     back = [back[0]] + [swap(back[i], i) for i in range(1, PLANE)]
 
     total = sum(
@@ -512,12 +504,10 @@
     outs = call(
         outputs_kernel,
         "outputs",
-        [anywhere] * 3 + [vmem] * (4 + PLANE),
+        [vmem] * (7 + PLANE),
         [anywhere] * 3,
         [shaped((rows, groups, length), BF16)] * 3,
         [
-            pltpu.VMEM((3, PLANE, rows, part, length), BF16),
-            pltpu.SemaphoreType.DMA((3, PLANE)),
             pltpu.VMEM((3, PLANE, rows, part, length), BF16),
             pltpu.SemaphoreType.DMA((3, PLANE)),
             plane_f32,

time: 44 us -> 36.8 us (0.84)
  local copies, waits for them, and re-layouts: 4.87 us -> 0.02 us
  waiting for transfers between devices: 7.93 us -> 4.92 us
  Pallas kernels: 16.8 us -> 17.7 us
    unnamed x18 -> x10, local copies, waits for them, and re-layouts: 4.87 us -> 0.02 us
    ppermute x9, waiting for transfers between devices: 7.93 us -> 4.92 us  [swap(): return lax.ppermute(x, 'ctx', [(i, i ^ bits) for i in range(count)])]
    pallas_call x4, Pallas kernels: 13 us -> 13.9 us  [the longest x1 5.3 us: per_device(): call(local_kernel, 'local', [vmem] * 5, [vmem] * 4, [natural] * 2 + [tabl...]
  transfers between devices with their start and end apart: 10 -> 10, of which waited for: 3 -> 4; matrix products, arithmetic and copies ran while one was open for 0% -> 0% of each run, Pallas kernels for 27% -> 31%
where the time goes in v3:
time: 36.8 us; the launch traced here: 36.7 us
  Pallas kernels  17.7 us (48%)
  starting transfers between devices  12.5 us (34%)
  waiting for transfers between devices  4.92 us (13%)
  between operations  0.78 us (2%)
  other arithmetic  0.69 us (2%)
    ppermute x9, starting transfers between devices, swap(): return lax.ppermute(x, 'ctx', [(i, i ^ bits) for i in range(count)])  12.5 us
    pallas_call x1, Pallas kernels, per_device(): call(local_kernel, 'local', [vmem] * 5, [vmem] * 4, [natural] * 2 + [tabl...  5.3 us
    ppermute x9, waiting for transfers between devices, swap(): return lax.ppermute(x, 'ctx', [(i, i ^ bits) for i in range(count)])  4.92 us
    pallas_call x1, Pallas kernels, per_device(): call(states_kernel, 'states', [anywhere] * 5, [vmem] * (3 + PLANE), [grou...  4.59 us
    pallas_call x1, Pallas kernels, per_device(): call(sums_kernel, 'sums', [vmem] * 3, vmem, shaped((2 * modes, lanes), F3...  3.12 us
    pallas_call x1, Pallas kernels, per_device(): call(outputs_kernel, 'outputs', [vmem] * (7 + PLANE), [anywhere] * 3, [sh...  3.11 us
    pallas_call x1, Pallas kernels, per_device(): call(functools.partial(line_kernel, length), 'line', [vmem] * (2 + PLANE...  0.85 us
    pallas_call x1, Pallas kernels, per_device(): call(functools.partial(plane_kernel, length), 'plane', [vmem] * (2 + PLAN...  0.75 us
  transfers between devices with their start and end apart: 10, of which 4 were waited for; matrix products, arithmetic and copies ran while one was open for 0% of the time, Pallas kernels for 31%

profile of v3, /device:TPU:0, one launch (start us, length us, event | category | flops | bytes accessed | tf_op | source)
XLA Modules:
  0.0 36.7 jit_solution(17913785674101195740)
XLA Ops:
  0.6 4.6 %states.1 = (bf16[64,32,128]{2,1,0:T(8,128)(2,1)S(1)}, bf16[64,32,128]{2,1,0:T(8,128)(2,1)S(1)}, f32[32,128]{1,0:T(8,128)S(1)}, bf16[8,32,128]{2,1,0:T(8,128)(2,...) custom-call(f32[16,64]{1,0:T(8,128)} %bitcast.21, ...), custom_call_target="tpu_custom_call" | custom-call | flops 1000000000 | bytes 4000000 | tf_op jit(solution)/shard_map/states/pallas_call | solution.py:425
  5.2 0.0 copy-start.3
  5.2 3.0 %collective-permute-start = (bf16[8,32,128]{2,1,0:T(8,128)(2,1)S(1)}, bf16[8,32,128]{2,1,0:T(8,128)(2,1)S(1)}, u32[]{:S(2)}, u32[]{:S(2)}) collective-permute-start(bf16[8,32,128]{2,1,0:T(8,128)(2,1)S(1)} %get-tuple-element.27), channel_id=1, source_target_pairs={{0,2},{2,0},{4,6},{6,4},{8,10},{10,8},{12,14},{14,12},{16,18},{18,... | collective-permute-start | bytes 196616 | tf_op jit(solution)/shard_map/ppermute | solution.py:446
  8.3 1.5 %collective-permute-start.1 = (bf16[8,32,128]{2,1,0:T(8,128)(2,1)S(1)}, bf16[8,32,128]{2,1,0:T(8,128)(2,1)S(1)}, u32[]{:S(2)}, u32[]{:S(2)}) collective-permute-start(bf16[8,32,128]{2,1,0:T(8,128)(2,1)S(1)} %get-tuple-element.28), channel_id=1, source_target_pairs={{0,4},{2,6},{4,0},{6,2},{8,12},{10,14},{12,8},{14,10},{16,20},{18,... | collective-permute-start | bytes 196616 | tf_op jit(solution)/shard_map/ppermute | solution.py:446
  9.8 0.0 collective-permute-start.2
  9.8 3.1 %sums.1.refs_4_ = f32[32,128]{1,0:T(8,128)S(1)} custom-call(bf16[64,32,128]{2,1,0:T(8,128)(2,1)S(1)} %get-tuple-element.23.gx_ref, bf16[64,32,128]{2,1,0:T(8,128)(2,1)S(1)} %get-tuple-element.24.cx_ref, f32[16,64]{1,0:T(8,128)S(1)} %bitcast.22), custom_call_target="tpu_custom_call" | custom-call | flops 1000000000 | bytes 4000000 | tf_op jit(solution)/shard_map/sums/pallas_call | solution.py:449
  12.9 0.0 collective-permute-done.refs_1_
  13.0 2.0 %collective-permute-done.2.refs_3_ = bf16[8,32,128]{2,1,0:T(8,128)(2,1)S(1)} collective-permute-done((bf16[8,32,128]{2,1,0:T(8,128)(2,1)S(1)}, bf16[8,32,128]{2,1,0:T(8,128)(2,1)S(1)}, u32[]{:S(2)}, u32[]{:S(2)}) %collective-permute-start.2) | collective-permute-done | bytes 65568 | tf_op jit(solution)/shard_map/ppermute | solution.py:446
  15.0 0.7 %plane.1.after_ref.refs_4_ = bf16[288,128]{1,0:T(8,128)(2,1)S(1)} custom-call(f32[32,128]{1,0:T(8,128)S(1)} %get-tuple-element.25.rate_ref, bf16[8,32,128]{2,1,0:T(8,128)(2,1)S(1)} %get-tuple-element.26.refs_0_, bf16[8,32,128]{2,1,0:T(8,128)(2,1)S(1)} %collective-permute-done.refs_1_, bf16[8,32,128]{2,1,0:T(8,128)(2,1)S(1)} %collective-permute-done.1.refs_2_, ...), custom_call_target="tpu_custom_call" | custom-call | flops 10000000 | bytes 1000000 | tf_op jit(solution)/shard_map/plane/pallas_call | solution.py:460
  15.7 3.6 %collective-permute-start.5 = (bf16[288,128]{1,0:T(8,128)(2,1)S(1)}, bf16[288,128]{1,0:T(8,128)(2,1)S(1)}, u32[]{:S(2)}, u32[]{:S(2)}) collective-permute-start(bf16[288,128]{1,0:T(8,128)(2,1)S(1)} %plane.1.after_ref.refs_4_), channel_id=1, source_target_pairs={{0,24},{2,26},{4,28},{6,30},{8,16},{10,18},{12,20},{14,22},{16,8},... | collective-permute-start | bytes 221192 | tf_op jit(solution)/shard_map/ppermute | solution.py:446
  19.3 0.8 %collective-permute-start.3 = (bf16[288,128]{1,0:T(8,128)(2,1)S(1)}, bf16[288,128]{1,0:T(8,128)(2,1)S(1)}, u32[]{:S(2)}, u32[]{:S(2)}) collective-permute-start(bf16[288,128]{1,0:T(8,128)(2,1)S(1)} %plane.1.after_ref.refs_4_), channel_id=1, source_target_pairs={{0,8},{2,10},{4,12},{6,14},{8,0},{10,2},{12,4},{14,6},{16,24},{18,... | collective-permute-start | bytes 221192 | tf_op jit(solution)/shard_map/ppermute | solution.py:446
  20.1 5.3 %local.1 = (f32[4,512,128]{2,1,0:T(8,128)S(1)}, f32[4,512,128]{2,1,0:T(8,128)S(1)}, bf16[64,16,128]{2,1,0:T(8,128)(2,1)S(1)}, bf16[64,16,128]{2,1,0:T(8,128)(2,1)S(1)}) custom-call(bf16[64,32,128]{2,1,0:T(8,128)(2,1)S(1)} %get-tuple-element.23.gx_ref, bf16[64,32,128]{2,1,0:T(8,128)(2,1)S(1)} %get-tuple-element.24.cx_ref, f32[16,64]{1,0:T(8,128)S(1)} %bitcast.23, ...), custom_call_target="tpu_custom_call" | custom-call | flops 1000000000 | bytes 4000000 | tf_op jit(solution)/shard_map/local/pallas_call | solution.py:473
  25.4 0.0 copy-start
  25.5 0.9 %line.1 = (bf16[160,128]{1,0:T(8,128)(2,1)S(1)}, bf16[160,128]{1,0:T(8,128)(2,1)S(1)}, bf16[160,128]{1,0:T(8,128)(2,1)S(1)}, bf16[160,128]{1,0:T(8,128)(2,1)S(1)}) custom-call(f32[32,128]{1,0:T(8,128)S(1)} %get-tuple-element.25.rate_ref, bf16[64,16,128]{2,1,0:T(8,128)(2,1)S(1)} %get-tuple-element.32.after_ref.wl_ref, ...), custom_call_target="tpu_custom_call" | custom-call | flops 10000000 | bytes 1000000 | tf_op jit(solution)/shard_map/line/pallas_call | solution.py:483
  26.3 0.6 %collective-permute-start.6 = (bf16[160,128]{1,0:T(8,128)(2,1)S(1)}, bf16[160,128]{1,0:T(8,128)(2,1)S(1)}, u32[]{:S(2)}, u32[]{:S(2)}) collective-permute-start(bf16[160,128]{1,0:T(8,128)(2,1)S(1)} %get-tuple-element.35), channel_id=1, source_target_pairs={{0,2},{2,0},{4,6},{6,4},{8,10},{10,8},{12,14},{14,12},{16,18},{18,... | collective-permute-start | bytes 122888 | tf_op jit(solution)/shard_map/ppermute | solution.py:446
  26.9 1.0 %collective-permute-start.7 = (bf16[160,128]{1,0:T(8,128)(2,1)S(1)}, bf16[160,128]{1,0:T(8,128)(2,1)S(1)}, u32[]{:S(2)}, u32[]{:S(2)}) collective-permute-start(bf16[160,128]{1,0:T(8,128)(2,1)S(1)} %get-tuple-element.36), channel_id=1, source_target_pairs={{0,4},{2,6},{4,0},{6,2},{8,12},{10,14},{12,8},{14,10},{16,20},{18,... | collective-permute-start | bytes 122888 | tf_op jit(solution)/shard_map/ppermute | solution.py:446
  27.9 2.0 %collective-permute-start.8 = (bf16[160,128]{1,0:T(8,128)(2,1)S(1)}, bf16[160,128]{1,0:T(8,128)(2,1)S(1)}, u32[]{:S(2)}, u32[]{:S(2)}) collective-permute-start(bf16[160,128]{1,0:T(8,128)(2,1)S(1)} %get-tuple-element.37), channel_id=1, source_target_pairs={{0,6},{2,4},{4,2},{6,0},{8,14},{10,12},{12,10},{14,8},{16,22},{18,... | collective-permute-start | bytes 122888 | tf_op jit(solution)/shard_map/ppermute | solution.py:446
  29.9 0.5 %collective-permute-done.6.refs_1_ = bf16[160,128]{1,0:T(8,128)(2,1)S(1)} collective-permute-done((bf16[160,128]{1,0:T(8,128)(2,1)S(1)}, bf16[160,128]{1,0:T(8,128)(2,1)S(1)}, u32[]{:S(2)}, u32[]{:S(2)}) %collective-permute-start.6) | collective-permute-done | bytes 40992 | tf_op jit(solution)/shard_map/ppermute | solution.py:446
  30.4 0.7 %collective-permute-done.7.refs_2_ = bf16[160,128]{1,0:T(8,128)(2,1)S(1)} collective-permute-done((bf16[160,128]{1,0:T(8,128)(2,1)S(1)}, bf16[160,128]{1,0:T(8,128)(2,1)S(1)}, u32[]{:S(2)}, u32[]{:S(2)}) %collective-permute-start.7) | collective-permute-done | bytes 40992 | tf_op jit(solution)/shard_map/ppermute | solution.py:446
  31.1 1.7 %collective-permute-done.8.refs_3_ = bf16[160,128]{1,0:T(8,128)(2,1)S(1)} collective-permute-done((bf16[160,128]{1,0:T(8,128)(2,1)S(1)}, bf16[160,128]{1,0:T(8,128)(2,1)S(1)}, u32[]{:S(2)}, u32[]{:S(2)}) %collective-permute-start.8) | collective-permute-done | bytes 40992 | tf_op jit(solution)/shard_map/ppermute | solution.py:446
  32.8 0.1 add_add_fusion
  32.9 0.0 collective-permute-start.9
  32.9 3.1 %outputs.1 = (bf16[32,64,128]{2,1,0:T(8,128)(2,1)}, bf16[32,64,128]{2,1,0:T(8,128)(2,1)}, bf16[32,64,128]{2,1,0:T(8,128)(2,1)}) custom-call(bf16[32,64,128]{2,1,0:T(8,128)(2,1)S(1)} %bitcast.16, bf16[32,64,128]{2,1,0:T(8,128)(2,1)S(1)} %bitcast.18, bf16[32,64,128]{2,1,0:T(8,128)(2,1)S(1)} %bitcast.20, f32[4,512,128]{2,1,0:T(8,128)S(1)} %get-tuple-element.30.conv_ref, ...), custom_call_target="tpu_custom_call" | custom-call | flops 1000000000 | bytes 5000000 | tf_op jit(solution)/shard_map/outputs/pallas_call | solution.py:504
  36.1 0.6 %fusion.1 = (f32[64,16]{0,1:T(8,128)}, f32[64,16]{0,1:T(8,128)}) fusion(f32[32,64]{1,0:T(8,128)S(1)} %add.31, f32[64,16]{0,1:T(8,128)S(1)} %copy-done.4, f32[64,16]{0,1:T(8,128)S(1)} %copy-done.3), kind=kLoop, calls=%fused_computation.3 | loop fusion | flops 5120 | bytes 24576 | tf_op jit(solution)/shard_map/transpose | solution.py:526
  (15 shorter events, 0.0 us)
Async XLA Ops:
  5.2 4.6 %copy-start.3 = (f32[64,16]{0,1:T(8,128)S(1)}, f32[64,16]{0,1:T(8,128)}, u32[]{:S(2)}) copy-start(f32[64,16]{0,1:T(8,128)} %param.11) | copy-start | bytes 12292
  5.2 7.7 %collective-permute-start = (bf16[8,32,128]{2,1,0:T(8,128)(2,1)S(1)}, bf16[8,32,128]{2,1,0:T(8,128)(2,1)S(1)}, u32[]{:S(2)}, u32[]{:S(2)}) collective-permute-start(bf16[8,32,128]{2,1,0:T(8,128)(2,1)S(1)} %get-tuple-element.27), channel_id=1, source_target_pairs={{0,2},{2,0},{4,6},{6,4},{8,10},{10,8},{12,14},{14,12},{16,18},{18,... | collective-permute-start | bytes 196616 | tf_op jit(solution)/shard_map/ppermute | solution.py:446
  8.3 4.7 %collective-permute-start.1 = (bf16[8,32,128]{2,1,0:T(8,128)(2,1)S(1)}, bf16[8,32,128]{2,1,0:T(8,128)(2,1)S(1)}, u32[]{:S(2)}, u32[]{:S(2)}) collective-permute-start(bf16[8,32,128]{2,1,0:T(8,128)(2,1)S(1)} %get-tuple-element.28), channel_id=1, source_target_pairs={{0,4},{2,6},{4,0},{6,2},{8,12},{10,14},{12,8},{14,10},{16,20},{18,... | collective-permute-start | bytes 196616 | tf_op jit(solution)/shard_map/ppermute | solution.py:446
  9.8 5.2 %collective-permute-start.2 = (bf16[8,32,128]{2,1,0:T(8,128)(2,1)S(1)}, bf16[8,32,128]{2,1,0:T(8,128)(2,1)S(1)}, u32[]{:S(2)}, u32[]{:S(2)}) collective-permute-start(bf16[8,32,128]{2,1,0:T(8,128)(2,1)S(1)} %get-tuple-element.29), channel_id=1, source_target_pairs={{0,6},{2,4},{4,2},{6,0},{8,14},{10,12},{12,10},{14,8},{16,22},{18,... | collective-permute-start | bytes 196616 | tf_op jit(solution)/shard_map/ppermute | solution.py:446
  15.0 5.2 %copy-start.4 = (f32[64,16]{0,1:T(8,128)S(1)}, f32[64,16]{0,1:T(8,128)}, u32[]{:S(2)}) copy-start(f32[64,16]{0,1:T(8,128)} %param.10) | copy-start | bytes 12292
  15.7 9.7 %collective-permute-start.5 = (bf16[288,128]{1,0:T(8,128)(2,1)S(1)}, bf16[288,128]{1,0:T(8,128)(2,1)S(1)}, u32[]{:S(2)}, u32[]{:S(2)}) collective-permute-start(bf16[288,128]{1,0:T(8,128)(2,1)S(1)} %plane.1.after_ref.refs_4_), channel_id=1, source_target_pairs={{0,24},{2,26},{4,28},{6,30},{8,16},{10,18},{12,20},{14,22},{16,8},... | collective-permute-start | bytes 221192 | tf_op jit(solution)/shard_map/ppermute | solution.py:446
  19.3 6.1 %collective-permute-start.4 = (bf16[288,128]{1,0:T(8,128)(2,1)S(1)}, bf16[288,128]{1,0:T(8,128)(2,1)S(1)}, u32[]{:S(2)}, u32[]{:S(2)}) collective-permute-start(bf16[288,128]{1,0:T(8,128)(2,1)S(1)} %plane.1.after_ref.refs_4_), channel_id=1, source_target_pairs={{0,16},{2,18},{4,20},{6,22},{8,24},{10,26},{12,28},{14,30},{16,0},... | collective-permute-start | bytes 221192 | tf_op jit(solution)/shard_map/ppermute | solution.py:446
  19.3 6.1 %collective-permute-start.3 = (bf16[288,128]{1,0:T(8,128)(2,1)S(1)}, bf16[288,128]{1,0:T(8,128)(2,1)S(1)}, u32[]{:S(2)}, u32[]{:S(2)}) collective-permute-start(bf16[288,128]{1,0:T(8,128)(2,1)S(1)} %plane.1.after_ref.refs_4_), channel_id=1, source_target_pairs={{0,8},{2,10},{4,12},{6,14},{8,0},{10,2},{12,4},{14,6},{16,24},{18,... | collective-permute-start | bytes 221192 | tf_op jit(solution)/shard_map/ppermute | solution.py:446
  20.1 12.8 %copy-start.1 = (bf16[2048,128]{1,0:T(8,128)(2,1)S(1)}, bf16[2048,128]{1,0:T(8,128)(2,1)}, u32[]{:S(2)}) copy-start(bf16[2048,128]{1,0:T(8,128)(2,1)} %param.8) | copy-start | bytes 1572868
  20.1 12.8 %copy-start.2 = (bf16[2048,128]{1,0:T(8,128)(2,1)S(1)}, bf16[2048,128]{1,0:T(8,128)(2,1)}, u32[]{:S(2)}) copy-start(bf16[2048,128]{1,0:T(8,128)(2,1)} %param.9) | copy-start | bytes 1572868
  25.4 7.5 %copy-start = (bf16[2048,128]{1,0:T(8,128)(2,1)S(1)}, bf16[2048,128]{1,0:T(8,128)(2,1)}, u32[]{:S(2)}) copy-start(bf16[2048,128]{1,0:T(8,128)(2,1)} %param.7) | copy-start | bytes 1572868
  26.3 4.1 %collective-permute-start.6 = (bf16[160,128]{1,0:T(8,128)(2,1)S(1)}, bf16[160,128]{1,0:T(8,128)(2,1)S(1)}, u32[]{:S(2)}, u32[]{:S(2)}) collective-permute-start(bf16[160,128]{1,0:T(8,128)(2,1)S(1)} %get-tuple-element.35), channel_id=1, source_target_pairs={{0,2},{2,0},{4,6},{6,4},{8,10},{10,8},{12,14},{14,12},{16,18},{18,... | collective-permute-start | bytes 122888 | tf_op jit(solution)/shard_map/ppermute | solution.py:446
  26.9 4.1 %collective-permute-start.7 = (bf16[160,128]{1,0:T(8,128)(2,1)S(1)}, bf16[160,128]{1,0:T(8,128)(2,1)S(1)}, u32[]{:S(2)}, u32[]{:S(2)}) collective-permute-start(bf16[160,128]{1,0:T(8,128)(2,1)S(1)} %get-tuple-element.36), channel_id=1, source_target_pairs={{0,4},{2,6},{4,0},{6,2},{8,12},{10,14},{12,8},{14,10},{16,20},{18,... | collective-permute-start | bytes 122888 | tf_op jit(solution)/shard_map/ppermute | solution.py:446
  27.9 4.9 %collective-permute-start.8 = (bf16[160,128]{1,0:T(8,128)(2,1)S(1)}, bf16[160,128]{1,0:T(8,128)(2,1)S(1)}, u32[]{:S(2)}, u32[]{:S(2)}) collective-permute-start(bf16[160,128]{1,0:T(8,128)(2,1)S(1)} %get-tuple-element.37), channel_id=1, source_target_pairs={{0,6},{2,4},{4,2},{6,0},{8,14},{10,12},{12,10},{14,8},{16,22},{18,... | collective-permute-start | bytes 122888 | tf_op jit(solution)/shard_map/ppermute | solution.py:446
  32.9 3.2 %collective-permute-start.9 = (f32[32,64]{1,0:T(8,128)S(1)}, f32[32,64]{1,0:T(8,128)S(1)}, u32[]{:S(2)}, u32[]{:S(2)}) collective-permute-start(f32[32,64]{1,0:T(8,128)S(1)} %add_add_fusion), channel_id=1, source_target_pairs={{0,1},{1,0},{2,3},{3,2},{4,5},{5,4},{6,7},{7,6},{8,9},{9,8},{10,11... | collective-permute-start | bytes 24584 | tf_op jit(solution)/shard_map/ppermute | solution.py:501

commit v4 on v3

v4 whole, which is shorter than its diff:
```python
import functools
import math

import jax
import jax.numpy as jnp
from jax import lax
from jax.experimental import pallas as pl
from jax.experimental.pallas import tpu as pltpu
from jax.sharding import PartitionSpec as P

F32 = jnp.float32
BF16 = jnp.bfloat16
PLANE = 4
NT = (((1,), (1,)), ((), ()))
NN = (((1,), (0,)), ((), ()))
TN = (((0,), (0,)), ((), ()))


def dot(a, b, dims):
    return lax.dot_general(a, b, dims, preferred_element_type=F32)


def product(a, b):
    return (a.astype(F32) * b.astype(F32)).astype(BF16)


def column(table, group):
    return jnp.sum(jnp.where(lane_iota(table.shape) == group, table, 0.0), axis=1, keepdims=True)


def mirror_of(length):
    total = lane_iota((length, length)) + lax.broadcasted_iota(jnp.int32, (length, length), 0)
    return jnp.where(total == length - 1, 1.0, 0.0).astype(BF16)


def places():
    me = lax.axis_index("ctx")
    return lax.rem(me, PLANE), lax.div(me, PLANE)


def lane_iota(shape):
    return lax.broadcasted_iota(jnp.int32, shape, len(shape) - 1)


def states_kernel(dec_hbm, k_hbm, v_hbm, g_hbm, q_hbm, xc_ref, rate_ref, *rest):
    outs, rest = rest[:PLANE], rest[PLANE:]
    dec_ref, dec_sem, bufs, sems, w_ref, gs, cs, st_ref = rest
    place, _ = places()
    _, rows, part, length = bufs.shape[1:]
    modes, groups = dec_ref.shape
    quads = part // 4
    flat = rows * part
    sources = (k_hbm, v_hbm, g_hbm, q_hbm)

    def copy(which, quarter):
        return pltpu.make_async_copy(
            sources[which].at[:, pl.ds(quarter * part, part), :],
            bufs.at[which, quarter],
            sems.at[which, quarter],
        )

    rates_in = pltpu.make_async_copy(dec_hbm, dec_ref, dec_sem)
    rates_in.start()
    for quarter in range(PLANE):
        for which in range(4):
            copy(which, quarter).start()
    rates_in.wait()
    dec = dec_ref[...]
    behind = float(length) - lane_iota((modes, length)).astype(F32)
    wide = (modes, 8 * modes)
    target = lane_iota(wide) % (4 * modes) - lax.broadcasted_iota(jnp.int32, wide, 0)

    def weights(index, _):
        rates = jnp.zeros(wide, F32)
        for side in range(4):
            group = 4 * index + side
            rate = column(dec, group)
            basis = jnp.exp(-rate * behind)
            w_ref[group, 0] = basis.astype(BF16)
            w_ref[group, 1] = (behind * basis).astype(BF16)
            rates = jnp.where(target == side * modes, rate, rates)
        rate_ref[pl.ds(index, 1), :] = jnp.sum(rates, axis=0, keepdims=True)
        return 0

    lax.fori_loop(0, groups // 4, weights, 0, unroll=4)
    mirror = mirror_of(length)
    zero = jnp.zeros((modes, length), BF16)

    def load(quarter):
        for which in range(4):
            copy(which, quarter).wait()
        slot = quarter % 2
        x = product(bufs[0, quarter], bufs[1, quarter]).astype(F32)
        c = product(bufs[2, quarter], bufs[3, quarter]).reshape(flat, length)
        c = dot(c, mirror, NN).reshape(x.shape)
        for part8 in range(part // 8):
            gs[slot, part8] = x[:, 8 * part8 : 8 * part8 + 8].reshape(8 * rows, length)
            cs[slot, part8] = c[:, 8 * part8 : 8 * part8 + 8].reshape(8 * rows, length)

    def reduce(quarter):
        slot = quarter % 2
        for quad in range(quads):
            left, right = [], []
            for side in range(4):
                local = 4 * quad + side
                group = quarter * part + local
                both = jnp.concatenate(
                    [
                        gs[slot, local // 8, pl.ds(local % 8, rows, stride=8), :],
                        cs[slot, local // 8, pl.ds(local % 8, rows, stride=8), :],
                    ],
                    axis=0,
                ).astype(BF16)
                xc_ref[group] = both
                w = [zero] * 8
                w[side], w[4 + side] = w_ref[group, 0], w_ref[group, 1]
                left.append(both)
                right.append(jnp.concatenate(w, axis=0))
            st_ref[quarter, quad] = dot(
                jnp.concatenate(left, axis=1), jnp.concatenate(right, axis=1), NT
            ).astype(BF16)

    for quarter in range(PLANE + 1):
        if quarter < PLANE:
            load(quarter)
        if quarter > 0:
            reduce(quarter - 1)
    for quad in range(quads):
        for index, x in enumerate(in_order([st_ref[i, quad] for i in range(PLANE)], place)):
            outs[index][quad] = x


def sums_kernel(xc_ref, dec_ref, sums_ref, corr_ref):
    groups, rows, length = xc_ref.shape
    rows = rows // 2
    modes = dec_ref.shape[0]
    part = groups // PLANE
    paired = (
        lane_iota((length, length)) + lax.broadcasted_iota(jnp.int32, (length, length), 0) < length
    )

    def correlate(quarter, _):
        for local in range(part):
            group = quarter * part + local
            prods = jnp.where(paired, dot(xc_ref[group, :rows], xc_ref[group, rows:], TN), 0.0)
            prods = pltpu.roll(prods, 0, 1, stride=1, stride_axis=0)
            corr_ref[pl.ds(group, 1), :] = jnp.sum(prods, axis=0, keepdims=True)
        return 0

    lax.fori_loop(0, PLANE, correlate, 0)
    dec = dec_ref[...]
    lag = float(length - 1) - lane_iota((modes, length)).astype(F32)
    lane = lane_iota((modes, sums_ref.shape[1]))

    def contract(quarter, carry):
        plain, moment = carry
        for local in range(part):
            group = quarter * part + local
            terms = jnp.exp(-column(dec, group) * lag) * corr_ref[pl.ds(group, 1), :]
            plain = jnp.where(lane == group, jnp.sum(terms, axis=1, keepdims=True), plain)
            moment = jnp.where(lane == group, jnp.sum(terms * lag, axis=1, keepdims=True), moment)
        return plain, moment

    zero = jnp.zeros(lane.shape, F32)
    plain, moment = lax.fori_loop(0, PLANE, contract, (zero, zero))
    sums_ref[:modes] = plain
    sums_ref[modes:] = moment


def local_kernel(xc_ref, dec_ref, res_ref, after_ref, out_ref, taps_ref, toep_ref):
    groups, _, length = xc_ref.shape
    modes = dec_ref.shape[0]
    part = groups // PLANE
    dec, res = dec_ref[...], res_ref[...]
    ahead = lane_iota((modes, length)).astype(F32)
    later = lane_iota((length, length)) >= lax.broadcasted_iota(jnp.int32, (length, length), 0)

    def quarter_step(quarter, _):
        for local in range(part):
            group = quarter * part + local
            rate = column(dec, group)
            taps = column(res, group) * jnp.exp(-rate * ahead)
            taps_ref[group] = taps.astype(BF16)
            taps = jnp.sum(taps, axis=0, keepdims=True)
            toep = pltpu.roll(
                jnp.broadcast_to(taps, (length, length)), 0, 1, stride=1, stride_axis=0
            )
            toep_ref[local] = jnp.where(later, toep, 0.0).astype(BF16)
        for local in range(part):
            group = quarter * part + local
            out_ref[group] = dot(xc_ref[group], toep_ref[local], NN)
        return 0

    lax.fori_loop(0, PLANE, quarter_step, 0)


def split_pair(x, half):
    head = x.astype(BF16).astype(F32)
    tail = (x - head).astype(BF16).astype(F32)
    low = lane_iota(x.shape) < half
    return jnp.where(low, head, pltpu.roll(jnp.where(low, tail, 0.0), half, x.ndim - 1)).astype(BF16)


def join_pair(x, half):
    x = x.astype(F32)
    low = lane_iota(x.shape) < half
    return jnp.where(low, x + pltpu.roll(x, half, x.ndim - 1), 0.0)


def in_order(arrays, place):
    arrays, bit = list(arrays), 1
    while bit < len(arrays):
        swap = (place & bit) != 0
        new = list(arrays)
        for i in range(len(arrays)):
            new[i] = jnp.where(swap, arrays[i ^ bit], arrays[i])
        arrays, bit = new, 2 * bit
    return arrays


def advance(state, decay, gap):
    half = state.shape[2] // 2
    shifted = pltpu.roll(state, half, 2)
    return decay * (state + jnp.where(lane_iota(state.shape) >= half, gap * shifted, 0.0))


def scan_blocks(heads, tails, start, rate, gap):
    decay = jnp.exp(-rate * gap)
    state, before = start[0], []
    for head in heads:
        before.append(state)
        state = advance(state, decay, gap) + head
    other, after = start[1], []
    for tail in tails[::-1]:
        after.insert(0, other)
        other = advance(other, decay, gap) + tail
    return before, after, state, other


def pair_terms(before, tails, rate):
    half = rate.shape[2] // 2
    plain, moment = 0.0, 0.0
    for state, tail in zip(before, tails, strict=True):
        plain = plain + state * tail
        moment = moment + state * pltpu.roll(tail, half, 2)
    plain, moment = jnp.sum(plain, axis=1), jnp.sum(moment, axis=1)
    moment = moment + pltpu.roll(moment, half, 1) - pltpu.roll(plain, half, 1)
    return jnp.where(lane_iota(plain.shape) < half, plain, moment) * jnp.exp(rate[:, 0])


def spread(terms, place, acc, modes):
    quads = terms.shape[0]
    shape = (quads, acc.shape[1])
    group = lane_iota(shape) - 4 * quads * place
    row = lax.broadcasted_iota(jnp.int32, shape, 0)
    for side in range(4):
        chosen = jnp.where(group == 4 * row + side, 1.0, 0.0)
        turned = lax.dot_general(
            terms, chosen, TN, precision=lax.Precision.HIGHEST, preferred_element_type=F32
        )
        acc[:modes] += turned[side * modes : (side + 1) * modes]
        acc[modes:] += turned[(4 + side) * modes : (5 + side) * modes]


def own_rates(rate_ref, place, quads):
    rate = rate_ref[pl.ds(place * quads, quads), :]
    return rate.reshape(quads, 1, rate.shape[1])


def halves(blocks, rows):
    return [b[:, :rows] for b in blocks], [b[:, rows:] for b in blocks]


def plane_kernel(length, rate_ref, *refs):
    *msgs, sums_ref, out_ref, acc = refs
    place, _ = places()
    quads, rows, lanes = msgs[0].shape
    rows, flat = rows // 2, quads * rows
    modes = lanes // 8
    heads, tails = halves(in_order([m[...].astype(F32) for m in msgs], place), rows)
    rate = own_rates(rate_ref, place, quads)
    nothing = jnp.zeros_like(heads[0])
    before, _, head, tail = scan_blocks(heads, tails, (nothing, nothing), rate, float(length))
    both = jnp.concatenate([head, tail], axis=1)
    out_ref[:flat] = both.astype(BF16).reshape(flat, lanes)
    acc[...] = sums_ref[...]
    spread(pair_terms(before, tails, rate), place, acc, modes)
    out_ref[flat:] = split_pair(acc[...], lanes // 2)


def line_kernel(length, rate_ref, after_ref, *refs):
    count = len(refs) - 2 * PLANE - 1
    msgs, lines = refs[:PLANE], refs[PLANE : PLANE + count]
    outs, acc = refs[PLANE + count : -1], refs[-1]
    place, level = places()
    quads, rows, lanes = msgs[0].shape
    shape = (quads, rows, lanes)
    rows, flat = rows // 2, quads * rows
    modes = lanes // 8
    rate = own_rates(rate_ref, place, quads)
    heads, tails = halves(
        in_order([r[:flat].astype(F32).reshape(shape) for r in lines], level), rows
    )
    nothing = jnp.zeros_like(heads[0])
    before, after, _, _ = scan_blocks(
        heads, tails, (nothing, nothing), rate, float(PLANE * length)
    )
    total = join_pair(lines[0][flat:], lanes // 2)
    for r in lines[1:]:
        total = total + join_pair(r[flat:], lanes // 2)
    acc[...] = total
    spread(pair_terms(before, tails, rate), place, acc, modes)
    sums = split_pair(acc[...], lanes // 2)
    start = [nothing, nothing]
    for i in range(count):
        start[0] = jnp.where(level == i, before[i], start[0])
        start[1] = jnp.where(level == i, after[i], start[1])
    heads, tails = halves(in_order([m[...].astype(F32) for m in msgs], place), rows)
    before, after, _, _ = scan_blocks(heads, tails, start, rate, float(length))
    found = [jnp.concatenate(pair, axis=1) for pair in zip(before, after, strict=True)]
    found = in_order(found, place)
    low = lane_iota((quads // 2,) + shape[1:]) < lanes // 2
    for i in range(PLANE):
        packed = jnp.where(low, found[i][: quads // 2], pltpu.roll(found[i][quads // 2 :], lanes // 2, 2))
        outs[i][: flat // 2] = packed.astype(BF16).reshape(flat // 2, lanes)
        outs[i][flat // 2 :] = sums


def outputs_kernel(k_ref, v_ref, g_ref, near_ref, taps_ref, *refs):
    incoming, results = refs[:PLANE], refs[PLANE : PLANE + 3]
    outs, out_sems, cs, gs = refs[PLANE + 3 :]
    place, _ = places()
    _, rows, part, length = outs.shape[1:]
    modes = taps_ref.shape[1]
    quads = part // 4
    flat = quads * rows

    def store(which, quarter):
        return pltpu.make_async_copy(
            outs.at[which, quarter],
            results[which].at[:, pl.ds(quarter * part, part), :],
            out_sems.at[which, quarter],
        )

    mirror = mirror_of(length)
    zero = jnp.zeros((modes, length), BF16)

    def expand(quarter):
        slot = quarter % 2
        index = place ^ quarter
        state = incoming[0][:flat]
        for i in range(1, PLANE):
            state = jnp.where(index == i, incoming[i][:flat], state)
        for local in range(part):
            quad, side = local // 4, local % 4
            base = side + (4 if quad >= quads // 2 else 0)
            first = (quad % (quads // 2)) * 2 * rows
            taps = jnp.concatenate(
                [zero] * base + [taps_ref[quarter * part + local]] + [zero] * (7 - base), axis=0
            )
            both = dot(state[first : first + 2 * rows], taps, NN)
            both = both + near_ref[quarter * part + local]
            cs[slot, local // 8, pl.ds(local % 8, rows, stride=8), :] = both[:rows]
            gs[slot, local // 8, pl.ds(local % 8, rows, stride=8), :] = both[rows:]

    def finish(quarter):
        slot = quarter % 2
        shape = (rows, part, length)
        own = pl.ds(quarter * part, part)
        conv, ig = (
            jnp.concatenate(
                [ref[slot, i].reshape(rows, 8, length) for i in range(part // 8)], axis=1
            ).astype(BF16)
            for ref in (cs, gs)
        )
        ig = dot(ig.reshape(rows * part, length), mirror, NN).reshape(shape)
        outs[0, quarter] = product(g_ref[:, own, :], conv)
        outs[1, quarter] = product(ig, v_ref[:, own, :])
        outs[2, quarter] = product(ig, k_ref[:, own, :])
        for which in range(3):
            store(which, quarter).start()

    for quarter in range(PLANE + 1):
        if quarter < PLANE:
            expand(quarter)
        if quarter > 0:
            finish(quarter - 1)
    for quarter in range(PLANE):
        for which in range(3):
            store(which, quarter).wait()


def per_device(queries, keys_in, values_in, grad_out, residue, decay_rate):
    chans, length = queries.shape
    groups, modes = residue.shape
    count = lax.axis_size("ctx")
    tp = lax.axis_size("tp")
    depth = count // PLANE
    rows = chans // groups
    part = groups // PLANE
    quads = part // 4
    lanes = 8 * modes

    def cube(x):
        return x.reshape(rows, groups, length)

    query, key, value, grad = cube(queries), cube(keys_in), cube(values_in), cube(grad_out)
    decay, resid = decay_rate.T, residue.T
    vmem = pl.BlockSpec(memory_space=pltpu.VMEM)
    anywhere = pl.BlockSpec(memory_space=pltpu.HBM)

    def shaped(shape, dtype):
        return jax.ShapeDtypeStruct(shape, dtype)

    def call(kernel, name, in_specs, out_specs, out_shape, scratch, flops, size):
        return pl.pallas_call(
            kernel,
            in_specs=in_specs,
            out_specs=out_specs,
            out_shape=out_shape,
            scratch_shapes=scratch,
            cost_estimate=pl.CostEstimate(flops=flops, bytes_accessed=size, transcendentals=0),
            compiler_params=pltpu.CompilerParams(vmem_limit_bytes=16 * 2**20),
            name=name,
        )

    grouped = shaped((groups, 2 * rows, length), BF16)
    block = shaped((quads, 2 * rows, lanes), BF16)
    xc, rates, *own = call(
        states_kernel,
        "states",
        [anywhere] * 5,
        [vmem] * (2 + PLANE),
        [grouped, shaped((groups // 4, lanes), F32)] + [block] * PLANE,
        [
            pltpu.VMEM((modes, groups), F32),
            pltpu.SemaphoreType.DMA,
            pltpu.VMEM((4, PLANE, rows, part, length), BF16),
            pltpu.SemaphoreType.DMA((4, PLANE)),
            pltpu.VMEM((groups, 2, modes, length), BF16),
            pltpu.VMEM((2, part // 8, rows * 8, length), F32),
            pltpu.VMEM((2, part // 8, rows * 8, length), F32),
            pltpu.VMEM((PLANE, quads, 2 * rows, lanes), BF16),
        ],
        10**9,
        4 * 10**6,
    )(*(pltpu.with_memory_space_constraint(x, pltpu.HBM) for x in (decay, key, value, grad, query)))

    def swap(x, bits):
        return lax.ppermute(x, "ctx", [(i, i ^ bits) for i in range(count)])

    near = [own[0]] + [swap(own[i], i) for i in range(1, PLANE)]
    sums = call(
        sums_kernel,
        "sums",
        [vmem] * 2,
        vmem,
        shaped((2 * modes, lanes), F32),
        [pltpu.VMEM((groups, length), F32)],
        10**9,
        4 * 10**6,
    )(xc, decay)
    flat = quads * 2 * rows
    plane = call(
        functools.partial(plane_kernel, length),
        "plane",
        [vmem] * (2 + PLANE),
        vmem,
        shaped((flat + 2 * modes, lanes), BF16),
        [pltpu.VMEM((2 * modes, lanes), F32)],
        10**7,
        10**6,
    )(rates, *near, sums)
    line = [plane] + [swap(plane, PLANE * i) for i in range(1, depth)]
    table = shaped((groups, modes, length), BF16)
    near_part, taps = call(
        local_kernel,
        "local",
        [vmem] * 4,
        [vmem] * 2,
        [shaped((groups, 2 * rows, length), F32), table],
        [pltpu.VMEM((part, length, length), BF16)],
        10**9,
        4 * 10**6,
    )(xc, decay, resid, plane)
    back = call(
        functools.partial(line_kernel, length),
        "line",
        [vmem] * (2 + PLANE + depth),
        [vmem] * PLANE,
        [shaped((flat // 2 + 2 * modes, lanes), BF16)] * PLANE,
        [pltpu.VMEM((2 * modes, lanes), F32)],
        10**7,
        10**6,
    )(rates, taps, *near, *line)
    back = [back[0]] + [swap(back[i], i) for i in range(1, PLANE)]

    total = sum(
        b[flat // 2 :, : lanes // 2].astype(F32) + b[flat // 2 :, lanes // 2 :].astype(F32)
        for b in back
    )
    bit = 1
    while bit < tp:
        total = total + lax.ppermute(total, "tp", [(i, i ^ bit) for i in range(tp)])
        bit *= 2

    outs = call(
        outputs_kernel,
        "outputs",
        [vmem] * (5 + PLANE),
        [anywhere] * 3,
        [shaped((rows, groups, length), BF16)] * 3,
        [
            pltpu.VMEM((3, PLANE, rows, part, length), BF16),
            pltpu.SemaphoreType.DMA((3, PLANE)),
            pltpu.VMEM((2, part // 8, rows * 8, length), F32),
            pltpu.VMEM((2, part // 8, rows * 8, length), F32),
        ],
        10**9,
        5 * 10**6,
    )(key, value, grad, near_part, taps, *back)
    tokens = count * length
    plain, moment = total[:modes, :groups], total[modes:, :groups]
    return (
        outs[0].reshape(chans, length),
        outs[1].reshape(chans, length),
        outs[2].reshape(chans, length),
        (plain / tokens).T,
        (-(resid * decay) * moment / tokens).T,
    )


def solution(mesh):
    in_specs = (P("tp", "ctx"), P("tp", "ctx"), P("tp", "ctx"), P("tp", "ctx"), P(), P())
    out_specs = (P("tp", "ctx"), P("tp", "ctx"), P("tp", "ctx"), P(), P())
    return jax.shard_map(
        per_device, mesh=mesh, in_specs=in_specs, out_specs=out_specs, check_vma=False
    )
```

time: 36.8 us -> 34.5 us (0.938)
  Pallas kernels: 17.7 us -> 15.5 us
    pallas_call x4, Pallas kernels: 16.1 us -> 13.7 us  [the longest x1 5.08 us: per_device(): call(local_kernel, 'local', [vmem] * 4, [vmem] * 2, [shaped((groups, 2 *...]
  transfers between devices with their start and end apart: 10 -> 10, of which waited for: 4 -> 4; matrix products, arithmetic and copies ran while one was open for 0% -> 0% of each run, Pallas kernels for 31% -> 29%
where the time goes in v4:
time: 34.5 us; the launch traced here: 34.4 us
  Pallas kernels  15.5 us (45%)
  starting transfers between devices  12.5 us (36%)
  waiting for transfers between devices  4.91 us (14%)
  between operations  0.77 us (2%)
  other arithmetic  0.69 us (2%)
    ppermute x9, starting transfers between devices, swap(): return lax.ppermute(x, 'ctx', [(i, i ^ bits) for i in range(count)])  12.5 us
    pallas_call x1, Pallas kernels, per_device(): call(local_kernel, 'local', [vmem] * 4, [vmem] * 2, [shaped((groups, 2 *...  5.08 us
    ppermute x9, waiting for transfers between devices, swap(): return lax.ppermute(x, 'ctx', [(i, i ^ bits) for i in range(count)])  4.91 us
    pallas_call x1, Pallas kernels, per_device(): call(states_kernel, 'states', [anywhere] * 5, [vmem] * (2 + PLANE), [grou...  3.61 us
    pallas_call x1, Pallas kernels, per_device(): call(sums_kernel, 'sums', [vmem] * 2, vmem, shaped((2 * modes, lanes), F3...  3.12 us
    pallas_call x1, Pallas kernels, per_device(): call(outputs_kernel, 'outputs', [vmem] * (5 + PLANE), [anywhere] * 3, [sh...  1.93 us
    pallas_call x1, Pallas kernels, per_device(): call(functools.partial(line_kernel, length), 'line', [vmem] * (2 + PLANE...  0.92 us
    pallas_call x1, Pallas kernels, per_device(): call(functools.partial(plane_kernel, length), 'plane', [vmem] * (2 + PLAN...  0.81 us
  transfers between devices with their start and end apart: 10, of which 4 were waited for; matrix products, arithmetic and copies ran while one was open for 0% of the time, Pallas kernels for 29%

profile of v4, /device:TPU:0, one launch (start us, length us, event | category | flops | bytes accessed | tf_op | source)
XLA Modules:
  0.0 34.4 jit_solution(15535137822930765612)
XLA Ops:
  0.6 3.6 %states.1 = (bf16[64,64,128]{2,1,0:T(8,128)(2,1)S(1)}, f32[16,128]{1,0:T(8,128)S(1)}, bf16[4,64,128]{2,1,0:T(8,128)(2,1)S(1)}, bf16[4,64,128]{2,1,0:T(8,128)(2,1...) custom-call(f32[16,64]{1,0:T(8,128)} %bitcast.21, bf16[32,64,128]{2,1,0:T(8,128)(2,1)} %bitcast.15, ...), custom_call_target="tpu_custom_call" | custom-call | flops 1000000000 | bytes 4000000 | tf_op jit(solution)/shard_map/states/pallas_call | solution.py:429
  4.3 0.0 copy-start.4
  4.3 3.0 %collective-permute-start = (bf16[4,64,128]{2,1,0:T(8,128)(2,1)S(1)}, bf16[4,64,128]{2,1,0:T(8,128)(2,1)S(1)}, u32[]{:S(2)}, u32[]{:S(2)}) collective-permute-start(bf16[4,64,128]{2,1,0:T(8,128)(2,1)S(1)} %get-tuple-element.23), channel_id=1, source_target_pairs={{0,2},{2,0},{4,6},{6,4},{8,10},{10,8},{12,14},{14,12},{16,18},{18,... | collective-permute-start | bytes 196616 | tf_op jit(solution)/shard_map/ppermute | solution.py:450
  7.3 1.5 %collective-permute-start.1 = (bf16[4,64,128]{2,1,0:T(8,128)(2,1)S(1)}, bf16[4,64,128]{2,1,0:T(8,128)(2,1)S(1)}, u32[]{:S(2)}, u32[]{:S(2)}) collective-permute-start(bf16[4,64,128]{2,1,0:T(8,128)(2,1)S(1)} %get-tuple-element.24), channel_id=1, source_target_pairs={{0,4},{2,6},{4,0},{6,2},{8,12},{10,14},{12,8},{14,10},{16,20},{18,... | collective-permute-start | bytes 196616 | tf_op jit(solution)/shard_map/ppermute | solution.py:450
  8.8 0.0 collective-permute-start.2
  8.8 3.1 %sums.1.refs_4_ = f32[32,128]{1,0:T(8,128)S(1)} custom-call(bf16[64,64,128]{2,1,0:T(8,128)(2,1)S(1)} %get-tuple-element.20.xc_ref, f32[16,64]{1,0:T(8,128)S(1)} %bitcast.22), custom_call_target="tpu_custom_call" | custom-call | flops 1000000000 | bytes 4000000 | tf_op jit(solution)/shard_map/sums/pallas_call | solution.py:453
  12.0 0.0 collective-permute-done.refs_1_
  12.0 0.0 collective-permute-done.1.refs_2_
  12.0 2.0 %collective-permute-done.2.refs_3_ = bf16[4,64,128]{2,1,0:T(8,128)(2,1)S(1)} collective-permute-done((bf16[4,64,128]{2,1,0:T(8,128)(2,1)S(1)}, bf16[4,64,128]{2,1,0:T(8,128)(2,1)S(1)}, u32[]{:S(2)}, u32[]{:S(2)}) %collective-permute-start.2) | collective-permute-done | bytes 65568 | tf_op jit(solution)/shard_map/ppermute | solution.py:450
  14.0 0.8 %plane.1.after_ref.refs_4_ = bf16[288,128]{1,0:T(8,128)(2,1)S(1)} custom-call(f32[16,128]{1,0:T(8,128)S(1)} %get-tuple-element.21.rate_ref, bf16[4,64,128]{2,1,0:T(8,128)(2,1)S(1)} %get-tuple-element.22.refs_0_, bf16[4,64,128]{2,1,0:T(8,128)(2,1)S(1)} %collective-permute-done.refs_1_, bf16[4,64,128]{2,1,0:T(8,128)(2,1)S(1)} %collective-permute-done.1.refs_2_, ...), custom_call_target="tpu_custom_call" | custom-call | flops 10000000 | bytes 1000000 | tf_op jit(solution)/shard_map/plane/pallas_call | solution.py:464
  14.8 3.6 %collective-permute-start.5 = (bf16[288,128]{1,0:T(8,128)(2,1)S(1)}, bf16[288,128]{1,0:T(8,128)(2,1)S(1)}, u32[]{:S(2)}, u32[]{:S(2)}) collective-permute-start(bf16[288,128]{1,0:T(8,128)(2,1)S(1)} %plane.1.after_ref.refs_4_), channel_id=1, source_target_pairs={{0,24},{2,26},{4,28},{6,30},{8,16},{10,18},{12,20},{14,22},{16,8},... | collective-permute-start | bytes 221192 | tf_op jit(solution)/shard_map/ppermute | solution.py:450
  18.4 0.8 %collective-permute-start.3 = (bf16[288,128]{1,0:T(8,128)(2,1)S(1)}, bf16[288,128]{1,0:T(8,128)(2,1)S(1)}, u32[]{:S(2)}, u32[]{:S(2)}) collective-permute-start(bf16[288,128]{1,0:T(8,128)(2,1)S(1)} %plane.1.after_ref.refs_4_), channel_id=1, source_target_pairs={{0,8},{2,10},{4,12},{6,14},{8,0},{10,2},{12,4},{14,6},{16,24},{18,... | collective-permute-start | bytes 221192 | tf_op jit(solution)/shard_map/ppermute | solution.py:450
  19.2 5.1 %local.1 = (f32[64,64,128]{2,1,0:T(8,128)S(1)}, bf16[64,16,128]{2,1,0:T(8,128)(2,1)S(1)}) custom-call(bf16[64,64,128]{2,1,0:T(8,128)(2,1)S(1)} %get-tuple-element.20.xc_ref, f32[16,64]{1,0:T(8,128)S(1)} %bitcast.23, f32[16,64]{1,0:T(8,128)S(1)} %bitcast.24, bf16[288,128]{1,0:T(8,128)(2,1)S(1)} %plane.1.after_ref.refs_4_), custom_call_target="tpu_custom_call" | custom-call | flops 1000000000 | bytes 4000000 | tf_op jit(solution)/shard_map/local/pallas_call | solution.py:476
  24.3 0.9 %line.1 = (bf16[160,128]{1,0:T(8,128)(2,1)S(1)}, bf16[160,128]{1,0:T(8,128)(2,1)S(1)}, bf16[160,128]{1,0:T(8,128)(2,1)S(1)}, bf16[160,128]{1,0:T(8,128)(2,1)S(1)}) custom-call(f32[16,128]{1,0:T(8,128)S(1)} %get-tuple-element.21.rate_ref, bf16[64,16,128]{2,1,0:T(8,128)(2,1)S(1)} %get-tuple-element.27.after_ref.taps_ref, ...), custom_call_target="tpu_custom_call" | custom-call | flops 10000000 | bytes 1000000 | tf_op jit(solution)/shard_map/line/pallas_call | solution.py:486
  25.2 0.6 %collective-permute-start.6 = (bf16[160,128]{1,0:T(8,128)(2,1)S(1)}, bf16[160,128]{1,0:T(8,128)(2,1)S(1)}, u32[]{:S(2)}, u32[]{:S(2)}) collective-permute-start(bf16[160,128]{1,0:T(8,128)(2,1)S(1)} %get-tuple-element.29), channel_id=1, source_target_pairs={{0,2},{2,0},{4,6},{6,4},{8,10},{10,8},{12,14},{14,12},{16,18},{18,... | collective-permute-start | bytes 122888 | tf_op jit(solution)/shard_map/ppermute | solution.py:450
  25.8 1.0 %collective-permute-start.7 = (bf16[160,128]{1,0:T(8,128)(2,1)S(1)}, bf16[160,128]{1,0:T(8,128)(2,1)S(1)}, u32[]{:S(2)}, u32[]{:S(2)}) collective-permute-start(bf16[160,128]{1,0:T(8,128)(2,1)S(1)} %get-tuple-element.30), channel_id=1, source_target_pairs={{0,4},{2,6},{4,0},{6,2},{8,12},{10,14},{12,8},{14,10},{16,20},{18,... | collective-permute-start | bytes 122888 | tf_op jit(solution)/shard_map/ppermute | solution.py:450
  26.8 2.0 %collective-permute-start.8 = (bf16[160,128]{1,0:T(8,128)(2,1)S(1)}, bf16[160,128]{1,0:T(8,128)(2,1)S(1)}, u32[]{:S(2)}, u32[]{:S(2)}) collective-permute-start(bf16[160,128]{1,0:T(8,128)(2,1)S(1)} %get-tuple-element.31), channel_id=1, source_target_pairs={{0,6},{2,4},{4,2},{6,0},{8,14},{10,12},{12,10},{14,8},{16,22},{18,... | collective-permute-start | bytes 122888 | tf_op jit(solution)/shard_map/ppermute | solution.py:450
  28.8 0.5 %collective-permute-done.6.refs_1_ = bf16[160,128]{1,0:T(8,128)(2,1)S(1)} collective-permute-done((bf16[160,128]{1,0:T(8,128)(2,1)S(1)}, bf16[160,128]{1,0:T(8,128)(2,1)S(1)}, u32[]{:S(2)}, u32[]{:S(2)}) %collective-permute-start.6) | collective-permute-done | bytes 40992 | tf_op jit(solution)/shard_map/ppermute | solution.py:450
  29.3 0.8 %collective-permute-done.7.refs_2_ = bf16[160,128]{1,0:T(8,128)(2,1)S(1)} collective-permute-done((bf16[160,128]{1,0:T(8,128)(2,1)S(1)}, bf16[160,128]{1,0:T(8,128)(2,1)S(1)}, u32[]{:S(2)}, u32[]{:S(2)}) %collective-permute-start.7) | collective-permute-done | bytes 40992 | tf_op jit(solution)/shard_map/ppermute | solution.py:450
  30.1 1.6 %collective-permute-done.8.refs_3_ = bf16[160,128]{1,0:T(8,128)(2,1)S(1)} collective-permute-done((bf16[160,128]{1,0:T(8,128)(2,1)S(1)}, bf16[160,128]{1,0:T(8,128)(2,1)S(1)}, u32[]{:S(2)}, u32[]{:S(2)}) %collective-permute-start.8) | collective-permute-done | bytes 40992 | tf_op jit(solution)/shard_map/ppermute | solution.py:450
  31.7 0.1 add_add_fusion
  31.8 0.0 collective-permute-start.9
  31.8 1.9 %outputs.1 = (bf16[32,64,128]{2,1,0:T(8,128)(2,1)}, bf16[32,64,128]{2,1,0:T(8,128)(2,1)}, bf16[32,64,128]{2,1,0:T(8,128)(2,1)}) custom-call(bf16[32,64,128]{2,1,0:T(8,128)(2,1)S(1)} %bitcast.16, bf16[32,64,128]{2,1,0:T(8,128)(2,1)S(1)} %bitcast.18, bf16[32,64,128]{2,1,0:T(8,128)(2,1)S(1)} %bitcast.20, f32[64,64,128]{2,1,0:T(8,128)S(1)} %get-tuple-element.26.near_ref, ...), custom_call_target="tpu_custom_call" | custom-call | flops 1000000000 | bytes 5000000 | tf_op jit(solution)/shard_map/outputs/pallas_call | solution.py:507
  33.8 0.6 %fusion.1 = (f32[64,16]{0,1:T(8,128)}, f32[64,16]{0,1:T(8,128)}) fusion(f32[32,64]{1,0:T(8,128)S(1)} %add.31, f32[64,16]{0,1:T(8,128)S(1)} %copy-done.4, f32[64,16]{0,1:T(8,128)S(1)} %copy-done.3), kind=kLoop, calls=%fused_computation.3 | loop fusion | flops 5120 | bytes 24576 | tf_op jit(solution)/shard_map/transpose | solution.py:529
  (15 shorter events, 0.0 us)
Async XLA Ops:
  0.6 8.2 %copy-start.3 = (f32[64,16]{0,1:T(8,128)S(1)}, f32[64,16]{0,1:T(8,128)}, u32[]{:S(2)}) copy-start(f32[64,16]{0,1:T(8,128)} %param.11) | copy-start | bytes 12292
  4.3 14.9 %copy-start.4 = (f32[64,16]{0,1:T(8,128)S(1)}, f32[64,16]{0,1:T(8,128)}, u32[]{:S(2)}) copy-start(f32[64,16]{0,1:T(8,128)} %param.10) | copy-start | bytes 12292
  4.3 7.7 %collective-permute-start = (bf16[4,64,128]{2,1,0:T(8,128)(2,1)S(1)}, bf16[4,64,128]{2,1,0:T(8,128)(2,1)S(1)}, u32[]{:S(2)}, u32[]{:S(2)}) collective-permute-start(bf16[4,64,128]{2,1,0:T(8,128)(2,1)S(1)} %get-tuple-element.23), channel_id=1, source_target_pairs={{0,2},{2,0},{4,6},{6,4},{8,10},{10,8},{12,14},{14,12},{16,18},{18,... | collective-permute-start | bytes 196616 | tf_op jit(solution)/shard_map/ppermute | solution.py:450
  7.3 4.7 %collective-permute-start.1 = (bf16[4,64,128]{2,1,0:T(8,128)(2,1)S(1)}, bf16[4,64,128]{2,1,0:T(8,128)(2,1)S(1)}, u32[]{:S(2)}, u32[]{:S(2)}) collective-permute-start(bf16[4,64,128]{2,1,0:T(8,128)(2,1)S(1)} %get-tuple-element.24), channel_id=1, source_target_pairs={{0,4},{2,6},{4,0},{6,2},{8,12},{10,14},{12,8},{14,10},{16,20},{18,... | collective-permute-start | bytes 196616 | tf_op jit(solution)/shard_map/ppermute | solution.py:450
  8.8 5.2 %collective-permute-start.2 = (bf16[4,64,128]{2,1,0:T(8,128)(2,1)S(1)}, bf16[4,64,128]{2,1,0:T(8,128)(2,1)S(1)}, u32[]{:S(2)}, u32[]{:S(2)}) collective-permute-start(bf16[4,64,128]{2,1,0:T(8,128)(2,1)S(1)} %get-tuple-element.25), channel_id=1, source_target_pairs={{0,6},{2,4},{4,2},{6,0},{8,14},{10,12},{12,10},{14,8},{16,22},{18,... | collective-permute-start | bytes 196616 | tf_op jit(solution)/shard_map/ppermute | solution.py:450
  14.8 9.5 %collective-permute-start.5 = (bf16[288,128]{1,0:T(8,128)(2,1)S(1)}, bf16[288,128]{1,0:T(8,128)(2,1)S(1)}, u32[]{:S(2)}, u32[]{:S(2)}) collective-permute-start(bf16[288,128]{1,0:T(8,128)(2,1)S(1)} %plane.1.after_ref.refs_4_), channel_id=1, source_target_pairs={{0,24},{2,26},{4,28},{6,30},{8,16},{10,18},{12,20},{14,22},{16,8},... | collective-permute-start | bytes 221192 | tf_op jit(solution)/shard_map/ppermute | solution.py:450
  18.4 5.9 %collective-permute-start.4 = (bf16[288,128]{1,0:T(8,128)(2,1)S(1)}, bf16[288,128]{1,0:T(8,128)(2,1)S(1)}, u32[]{:S(2)}, u32[]{:S(2)}) collective-permute-start(bf16[288,128]{1,0:T(8,128)(2,1)S(1)} %plane.1.after_ref.refs_4_), channel_id=1, source_target_pairs={{0,16},{2,18},{4,20},{6,22},{8,24},{10,26},{12,28},{14,30},{16,0},... | collective-permute-start | bytes 221192 | tf_op jit(solution)/shard_map/ppermute | solution.py:450
  18.4 5.9 %collective-permute-start.3 = (bf16[288,128]{1,0:T(8,128)(2,1)S(1)}, bf16[288,128]{1,0:T(8,128)(2,1)S(1)}, u32[]{:S(2)}, u32[]{:S(2)}) collective-permute-start(bf16[288,128]{1,0:T(8,128)(2,1)S(1)} %plane.1.after_ref.refs_4_), channel_id=1, source_target_pairs={{0,8},{2,10},{4,12},{6,14},{8,0},{10,2},{12,4},{14,6},{16,24},{18,... | collective-permute-start | bytes 221192 | tf_op jit(solution)/shard_map/ppermute | solution.py:450
  19.2 12.6 %copy-start = (bf16[2048,128]{1,0:T(8,128)(2,1)S(1)}, bf16[2048,128]{1,0:T(8,128)(2,1)}, u32[]{:S(2)}) copy-start(bf16[2048,128]{1,0:T(8,128)(2,1)} %param.7) | copy-start | bytes 1572868
  19.2 12.6 %copy-start.1 = (bf16[2048,128]{1,0:T(8,128)(2,1)S(1)}, bf16[2048,128]{1,0:T(8,128)(2,1)}, u32[]{:S(2)}) copy-start(bf16[2048,128]{1,0:T(8,128)(2,1)} %param.8) | copy-start | bytes 1572868
  19.2 12.6 %copy-start.2 = (bf16[2048,128]{1,0:T(8,128)(2,1)S(1)}, bf16[2048,128]{1,0:T(8,128)(2,1)}, u32[]{:S(2)}) copy-start(bf16[2048,128]{1,0:T(8,128)(2,1)} %param.9) | copy-start | bytes 1572868
  25.2 4.1 %collective-permute-start.6 = (bf16[160,128]{1,0:T(8,128)(2,1)S(1)}, bf16[160,128]{1,0:T(8,128)(2,1)S(1)}, u32[]{:S(2)}, u32[]{:S(2)}) collective-permute-start(bf16[160,128]{1,0:T(8,128)(2,1)S(1)} %get-tuple-element.29), channel_id=1, source_target_pairs={{0,2},{2,0},{4,6},{6,4},{8,10},{10,8},{12,14},{14,12},{16,18},{18,... | collective-permute-start | bytes 122888 | tf_op jit(solution)/shard_map/ppermute | solution.py:450
  25.8 4.3 %collective-permute-start.7 = (bf16[160,128]{1,0:T(8,128)(2,1)S(1)}, bf16[160,128]{1,0:T(8,128)(2,1)S(1)}, u32[]{:S(2)}, u32[]{:S(2)}) collective-permute-start(bf16[160,128]{1,0:T(8,128)(2,1)S(1)} %get-tuple-element.30), channel_id=1, source_target_pairs={{0,4},{2,6},{4,0},{6,2},{8,12},{10,14},{12,8},{14,10},{16,20},{18,... | collective-permute-start | bytes 122888 | tf_op jit(solution)/shard_map/ppermute | solution.py:450
  26.8 4.9 %collective-permute-start.8 = (bf16[160,128]{1,0:T(8,128)(2,1)S(1)}, bf16[160,128]{1,0:T(8,128)(2,1)S(1)}, u32[]{:S(2)}, u32[]{:S(2)}) collective-permute-start(bf16[160,128]{1,0:T(8,128)(2,1)S(1)} %get-tuple-element.31), channel_id=1, source_target_pairs={{0,6},{2,4},{4,2},{6,0},{8,14},{10,12},{12,10},{14,8},{16,22},{18,... | collective-permute-start | bytes 122888 | tf_op jit(solution)/shard_map/ppermute | solution.py:450
  31.8 2.0 %collective-permute-start.9 = (f32[32,64]{1,0:T(8,128)S(1)}, f32[32,64]{1,0:T(8,128)S(1)}, u32[]{:S(2)}, u32[]{:S(2)}) collective-permute-start(f32[32,64]{1,0:T(8,128)S(1)} %add_add_fusion), channel_id=1, source_target_pairs={{0,1},{1,0},{2,3},{3,2},{4,5},{5,4},{6,7},{7,6},{8,9},{9,8},{10,11... | collective-permute-start | bytes 24584 | tf_op jit(solution)/shard_map/ppermute | solution.py:504

commit v5 on v4

--- a/solution.py
+++ b/solution.py
@@ -42,28 +42,69 @@
     return lax.broadcasted_iota(jnp.int32, shape, len(shape) - 1)
 
 
-def states_kernel(dec_hbm, k_hbm, v_hbm, g_hbm, q_hbm, xc_ref, rate_ref, *rest):
-    outs, rest = rest[:PLANE], rest[PLANE:]
-    dec_ref, dec_sem, bufs, sems, w_ref, gs, cs, st_ref = rest
+class Reducer:
+    def __init__(self, sources, bufs, sems, w_ref, gs, cs):
+        self.sources, self.bufs, self.sems, self.w_ref, self.gs, self.cs = (
+            sources, bufs, sems, w_ref, gs, cs
+        )
+        _, self.rows, self.part, self.length = bufs.shape[1:]
+        self.mirror = mirror_of(self.length)
+
+    def copies(self, slot, quarter):
+        return [
+            pltpu.make_async_copy(
+                source.at[:, pl.ds(pl.multiple_of(quarter * self.part, self.part), self.part), :],
+                self.bufs.at[which, slot],
+                self.sems.at[which, slot],
+            )
+            for which, source in enumerate(self.sources)
+        ]
+
+    def load(self, slot, quarter):
+        for copy in self.copies(slot, quarter):
+            copy.wait()
+        bufs, flat = self.bufs, self.rows * self.part
+        x = product(bufs[0, slot], bufs[1, slot]).astype(F32)
+        c = product(bufs[2, slot], bufs[3, slot]).reshape(flat, self.length)
+        c = dot(c, self.mirror, NN).reshape(x.shape)
+        for eight in range(self.part // 8):
+            span = slice(8 * eight, 8 * eight + 8)
+            self.gs[slot, eight] = x[:, span].reshape(8 * self.rows, self.length)
+            self.cs[slot, eight] = c[:, span].reshape(8 * self.rows, self.length)
+
+    def reduce(self, slot, quarter, xc_ref, out_ref):
+        zero = jnp.zeros(self.w_ref.shape[2:], BF16)
+        for quad in range(self.part // 4):
+            left, right = [], []
+            for side in range(4):
+                local = 4 * quad + side
+                group = quarter * self.part + local
+                where = pl.ds(local % 8, self.rows, stride=8)
+                both = jnp.concatenate(
+                    [ref[slot, local // 8, where, :] for ref in (self.gs, self.cs)], axis=0
+                ).astype(BF16)
+                xc_ref[local] = both
+                w = [zero] * 8
+                w[side], w[4 + side] = self.w_ref[group, 0], self.w_ref[group, 1]
+                left.append(both)
+                right.append(jnp.concatenate(w, axis=0))
+            out_ref[quad] = dot(
+                jnp.concatenate(left, axis=1), jnp.concatenate(right, axis=1), NT
+            ).astype(BF16)
+
+
+def states_kernel(dec_hbm, k_hbm, v_hbm, g_hbm, q_hbm, xc_ref, w_ref, rate_ref, *rest):
+    outs, rest = rest[: PLANE - 1], rest[PLANE - 1 :]
+    dec_ref, dec_sem, bufs, sems, gs, cs = rest
     place, _ = places()
-    _, rows, part, length = bufs.shape[1:]
     modes, groups = dec_ref.shape
-    quads = part // 4
-    flat = rows * part
-    sources = (k_hbm, v_hbm, g_hbm, q_hbm)
-
-    def copy(which, quarter):
-        return pltpu.make_async_copy(
-            sources[which].at[:, pl.ds(quarter * part, part), :],
-            bufs.at[which, quarter],
-            sems.at[which, quarter],
-        )
-
+    work = Reducer((k_hbm, v_hbm, g_hbm, q_hbm), bufs, sems, w_ref, gs, cs)
+    length = work.length
     rates_in = pltpu.make_async_copy(dec_hbm, dec_ref, dec_sem)
     rates_in.start()
-    for quarter in range(PLANE):
-        for which in range(4):
-            copy(which, quarter).start()
+    for slot in range(PLANE - 1):
+        for copy in work.copies(slot, place ^ (slot + 1)):
+            copy.start()
     rates_in.wait()
     dec = dec_ref[...]
     behind = float(length) - lane_iota((modes, length)).astype(F32)
@@ -83,71 +124,40 @@
         return 0
 
     lax.fori_loop(0, groups // 4, weights, 0, unroll=4)
-    mirror = mirror_of(length)
-    zero = jnp.zeros((modes, length), BF16)
-
-    def load(quarter):
-        for which in range(4):
-            copy(which, quarter).wait()
-        slot = quarter % 2
-        x = product(bufs[0, quarter], bufs[1, quarter]).astype(F32)
-        c = product(bufs[2, quarter], bufs[3, quarter]).reshape(flat, length)
-        c = dot(c, mirror, NN).reshape(x.shape)
-        for part8 in range(part // 8):
-            gs[slot, part8] = x[:, 8 * part8 : 8 * part8 + 8].reshape(8 * rows, length)
-            cs[slot, part8] = c[:, 8 * part8 : 8 * part8 + 8].reshape(8 * rows, length)
-
-    def reduce(quarter):
-        slot = quarter % 2
-        for quad in range(quads):
-            left, right = [], []
-            for side in range(4):
-                local = 4 * quad + side
-                group = quarter * part + local
-                both = jnp.concatenate(
-                    [
-                        gs[slot, local // 8, pl.ds(local % 8, rows, stride=8), :],
-                        cs[slot, local // 8, pl.ds(local % 8, rows, stride=8), :],
-                    ],
-                    axis=0,
-                ).astype(BF16)
-                xc_ref[group] = both
-                w = [zero] * 8
-                w[side], w[4 + side] = w_ref[group, 0], w_ref[group, 1]
-                left.append(both)
-                right.append(jnp.concatenate(w, axis=0))
-            st_ref[quarter, quad] = dot(
-                jnp.concatenate(left, axis=1), jnp.concatenate(right, axis=1), NT
-            ).astype(BF16)
-
-    for quarter in range(PLANE + 1):
-        if quarter < PLANE:
-            load(quarter)
-        if quarter > 0:
-            reduce(quarter - 1)
-    for quad in range(quads):
-        for index, x in enumerate(in_order([st_ref[i, quad] for i in range(PLANE)], place)):
-            outs[index][quad] = x
-
-
-def sums_kernel(xc_ref, dec_ref, sums_ref, corr_ref):
-    groups, rows, length = xc_ref.shape
+    for slot in range(PLANE):
+        if slot < PLANE - 1:
+            work.load(slot, place ^ (slot + 1))
+        if slot > 0:
+            work.reduce(slot - 1, place ^ slot, xc_ref.at[slot - 1], outs[slot - 1])
+
+
+def sums_kernel(k_hbm, v_hbm, g_hbm, q_hbm, xc_ref, w_ref, dec_ref, own_ref, out_ref, sums_ref, *rest):
+    bufs, sems, gs, cs, corr_ref = rest
+    place, _ = places()
+    work = Reducer((k_hbm, v_hbm, g_hbm, q_hbm), bufs, sems, w_ref, gs, cs)
+    for copy in work.copies(0, place):
+        copy.start()
+    _, part, rows, length = xc_ref.shape
     rows = rows // 2
     modes = dec_ref.shape[0]
-    part = groups // PLANE
     paired = (
         lane_iota((length, length)) + lax.broadcasted_iota(jnp.int32, (length, length), 0) < length
     )
 
-    def correlate(quarter, _):
+    def correlate(ref, base):
         for local in range(part):
-            group = quarter * part + local
-            prods = jnp.where(paired, dot(xc_ref[group, :rows], xc_ref[group, rows:], TN), 0.0)
+            prods = jnp.where(paired, dot(ref[local, :rows], ref[local, rows:], TN), 0.0)
             prods = pltpu.roll(prods, 0, 1, stride=1, stride_axis=0)
-            corr_ref[pl.ds(group, 1), :] = jnp.sum(prods, axis=0, keepdims=True)
+            corr_ref[pl.ds(base + local, 1), :] = jnp.sum(prods, axis=0, keepdims=True)
+
+    def others(slot, _):
+        correlate(xc_ref.at[slot], part * (place ^ (slot + 1)))
         return 0
 
-    lax.fori_loop(0, PLANE, correlate, 0)
+    lax.fori_loop(0, PLANE - 1, others, 0)
+    work.load(0, place)
+    work.reduce(0, place, own_ref, out_ref)
+    correlate(own_ref, part * place)
     dec = dec_ref[...]
     lag = float(length - 1) - lane_iota((modes, length)).astype(F32)
     lane = lane_iota((modes, sums_ref.shape[1]))
@@ -167,31 +177,34 @@
     sums_ref[modes:] = moment
 
 
-def local_kernel(xc_ref, dec_ref, res_ref, after_ref, out_ref, taps_ref, toep_ref):
-    groups, _, length = xc_ref.shape
+def local_kernel(own_ref, xc_ref, dec_ref, res_ref, after_ref, out_ref, taps_ref, toep_ref):
+    _, part, _, length = xc_ref.shape
     modes = dec_ref.shape[0]
-    part = groups // PLANE
+    place, _ = places()
     dec, res = dec_ref[...], res_ref[...]
     ahead = lane_iota((modes, length)).astype(F32)
     later = lane_iota((length, length)) >= lax.broadcasted_iota(jnp.int32, (length, length), 0)
 
-    def quarter_step(quarter, _):
+    def convolve(index, ref):
         for local in range(part):
-            group = quarter * part + local
-            rate = column(dec, group)
-            taps = column(res, group) * jnp.exp(-rate * ahead)
-            taps_ref[group] = taps.astype(BF16)
+            group = (place ^ index) * part + local
+            taps = column(res, group) * jnp.exp(-column(dec, group) * ahead)
+            taps_ref[index, local] = taps.astype(BF16)
             taps = jnp.sum(taps, axis=0, keepdims=True)
             toep = pltpu.roll(
                 jnp.broadcast_to(taps, (length, length)), 0, 1, stride=1, stride_axis=0
             )
             toep_ref[local] = jnp.where(later, toep, 0.0).astype(BF16)
         for local in range(part):
-            group = quarter * part + local
-            out_ref[group] = dot(xc_ref[group], toep_ref[local], NN)
+            out_ref[index, local] = dot(ref[local], toep_ref[local], NN)
+
+    convolve(0, own_ref)
+
+    def others(index, _):
+        convolve(index, xc_ref.at[index - 1])
         return 0
 
-    lax.fori_loop(0, PLANE, quarter_step, 0)
+    lax.fori_loop(1, PLANE, others, 0)
 
 
 def split_pair(x, half):
@@ -326,68 +339,65 @@
         outs[i][flat // 2 :] = sums
 
 
-def outputs_kernel(k_ref, v_ref, g_ref, near_ref, taps_ref, *refs):
-    incoming, results = refs[:PLANE], refs[PLANE : PLANE + 3]
-    outs, out_sems, cs, gs = refs[PLANE + 3 :]
+def outputs_kernel(index, tokens, k_ref, v_ref, g_ref, near_ref, taps_ref, state_ref, *refs):
+    last = index == PLANE - 1
+    if last:
+        (total_ref, dec_ref, res_ref), refs = refs[:3], refs[3:]
+    if index > 0:
+        refs = refs[3:]
+    results, refs = refs[:3], refs[3:]
+    if last:
+        grads, refs = refs[:2], refs[2:]
+    outs, sems, cs, gs, *rest = refs
     place, _ = places()
-    _, rows, part, length = outs.shape[1:]
-    modes = taps_ref.shape[1]
+    _, rows, part, length = outs.shape
+    modes = taps_ref.shape[2]
     quads = part // 4
-    flat = quads * rows
-
-    def store(which, quarter):
-        return pltpu.make_async_copy(
-            outs.at[which, quarter],
-            results[which].at[:, pl.ds(quarter * part, part), :],
-            out_sems.at[which, quarter],
-        )
-
+    quarter = place ^ index
+    own = pl.ds(pl.multiple_of(quarter * part, part), part)
+    stores = [
+        pltpu.make_async_copy(outs.at[which], results[which].at[:, own, :], sems.at[which])
+        for which in range(3)
+    ]
+    if last:
+        sums, sums_sems = rest
+        groups = dec_ref.shape[1]
+        sums[0] = total_ref[:modes, :groups] / tokens
+        sums[1] = -(res_ref[...] * dec_ref[...]) * total_ref[modes:, :groups] / tokens
+        stores += [
+            pltpu.make_async_copy(sums.at[which], grads[which], sums_sems.at[which])
+            for which in range(2)
+        ]
+        for copy in stores[3:]:
+            copy.start()
     mirror = mirror_of(length)
     zero = jnp.zeros((modes, length), BF16)
-
-    def expand(quarter):
-        slot = quarter % 2
-        index = place ^ quarter
-        state = incoming[0][:flat]
-        for i in range(1, PLANE):
-            state = jnp.where(index == i, incoming[i][:flat], state)
-        for local in range(part):
-            quad, side = local // 4, local % 4
-            base = side + (4 if quad >= quads // 2 else 0)
-            first = (quad % (quads // 2)) * 2 * rows
-            taps = jnp.concatenate(
-                [zero] * base + [taps_ref[quarter * part + local]] + [zero] * (7 - base), axis=0
-            )
-            both = dot(state[first : first + 2 * rows], taps, NN)
-            both = both + near_ref[quarter * part + local]
-            cs[slot, local // 8, pl.ds(local % 8, rows, stride=8), :] = both[:rows]
-            gs[slot, local // 8, pl.ds(local % 8, rows, stride=8), :] = both[rows:]
-
-    def finish(quarter):
-        slot = quarter % 2
-        shape = (rows, part, length)
-        own = pl.ds(quarter * part, part)
-        conv, ig = (
-            jnp.concatenate(
-                [ref[slot, i].reshape(rows, 8, length) for i in range(part // 8)], axis=1
-            ).astype(BF16)
-            for ref in (cs, gs)
+    for local in range(part):
+        quad, side = local // 4, local % 4
+        base = side + (4 if quad >= quads // 2 else 0)
+        first = (quad % (quads // 2)) * 2 * rows
+        taps = jnp.concatenate(
+            [zero] * base + [taps_ref[index, local]] + [zero] * (7 - base), axis=0
         )
-        ig = dot(ig.reshape(rows * part, length), mirror, NN).reshape(shape)
-        outs[0, quarter] = product(g_ref[:, own, :], conv)
-        outs[1, quarter] = product(ig, v_ref[:, own, :])
-        outs[2, quarter] = product(ig, k_ref[:, own, :])
-        for which in range(3):
-            store(which, quarter).start()
-
-    for quarter in range(PLANE + 1):
-        if quarter < PLANE:
-            expand(quarter)
-        if quarter > 0:
-            finish(quarter - 1)
-    for quarter in range(PLANE):
-        for which in range(3):
-            store(which, quarter).wait()
+        both = dot(state_ref[first : first + 2 * rows], taps, NN) + near_ref[index, local]
+        cs[local // 8, pl.ds(local % 8, rows, stride=8), :] = both[:rows]
+        gs[local // 8, pl.ds(local % 8, rows, stride=8), :] = both[rows:]
+    shape = (rows, part, length)
+    conv, ig = (
+        jnp.concatenate(
+            [ref[i].reshape(rows, 8, length) for i in range(part // 8)], axis=1
+        ).astype(BF16)
+        for ref in (cs, gs)
+    )
+    outs[0] = product(g_ref[:, own, :], conv)
+    stores[0].start()
+    ig = dot(ig.reshape(rows * part, length), mirror, NN).reshape(shape)
+    outs[1] = product(ig, v_ref[:, own, :])
+    stores[1].start()
+    outs[2] = product(ig, k_ref[:, own, :])
+    stores[2].start()
+    for copy in stores:
+        copy.wait()
 
 
 def per_device(queries, keys_in, values_in, grad_out, residue, decay_rate):
@@ -412,7 +422,7 @@
     def shaped(shape, dtype):
         return jax.ShapeDtypeStruct(shape, dtype)
 
-    def call(kernel, name, in_specs, out_specs, out_shape, scratch, flops, size):
+    def call(kernel, name, in_specs, out_specs, out_shape, scratch, flops, size, aliases=None):
         return pl.pallas_call(
             kernel,
             in_specs=in_specs,
@@ -421,45 +431,52 @@
             scratch_shapes=scratch,
             cost_estimate=pl.CostEstimate(flops=flops, bytes_accessed=size, transcendentals=0),
             compiler_params=pltpu.CompilerParams(vmem_limit_bytes=16 * 2**20),
+            input_output_aliases=aliases or {},
             name=name,
         )
 
-    grouped = shaped((groups, 2 * rows, length), BF16)
+    def in_hbm(*arrays):
+        return [pltpu.with_memory_space_constraint(x, pltpu.HBM) for x in arrays]
+
+    def reducer(slots):
+        return [
+            pltpu.VMEM((4, slots, rows, part, length), BF16),
+            pltpu.SemaphoreType.DMA((4, slots)),
+        ] + [pltpu.VMEM((slots, part // 8, rows * 8, length), F32)] * 2
+
+    quarter = (part, 2 * rows, length)
     block = shaped((quads, 2 * rows, lanes), BF16)
-    xc, rates, *own = call(
+    xc, weights, rates, *own = call(
         states_kernel,
         "states",
         [anywhere] * 5,
         [vmem] * (2 + PLANE),
-        [grouped, shaped((groups // 4, lanes), F32)] + [block] * PLANE,
         [
-            pltpu.VMEM((modes, groups), F32),
-            pltpu.SemaphoreType.DMA,
-            pltpu.VMEM((4, PLANE, rows, part, length), BF16),
-            pltpu.SemaphoreType.DMA((4, PLANE)),
-            pltpu.VMEM((groups, 2, modes, length), BF16),
-            pltpu.VMEM((2, part // 8, rows * 8, length), F32),
-            pltpu.VMEM((2, part // 8, rows * 8, length), F32),
-            pltpu.VMEM((PLANE, quads, 2 * rows, lanes), BF16),
-        ],
+            shaped((PLANE - 1,) + quarter, BF16),
+            shaped((groups, 2, modes, length), BF16),
+            shaped((groups // 4, lanes), F32),
+        ]
+        + [block] * (PLANE - 1),
+        [pltpu.VMEM((modes, groups), F32), pltpu.SemaphoreType.DMA] + reducer(PLANE - 1),
         10**9,
         4 * 10**6,
-    )(*(pltpu.with_memory_space_constraint(x, pltpu.HBM) for x in (decay, key, value, grad, query)))
+    )(*in_hbm(decay, key, value, grad, query))
 
     def swap(x, bits):
         return lax.ppermute(x, "ctx", [(i, i ^ bits) for i in range(count)])
 
-    near = [own[0]] + [swap(own[i], i) for i in range(1, PLANE)]
-    sums = call(
+    near = [swap(own[i - 1], i) for i in range(1, PLANE)]
+    xo, mine, sums = call(
         sums_kernel,
         "sums",
-        [vmem] * 2,
-        vmem,
-        shaped((2 * modes, lanes), F32),
-        [pltpu.VMEM((groups, length), F32)],
+        [anywhere] * 4 + [vmem] * 3,
+        [vmem] * 3,
+        [shaped(quarter, BF16), block, shaped((2 * modes, lanes), F32)],
+        reducer(1) + [pltpu.VMEM((groups, length), F32)],
         10**9,
         4 * 10**6,
-    )(xc, decay)
+    )(*in_hbm(key, value, grad, query), xc, weights, decay)
+    near = [mine] + near
     flat = quads * 2 * rows
     plane = call(
         functools.partial(plane_kernel, length),
@@ -472,17 +489,19 @@
         10**6,
     )(rates, *near, sums)
     line = [plane] + [swap(plane, PLANE * i) for i in range(1, depth)]
-    table = shaped((groups, modes, length), BF16)
     near_part, taps = call(
         local_kernel,
         "local",
-        [vmem] * 4,
+        [vmem] * 5,
         [vmem] * 2,
-        [shaped((groups, 2 * rows, length), F32), table],
+        [
+            shaped((PLANE,) + quarter, F32),
+            shaped((PLANE, part, modes, length), BF16),
+        ],
         [pltpu.VMEM((part, length, length), BF16)],
         10**9,
         4 * 10**6,
-    )(xc, decay, resid, plane)
+    )(xo, xc, decay, resid, plane)
     back = call(
         functools.partial(line_kernel, length),
         "line",
@@ -504,30 +523,34 @@
         total = total + lax.ppermute(total, "tp", [(i, i ^ bit) for i in range(tp)])
         bit *= 2
 
-    outs = call(
-        outputs_kernel,
-        "outputs",
-        [vmem] * (5 + PLANE),
-        [anywhere] * 3,
-        [shaped((rows, groups, length), BF16)] * 3,
-        [
-            pltpu.VMEM((3, PLANE, rows, part, length), BF16),
-            pltpu.SemaphoreType.DMA((3, PLANE)),
-            pltpu.VMEM((2, part // 8, rows * 8, length), F32),
-            pltpu.VMEM((2, part // 8, rows * 8, length), F32),
-        ],
-        10**9,
-        5 * 10**6,
-    )(key, value, grad, near_part, taps, *back)
     tokens = count * length
-    plain, moment = total[:modes, :groups], total[modes:, :groups]
-    return (
-        outs[0].reshape(chans, length),
-        outs[1].reshape(chans, length),
-        outs[2].reshape(chans, length),
-        (plain / tokens).T,
-        (-(resid * decay) * moment / tokens).T,
-    )
+    outs = ()
+    for index in range(PLANE):
+        last = index == PLANE - 1
+        extra = (total, decay, resid) if last else ()
+        *outs, = call(
+            functools.partial(outputs_kernel, index, tokens),
+            f"outputs{index}",
+            [vmem] * (6 + len(extra)) + [anywhere] * len(outs),
+            [anywhere] * (5 if last else 3),
+            [shaped((rows, groups, length), BF16)] * 3
+            + [shaped((modes, groups), F32)] * (2 if last else 0),
+            [
+                pltpu.VMEM((3, rows, part, length), BF16),
+                pltpu.SemaphoreType.DMA((3,)),
+                pltpu.VMEM((part // 8, rows * 8, length), F32),
+                pltpu.VMEM((part // 8, rows * 8, length), F32),
+            ]
+            + (
+                [pltpu.VMEM((2, modes, groups), F32), pltpu.SemaphoreType.DMA((2,))]
+                if last
+                else []
+            ),
+            2 * 10**8,
+            10**6,
+            {6 + len(extra) + i: i for i in range(len(outs))},
+        )(key, value, grad, near_part, taps, back[index], *extra, *outs)
+    return (*(x.reshape(chans, length) for x in outs[:3]), outs[3].T, outs[4].T)
 
 
 def solution(mesh):

time: 34.5 us -> 34.5 us (level)
  Pallas kernels: 15.5 us -> 18 us
  waiting for transfers between devices: 4.91 us -> 2.96 us
  other arithmetic: 0.69 us -> 0.08 us
    pallas_call x4 -> x7, Pallas kernels: 13.7 us -> 16.3 us  [the longest x1 5.03 us: per_device(): call(local_kernel, 'local', [vmem] * 5, [vmem] * 2, [shaped((PLANE,) + qu...]
    ppermute x9, waiting for transfers between devices: 4.91 us -> 2.96 us  [swap(): return lax.ppermute(x, 'ctx', [(i, i ^ bits) for i in range(count)])]
    transpose x1 -> x0, other arithmetic: 0.61 us -> none  [per_device(): return (outs[0].reshape(chans, length), outs[1].reshape(chans, length), o...]
  transfers between devices with their start and end apart: 10 -> 10, of which waited for: 4 -> 4; matrix products, arithmetic and copies ran while one was open for 0% -> 0% of each run, Pallas kernels for 29% -> 35%
where the time goes in v5:
time: 34.5 us; the launch traced here: 34.3 us
  Pallas kernels  18 us (52%)
  starting transfers between devices  12.5 us (36%)
  waiting for transfers between devices  2.96 us (9%)
  between operations  0.77 us (2%)
    ppermute x9, starting transfers between devices, swap(): return lax.ppermute(x, 'ctx', [(i, i ^ bits) for i in range(count)])  12.5 us
    pallas_call x1, Pallas kernels, per_device(): call(local_kernel, 'local', [vmem] * 5, [vmem] * 2, [shaped((PLANE,) + qu...  5.03 us
    pallas_call x4, Pallas kernels, per_device(): call(functools.partial(outputs_kernel, index, tokens), f'outputs{index}',...  4.72 us
    pallas_call x1, Pallas kernels, per_device(): call(sums_kernel, 'sums', [anywhere] * 4 + [vmem] * 3, [vmem] * 3, [shape...  3.46 us
    pallas_call x1, Pallas kernels, per_device(): call(states_kernel, 'states', [anywhere] * 5, [vmem] * (2 + PLANE), [shap...  3.04 us
    ppermute x9, waiting for transfers between devices, swap(): return lax.ppermute(x, 'ctx', [(i, i ^ bits) for i in range(count)])  2.96 us
    pallas_call x1, Pallas kernels, per_device(): call(functools.partial(line_kernel, length), 'line', [vmem] * (2 + PLANE...  0.92 us
    pallas_call x1, Pallas kernels, per_device(): call(functools.partial(plane_kernel, length), 'plane', [vmem] * (2 + PLAN...  0.81 us
  transfers between devices with their start and end apart: 10, of which 4 were waited for; matrix products, arithmetic and copies ran while one was open for 0% of the time, Pallas kernels for 35%

profile of v5, /device:TPU:0, one launch (start us, length us, event | category | flops | bytes accessed | tf_op | source)
XLA Modules:
  0.0 34.3 jit_solution(12976129457580504224)
XLA Ops:
  0.6 3.0 %states.1 = (bf16[3,16,64,128]{3,2,1,0:T(8,128)(2,1)S(1)}, bf16[64,2,16,128]{3,2,1,0:T(8,128)(2,1)S(1)}, f32[16,128]{1,0:T(8,128)S(1)}, bf16[4,64,128]{2,1,0:T(8...) custom-call(f32[16,64]{1,0:T(8,128)} %bitcast.29, bf16[32,64,128]{2,1,0:T(8,128)(2,1)} %bitcast.11, ...), custom_call_target="tpu_custom_call" | custom-call | flops 1000000000 | bytes 4000000 | tf_op jit(solution)/shard_map/states/pallas_call | solution.py:449
  3.7 0.0 copy-start.4
  3.7 3.0 %collective-permute-start = (bf16[4,64,128]{2,1,0:T(8,128)(2,1)S(1)}, bf16[4,64,128]{2,1,0:T(8,128)(2,1)S(1)}, u32[]{:S(2)}, u32[]{:S(2)}) collective-permute-start(bf16[4,64,128]{2,1,0:T(8,128)(2,1)S(1)} %get-tuple-element.39), channel_id=1, source_target_pairs={{0,2},{2,0},{4,6},{6,4},{8,10},{10,8},{12,14},{14,12},{16,18},{18,... | collective-permute-start | bytes 196616 | tf_op jit(solution)/shard_map/ppermute | solution.py:466
  6.7 1.5 %collective-permute-start.1 = (bf16[4,64,128]{2,1,0:T(8,128)(2,1)S(1)}, bf16[4,64,128]{2,1,0:T(8,128)(2,1)S(1)}, u32[]{:S(2)}, u32[]{:S(2)}) collective-permute-start(bf16[4,64,128]{2,1,0:T(8,128)(2,1)S(1)} %get-tuple-element.40), channel_id=1, source_target_pairs={{0,4},{2,6},{4,0},{6,2},{8,12},{10,14},{12,8},{14,10},{16,20},{18,... | collective-permute-start | bytes 196616 | tf_op jit(solution)/shard_map/ppermute | solution.py:466
  8.2 0.0 collective-permute-start.2
  8.3 3.5 %sums.1 = (bf16[16,64,128]{2,1,0:T(8,128)(2,1)S(1)}, bf16[4,64,128]{2,1,0:T(8,128)(2,1)S(1)}, f32[32,128]{1,0:T(8,128)S(1)}) custom-call(bf16[32,64,128]{2,1,0:T(8,128)(2,1)} %bitcast.12, bf16[32,64,128]{2,1,0:T(8,128)(2,1)} %bitcast.18, bf16[32,64,128]{2,1,0:T(8,128)(2,1)} %bitcast.24, bf16[32,64,128]{2,1,0:T(8,128)(2,1)} %bitcast.39, ...), custom_call_target="tpu_custom_call" | custom-call | flops 1000000000 | bytes 4000000 | tf_op jit(solution)/shard_map/sums/pallas_call | solution.py:469
  11.7 1.6 %collective-permute-done.2.refs_3_ = bf16[4,64,128]{2,1,0:T(8,128)(2,1)S(1)} collective-permute-done((bf16[4,64,128]{2,1,0:T(8,128)(2,1)S(1)}, bf16[4,64,128]{2,1,0:T(8,128)(2,1)S(1)}, u32[]{:S(2)}, u32[]{:S(2)}) %collective-permute-start.2) | collective-permute-done | bytes 65568 | tf_op jit(solution)/shard_map/ppermute | solution.py:466
  13.4 0.8 %plane.1.after_ref.refs_4_ = bf16[288,128]{1,0:T(8,128)(2,1)S(1)} custom-call(f32[16,128]{1,0:T(8,128)S(1)} %get-tuple-element.37.rate_ref, bf16[4,64,128]{2,1,0:T(8,128)(2,1)S(1)} %get-tuple-element.38.refs_0_, bf16[4,64,128]{2,1,0:T(8,128)(2,1)S(1)} %collective-permute-done.refs_1_, bf16[4,64,128]{2,1,0:T(8,128)(2,1)S(1)} %collective-permute-done.1.refs_2_, ...), custom_call_target="tpu_custom_call" | custom-call | flops 10000000 | bytes 1000000 | tf_op jit(solution)/shard_map/plane/pallas_call | solution.py:481
  14.2 3.6 %collective-permute-start.5 = (bf16[288,128]{1,0:T(8,128)(2,1)S(1)}, bf16[288,128]{1,0:T(8,128)(2,1)S(1)}, u32[]{:S(2)}, u32[]{:S(2)}) collective-permute-start(bf16[288,128]{1,0:T(8,128)(2,1)S(1)} %plane.1.after_ref.refs_4_), channel_id=1, source_target_pairs={{0,24},{2,26},{4,28},{6,30},{8,16},{10,18},{12,20},{14,22},{16,8},... | collective-permute-start | bytes 221192 | tf_op jit(solution)/shard_map/ppermute | solution.py:466
  17.8 0.8 %collective-permute-start.3 = (bf16[288,128]{1,0:T(8,128)(2,1)S(1)}, bf16[288,128]{1,0:T(8,128)(2,1)S(1)}, u32[]{:S(2)}, u32[]{:S(2)}) collective-permute-start(bf16[288,128]{1,0:T(8,128)(2,1)S(1)} %plane.1.after_ref.refs_4_), channel_id=1, source_target_pairs={{0,8},{2,10},{4,12},{6,14},{8,0},{10,2},{12,4},{14,6},{16,24},{18,... | collective-permute-start | bytes 221192 | tf_op jit(solution)/shard_map/ppermute | solution.py:466
  18.6 5.0 %local.1 = (f32[4,16,64,128]{3,2,1,0:T(8,128)S(1)}, bf16[4,16,16,128]{3,2,1,0:T(8,128)(2,1)S(1)}) custom-call(bf16[16,64,128]{2,1,0:T(8,128)(2,1)S(1)} %get-tuple-element.36.own_ref, bf16[3,16,64,128]{3,2,1,0:T(8,128)(2,1)S(1)} %get-tuple-element.34.xc_ref, f32[16,64]{1,0:T(8,128)S(1)} %bitcast.31, f32[16,64]{1,0:T(8,128)S(1)} %bitcast.33, ...), custom_call_target="tpu_custom_call" | custom-call | flops 1000000000 | bytes 4000000 | tf_op jit(solution)/shard_map/local/pallas_call | solution.py:492
  23.7 0.9 %line.1 = (bf16[160,128]{1,0:T(8,128)(2,1)S(1)}, bf16[160,128]{1,0:T(8,128)(2,1)S(1)}, bf16[160,128]{1,0:T(8,128)(2,1)S(1)}, bf16[160,128]{1,0:T(8,128)(2,1)S(1)}) custom-call(f32[16,128]{1,0:T(8,128)S(1)} %get-tuple-element.37.rate_ref, bf16[4,16,16,128]{3,2,1,0:T(8,128)(2,1)S(1)} %get-tuple-element.44.after_ref.taps_ref, ...), custom_call_target="tpu_custom_call" | custom-call | flops 10000000 | bytes 1000000 | tf_op jit(solution)/shard_map/line/pallas_call | solution.py:505
  24.6 1.3 %collective-permute-start.6 = (bf16[160,128]{1,0:T(8,128)(2,1)S(1)}, bf16[160,128]{1,0:T(8,128)(2,1)S(1)}, u32[]{:S(2)}, u32[]{:S(2)}) collective-permute-start(bf16[160,128]{1,0:T(8,128)(2,1)S(1)} %get-tuple-element.45), channel_id=1, source_target_pairs={{0,6},{2,4},{4,2},{6,0},{8,14},{10,12},{12,10},{14,8},{16,22},{18,... | collective-permute-start | bytes 122888 | tf_op jit(solution)/shard_map/ppermute | solution.py:466
  25.9 0.7 %collective-permute-start.7 = (bf16[160,128]{1,0:T(8,128)(2,1)S(1)}, bf16[160,128]{1,0:T(8,128)(2,1)S(1)}, u32[]{:S(2)}, u32[]{:S(2)}) collective-permute-start(bf16[160,128]{1,0:T(8,128)(2,1)S(1)} %get-tuple-element.47), channel_id=1, source_target_pairs={{0,2},{2,0},{4,6},{6,4},{8,10},{10,8},{12,14},{14,12},{16,18},{18,... | collective-permute-start | bytes 122888 | tf_op jit(solution)/shard_map/ppermute | solution.py:466
  26.6 1.5 %collective-permute-start.8 = (bf16[160,128]{1,0:T(8,128)(2,1)S(1)}, bf16[160,128]{1,0:T(8,128)(2,1)S(1)}, u32[]{:S(2)}, u32[]{:S(2)}) collective-permute-start(bf16[160,128]{1,0:T(8,128)(2,1)S(1)} %get-tuple-element.48), channel_id=1, source_target_pairs={{0,4},{2,6},{4,0},{6,2},{8,12},{10,14},{12,8},{14,10},{16,20},{18,... | collective-permute-start | bytes 122888 | tf_op jit(solution)/shard_map/ppermute | solution.py:466
  28.2 1.2 %outputs0.1 = (bf16[32,64,128]{2,1,0:T(8,128)(2,1)}, bf16[32,64,128]{2,1,0:T(8,128)(2,1)}, bf16[32,64,128]{2,1,0:T(8,128)(2,1)}) custom-call(bf16[32,64,128]{2,1,0:T(8,128)(2,1)S(1)} %bitcast.13, bf16[32,64,128]{2,1,0:T(8,128)(2,1)S(1)} %bitcast.19, bf16[32,64,128]{2,1,0:T(8,128)(2,1)S(1)} %bitcast.25, f32[4,16,64,128]{3,2,1,0:T(8,128)S(1)} %get-tuple-element.43.near_ref, ...), custom_call_target="tpu_custom_call" | custom-call | flops 200000000 | bytes 1000000 | tf_op jit(solution)/shard_map/outputs0/pallas_call | solution.py:531
  29.3 0.2 collective-permute-done.6.state_ref
  29.6 0.4 %collective-permute-done.7.state_ref = bf16[160,128]{1,0:T(8,128)(2,1)S(1)} collective-permute-done((bf16[160,128]{1,0:T(8,128)(2,1)S(1)}, bf16[160,128]{1,0:T(8,128)(2,1)S(1)}, u32[]{:S(2)}, u32[]{:S(2)}) %collective-permute-start.7) | collective-permute-done | bytes 40992 | tf_op jit(solution)/shard_map/ppermute | solution.py:466
  29.9 0.7 %collective-permute-done.8.state_ref = bf16[160,128]{1,0:T(8,128)(2,1)S(1)} collective-permute-done((bf16[160,128]{1,0:T(8,128)(2,1)S(1)}, bf16[160,128]{1,0:T(8,128)(2,1)S(1)}, u32[]{:S(2)}, u32[]{:S(2)}) %collective-permute-start.8) | collective-permute-done | bytes 40992 | tf_op jit(solution)/shard_map/ppermute | solution.py:466
  30.6 0.1 add_add_fusion
  30.7 0.0 collective-permute-start.9
  30.7 1.2 %outputs1.1 = (bf16[32,64,128]{2,1,0:T(8,128)(2,1)}, bf16[32,64,128]{2,1,0:T(8,128)(2,1)}, bf16[32,64,128]{2,1,0:T(8,128)(2,1)}) custom-call(bf16[32,64,128]{2,1,0:T(8,128)(2,1)S(1)} %bitcast.14, bf16[32,64,128]{2,1,0:T(8,128)(2,1)S(1)} %bitcast.20, bf16[32,64,128]{2,1,0:T(8,128)(2,1)S(1)} %bitcast.26, ...), custom_call_target="tpu_custom_call", output_to_operand_aliasing={{0}: (6, {}), {1}: (7, {}), {2}: (8, {})} | custom-call | flops 200000000 | bytes 1000000 | tf_op jit(solution)/shard_map/outputs1/pallas_call | solution.py:531
  31.9 1.2 %outputs2.1 = (bf16[32,64,128]{2,1,0:T(8,128)(2,1)}, bf16[32,64,128]{2,1,0:T(8,128)(2,1)}, bf16[32,64,128]{2,1,0:T(8,128)(2,1)}) custom-call(bf16[32,64,128]{2,1,0:T(8,128)(2,1)S(1)} %bitcast.15, bf16[32,64,128]{2,1,0:T(8,128)(2,1)S(1)} %bitcast.21, bf16[32,64,128]{2,1,0:T(8,128)(2,1)S(1)} %bitcast.27, ...), custom_call_target="tpu_custom_call", output_to_operand_aliasing={{0}: (6, {}), {1}: (7, {}), {2}: (8, {})} | custom-call | flops 200000000 | bytes 1000000 | tf_op jit(solution)/shard_map/outputs2/pallas_call | solution.py:531
  33.1 1.2 %outputs3.1 = (bf16[32,64,128]{2,1,0:T(8,128)(2,1)}, bf16[32,64,128]{2,1,0:T(8,128)(2,1)}, bf16[32,64,128]{2,1,0:T(8,128)(2,1)}, f32[16,64]{1,0:T(8,128)}, f32[16,64]{1,0:T(8,128)}) custom-call(bf16[32,64,128]{2,1,0:T(8,128)(2,1)S(1)} %bitcast.16, bf16[32,64,128]{2,1,0:T(8,128)(2,1)S(1)} %bitcast.22, ...), custom_call_target="tpu_custom_call", output_to_operand_aliasing={{0}: (9, {}), {1}: (10, {}), {2}: (11, {})} | custom-call | flops 200000000 | bytes 1000000 | tf_op jit(solution)/shard_map/outputs3/pallas_call | solution.py:531
  (17 shorter events, 0.0 us)
Async XLA Ops:
  0.6 7.6 %copy-start.3 = (f32[64,16]{0,1:T(8,128)S(1)}, f32[64,16]{0,1:T(8,128)}, u32[]{:S(2)}) copy-start(f32[64,16]{0,1:T(8,128)} %param.11) | copy-start | bytes 12292
  3.7 14.9 %copy-start.4 = (f32[64,16]{0,1:T(8,128)S(1)}, f32[64,16]{0,1:T(8,128)}, u32[]{:S(2)}) copy-start(f32[64,16]{0,1:T(8,128)} %param.10) | copy-start | bytes 12292
  3.7 8.0 %collective-permute-start = (bf16[4,64,128]{2,1,0:T(8,128)(2,1)S(1)}, bf16[4,64,128]{2,1,0:T(8,128)(2,1)S(1)}, u32[]{:S(2)}, u32[]{:S(2)}) collective-permute-start(bf16[4,64,128]{2,1,0:T(8,128)(2,1)S(1)} %get-tuple-element.39), channel_id=1, source_target_pairs={{0,2},{2,0},{4,6},{6,4},{8,10},{10,8},{12,14},{14,12},{16,18},{18,... | collective-permute-start | bytes 196616 | tf_op jit(solution)/shard_map/ppermute | solution.py:466
  6.7 5.0 %collective-permute-start.1 = (bf16[4,64,128]{2,1,0:T(8,128)(2,1)S(1)}, bf16[4,64,128]{2,1,0:T(8,128)(2,1)S(1)}, u32[]{:S(2)}, u32[]{:S(2)}) collective-permute-start(bf16[4,64,128]{2,1,0:T(8,128)(2,1)S(1)} %get-tuple-element.40), channel_id=1, source_target_pairs={{0,4},{2,6},{4,0},{6,2},{8,12},{10,14},{12,8},{14,10},{16,20},{18,... | collective-permute-start | bytes 196616 | tf_op jit(solution)/shard_map/ppermute | solution.py:466
  8.2 5.2 %collective-permute-start.2 = (bf16[4,64,128]{2,1,0:T(8,128)(2,1)S(1)}, bf16[4,64,128]{2,1,0:T(8,128)(2,1)S(1)}, u32[]{:S(2)}, u32[]{:S(2)}) collective-permute-start(bf16[4,64,128]{2,1,0:T(8,128)(2,1)S(1)} %get-tuple-element.41), channel_id=1, source_target_pairs={{0,6},{2,4},{4,2},{6,0},{8,14},{10,12},{12,10},{14,8},{16,22},{18,... | collective-permute-start | bytes 196616 | tf_op jit(solution)/shard_map/ppermute | solution.py:466
  14.2 9.4 %collective-permute-start.5 = (bf16[288,128]{1,0:T(8,128)(2,1)S(1)}, bf16[288,128]{1,0:T(8,128)(2,1)S(1)}, u32[]{:S(2)}, u32[]{:S(2)}) collective-permute-start(bf16[288,128]{1,0:T(8,128)(2,1)S(1)} %plane.1.after_ref.refs_4_), channel_id=1, source_target_pairs={{0,24},{2,26},{4,28},{6,30},{8,16},{10,18},{12,20},{14,22},{16,8},... | collective-permute-start | bytes 221192 | tf_op jit(solution)/shard_map/ppermute | solution.py:466
  17.8 5.8 %collective-permute-start.4 = (bf16[288,128]{1,0:T(8,128)(2,1)S(1)}, bf16[288,128]{1,0:T(8,128)(2,1)S(1)}, u32[]{:S(2)}, u32[]{:S(2)}) collective-permute-start(bf16[288,128]{1,0:T(8,128)(2,1)S(1)} %plane.1.after_ref.refs_4_), channel_id=1, source_target_pairs={{0,16},{2,18},{4,20},{6,22},{8,24},{10,26},{12,28},{14,30},{16,0},... | collective-permute-start | bytes 221192 | tf_op jit(solution)/shard_map/ppermute | solution.py:466
  17.8 5.9 %collective-permute-start.3 = (bf16[288,128]{1,0:T(8,128)(2,1)S(1)}, bf16[288,128]{1,0:T(8,128)(2,1)S(1)}, u32[]{:S(2)}, u32[]{:S(2)}) collective-permute-start(bf16[288,128]{1,0:T(8,128)(2,1)S(1)} %plane.1.after_ref.refs_4_), channel_id=1, source_target_pairs={{0,8},{2,10},{4,12},{6,14},{8,0},{10,2},{12,4},{14,6},{16,24},{18,... | collective-permute-start | bytes 221192 | tf_op jit(solution)/shard_map/ppermute | solution.py:466
  18.6 9.6 %copy-start = (bf16[2048,128]{1,0:T(8,128)(2,1)S(1)}, bf16[2048,128]{1,0:T(8,128)(2,1)}, u32[]{:S(2)}) copy-start(bf16[2048,128]{1,0:T(8,128)(2,1)} %param.7) | copy-start | bytes 1572868
  18.6 9.6 %copy-start.1 = (bf16[2048,128]{1,0:T(8,128)(2,1)S(1)}, bf16[2048,128]{1,0:T(8,128)(2,1)}, u32[]{:S(2)}) copy-start(bf16[2048,128]{1,0:T(8,128)(2,1)} %param.8) | copy-start | bytes 1572868
  18.6 9.6 %copy-start.2 = (bf16[2048,128]{1,0:T(8,128)(2,1)S(1)}, bf16[2048,128]{1,0:T(8,128)(2,1)}, u32[]{:S(2)}) copy-start(bf16[2048,128]{1,0:T(8,128)(2,1)} %param.9) | copy-start | bytes 1572868
  24.6 5.0 %collective-permute-start.6 = (bf16[160,128]{1,0:T(8,128)(2,1)S(1)}, bf16[160,128]{1,0:T(8,128)(2,1)S(1)}, u32[]{:S(2)}, u32[]{:S(2)}) collective-permute-start(bf16[160,128]{1,0:T(8,128)(2,1)S(1)} %get-tuple-element.45), channel_id=1, source_target_pairs={{0,6},{2,4},{4,2},{6,0},{8,14},{10,12},{12,10},{14,8},{16,22},{18,... | collective-permute-start | bytes 122888 | tf_op jit(solution)/shard_map/ppermute | solution.py:466
  25.9 4.0 %collective-permute-start.7 = (bf16[160,128]{1,0:T(8,128)(2,1)S(1)}, bf16[160,128]{1,0:T(8,128)(2,1)S(1)}, u32[]{:S(2)}, u32[]{:S(2)}) collective-permute-start(bf16[160,128]{1,0:T(8,128)(2,1)S(1)} %get-tuple-element.47), channel_id=1, source_target_pairs={{0,2},{2,0},{4,6},{6,4},{8,10},{10,8},{12,14},{14,12},{16,18},{18,... | collective-permute-start | bytes 122888 | tf_op jit(solution)/shard_map/ppermute | solution.py:466
  26.6 4.0 %collective-permute-start.8 = (bf16[160,128]{1,0:T(8,128)(2,1)S(1)}, bf16[160,128]{1,0:T(8,128)(2,1)S(1)}, u32[]{:S(2)}, u32[]{:S(2)}) collective-permute-start(bf16[160,128]{1,0:T(8,128)(2,1)S(1)} %get-tuple-element.48), channel_id=1, source_target_pairs={{0,4},{2,6},{4,0},{6,2},{8,12},{10,14},{12,8},{14,10},{16,20},{18,... | collective-permute-start | bytes 122888 | tf_op jit(solution)/shard_map/ppermute | solution.py:466
  30.7 2.4 %collective-permute-start.9 = (f32[32,64]{1,0:T(8,128)S(1)}, f32[32,64]{1,0:T(8,128)S(1)}, u32[]{:S(2)}, u32[]{:S(2)}) collective-permute-start(f32[32,64]{1,0:T(8,128)S(1)} %add_add_fusion), channel_id=1, source_target_pairs={{0,1},{1,0},{2,3},{3,2},{4,5},{5,4},{6,7},{7,6},{8,9},{9,8},{10,11... | collective-permute-start | bytes 24584 | tf_op jit(solution)/shard_map/ppermute | solution.py:523

commit v6 on v5

--- a/solution.py
+++ b/solution.py
@@ -1,5 +1,4 @@
 import functools
-import math
 
 import jax
 import jax.numpy as jnp
@@ -178,25 +177,33 @@
 
 
 def local_kernel(own_ref, xc_ref, dec_ref, res_ref, after_ref, out_ref, taps_ref, toep_ref):
-    _, part, _, length = xc_ref.shape
+    _, part, rows, length = xc_ref.shape
+    rows = rows // 2
     modes = dec_ref.shape[0]
     place, _ = places()
     dec, res = dec_ref[...], res_ref[...]
     ahead = lane_iota((modes, length)).astype(F32)
     later = lane_iota((length, length)) >= lax.broadcasted_iota(jnp.int32, (length, length), 0)
+    mirror = mirror_of(length)
 
     def convolve(index, ref):
         for local in range(part):
             group = (place ^ index) * part + local
-            taps = column(res, group) * jnp.exp(-column(dec, group) * ahead)
-            taps_ref[index, local] = taps.astype(BF16)
+            rate, weight = column(dec, group), column(res, group)
+            taps = weight * jnp.exp(-rate * ahead)
+            taps_ref[index, local, 0] = taps.astype(BF16)
+            back = weight * jnp.exp(-rate * (float(length - 1) - ahead))
+            taps_ref[index, local, 1] = back.astype(BF16)
             taps = jnp.sum(taps, axis=0, keepdims=True)
             toep = pltpu.roll(
                 jnp.broadcast_to(taps, (length, length)), 0, 1, stride=1, stride_axis=0
             )
             toep_ref[local] = jnp.where(later, toep, 0.0).astype(BF16)
         for local in range(part):
-            out_ref[index, local] = dot(ref[local], toep_ref[local], NN)
+            toep = toep_ref[local]
+            out_ref[index, local, :rows] = dot(ref[local, :rows], toep, NN)
+            tokens = dot(ref[local, rows:], mirror, NN).astype(BF16)
+            out_ref[index, local, rows:] = dot(tokens, toep, NT)
 
     convolve(0, own_ref)
 
@@ -339,68 +346,65 @@
         outs[i][flat // 2 :] = sums
 
 
-def outputs_kernel(index, tokens, k_ref, v_ref, g_ref, near_ref, taps_ref, state_ref, *refs):
-    last = index == PLANE - 1
-    if last:
-        (total_ref, dec_ref, res_ref), refs = refs[:3], refs[3:]
-    if index > 0:
-        refs = refs[3:]
-    results, refs = refs[:3], refs[3:]
-    if last:
-        grads, refs = refs[:2], refs[2:]
-    outs, sems, cs, gs, *rest = refs
+def outputs_kernel(indices, k_ref, v_ref, g_ref, near_ref, taps_ref, *refs):
+    count = len(indices)
+    states, refs = refs[:count], refs[count:]
+    results, (outs, sems, cs, gs) = refs[-7:-4], refs[-4:]
     place, _ = places()
-    _, rows, part, length = outs.shape
-    modes = taps_ref.shape[2]
+    _, _, rows, part, length = outs.shape
+    modes = taps_ref.shape[3]
     quads = part // 4
-    quarter = place ^ index
-    own = pl.ds(pl.multiple_of(quarter * part, part), part)
-    stores = [
-        pltpu.make_async_copy(outs.at[which], results[which].at[:, own, :], sems.at[which])
-        for which in range(3)
+    zero = jnp.zeros((modes, length), BF16)
+    spans = [
+        pl.ds(pl.multiple_of((place ^ index) * part, part), part) for index in indices
     ]
-    if last:
-        sums, sums_sems = rest
-        groups = dec_ref.shape[1]
-        sums[0] = total_ref[:modes, :groups] / tokens
-        sums[1] = -(res_ref[...] * dec_ref[...]) * total_ref[modes:, :groups] / tokens
-        stores += [
-            pltpu.make_async_copy(sums.at[which], grads[which], sums_sems.at[which])
-            for which in range(2)
-        ]
-        for copy in stores[3:]:
-            copy.start()
-    mirror = mirror_of(length)
-    zero = jnp.zeros((modes, length), BF16)
-    for local in range(part):
-        quad, side = local // 4, local % 4
-        base = side + (4 if quad >= quads // 2 else 0)
-        first = (quad % (quads // 2)) * 2 * rows
-        taps = jnp.concatenate(
-            [zero] * base + [taps_ref[index, local]] + [zero] * (7 - base), axis=0
+
+    def store(which, slot):
+        return pltpu.make_async_copy(
+            outs.at[which, slot], results[which].at[:, spans[slot], :], sems.at[which, slot]
         )
-        both = dot(state_ref[first : first + 2 * rows], taps, NN) + near_ref[index, local]
-        cs[local // 8, pl.ds(local % 8, rows, stride=8), :] = both[:rows]
-        gs[local // 8, pl.ds(local % 8, rows, stride=8), :] = both[rows:]
-    shape = (rows, part, length)
-    conv, ig = (
-        jnp.concatenate(
-            [ref[i].reshape(rows, 8, length) for i in range(part // 8)], axis=1
-        ).astype(BF16)
-        for ref in (cs, gs)
-    )
-    outs[0] = product(g_ref[:, own, :], conv)
-    stores[0].start()
-    ig = dot(ig.reshape(rows * part, length), mirror, NN).reshape(shape)
-    outs[1] = product(ig, v_ref[:, own, :])
-    stores[1].start()
-    outs[2] = product(ig, k_ref[:, own, :])
-    stores[2].start()
-    for copy in stores:
-        copy.wait()
-
-
-def per_device(queries, keys_in, values_in, grad_out, residue, decay_rate):
+
+    def expand(slot):
+        index, state_ref = indices[slot], states[slot]
+        for local in range(part):
+            quad, side = local // 4, local % 4
+            base = side + (4 if quad >= quads // 2 else 0)
+            first = (quad % (quads // 2)) * 2 * rows
+            for half, ref in enumerate((cs, gs)):
+                taps = jnp.concatenate(
+                    [zero] * base + [taps_ref[index, local, half]] + [zero] * (7 - base), axis=0
+                )
+                where = slice(half * rows, (half + 1) * rows)
+                state = state_ref[first + half * rows : first + (half + 1) * rows]
+                ref[slot, local // 8, pl.ds(local % 8, rows, stride=8), :] = (
+                    dot(state, taps, NN) + near_ref[index, local, where]
+                )
+
+    def finish(slot):
+        conv, ig = (
+            jnp.concatenate(
+                [ref[slot, i].reshape(rows, 8, length) for i in range(part // 8)], axis=1
+            ).astype(BF16)
+            for ref in (cs, gs)
+        )
+        own = spans[slot]
+        outs[0, slot] = product(g_ref[:, own, :], conv)
+        outs[1, slot] = product(ig, v_ref[:, own, :])
+        outs[2, slot] = product(ig, k_ref[:, own, :])
+        for which in range(3):
+            store(which, slot).start()
+
+    for slot in range(count + 1):
+        if slot < count:
+            expand(slot)
+        if slot > 0:
+            finish(slot - 1)
+    for slot in range(count):
+        for which in range(3):
+            store(which, slot).wait()
+
+
+def gradients(queries, keys_in, values_in, grad_out, residue, decay_rate):
     chans, length = queries.shape
     groups, modes = residue.shape
     count = lax.axis_size("ctx")
@@ -422,7 +426,7 @@
     def shaped(shape, dtype):
         return jax.ShapeDtypeStruct(shape, dtype)
 
-    def call(kernel, name, in_specs, out_specs, out_shape, scratch, flops, size, aliases=None):
+    def call(kernel, in_specs, out_specs, out_shape, scratch, flops, size, aliases=None):
         return pl.pallas_call(
             kernel,
             in_specs=in_specs,
@@ -432,7 +436,6 @@
             cost_estimate=pl.CostEstimate(flops=flops, bytes_accessed=size, transcendentals=0),
             compiler_params=pltpu.CompilerParams(vmem_limit_bytes=16 * 2**20),
             input_output_aliases=aliases or {},
-            name=name,
         )
 
     def in_hbm(*arrays):
@@ -448,7 +451,6 @@
     block = shaped((quads, 2 * rows, lanes), BF16)
     xc, weights, rates, *own = call(
         states_kernel,
-        "states",
         [anywhere] * 5,
         [vmem] * (2 + PLANE),
         [
@@ -468,7 +470,6 @@
     near = [swap(own[i - 1], i) for i in range(1, PLANE)]
     xo, mine, sums = call(
         sums_kernel,
-        "sums",
         [anywhere] * 4 + [vmem] * 3,
         [vmem] * 3,
         [shaped(quarter, BF16), block, shaped((2 * modes, lanes), F32)],
@@ -480,7 +481,6 @@
     flat = quads * 2 * rows
     plane = call(
         functools.partial(plane_kernel, length),
-        "plane",
         [vmem] * (2 + PLANE),
         vmem,
         shaped((flat + 2 * modes, lanes), BF16),
@@ -491,20 +491,18 @@
     line = [plane] + [swap(plane, PLANE * i) for i in range(1, depth)]
     near_part, taps = call(
         local_kernel,
-        "local",
         [vmem] * 5,
         [vmem] * 2,
         [
             shaped((PLANE,) + quarter, F32),
-            shaped((PLANE, part, modes, length), BF16),
+            shaped((PLANE, part, 2, modes, length), BF16),
         ],
         [pltpu.VMEM((part, length, length), BF16)],
         10**9,
         4 * 10**6,
     )(xo, xc, decay, resid, plane)
-    back = call(
+    sent = call(
         functools.partial(line_kernel, length),
-        "line",
         [vmem] * (2 + PLANE + depth),
         [vmem] * PLANE,
         [shaped((flat // 2 + 2 * modes, lanes), BF16)] * PLANE,
@@ -512,7 +510,9 @@
         10**7,
         10**6,
     )(rates, taps, *near, *line)
-    back = [back[0]] + [swap(back[i], i) for i in range(1, PLANE)]
+    back = [sent[0]]
+    for i in range(1, PLANE):
+        back.append(swap(sent[i], i))
 
     total = sum(
         b[flat // 2 :, : lanes // 2].astype(F32) + b[flat // 2 :, lanes // 2 :].astype(F32)
@@ -523,39 +523,36 @@
         total = total + lax.ppermute(total, "tp", [(i, i ^ bit) for i in range(tp)])
         bit *= 2
 
+    outs = ()
+    for indices in ((0,), tuple(range(1, PLANE - 1)), (PLANE - 1,)):
+        slots = len(indices)
+        outs = call(
+            functools.partial(outputs_kernel, indices),
+            [vmem] * (5 + slots) + [anywhere] * len(outs),
+            [anywhere] * 3,
+            [shaped((rows, groups, length), BF16)] * 3,
+            [
+                pltpu.VMEM((3, slots, rows, part, length), BF16),
+                pltpu.SemaphoreType.DMA((3, slots)),
+                pltpu.VMEM((slots, part // 8, rows * 8, length), F32),
+                pltpu.VMEM((slots, part // 8, rows * 8, length), F32),
+            ],
+            2 * 10**8 * slots,
+            10**6 * slots,
+            {5 + slots + i: i for i in range(len(outs))},
+        )(key, value, grad, near_part, taps, *(back[i] for i in indices), *outs)
     tokens = count * length
-    outs = ()
-    for index in range(PLANE):
-        last = index == PLANE - 1
-        extra = (total, decay, resid) if last else ()
-        *outs, = call(
-            functools.partial(outputs_kernel, index, tokens),
-            f"outputs{index}",
-            [vmem] * (6 + len(extra)) + [anywhere] * len(outs),
-            [anywhere] * (5 if last else 3),
-            [shaped((rows, groups, length), BF16)] * 3
-            + [shaped((modes, groups), F32)] * (2 if last else 0),
-            [
-                pltpu.VMEM((3, rows, part, length), BF16),
-                pltpu.SemaphoreType.DMA((3,)),
-                pltpu.VMEM((part // 8, rows * 8, length), F32),
-                pltpu.VMEM((part // 8, rows * 8, length), F32),
-            ]
-            + (
-                [pltpu.VMEM((2, modes, groups), F32), pltpu.SemaphoreType.DMA((2,))]
-                if last
-                else []
-            ),
-            2 * 10**8,
-            10**6,
-            {6 + len(extra) + i: i for i in range(len(outs))},
-        )(key, value, grad, near_part, taps, back[index], *extra, *outs)
-    return (*(x.reshape(chans, length) for x in outs[:3]), outs[3].T, outs[4].T)
+    plain, moment = total[:modes, :groups], total[modes:, :groups]
+    return (
+        *(x.reshape(chans, length) for x in outs),
+        (plain / tokens).T,
+        (-(resid * decay) * moment / tokens).T,
+    )
 
 
 def solution(mesh):
     in_specs = (P("tp", "ctx"), P("tp", "ctx"), P("tp", "ctx"), P("tp", "ctx"), P(), P())
     out_specs = (P("tp", "ctx"), P("tp", "ctx"), P("tp", "ctx"), P(), P())
     return jax.shard_map(
-        per_device, mesh=mesh, in_specs=in_specs, out_specs=out_specs, check_vma=False
+        gradients, mesh=mesh, in_specs=in_specs, out_specs=out_specs, check_vma=False
     )

time: 34.5 us -> 35.1 us (1.017)
  other arithmetic: 0.08 us -> 0.69 us
    transpose x0 -> x1, other arithmetic: none -> 0.61 us  [gradients(): return (*(x.reshape(chans, length) for x in outs), (plain / tokens).T, (-...]
    pallas_call x9 -> x8, Pallas kernels: 18 us -> 18 us  [the longest x1 5.88 us: gradients(): call(local_kernel, [vmem] * 5, [vmem] * 2, [shaped((PLANE,) + quarter, F3...]
  transfers between devices with their start and end apart: 10 -> 10, of which waited for: 4 -> 4; matrix products, arithmetic and copies ran while one was open for 0% -> 0% of each run, Pallas kernels for 35% -> 38%
where the time goes in v6:
time: 35.1 us; the launch traced here: 35 us
  Pallas kernels  18 us (51%)
  starting transfers between devices  12.5 us (36%)
  waiting for transfers between devices  2.99 us (9%)
  between operations  0.76 us (2%)
  other arithmetic  0.69 us (2%)
    ppermute x9, starting transfers between devices, swap(): return lax.ppermute(x, 'ctx', [(i, i ^ bits) for i in range(count)])  12.5 us
    pallas_call x1, Pallas kernels, gradients(): call(local_kernel, [vmem] * 5, [vmem] * 2, [shaped((PLANE,) + quarter, F3...  5.88 us
    pallas_call x3, Pallas kernels, gradients(): call(functools.partial(outputs_kernel, indices), [vmem] * (5 + slots) + [...  3.92 us
    pallas_call x1, Pallas kernels, gradients(): call(sums_kernel, [anywhere] * 4 + [vmem] * 3, [vmem] * 3, [shaped(quarte...  3.45 us
    pallas_call x1, Pallas kernels, gradients(): call(states_kernel, [anywhere] * 5, [vmem] * (2 + PLANE), [shaped((PLANE...  3.04 us
    ppermute x9, waiting for transfers between devices, swap(): return lax.ppermute(x, 'ctx', [(i, i ^ bits) for i in range(count)])  2.98 us
    pallas_call x1, Pallas kernels, gradients(): call(functools.partial(line_kernel, length), [vmem] * (2 + PLANE + depth)...  0.91 us
    pallas_call x1, Pallas kernels, gradients(): call(functools.partial(plane_kernel, length), [vmem] * (2 + PLANE), vmem,...  0.81 us
  transfers between devices with their start and end apart: 10, of which 4 were waited for; matrix products, arithmetic and copies ran while one was open for 0% of the time, Pallas kernels for 38%

profile of v6, /device:TPU:0, one launch (start us, length us, event | category | flops | bytes accessed | tf_op | source)
XLA Modules:
  0.0 35.0 jit_solution(4650875328949374061)
XLA Ops:
  0.6 3.0 %shard_map.101 = (bf16[3,16,64,128]{3,2,1,0:T(8,128)(2,1)S(1)}, bf16[64,2,16,128]{3,2,1,0:T(8,128)(2,1)S(1)}, f32[16,128]{1,0:T(8,128)S(1)}, bf16[4,64,128]{2,1,...) custom-call(f32[16,64]{1,0:T(8,128)} %bitcast.30, bf16[32,64,128]{2,1,0:T(8,128)(2,1)} %bitcast.15, ...), custom_call_target="tpu_custom_call" | custom-call | flops 1000000000 | bytes 4000000 | tf_op jit(solution)/shard_map/pallas_call | solution.py:452
  3.7 3.0 %collective-permute-start = (bf16[4,64,128]{2,1,0:T(8,128)(2,1)S(1)}, bf16[4,64,128]{2,1,0:T(8,128)(2,1)S(1)}, u32[]{:S(2)}, u32[]{:S(2)}) collective-permute-start(bf16[4,64,128]{2,1,0:T(8,128)(2,1)S(1)} %get-tuple-element.34), channel_id=1, source_target_pairs={{0,2},{2,0},{4,6},{6,4},{8,10},{10,8},{12,14},{14,12},{16,18},{18,... | collective-permute-start | bytes 196616 | tf_op jit(solution)/shard_map/ppermute | solution.py:468
  6.7 1.5 %collective-permute-start.1 = (bf16[4,64,128]{2,1,0:T(8,128)(2,1)S(1)}, bf16[4,64,128]{2,1,0:T(8,128)(2,1)S(1)}, u32[]{:S(2)}, u32[]{:S(2)}) collective-permute-start(bf16[4,64,128]{2,1,0:T(8,128)(2,1)S(1)} %get-tuple-element.35), channel_id=1, source_target_pairs={{0,4},{2,6},{4,0},{6,2},{8,12},{10,14},{12,8},{14,10},{16,20},{18,... | collective-permute-start | bytes 196616 | tf_op jit(solution)/shard_map/ppermute | solution.py:468
  8.2 0.0 collective-permute-start.2
  8.2 3.4 %shard_map.102 = (bf16[16,64,128]{2,1,0:T(8,128)(2,1)S(1)}, bf16[4,64,128]{2,1,0:T(8,128)(2,1)S(1)}, f32[32,128]{1,0:T(8,128)S(1)}) custom-call(bf16[32,64,128]{2,1,0:T(8,128)(2,1)} %bitcast.16, bf16[32,64,128]{2,1,0:T(8,128)(2,1)} %bitcast.21, bf16[32,64,128]{2,1,0:T(8,128)(2,1)} %bitcast.26, bf16[32,64,128]{2,1,0:T(8,128)(2,1)} %bitcast.38, ...), custom_call_target="tpu_custom_call" | custom-call | flops 1000000000 | bytes 4000000 | tf_op jit(solution)/shard_map/pallas_call | solution.py:471
  11.7 1.7 %collective-permute-done.2.refs_3_ = bf16[4,64,128]{2,1,0:T(8,128)(2,1)S(1)} collective-permute-done((bf16[4,64,128]{2,1,0:T(8,128)(2,1)S(1)}, bf16[4,64,128]{2,1,0:T(8,128)(2,1)S(1)}, u32[]{:S(2)}, u32[]{:S(2)}) %collective-permute-start.2) | collective-permute-done | bytes 65568 | tf_op jit(solution)/shard_map/ppermute | solution.py:468
  13.4 0.8 %shard_map.103.after_ref.refs_4_ = bf16[288,128]{1,0:T(8,128)(2,1)S(1)} custom-call(f32[16,128]{1,0:T(8,128)S(1)} %get-tuple-element.32.rate_ref, bf16[4,64,128]{2,1,0:T(8,128)(2,1)S(1)} %get-tuple-element.33.refs_0_, bf16[4,64,128]{2,1,0:T(8,128)(2,1)S(1)} %collective-permute-done.refs_1_, bf16[4,64,128]{2,1,0:T(8,128)(2,1)S(1)} %collective-permute-done.1.refs_2_, ...), custom_call_target="tpu_custom_call" | custom-call | flops 10000000 | bytes 1000000 | tf_op jit(solution)/shard_map/pallas_call | solution.py:482
  14.2 3.6 %collective-permute-start.5 = (bf16[288,128]{1,0:T(8,128)(2,1)S(1)}, bf16[288,128]{1,0:T(8,128)(2,1)S(1)}, u32[]{:S(2)}, u32[]{:S(2)}) collective-permute-start(bf16[288,128]{1,0:T(8,128)(2,1)S(1)} %shard_map.103.after_ref.refs_4_), channel_id=1, source_target_pairs={{0,24},{2,26},{4,28},{6,30},{8,16},{10,18},{12,20},{14,22},{16,8},... | collective-permute-start | bytes 221192 | tf_op jit(solution)/shard_map/ppermute | solution.py:468
  17.8 0.8 %collective-permute-start.3 = (bf16[288,128]{1,0:T(8,128)(2,1)S(1)}, bf16[288,128]{1,0:T(8,128)(2,1)S(1)}, u32[]{:S(2)}, u32[]{:S(2)}) collective-permute-start(bf16[288,128]{1,0:T(8,128)(2,1)S(1)} %shard_map.103.after_ref.refs_4_), channel_id=1, source_target_pairs={{0,8},{2,10},{4,12},{6,14},{8,0},{10,2},{12,4},{14,6},{16,24},{18,... | collective-permute-start | bytes 221192 | tf_op jit(solution)/shard_map/ppermute | solution.py:468
  18.6 5.9 %shard_map.104 = (f32[4,16,64,128]{3,2,1,0:T(8,128)S(1)}, bf16[4,16,2,16,128]{4,3,2,1,0:T(8,128)(2,1)S(1)}) custom-call(bf16[16,64,128]{2,1,0:T(8,128)(2,1)S(1)} %get-tuple-element.31.own_ref, bf16[3,16,64,128]{3,2,1,0:T(8,128)(2,1)S(1)} %get-tuple-element.29.xc_ref, f32[16,64]{1,0:T(8,128)S(1)} %bitcast.32, f32[16,64]{1,0:T(8,128)S(1)} %bitcast.33, ...), custom_call_target="tpu_custom_call" | custom-call | flops 1000000000 | bytes 4000000 | tf_op jit(solution)/shard_map/pallas_call | solution.py:492
  24.5 0.0 collective-permute-done.3.refs_5_
  24.5 0.9 %shard_map.105 = (bf16[160,128]{1,0:T(8,128)(2,1)S(1)}, bf16[160,128]{1,0:T(8,128)(2,1)S(1)}, bf16[160,128]{1,0:T(8,128)(2,1)S(1)}, bf16[160,128]{1,0:T(8,128)(2,1)S(1)}) custom-call(f32[16,128]{1,0:T(8,128)S(1)} %get-tuple-element.32.rate_ref, bf16[4,16,2,16,128]{4,3,2,1,0:T(8,128)(2,1)S(1)} %get-tuple-element.39.after_ref.taps_ref, ...), custom_call_target="tpu_custom_call" | custom-call | flops 10000000 | bytes 1000000 | tf_op jit(solution)/shard_map/pallas_call | solution.py:504
  25.5 1.3 %collective-permute-start.6 = (bf16[160,128]{1,0:T(8,128)(2,1)S(1)}, bf16[160,128]{1,0:T(8,128)(2,1)S(1)}, u32[]{:S(2)}, u32[]{:S(2)}) collective-permute-start(bf16[160,128]{1,0:T(8,128)(2,1)S(1)} %get-tuple-element.40), channel_id=1, source_target_pairs={{0,6},{2,4},{4,2},{6,0},{8,14},{10,12},{12,10},{14,8},{16,22},{18,... | collective-permute-start | bytes 122888 | tf_op jit(solution)/shard_map/ppermute | solution.py:468
  26.8 0.7 %collective-permute-start.7 = (bf16[160,128]{1,0:T(8,128)(2,1)S(1)}, bf16[160,128]{1,0:T(8,128)(2,1)S(1)}, u32[]{:S(2)}, u32[]{:S(2)}) collective-permute-start(bf16[160,128]{1,0:T(8,128)(2,1)S(1)} %get-tuple-element.41), channel_id=1, source_target_pairs={{0,2},{2,0},{4,6},{6,4},{8,10},{10,8},{12,14},{14,12},{16,18},{18,... | collective-permute-start | bytes 122888 | tf_op jit(solution)/shard_map/ppermute | solution.py:468
  27.5 1.5 %collective-permute-start.8 = (bf16[160,128]{1,0:T(8,128)(2,1)S(1)}, bf16[160,128]{1,0:T(8,128)(2,1)S(1)}, u32[]{:S(2)}, u32[]{:S(2)}) collective-permute-start(bf16[160,128]{1,0:T(8,128)(2,1)S(1)} %get-tuple-element.42), channel_id=1, source_target_pairs={{0,4},{2,6},{4,0},{6,2},{8,12},{10,14},{12,8},{14,10},{16,20},{18,... | collective-permute-start | bytes 122888 | tf_op jit(solution)/shard_map/ppermute | solution.py:468
  29.0 1.2 %shard_map.106 = (bf16[32,64,128]{2,1,0:T(8,128)(2,1)}, bf16[32,64,128]{2,1,0:T(8,128)(2,1)}, bf16[32,64,128]{2,1,0:T(8,128)(2,1)}) custom-call(bf16[32,64,128]{2,1,0:T(8,128)(2,1)S(1)} %bitcast.17, bf16[32,64,128]{2,1,0:T(8,128)(2,1)S(1)} %bitcast.22, bf16[32,64,128]{2,1,0:T(8,128)(2,1)S(1)} %bitcast.27, f32[4,16,64,128]{3,2,1,0:T(8,128)S(1)} %get-tuple-element.38.near_ref, ...), custom_call_target="tpu_custom_call" | custom-call | flops 200000000 | bytes 1000000 | tf_op jit(solution)/shard_map/pallas_call | solution.py:529
  30.2 0.2 collective-permute-done.6.refs_0_
  30.4 0.4 %collective-permute-done.7.refs_0_ = bf16[160,128]{1,0:T(8,128)(2,1)S(1)} collective-permute-done((bf16[160,128]{1,0:T(8,128)(2,1)S(1)}, bf16[160,128]{1,0:T(8,128)(2,1)S(1)}, u32[]{:S(2)}, u32[]{:S(2)}) %collective-permute-start.7) | collective-permute-done | bytes 40992 | tf_op jit(solution)/shard_map/ppermute | solution.py:468
  30.8 0.7 %collective-permute-done.8.refs_1_ = bf16[160,128]{1,0:T(8,128)(2,1)S(1)} collective-permute-done((bf16[160,128]{1,0:T(8,128)(2,1)S(1)}, bf16[160,128]{1,0:T(8,128)(2,1)S(1)}, u32[]{:S(2)}, u32[]{:S(2)}) %collective-permute-start.8) | collective-permute-done | bytes 40992 | tf_op jit(solution)/shard_map/ppermute | solution.py:468
  31.5 0.1 add_add_fusion
  31.6 0.0 collective-permute-start.9
  31.6 1.5 %shard_map.107 = (bf16[32,64,128]{2,1,0:T(8,128)(2,1)}, bf16[32,64,128]{2,1,0:T(8,128)(2,1)}, bf16[32,64,128]{2,1,0:T(8,128)(2,1)}) custom-call(bf16[32,64,128]{2,1,0:T(8,128)(2,1)S(1)} %bitcast.18, bf16[32,64,128]{2,1,0:T(8,128)(2,1)S(1)} %bitcast.23, bf16[32,64,128]{2,1,0:T(8,128)(2,1)S(1)} %bitcast.28, ...), custom_call_target="tpu_custom_call", output_to_operand_aliasing={{0}: (7, {}), {1}: (8, {}), {2}: (9, {})} | custom-call | flops 400000000 | bytes 2000000 | tf_op jit(solution)/shard_map/pallas_call | solution.py:529
  33.1 1.2 %shard_map.108 = (bf16[32,64,128]{2,1,0:T(8,128)(2,1)}, bf16[32,64,128]{2,1,0:T(8,128)(2,1)}, bf16[32,64,128]{2,1,0:T(8,128)(2,1)}) custom-call(bf16[32,64,128]{2,1,0:T(8,128)(2,1)S(1)} %bitcast.19, bf16[32,64,128]{2,1,0:T(8,128)(2,1)S(1)} %bitcast.24, bf16[32,64,128]{2,1,0:T(8,128)(2,1)S(1)} %bitcast.29, ...), custom_call_target="tpu_custom_call", output_to_operand_aliasing={{0}: (6, {}), {1}: (7, {}), {2}: (8, {})} | custom-call | flops 200000000 | bytes 1000000 | tf_op jit(solution)/shard_map/pallas_call | solution.py:529
  34.4 0.6 %fusion.1 = (f32[64,16]{0,1:T(8,128)}, f32[64,16]{0,1:T(8,128)}) fusion(f32[32,64]{1,0:T(8,128)S(1)} %add.31, f32[64,16]{0,1:T(8,128)S(1)} %copy-done.4, f32[64,16]{0,1:T(8,128)S(1)} %copy-done.3), kind=kLoop, calls=%fused_computation.3 | loop fusion | flops 5120 | bytes 24576 | tf_op jit(solution)/shard_map/transpose | solution.py:549
  (17 shorter events, 0.0 us)
Async XLA Ops:
  0.6 7.6 %copy-start.3 = (f32[64,16]{0,1:T(8,128)S(1)}, f32[64,16]{0,1:T(8,128)}, u32[]{:S(2)}) copy-start(f32[64,16]{0,1:T(8,128)} %param.11) | copy-start | bytes 12292
  3.7 14.9 %copy-start.4 = (f32[64,16]{0,1:T(8,128)S(1)}, f32[64,16]{0,1:T(8,128)}, u32[]{:S(2)}) copy-start(f32[64,16]{0,1:T(8,128)} %param.10) | copy-start | bytes 12292
  3.7 8.0 %collective-permute-start = (bf16[4,64,128]{2,1,0:T(8,128)(2,1)S(1)}, bf16[4,64,128]{2,1,0:T(8,128)(2,1)S(1)}, u32[]{:S(2)}, u32[]{:S(2)}) collective-permute-start(bf16[4,64,128]{2,1,0:T(8,128)(2,1)S(1)} %get-tuple-element.34), channel_id=1, source_target_pairs={{0,2},{2,0},{4,6},{6,4},{8,10},{10,8},{12,14},{14,12},{16,18},{18,... | collective-permute-start | bytes 196616 | tf_op jit(solution)/shard_map/ppermute | solution.py:468
  6.7 5.0 %collective-permute-start.1 = (bf16[4,64,128]{2,1,0:T(8,128)(2,1)S(1)}, bf16[4,64,128]{2,1,0:T(8,128)(2,1)S(1)}, u32[]{:S(2)}, u32[]{:S(2)}) collective-permute-start(bf16[4,64,128]{2,1,0:T(8,128)(2,1)S(1)} %get-tuple-element.35), channel_id=1, source_target_pairs={{0,4},{2,6},{4,0},{6,2},{8,12},{10,14},{12,8},{14,10},{16,20},{18,... | collective-permute-start | bytes 196616 | tf_op jit(solution)/shard_map/ppermute | solution.py:468
  8.2 5.2 %collective-permute-start.2 = (bf16[4,64,128]{2,1,0:T(8,128)(2,1)S(1)}, bf16[4,64,128]{2,1,0:T(8,128)(2,1)S(1)}, u32[]{:S(2)}, u32[]{:S(2)}) collective-permute-start(bf16[4,64,128]{2,1,0:T(8,128)(2,1)S(1)} %get-tuple-element.36), channel_id=1, source_target_pairs={{0,6},{2,4},{4,2},{6,0},{8,14},{10,12},{12,10},{14,8},{16,22},{18,... | collective-permute-start | bytes 196616 | tf_op jit(solution)/shard_map/ppermute | solution.py:468
  14.2 10.3 %collective-permute-start.5 = (bf16[288,128]{1,0:T(8,128)(2,1)S(1)}, bf16[288,128]{1,0:T(8,128)(2,1)S(1)}, u32[]{:S(2)}, u32[]{:S(2)}) collective-permute-start(bf16[288,128]{1,0:T(8,128)(2,1)S(1)} %shard_map.103.after_ref.refs_4_), channel_id=1, source_target_pairs={{0,24},{2,26},{4,28},{6,30},{8,16},{10,18},{12,20},{14,22},{16,8},... | collective-permute-start | bytes 221192 | tf_op jit(solution)/shard_map/ppermute | solution.py:468
  17.8 6.7 %collective-permute-start.4 = (bf16[288,128]{1,0:T(8,128)(2,1)S(1)}, bf16[288,128]{1,0:T(8,128)(2,1)S(1)}, u32[]{:S(2)}, u32[]{:S(2)}) collective-permute-start(bf16[288,128]{1,0:T(8,128)(2,1)S(1)} %shard_map.103.after_ref.refs_4_), channel_id=1, source_target_pairs={{0,16},{2,18},{4,20},{6,22},{8,24},{10,26},{12,28},{14,30},{16,0},... | collective-permute-start | bytes 221192 | tf_op jit(solution)/shard_map/ppermute | solution.py:468
  17.8 6.7 %collective-permute-start.3 = (bf16[288,128]{1,0:T(8,128)(2,1)S(1)}, bf16[288,128]{1,0:T(8,128)(2,1)S(1)}, u32[]{:S(2)}, u32[]{:S(2)}) collective-permute-start(bf16[288,128]{1,0:T(8,128)(2,1)S(1)} %shard_map.103.after_ref.refs_4_), channel_id=1, source_target_pairs={{0,8},{2,10},{4,12},{6,14},{8,0},{10,2},{12,4},{14,6},{16,24},{18,... | collective-permute-start | bytes 221192 | tf_op jit(solution)/shard_map/ppermute | solution.py:468
  18.6 10.4 %copy-start = (bf16[2048,128]{1,0:T(8,128)(2,1)S(1)}, bf16[2048,128]{1,0:T(8,128)(2,1)}, u32[]{:S(2)}) copy-start(bf16[2048,128]{1,0:T(8,128)(2,1)} %param.7) | copy-start | bytes 1572868
  18.6 10.4 %copy-start.1 = (bf16[2048,128]{1,0:T(8,128)(2,1)S(1)}, bf16[2048,128]{1,0:T(8,128)(2,1)}, u32[]{:S(2)}) copy-start(bf16[2048,128]{1,0:T(8,128)(2,1)} %param.8) | copy-start | bytes 1572868
  18.6 10.4 %copy-start.2 = (bf16[2048,128]{1,0:T(8,128)(2,1)S(1)}, bf16[2048,128]{1,0:T(8,128)(2,1)}, u32[]{:S(2)}) copy-start(bf16[2048,128]{1,0:T(8,128)(2,1)} %param.9) | copy-start | bytes 1572868
  25.5 5.0 %collective-permute-start.6 = (bf16[160,128]{1,0:T(8,128)(2,1)S(1)}, bf16[160,128]{1,0:T(8,128)(2,1)S(1)}, u32[]{:S(2)}, u32[]{:S(2)}) collective-permute-start(bf16[160,128]{1,0:T(8,128)(2,1)S(1)} %get-tuple-element.40), channel_id=1, source_target_pairs={{0,6},{2,4},{4,2},{6,0},{8,14},{10,12},{12,10},{14,8},{16,22},{18,... | collective-permute-start | bytes 122888 | tf_op jit(solution)/shard_map/ppermute | solution.py:468
  26.8 4.0 %collective-permute-start.7 = (bf16[160,128]{1,0:T(8,128)(2,1)S(1)}, bf16[160,128]{1,0:T(8,128)(2,1)S(1)}, u32[]{:S(2)}, u32[]{:S(2)}) collective-permute-start(bf16[160,128]{1,0:T(8,128)(2,1)S(1)} %get-tuple-element.41), channel_id=1, source_target_pairs={{0,2},{2,0},{4,6},{6,4},{8,10},{10,8},{12,14},{14,12},{16,18},{18,... | collective-permute-start | bytes 122888 | tf_op jit(solution)/shard_map/ppermute | solution.py:468
  27.5 4.0 %collective-permute-start.8 = (bf16[160,128]{1,0:T(8,128)(2,1)S(1)}, bf16[160,128]{1,0:T(8,128)(2,1)S(1)}, u32[]{:S(2)}, u32[]{:S(2)}) collective-permute-start(bf16[160,128]{1,0:T(8,128)(2,1)S(1)} %get-tuple-element.42), channel_id=1, source_target_pairs={{0,4},{2,6},{4,0},{6,2},{8,12},{10,14},{12,8},{14,10},{16,20},{18,... | collective-permute-start | bytes 122888 | tf_op jit(solution)/shard_map/ppermute | solution.py:468
  31.6 2.8 %collective-permute-start.9 = (f32[32,64]{1,0:T(8,128)S(1)}, f32[32,64]{1,0:T(8,128)S(1)}, u32[]{:S(2)}, u32[]{:S(2)}) collective-permute-start(f32[32,64]{1,0:T(8,128)S(1)} %add_add_fusion), channel_id=1, source_target_pairs={{0,1},{1,0},{2,3},{3,2},{4,5},{5,4},{6,7},{7,6},{8,9},{9,8},{10,11... | collective-permute-start | bytes 24584 | tf_op jit(solution)/shard_map/ppermute | solution.py:523

commit v7 on v6

--- a/solution.py
+++ b/solution.py
@@ -176,34 +176,51 @@
     sums_ref[modes:] = moment
 
 
-def local_kernel(own_ref, xc_ref, dec_ref, res_ref, after_ref, out_ref, taps_ref, toep_ref):
-    _, part, rows, length = xc_ref.shape
-    rows = rows // 2
+def local_kernel(own_ref, xc_ref, dec_ref, res_ref, after_ref, out_ref, taps_ref, *scratch):
+    toep_ref, rows_ref, bands_ref = scratch
+    _, part, _, length = xc_ref.shape
     modes = dec_ref.shape[0]
     place, _ = places()
     dec, res = dec_ref[...], res_ref[...]
     ahead = lane_iota((modes, length)).astype(F32)
-    later = lane_iota((length, length)) >= lax.broadcasted_iota(jnp.int32, (length, length), 0)
-    mirror = mirror_of(length)
+    step = 16
+    lane = lane_iota((step, length))
+    row = lax.broadcasted_iota(jnp.int32, (step, length), 0)
+
+    def each(body):
+        def run(index, _):
+            body(index)
+            return 0
+
+        lax.fori_loop(0, PLANE, run, 0)
+
+    @each
+    def _(index):
+        first_group = (place ^ index) * part
+        for local in range(part):
+            rate, weight = column(dec, first_group + local), column(res, first_group + local)
+            taps = weight * jnp.exp(-rate * ahead)
+            taps_ref[index, local] = taps.astype(BF16)
+            rows_ref[index, local : local + 1] = jnp.sum(taps, axis=0, keepdims=True)
+
+    @each
+    def _(index):
+        for local in range(part):
+            taps = jnp.broadcast_to(rows_ref[index, local : local + 1], (step, length))
+            bands_ref[index, local] = pltpu.roll(taps, 0, 1, stride=1, stride_axis=0).astype(BF16)
+
+    @each
+    def _(index):
+        for local in range(part):
+            band = bands_ref[index, local]
+            for first in range(0, length, step):
+                toep_ref[index, local, first : first + step] = jnp.where(
+                    lane >= row + first, pltpu.roll(band, first, 1), 0.0
+                )
 
     def convolve(index, ref):
         for local in range(part):
-            group = (place ^ index) * part + local
-            rate, weight = column(dec, group), column(res, group)
-            taps = weight * jnp.exp(-rate * ahead)
-            taps_ref[index, local, 0] = taps.astype(BF16)
-            back = weight * jnp.exp(-rate * (float(length - 1) - ahead))
-            taps_ref[index, local, 1] = back.astype(BF16)
-            taps = jnp.sum(taps, axis=0, keepdims=True)
-            toep = pltpu.roll(
-                jnp.broadcast_to(taps, (length, length)), 0, 1, stride=1, stride_axis=0
-            )
-            toep_ref[local] = jnp.where(later, toep, 0.0).astype(BF16)
-        for local in range(part):
-            toep = toep_ref[local]
-            out_ref[index, local, :rows] = dot(ref[local, :rows], toep, NN)
-            tokens = dot(ref[local, rows:], mirror, NN).astype(BF16)
-            out_ref[index, local, rows:] = dot(tokens, toep, NT)
+            out_ref[index, local] = dot(ref[local], toep_ref[index, local], NN)
 
     convolve(0, own_ref)
 
@@ -352,8 +369,9 @@
     results, (outs, sems, cs, gs) = refs[-7:-4], refs[-4:]
     place, _ = places()
     _, _, rows, part, length = outs.shape
-    modes = taps_ref.shape[3]
+    modes = taps_ref.shape[2]
     quads = part // 4
+    mirror = mirror_of(length)
     zero = jnp.zeros((modes, length), BF16)
     spans = [
         pl.ds(pl.multiple_of((place ^ index) * part, part), part) for index in indices
@@ -370,15 +388,13 @@
             quad, side = local // 4, local % 4
             base = side + (4 if quad >= quads // 2 else 0)
             first = (quad % (quads // 2)) * 2 * rows
-            for half, ref in enumerate((cs, gs)):
-                taps = jnp.concatenate(
-                    [zero] * base + [taps_ref[index, local, half]] + [zero] * (7 - base), axis=0
-                )
-                where = slice(half * rows, (half + 1) * rows)
-                state = state_ref[first + half * rows : first + (half + 1) * rows]
-                ref[slot, local // 8, pl.ds(local % 8, rows, stride=8), :] = (
-                    dot(state, taps, NN) + near_ref[index, local, where]
-                )
+            taps = jnp.concatenate(
+                [zero] * base + [taps_ref[index, local]] + [zero] * (7 - base), axis=0
+            )
+            both = dot(state_ref[first : first + 2 * rows], taps, NN) + near_ref[index, local]
+            where = pl.ds(local % 8, rows, stride=8)
+            cs[slot, local // 8, where, :] = both[:rows]
+            gs[slot, local // 8, where, :] = both[rows:]
 
     def finish(slot):
         conv, ig = (
@@ -389,6 +405,7 @@
         )
         own = spans[slot]
         outs[0, slot] = product(g_ref[:, own, :], conv)
+        ig = dot(ig.reshape(rows * part, length), mirror, NN).reshape(conv.shape)
         outs[1, slot] = product(ig, v_ref[:, own, :])
         outs[2, slot] = product(ig, k_ref[:, own, :])
         for which in range(3):
@@ -495,9 +512,13 @@
         [vmem] * 2,
         [
             shaped((PLANE,) + quarter, F32),
-            shaped((PLANE, part, 2, modes, length), BF16),
+            shaped((PLANE, part, modes, length), BF16),
         ],
-        [pltpu.VMEM((part, length, length), BF16)],
+        [
+            pltpu.VMEM((PLANE, part, length, length), BF16),
+            pltpu.VMEM((PLANE, part, length), F32),
+            pltpu.VMEM((PLANE, part, 16, length), BF16),
+        ],
         10**9,
         4 * 10**6,
     )(xo, xc, decay, resid, plane)

time: 35.1 us -> 34.1 us (0.972)
  Pallas kernels: 18 us -> 14.9 us
  waiting for transfers between devices: 2.99 us -> 5.04 us
    pallas_call x1, Pallas kernels: 5.88 us -> 2.8 us  [gradients(): call(local_kernel, [vmem] * 5, [vmem] * 2, [shaped((PLANE,) + quarter, F3...]
    ppermute x9, waiting for transfers between devices: 2.98 us -> 5.04 us  [swap(): return lax.ppermute(x, 'ctx', [(i, i ^ bits) for i in range(count)])]
  transfers between devices with their start and end apart: 10 -> 10, of which waited for: 4 -> 5; matrix products, arithmetic and copies ran while one was open for 0% -> 0% of each run, Pallas kernels for 38% -> 30%
where the time goes in v7:
time: 34.1 us; the launch traced here: 33.9 us
  Pallas kernels  14.9 us (44%)
  starting transfers between devices  12.5 us (37%)
  waiting for transfers between devices  5.04 us (15%)
  between operations  0.76 us (2%)
  other arithmetic  0.69 us (2%)
    ppermute x9, starting transfers between devices, swap(): return lax.ppermute(x, 'ctx', [(i, i ^ bits) for i in range(count)])  12.5 us
    ppermute x9, waiting for transfers between devices, swap(): return lax.ppermute(x, 'ctx', [(i, i ^ bits) for i in range(count)])  5.04 us
    pallas_call x3, Pallas kernels, gradients(): call(functools.partial(outputs_kernel, indices), [vmem] * (5 + slots) + [...  3.88 us
    pallas_call x1, Pallas kernels, gradients(): call(sums_kernel, [anywhere] * 4 + [vmem] * 3, [vmem] * 3, [shaped(quarte...  3.45 us
    pallas_call x1, Pallas kernels, gradients(): call(states_kernel, [anywhere] * 5, [vmem] * (2 + PLANE), [shaped((PLANE...  3.04 us
    pallas_call x1, Pallas kernels, gradients(): call(local_kernel, [vmem] * 5, [vmem] * 2, [shaped((PLANE,) + quarter, F3...  2.8 us
    pallas_call x1, Pallas kernels, gradients(): call(functools.partial(line_kernel, length), [vmem] * (2 + PLANE + depth)...  0.91 us
    pallas_call x1, Pallas kernels, gradients(): call(functools.partial(plane_kernel, length), [vmem] * (2 + PLANE), vmem,...  0.81 us
  transfers between devices with their start and end apart: 10, of which 5 were waited for; matrix products, arithmetic and copies ran while one was open for 0% of the time, Pallas kernels for 30%

profile of v7, /device:TPU:0, one launch (start us, length us, event | category | flops | bytes accessed | tf_op | source)
XLA Modules:
  0.0 33.9 jit_solution(6456133858322637770)
XLA Ops:
  0.6 3.0 %shard_map.101 = (bf16[3,16,64,128]{3,2,1,0:T(8,128)(2,1)S(1)}, bf16[64,2,16,128]{3,2,1,0:T(8,128)(2,1)S(1)}, f32[16,128]{1,0:T(8,128)S(1)}, bf16[4,64,128]{2,1,...) custom-call(f32[16,64]{1,0:T(8,128)} %bitcast.30, bf16[32,64,128]{2,1,0:T(8,128)(2,1)} %bitcast.15, ...), custom_call_target="tpu_custom_call" | custom-call | flops 1000000000 | bytes 4000000 | tf_op jit(solution)/shard_map/pallas_call | solution.py:469
  3.7 3.0 %collective-permute-start = (bf16[4,64,128]{2,1,0:T(8,128)(2,1)S(1)}, bf16[4,64,128]{2,1,0:T(8,128)(2,1)S(1)}, u32[]{:S(2)}, u32[]{:S(2)}) collective-permute-start(bf16[4,64,128]{2,1,0:T(8,128)(2,1)S(1)} %get-tuple-element.34), channel_id=1, source_target_pairs={{0,2},{2,0},{4,6},{6,4},{8,10},{10,8},{12,14},{14,12},{16,18},{18,... | collective-permute-start | bytes 196616 | tf_op jit(solution)/shard_map/ppermute | solution.py:485
  6.7 1.5 %collective-permute-start.1 = (bf16[4,64,128]{2,1,0:T(8,128)(2,1)S(1)}, bf16[4,64,128]{2,1,0:T(8,128)(2,1)S(1)}, u32[]{:S(2)}, u32[]{:S(2)}) collective-permute-start(bf16[4,64,128]{2,1,0:T(8,128)(2,1)S(1)} %get-tuple-element.35), channel_id=1, source_target_pairs={{0,4},{2,6},{4,0},{6,2},{8,12},{10,14},{12,8},{14,10},{16,20},{18,... | collective-permute-start | bytes 196616 | tf_op jit(solution)/shard_map/ppermute | solution.py:485
  8.2 0.0 collective-permute-start.2
  8.2 3.5 %shard_map.102 = (bf16[16,64,128]{2,1,0:T(8,128)(2,1)S(1)}, bf16[4,64,128]{2,1,0:T(8,128)(2,1)S(1)}, f32[32,128]{1,0:T(8,128)S(1)}) custom-call(bf16[32,64,128]{2,1,0:T(8,128)(2,1)} %bitcast.16, bf16[32,64,128]{2,1,0:T(8,128)(2,1)} %bitcast.21, bf16[32,64,128]{2,1,0:T(8,128)(2,1)} %bitcast.26, bf16[32,64,128]{2,1,0:T(8,128)(2,1)} %bitcast.38, ...), custom_call_target="tpu_custom_call" | custom-call | flops 1000000000 | bytes 4000000 | tf_op jit(solution)/shard_map/pallas_call | solution.py:488
  11.7 1.7 %collective-permute-done.2.refs_3_ = bf16[4,64,128]{2,1,0:T(8,128)(2,1)S(1)} collective-permute-done((bf16[4,64,128]{2,1,0:T(8,128)(2,1)S(1)}, bf16[4,64,128]{2,1,0:T(8,128)(2,1)S(1)}, u32[]{:S(2)}, u32[]{:S(2)}) %collective-permute-start.2) | collective-permute-done | bytes 65568 | tf_op jit(solution)/shard_map/ppermute | solution.py:485
  13.4 0.8 %shard_map.103.after_ref.refs_4_ = bf16[288,128]{1,0:T(8,128)(2,1)S(1)} custom-call(f32[16,128]{1,0:T(8,128)S(1)} %get-tuple-element.32.rate_ref, bf16[4,64,128]{2,1,0:T(8,128)(2,1)S(1)} %get-tuple-element.33.refs_0_, bf16[4,64,128]{2,1,0:T(8,128)(2,1)S(1)} %collective-permute-done.refs_1_, bf16[4,64,128]{2,1,0:T(8,128)(2,1)S(1)} %collective-permute-done.1.refs_2_, ...), custom_call_target="tpu_custom_call" | custom-call | flops 10000000 | bytes 1000000 | tf_op jit(solution)/shard_map/pallas_call | solution.py:499
  14.2 3.6 %collective-permute-start.5 = (bf16[288,128]{1,0:T(8,128)(2,1)S(1)}, bf16[288,128]{1,0:T(8,128)(2,1)S(1)}, u32[]{:S(2)}, u32[]{:S(2)}) collective-permute-start(bf16[288,128]{1,0:T(8,128)(2,1)S(1)} %shard_map.103.after_ref.refs_4_), channel_id=1, source_target_pairs={{0,24},{2,26},{4,28},{6,30},{8,16},{10,18},{12,20},{14,22},{16,8},... | collective-permute-start | bytes 221192 | tf_op jit(solution)/shard_map/ppermute | solution.py:485
  17.8 0.8 %collective-permute-start.3 = (bf16[288,128]{1,0:T(8,128)(2,1)S(1)}, bf16[288,128]{1,0:T(8,128)(2,1)S(1)}, u32[]{:S(2)}, u32[]{:S(2)}) collective-permute-start(bf16[288,128]{1,0:T(8,128)(2,1)S(1)} %shard_map.103.after_ref.refs_4_), channel_id=1, source_target_pairs={{0,8},{2,10},{4,12},{6,14},{8,0},{10,2},{12,4},{14,6},{16,24},{18,... | collective-permute-start | bytes 221192 | tf_op jit(solution)/shard_map/ppermute | solution.py:485
  18.6 2.8 %shard_map.104 = (f32[4,16,64,128]{3,2,1,0:T(8,128)S(1)}, bf16[4,16,16,128]{3,2,1,0:T(8,128)(2,1)S(1)}) custom-call(bf16[16,64,128]{2,1,0:T(8,128)(2,1)S(1)} %get-tuple-element.31.own_ref, bf16[3,16,64,128]{3,2,1,0:T(8,128)(2,1)S(1)} %get-tuple-element.29.xc_ref, f32[16,64]{1,0:T(8,128)S(1)} %bitcast.32, f32[16,64]{1,0:T(8,128)S(1)} %bitcast.33, ...), custom_call_target="tpu_custom_call" | custom-call | flops 1000000000 | bytes 4000000 | tf_op jit(solution)/shard_map/pallas_call | solution.py:509
  21.4 1.6 %collective-permute-done.4.refs_6_ = bf16[288,128]{1,0:T(8,128)(2,1)S(1)} collective-permute-done((bf16[288,128]{1,0:T(8,128)(2,1)S(1)}, bf16[288,128]{1,0:T(8,128)(2,1)S(1)}, u32[]{:S(2)}, u32[]{:S(2)}) %collective-permute-start.4) | collective-permute-done | bytes 73760 | tf_op jit(solution)/shard_map/ppermute | solution.py:485
  23.1 0.9 %shard_map.105 = (bf16[160,128]{1,0:T(8,128)(2,1)S(1)}, bf16[160,128]{1,0:T(8,128)(2,1)S(1)}, bf16[160,128]{1,0:T(8,128)(2,1)S(1)}, bf16[160,128]{1,0:T(8,128)(2,1)S(1)}) custom-call(f32[16,128]{1,0:T(8,128)S(1)} %get-tuple-element.32.rate_ref, bf16[4,16,16,128]{3,2,1,0:T(8,128)(2,1)S(1)} %get-tuple-element.39.after_ref.taps_ref, ...), custom_call_target="tpu_custom_call" | custom-call | flops 10000000 | bytes 1000000 | tf_op jit(solution)/shard_map/pallas_call | solution.py:525
  24.0 1.8 %collective-permute-start.6 = (bf16[160,128]{1,0:T(8,128)(2,1)S(1)}, bf16[160,128]{1,0:T(8,128)(2,1)S(1)}, u32[]{:S(2)}, u32[]{:S(2)}) collective-permute-start(bf16[160,128]{1,0:T(8,128)(2,1)S(1)} %get-tuple-element.40), channel_id=1, source_target_pairs={{0,6},{2,4},{4,2},{6,0},{8,14},{10,12},{12,10},{14,8},{16,22},{18,... | collective-permute-start | bytes 122888 | tf_op jit(solution)/shard_map/ppermute | solution.py:485
  25.8 0.7 %collective-permute-start.7 = (bf16[160,128]{1,0:T(8,128)(2,1)S(1)}, bf16[160,128]{1,0:T(8,128)(2,1)S(1)}, u32[]{:S(2)}, u32[]{:S(2)}) collective-permute-start(bf16[160,128]{1,0:T(8,128)(2,1)S(1)} %get-tuple-element.41), channel_id=1, source_target_pairs={{0,2},{2,0},{4,6},{6,4},{8,10},{10,8},{12,14},{14,12},{16,18},{18,... | collective-permute-start | bytes 122888 | tf_op jit(solution)/shard_map/ppermute | solution.py:485
  26.5 1.1 %collective-permute-start.8 = (bf16[160,128]{1,0:T(8,128)(2,1)S(1)}, bf16[160,128]{1,0:T(8,128)(2,1)S(1)}, u32[]{:S(2)}, u32[]{:S(2)}) collective-permute-start(bf16[160,128]{1,0:T(8,128)(2,1)S(1)} %get-tuple-element.42), channel_id=1, source_target_pairs={{0,4},{2,6},{4,0},{6,2},{8,12},{10,14},{12,8},{14,10},{16,20},{18,... | collective-permute-start | bytes 122888 | tf_op jit(solution)/shard_map/ppermute | solution.py:485
  27.5 1.2 %shard_map.106 = (bf16[32,64,128]{2,1,0:T(8,128)(2,1)}, bf16[32,64,128]{2,1,0:T(8,128)(2,1)}, bf16[32,64,128]{2,1,0:T(8,128)(2,1)}) custom-call(bf16[32,64,128]{2,1,0:T(8,128)(2,1)S(1)} %bitcast.17, bf16[32,64,128]{2,1,0:T(8,128)(2,1)S(1)} %bitcast.22, bf16[32,64,128]{2,1,0:T(8,128)(2,1)S(1)} %bitcast.27, f32[4,16,64,128]{3,2,1,0:T(8,128)S(1)} %get-tuple-element.38.near_ref, ...), custom_call_target="tpu_custom_call" | custom-call | flops 200000000 | bytes 1000000 | tf_op jit(solution)/shard_map/pallas_call | solution.py:550
  28.8 0.2 collective-permute-done.6.refs_0_
  29.0 0.8 %collective-permute-done.7.refs_0_ = bf16[160,128]{1,0:T(8,128)(2,1)S(1)} collective-permute-done((bf16[160,128]{1,0:T(8,128)(2,1)S(1)}, bf16[160,128]{1,0:T(8,128)(2,1)S(1)}, u32[]{:S(2)}, u32[]{:S(2)}) %collective-permute-start.7) | collective-permute-done | bytes 40992 | tf_op jit(solution)/shard_map/ppermute | solution.py:485
  29.8 0.7 %collective-permute-done.8.refs_1_ = bf16[160,128]{1,0:T(8,128)(2,1)S(1)} collective-permute-done((bf16[160,128]{1,0:T(8,128)(2,1)S(1)}, bf16[160,128]{1,0:T(8,128)(2,1)S(1)}, u32[]{:S(2)}, u32[]{:S(2)}) %collective-permute-start.8) | collective-permute-done | bytes 40992 | tf_op jit(solution)/shard_map/ppermute | solution.py:485
  30.5 0.1 add_add_fusion
  30.6 0.0 collective-permute-start.9
  30.6 1.5 %shard_map.107 = (bf16[32,64,128]{2,1,0:T(8,128)(2,1)}, bf16[32,64,128]{2,1,0:T(8,128)(2,1)}, bf16[32,64,128]{2,1,0:T(8,128)(2,1)}) custom-call(bf16[32,64,128]{2,1,0:T(8,128)(2,1)S(1)} %bitcast.18, bf16[32,64,128]{2,1,0:T(8,128)(2,1)S(1)} %bitcast.23, bf16[32,64,128]{2,1,0:T(8,128)(2,1)S(1)} %bitcast.28, ...), custom_call_target="tpu_custom_call", output_to_operand_aliasing={{0}: (7, {}), {1}: (8, {}), {2}: (9, {})} | custom-call | flops 400000000 | bytes 2000000 | tf_op jit(solution)/shard_map/pallas_call | solution.py:550
  32.1 1.2 %shard_map.108 = (bf16[32,64,128]{2,1,0:T(8,128)(2,1)}, bf16[32,64,128]{2,1,0:T(8,128)(2,1)}, bf16[32,64,128]{2,1,0:T(8,128)(2,1)}) custom-call(bf16[32,64,128]{2,1,0:T(8,128)(2,1)S(1)} %bitcast.19, bf16[32,64,128]{2,1,0:T(8,128)(2,1)S(1)} %bitcast.24, bf16[32,64,128]{2,1,0:T(8,128)(2,1)S(1)} %bitcast.29, ...), custom_call_target="tpu_custom_call", output_to_operand_aliasing={{0}: (6, {}), {1}: (7, {}), {2}: (8, {})} | custom-call | flops 200000000 | bytes 1000000 | tf_op jit(solution)/shard_map/pallas_call | solution.py:550
  33.3 0.6 %fusion.1 = (f32[64,16]{0,1:T(8,128)}, f32[64,16]{0,1:T(8,128)}) fusion(f32[32,64]{1,0:T(8,128)S(1)} %add.31, f32[64,16]{0,1:T(8,128)S(1)} %copy-done.4, f32[64,16]{0,1:T(8,128)S(1)} %copy-done.3), kind=kLoop, calls=%fused_computation.3 | loop fusion | flops 5120 | bytes 24576 | tf_op jit(solution)/shard_map/transpose | solution.py:570
  (17 shorter events, 0.0 us)
Async XLA Ops:
  0.6 7.6 %copy-start.3 = (f32[64,16]{0,1:T(8,128)S(1)}, f32[64,16]{0,1:T(8,128)}, u32[]{:S(2)}) copy-start(f32[64,16]{0,1:T(8,128)} %param.11) | copy-start | bytes 12292
  3.7 14.9 %copy-start.4 = (f32[64,16]{0,1:T(8,128)S(1)}, f32[64,16]{0,1:T(8,128)}, u32[]{:S(2)}) copy-start(f32[64,16]{0,1:T(8,128)} %param.10) | copy-start | bytes 12292
  3.7 8.0 %collective-permute-start = (bf16[4,64,128]{2,1,0:T(8,128)(2,1)S(1)}, bf16[4,64,128]{2,1,0:T(8,128)(2,1)S(1)}, u32[]{:S(2)}, u32[]{:S(2)}) collective-permute-start(bf16[4,64,128]{2,1,0:T(8,128)(2,1)S(1)} %get-tuple-element.34), channel_id=1, source_target_pairs={{0,2},{2,0},{4,6},{6,4},{8,10},{10,8},{12,14},{14,12},{16,18},{18,... | collective-permute-start | bytes 196616 | tf_op jit(solution)/shard_map/ppermute | solution.py:485
  6.7 5.0 %collective-permute-start.1 = (bf16[4,64,128]{2,1,0:T(8,128)(2,1)S(1)}, bf16[4,64,128]{2,1,0:T(8,128)(2,1)S(1)}, u32[]{:S(2)}, u32[]{:S(2)}) collective-permute-start(bf16[4,64,128]{2,1,0:T(8,128)(2,1)S(1)} %get-tuple-element.35), channel_id=1, source_target_pairs={{0,4},{2,6},{4,0},{6,2},{8,12},{10,14},{12,8},{14,10},{16,20},{18,... | collective-permute-start | bytes 196616 | tf_op jit(solution)/shard_map/ppermute | solution.py:485
  8.2 5.2 %collective-permute-start.2 = (bf16[4,64,128]{2,1,0:T(8,128)(2,1)S(1)}, bf16[4,64,128]{2,1,0:T(8,128)(2,1)S(1)}, u32[]{:S(2)}, u32[]{:S(2)}) collective-permute-start(bf16[4,64,128]{2,1,0:T(8,128)(2,1)S(1)} %get-tuple-element.36), channel_id=1, source_target_pairs={{0,6},{2,4},{4,2},{6,0},{8,14},{10,12},{12,10},{14,8},{16,22},{18,... | collective-permute-start | bytes 196616 | tf_op jit(solution)/shard_map/ppermute | solution.py:485
  14.2 7.2 %collective-permute-start.5 = (bf16[288,128]{1,0:T(8,128)(2,1)S(1)}, bf16[288,128]{1,0:T(8,128)(2,1)S(1)}, u32[]{:S(2)}, u32[]{:S(2)}) collective-permute-start(bf16[288,128]{1,0:T(8,128)(2,1)S(1)} %shard_map.103.after_ref.refs_4_), channel_id=1, source_target_pairs={{0,24},{2,26},{4,28},{6,30},{8,16},{10,18},{12,20},{14,22},{16,8},... | collective-permute-start | bytes 221192 | tf_op jit(solution)/shard_map/ppermute | solution.py:485
  17.8 5.3 %collective-permute-start.4 = (bf16[288,128]{1,0:T(8,128)(2,1)S(1)}, bf16[288,128]{1,0:T(8,128)(2,1)S(1)}, u32[]{:S(2)}, u32[]{:S(2)}) collective-permute-start(bf16[288,128]{1,0:T(8,128)(2,1)S(1)} %shard_map.103.after_ref.refs_4_), channel_id=1, source_target_pairs={{0,16},{2,18},{4,20},{6,22},{8,24},{10,26},{12,28},{14,30},{16,0},... | collective-permute-start | bytes 221192 | tf_op jit(solution)/shard_map/ppermute | solution.py:485
  17.8 5.3 %collective-permute-start.3 = (bf16[288,128]{1,0:T(8,128)(2,1)S(1)}, bf16[288,128]{1,0:T(8,128)(2,1)S(1)}, u32[]{:S(2)}, u32[]{:S(2)}) collective-permute-start(bf16[288,128]{1,0:T(8,128)(2,1)S(1)} %shard_map.103.after_ref.refs_4_), channel_id=1, source_target_pairs={{0,8},{2,10},{4,12},{6,14},{8,0},{10,2},{12,4},{14,6},{16,24},{18,... | collective-permute-start | bytes 221192 | tf_op jit(solution)/shard_map/ppermute | solution.py:485
  18.6 8.9 %copy-start = (bf16[2048,128]{1,0:T(8,128)(2,1)S(1)}, bf16[2048,128]{1,0:T(8,128)(2,1)}, u32[]{:S(2)}) copy-start(bf16[2048,128]{1,0:T(8,128)(2,1)} %param.7) | copy-start | bytes 1572868
  18.6 8.9 %copy-start.1 = (bf16[2048,128]{1,0:T(8,128)(2,1)S(1)}, bf16[2048,128]{1,0:T(8,128)(2,1)}, u32[]{:S(2)}) copy-start(bf16[2048,128]{1,0:T(8,128)(2,1)} %param.8) | copy-start | bytes 1572868
  18.6 8.9 %copy-start.2 = (bf16[2048,128]{1,0:T(8,128)(2,1)S(1)}, bf16[2048,128]{1,0:T(8,128)(2,1)}, u32[]{:S(2)}) copy-start(bf16[2048,128]{1,0:T(8,128)(2,1)} %param.9) | copy-start | bytes 1572868
  24.0 5.0 %collective-permute-start.6 = (bf16[160,128]{1,0:T(8,128)(2,1)S(1)}, bf16[160,128]{1,0:T(8,128)(2,1)S(1)}, u32[]{:S(2)}, u32[]{:S(2)}) collective-permute-start(bf16[160,128]{1,0:T(8,128)(2,1)S(1)} %get-tuple-element.40), channel_id=1, source_target_pairs={{0,6},{2,4},{4,2},{6,0},{8,14},{10,12},{12,10},{14,8},{16,22},{18,... | collective-permute-start | bytes 122888 | tf_op jit(solution)/shard_map/ppermute | solution.py:485
  25.8 4.0 %collective-permute-start.7 = (bf16[160,128]{1,0:T(8,128)(2,1)S(1)}, bf16[160,128]{1,0:T(8,128)(2,1)S(1)}, u32[]{:S(2)}, u32[]{:S(2)}) collective-permute-start(bf16[160,128]{1,0:T(8,128)(2,1)S(1)} %get-tuple-element.41), channel_id=1, source_target_pairs={{0,2},{2,0},{4,6},{6,4},{8,10},{10,8},{12,14},{14,12},{16,18},{18,... | collective-permute-start | bytes 122888 | tf_op jit(solution)/shard_map/ppermute | solution.py:485
  26.5 4.0 %collective-permute-start.8 = (bf16[160,128]{1,0:T(8,128)(2,1)S(1)}, bf16[160,128]{1,0:T(8,128)(2,1)S(1)}, u32[]{:S(2)}, u32[]{:S(2)}) collective-permute-start(bf16[160,128]{1,0:T(8,128)(2,1)S(1)} %get-tuple-element.42), channel_id=1, source_target_pairs={{0,4},{2,6},{4,0},{6,2},{8,12},{10,14},{12,8},{14,10},{16,20},{18,... | collective-permute-start | bytes 122888 | tf_op jit(solution)/shard_map/ppermute | solution.py:485
  30.6 2.7 %collective-permute-start.9 = (f32[32,64]{1,0:T(8,128)S(1)}, f32[32,64]{1,0:T(8,128)S(1)}, u32[]{:S(2)}, u32[]{:S(2)}) collective-permute-start(f32[32,64]{1,0:T(8,128)S(1)} %add_add_fusion), channel_id=1, source_target_pairs={{0,1},{1,0},{2,3},{3,2},{4,5},{5,4},{6,7},{7,6},{8,9},{9,8},{10,11... | collective-permute-start | bytes 24584 | tf_op jit(solution)/shard_map/ppermute | solution.py:544

commit v8 on v7

--- a/solution.py
+++ b/solution.py
@@ -20,7 +20,7 @@
 
 
 def product(a, b):
-    return (a.astype(F32) * b.astype(F32)).astype(BF16)
+    return a.astype(BF16) * b.astype(BF16)
 
 
 def column(table, group):
@@ -72,9 +72,10 @@
             self.cs[slot, eight] = c[:, span].reshape(8 * self.rows, self.length)
 
     def reduce(self, slot, quarter, xc_ref, out_ref):
-        zero = jnp.zeros(self.w_ref.shape[2:], BF16)
+        modes = self.w_ref.shape[2]
+        lane = lane_iota((2 * self.rows, 8 * modes)) % (4 * modes)
         for quad in range(self.part // 4):
-            left, right = [], []
+            left, right = [], [[], []]
             for side in range(4):
                 local = 4 * quad + side
                 group = quarter * self.part + local
@@ -83,13 +84,17 @@
                     [ref[slot, local // 8, where, :] for ref in (self.gs, self.cs)], axis=0
                 ).astype(BF16)
                 xc_ref[local] = both
-                w = [zero] * 8
-                w[side], w[4 + side] = self.w_ref[group, 0], self.w_ref[group, 1]
                 left.append(both)
-                right.append(jnp.concatenate(w, axis=0))
-            out_ref[quad] = dot(
-                jnp.concatenate(left, axis=1), jnp.concatenate(right, axis=1), NT
-            ).astype(BF16)
+                right[0].append(self.w_ref[group, 0])
+                right[1].append(self.w_ref[group, 1])
+            every = dot(
+                jnp.concatenate(left, axis=0), jnp.concatenate(right[0] + right[1], axis=0), NT
+            )
+            every = every.reshape(4, 2 * self.rows, 8 * modes)
+            found = every[0]
+            for side in range(1, 4):
+                found = jnp.where(lane >= side * modes, every[side], found)
+            out_ref[quad] = found.astype(BF16)
 
 
 def states_kernel(dec_hbm, k_hbm, v_hbm, g_hbm, q_hbm, xc_ref, w_ref, rate_ref, *rest):
@@ -286,17 +291,22 @@
 
 
 def spread(terms, place, acc, modes):
-    quads = terms.shape[0]
-    shape = (quads, acc.shape[1])
-    group = lane_iota(shape) - 4 * quads * place
-    row = lax.broadcasted_iota(jnp.int32, shape, 0)
+    quads, lanes = terms.shape
+    parts = []
+    for _ in range(3):
+        parts.append(terms.astype(BF16))
+        terms = terms - parts[-1].astype(F32)
+    parts = jnp.concatenate([x.astype(F32) for x in parts], axis=0)
+    shape = (3 * quads, 4 * lanes)
+    lane = lane_iota(shape)
+    row = lax.broadcasted_iota(jnp.int32, shape, 0) % quads
+    group = lane % lanes - 4 * quads * place
+    chosen = jnp.where(group == 4 * row + lane // lanes, 1.0, 0.0)
+    turned = dot(parts.astype(BF16), chosen.astype(BF16), TN)
     for side in range(4):
-        chosen = jnp.where(group == 4 * row + side, 1.0, 0.0)
-        turned = lax.dot_general(
-            terms, chosen, TN, precision=lax.Precision.HIGHEST, preferred_element_type=F32
-        )
-        acc[:modes] += turned[side * modes : (side + 1) * modes]
-        acc[modes:] += turned[(4 + side) * modes : (5 + side) * modes]
+        span = slice(side * lanes, (side + 1) * lanes)
+        acc[:modes] += turned[side * modes : (side + 1) * modes, span]
+        acc[modes:] += turned[(4 + side) * modes : (5 + side) * modes, span]
 
 
 def own_rates(rate_ref, place, quads):
@@ -372,7 +382,6 @@
     modes = taps_ref.shape[2]
     quads = part // 4
     mirror = mirror_of(length)
-    zero = jnp.zeros((modes, length), BF16)
     spans = [
         pl.ds(pl.multiple_of((place ^ index) * part, part), part) for index in indices
     ]
@@ -384,17 +393,23 @@
 
     def expand(slot):
         index, state_ref = indices[slot], states[slot]
-        for local in range(part):
-            quad, side = local // 4, local % 4
-            base = side + (4 if quad >= quads // 2 else 0)
-            first = (quad % (quads // 2)) * 2 * rows
-            taps = jnp.concatenate(
-                [zero] * base + [taps_ref[index, local]] + [zero] * (7 - base), axis=0
-            )
-            both = dot(state_ref[first : first + 2 * rows], taps, NN) + near_ref[index, local]
-            where = pl.ds(local % 8, rows, stride=8)
-            cs[slot, local // 8, where, :] = both[:rows]
-            gs[slot, local // 8, where, :] = both[rows:]
+        half = quads // 2
+        lane = lane_iota((2 * rows, 8 * modes))
+        for quad in range(half):
+            state = state_ref[2 * rows * quad : 2 * rows * (quad + 1)]
+            locals_ = [4 * (quad + half * (i // 4)) + i % 4 for i in range(8)]
+            left = [
+                jnp.where((lane >= modes * i) & (lane < modes * (i + 1)), state, 0.0)
+                for i in range(8)
+            ]
+            right = [taps_ref[index, local] for local in locals_]
+            every = dot(jnp.concatenate(left, axis=0), jnp.concatenate(right, axis=0), NN)
+            every = every.reshape(8, 2 * rows, length)
+            for i, local in enumerate(locals_):
+                both = every[i] + near_ref[index, local]
+                where = pl.ds(local % 8, rows, stride=8)
+                cs[slot, local // 8, where, :] = both[:rows]
+                gs[slot, local // 8, where, :] = both[rows:]
 
     def finish(slot):
         conv, ig = (

time: 34.1 us -> 33.6 us (0.985)
  Pallas kernels: 14.9 us -> 14.5 us
where the time goes in v8:
time: 33.6 us; the launch traced here: 33.5 us
  Pallas kernels  14.5 us (43%)
  starting transfers between devices  12.5 us (37%)
  waiting for transfers between devices  5.02 us (15%)
  between operations  0.76 us (2%)
  other arithmetic  0.69 us (2%)
    ppermute x9, starting transfers between devices, swap(): return lax.ppermute(x, 'ctx', [(i, i ^ bits) for i in range(count)])  12.5 us
    ppermute x9, waiting for transfers between devices, swap(): return lax.ppermute(x, 'ctx', [(i, i ^ bits) for i in range(count)])  5.02 us
    pallas_call x3, Pallas kernels, gradients(): call(functools.partial(outputs_kernel, indices), [vmem] * (5 + slots) + [...  3.97 us
    pallas_call x1, Pallas kernels, gradients(): call(sums_kernel, [anywhere] * 4 + [vmem] * 3, [vmem] * 3, [shaped(quarte...  3.41 us
    pallas_call x1, Pallas kernels, gradients(): call(states_kernel, [anywhere] * 5, [vmem] * (2 + PLANE), [shaped((PLANE...  2.86 us
    pallas_call x1, Pallas kernels, gradients(): call(local_kernel, [vmem] * 5, [vmem] * 2, [shaped((PLANE,) + quarter, F3...  2.8 us
    pallas_call x1, Pallas kernels, gradients(): call(functools.partial(line_kernel, length), [vmem] * (2 + PLANE + depth)...  0.8 us
  transfers between devices with their start and end apart: 10, of which 5 were waited for; matrix products, arithmetic and copies ran while one was open for 0% of the time, Pallas kernels for 30%

profile of v8, /device:TPU:0, one launch (start us, length us, event | category | flops | bytes accessed | tf_op | source)
XLA Modules:
  0.0 33.5 jit_solution(17712477435757066380)
XLA Ops:
  0.6 2.9 %shard_map.101 = (bf16[3,16,64,128]{3,2,1,0:T(8,128)(2,1)S(1)}, bf16[64,2,16,128]{3,2,1,0:T(8,128)(2,1)S(1)}, f32[16,128]{1,0:T(8,128)S(1)}, bf16[4,64,128]{2,1,...) custom-call(f32[16,64]{1,0:T(8,128)} %bitcast.30, bf16[32,64,128]{2,1,0:T(8,128)(2,1)} %bitcast.15, ...), custom_call_target="tpu_custom_call" | custom-call | flops 1000000000 | bytes 4000000 | tf_op jit(solution)/shard_map/pallas_call | solution.py:484
  3.5 3.0 %collective-permute-start = (bf16[4,64,128]{2,1,0:T(8,128)(2,1)S(1)}, bf16[4,64,128]{2,1,0:T(8,128)(2,1)S(1)}, u32[]{:S(2)}, u32[]{:S(2)}) collective-permute-start(bf16[4,64,128]{2,1,0:T(8,128)(2,1)S(1)} %get-tuple-element.34), channel_id=1, source_target_pairs={{0,2},{2,0},{4,6},{6,4},{8,10},{10,8},{12,14},{14,12},{16,18},{18,... | collective-permute-start | bytes 196616 | tf_op jit(solution)/shard_map/ppermute | solution.py:500
  6.5 1.5 %collective-permute-start.1 = (bf16[4,64,128]{2,1,0:T(8,128)(2,1)S(1)}, bf16[4,64,128]{2,1,0:T(8,128)(2,1)S(1)}, u32[]{:S(2)}, u32[]{:S(2)}) collective-permute-start(bf16[4,64,128]{2,1,0:T(8,128)(2,1)S(1)} %get-tuple-element.35), channel_id=1, source_target_pairs={{0,4},{2,6},{4,0},{6,2},{8,12},{10,14},{12,8},{14,10},{16,20},{18,... | collective-permute-start | bytes 196616 | tf_op jit(solution)/shard_map/ppermute | solution.py:500
  8.0 0.0 collective-permute-start.2
  8.1 3.4 %shard_map.102 = (bf16[16,64,128]{2,1,0:T(8,128)(2,1)S(1)}, bf16[4,64,128]{2,1,0:T(8,128)(2,1)S(1)}, f32[32,128]{1,0:T(8,128)S(1)}) custom-call(bf16[32,64,128]{2,1,0:T(8,128)(2,1)} %bitcast.16, bf16[32,64,128]{2,1,0:T(8,128)(2,1)} %bitcast.21, bf16[32,64,128]{2,1,0:T(8,128)(2,1)} %bitcast.26, bf16[32,64,128]{2,1,0:T(8,128)(2,1)} %bitcast.38, ...), custom_call_target="tpu_custom_call" | custom-call | flops 1000000000 | bytes 4000000 | tf_op jit(solution)/shard_map/pallas_call | solution.py:503
  11.5 1.7 %collective-permute-done.2.refs_3_ = bf16[4,64,128]{2,1,0:T(8,128)(2,1)S(1)} collective-permute-done((bf16[4,64,128]{2,1,0:T(8,128)(2,1)S(1)}, bf16[4,64,128]{2,1,0:T(8,128)(2,1)S(1)}, u32[]{:S(2)}, u32[]{:S(2)}) %collective-permute-start.2) | collective-permute-done | bytes 65568 | tf_op jit(solution)/shard_map/ppermute | solution.py:500
  13.2 0.6 %shard_map.103.after_ref.refs_4_ = bf16[288,128]{1,0:T(8,128)(2,1)S(1)} custom-call(f32[16,128]{1,0:T(8,128)S(1)} %get-tuple-element.32.rate_ref, bf16[4,64,128]{2,1,0:T(8,128)(2,1)S(1)} %get-tuple-element.33.refs_0_, bf16[4,64,128]{2,1,0:T(8,128)(2,1)S(1)} %collective-permute-done.refs_1_, bf16[4,64,128]{2,1,0:T(8,128)(2,1)S(1)} %collective-permute-done.1.refs_2_, ...), custom_call_target="tpu_custom_call" | custom-call | flops 10000000 | bytes 1000000 | tf_op jit(solution)/shard_map/pallas_call | solution.py:514
  13.8 3.6 %collective-permute-start.5 = (bf16[288,128]{1,0:T(8,128)(2,1)S(1)}, bf16[288,128]{1,0:T(8,128)(2,1)S(1)}, u32[]{:S(2)}, u32[]{:S(2)}) collective-permute-start(bf16[288,128]{1,0:T(8,128)(2,1)S(1)} %shard_map.103.after_ref.refs_4_), channel_id=1, source_target_pairs={{0,24},{2,26},{4,28},{6,30},{8,16},{10,18},{12,20},{14,22},{16,8},... | collective-permute-start | bytes 221192 | tf_op jit(solution)/shard_map/ppermute | solution.py:500
  17.5 0.8 %collective-permute-start.3 = (bf16[288,128]{1,0:T(8,128)(2,1)S(1)}, bf16[288,128]{1,0:T(8,128)(2,1)S(1)}, u32[]{:S(2)}, u32[]{:S(2)}) collective-permute-start(bf16[288,128]{1,0:T(8,128)(2,1)S(1)} %shard_map.103.after_ref.refs_4_), channel_id=1, source_target_pairs={{0,8},{2,10},{4,12},{6,14},{8,0},{10,2},{12,4},{14,6},{16,24},{18,... | collective-permute-start | bytes 221192 | tf_op jit(solution)/shard_map/ppermute | solution.py:500
  18.3 2.8 %shard_map.104 = (f32[4,16,64,128]{3,2,1,0:T(8,128)S(1)}, bf16[4,16,16,128]{3,2,1,0:T(8,128)(2,1)S(1)}) custom-call(bf16[16,64,128]{2,1,0:T(8,128)(2,1)S(1)} %get-tuple-element.31.own_ref, bf16[3,16,64,128]{3,2,1,0:T(8,128)(2,1)S(1)} %get-tuple-element.29.xc_ref, f32[16,64]{1,0:T(8,128)S(1)} %bitcast.32, f32[16,64]{1,0:T(8,128)S(1)} %bitcast.33, ...), custom_call_target="tpu_custom_call" | custom-call | flops 1000000000 | bytes 4000000 | tf_op jit(solution)/shard_map/pallas_call | solution.py:524
  21.1 1.6 %collective-permute-done.4.refs_6_ = bf16[288,128]{1,0:T(8,128)(2,1)S(1)} collective-permute-done((bf16[288,128]{1,0:T(8,128)(2,1)S(1)}, bf16[288,128]{1,0:T(8,128)(2,1)S(1)}, u32[]{:S(2)}, u32[]{:S(2)}) %collective-permute-start.4) | collective-permute-done | bytes 73760 | tf_op jit(solution)/shard_map/ppermute | solution.py:500
  22.7 0.8 %shard_map.105 = (bf16[160,128]{1,0:T(8,128)(2,1)S(1)}, bf16[160,128]{1,0:T(8,128)(2,1)S(1)}, bf16[160,128]{1,0:T(8,128)(2,1)S(1)}, bf16[160,128]{1,0:T(8,128)(2,1)S(1)}) custom-call(f32[16,128]{1,0:T(8,128)S(1)} %get-tuple-element.32.rate_ref, bf16[4,16,16,128]{3,2,1,0:T(8,128)(2,1)S(1)} %get-tuple-element.39.after_ref.taps_ref, ...), custom_call_target="tpu_custom_call" | custom-call | flops 10000000 | bytes 1000000 | tf_op jit(solution)/shard_map/pallas_call | solution.py:540
  23.5 1.7 %collective-permute-start.6 = (bf16[160,128]{1,0:T(8,128)(2,1)S(1)}, bf16[160,128]{1,0:T(8,128)(2,1)S(1)}, u32[]{:S(2)}, u32[]{:S(2)}) collective-permute-start(bf16[160,128]{1,0:T(8,128)(2,1)S(1)} %get-tuple-element.40), channel_id=1, source_target_pairs={{0,6},{2,4},{4,2},{6,0},{8,14},{10,12},{12,10},{14,8},{16,22},{18,... | collective-permute-start | bytes 122888 | tf_op jit(solution)/shard_map/ppermute | solution.py:500
  25.3 0.7 %collective-permute-start.7 = (bf16[160,128]{1,0:T(8,128)(2,1)S(1)}, bf16[160,128]{1,0:T(8,128)(2,1)S(1)}, u32[]{:S(2)}, u32[]{:S(2)}) collective-permute-start(bf16[160,128]{1,0:T(8,128)(2,1)S(1)} %get-tuple-element.41), channel_id=1, source_target_pairs={{0,2},{2,0},{4,6},{6,4},{8,10},{10,8},{12,14},{14,12},{16,18},{18,... | collective-permute-start | bytes 122888 | tf_op jit(solution)/shard_map/ppermute | solution.py:500
  26.0 1.1 %collective-permute-start.8 = (bf16[160,128]{1,0:T(8,128)(2,1)S(1)}, bf16[160,128]{1,0:T(8,128)(2,1)S(1)}, u32[]{:S(2)}, u32[]{:S(2)}) collective-permute-start(bf16[160,128]{1,0:T(8,128)(2,1)S(1)} %get-tuple-element.42), channel_id=1, source_target_pairs={{0,4},{2,6},{4,0},{6,2},{8,12},{10,14},{12,8},{14,10},{16,20},{18,... | collective-permute-start | bytes 122888 | tf_op jit(solution)/shard_map/ppermute | solution.py:500
  27.1 1.3 %shard_map.106 = (bf16[32,64,128]{2,1,0:T(8,128)(2,1)}, bf16[32,64,128]{2,1,0:T(8,128)(2,1)}, bf16[32,64,128]{2,1,0:T(8,128)(2,1)}) custom-call(bf16[32,64,128]{2,1,0:T(8,128)(2,1)S(1)} %bitcast.17, bf16[32,64,128]{2,1,0:T(8,128)(2,1)S(1)} %bitcast.22, bf16[32,64,128]{2,1,0:T(8,128)(2,1)S(1)} %bitcast.27, f32[4,16,64,128]{3,2,1,0:T(8,128)S(1)} %get-tuple-element.38.near_ref, ...), custom_call_target="tpu_custom_call" | custom-call | flops 200000000 | bytes 1000000 | tf_op jit(solution)/shard_map/pallas_call | solution.py:565
  28.4 0.1 collective-permute-done.6.refs_0_
  28.5 0.8 %collective-permute-done.7.refs_0_ = bf16[160,128]{1,0:T(8,128)(2,1)S(1)} collective-permute-done((bf16[160,128]{1,0:T(8,128)(2,1)S(1)}, bf16[160,128]{1,0:T(8,128)(2,1)S(1)}, u32[]{:S(2)}, u32[]{:S(2)}) %collective-permute-start.7) | collective-permute-done | bytes 40992 | tf_op jit(solution)/shard_map/ppermute | solution.py:500
  29.3 0.7 %collective-permute-done.8.refs_1_ = bf16[160,128]{1,0:T(8,128)(2,1)S(1)} collective-permute-done((bf16[160,128]{1,0:T(8,128)(2,1)S(1)}, bf16[160,128]{1,0:T(8,128)(2,1)S(1)}, u32[]{:S(2)}, u32[]{:S(2)}) %collective-permute-start.8) | collective-permute-done | bytes 40992 | tf_op jit(solution)/shard_map/ppermute | solution.py:500
  30.0 0.1 add_add_fusion
  30.1 0.0 collective-permute-start.9
  30.1 1.4 %shard_map.107 = (bf16[32,64,128]{2,1,0:T(8,128)(2,1)}, bf16[32,64,128]{2,1,0:T(8,128)(2,1)}, bf16[32,64,128]{2,1,0:T(8,128)(2,1)}) custom-call(bf16[32,64,128]{2,1,0:T(8,128)(2,1)S(1)} %bitcast.18, bf16[32,64,128]{2,1,0:T(8,128)(2,1)S(1)} %bitcast.23, bf16[32,64,128]{2,1,0:T(8,128)(2,1)S(1)} %bitcast.28, ...), custom_call_target="tpu_custom_call", output_to_operand_aliasing={{0}: (7, {}), {1}: (8, {}), {2}: (9, {})} | custom-call | flops 400000000 | bytes 2000000 | tf_op jit(solution)/shard_map/pallas_call | solution.py:565
  31.6 1.3 %shard_map.108 = (bf16[32,64,128]{2,1,0:T(8,128)(2,1)}, bf16[32,64,128]{2,1,0:T(8,128)(2,1)}, bf16[32,64,128]{2,1,0:T(8,128)(2,1)}) custom-call(bf16[32,64,128]{2,1,0:T(8,128)(2,1)S(1)} %bitcast.19, bf16[32,64,128]{2,1,0:T(8,128)(2,1)S(1)} %bitcast.24, bf16[32,64,128]{2,1,0:T(8,128)(2,1)S(1)} %bitcast.29, ...), custom_call_target="tpu_custom_call", output_to_operand_aliasing={{0}: (6, {}), {1}: (7, {}), {2}: (8, {})} | custom-call | flops 200000000 | bytes 1000000 | tf_op jit(solution)/shard_map/pallas_call | solution.py:565
  32.9 0.6 %fusion.1 = (f32[64,16]{0,1:T(8,128)}, f32[64,16]{0,1:T(8,128)}) fusion(f32[32,64]{1,0:T(8,128)S(1)} %add.31, f32[64,16]{0,1:T(8,128)S(1)} %copy-done.4, f32[64,16]{0,1:T(8,128)S(1)} %copy-done.3), kind=kLoop, calls=%fused_computation.3 | loop fusion | flops 5120 | bytes 24576 | tf_op jit(solution)/shard_map/transpose | solution.py:585
  (17 shorter events, 0.0 us)
Async XLA Ops:
  0.6 7.4 %copy-start.3 = (f32[64,16]{0,1:T(8,128)S(1)}, f32[64,16]{0,1:T(8,128)}, u32[]{:S(2)}) copy-start(f32[64,16]{0,1:T(8,128)} %param.11) | copy-start | bytes 12292
  3.5 14.8 %copy-start.4 = (f32[64,16]{0,1:T(8,128)S(1)}, f32[64,16]{0,1:T(8,128)}, u32[]{:S(2)}) copy-start(f32[64,16]{0,1:T(8,128)} %param.10) | copy-start | bytes 12292
  3.5 8.0 %collective-permute-start = (bf16[4,64,128]{2,1,0:T(8,128)(2,1)S(1)}, bf16[4,64,128]{2,1,0:T(8,128)(2,1)S(1)}, u32[]{:S(2)}, u32[]{:S(2)}) collective-permute-start(bf16[4,64,128]{2,1,0:T(8,128)(2,1)S(1)} %get-tuple-element.34), channel_id=1, source_target_pairs={{0,2},{2,0},{4,6},{6,4},{8,10},{10,8},{12,14},{14,12},{16,18},{18,... | collective-permute-start | bytes 196616 | tf_op jit(solution)/shard_map/ppermute | solution.py:500
  6.5 5.0 %collective-permute-start.1 = (bf16[4,64,128]{2,1,0:T(8,128)(2,1)S(1)}, bf16[4,64,128]{2,1,0:T(8,128)(2,1)S(1)}, u32[]{:S(2)}, u32[]{:S(2)}) collective-permute-start(bf16[4,64,128]{2,1,0:T(8,128)(2,1)S(1)} %get-tuple-element.35), channel_id=1, source_target_pairs={{0,4},{2,6},{4,0},{6,2},{8,12},{10,14},{12,8},{14,10},{16,20},{18,... | collective-permute-start | bytes 196616 | tf_op jit(solution)/shard_map/ppermute | solution.py:500
  8.0 5.2 %collective-permute-start.2 = (bf16[4,64,128]{2,1,0:T(8,128)(2,1)S(1)}, bf16[4,64,128]{2,1,0:T(8,128)(2,1)S(1)}, u32[]{:S(2)}, u32[]{:S(2)}) collective-permute-start(bf16[4,64,128]{2,1,0:T(8,128)(2,1)S(1)} %get-tuple-element.36), channel_id=1, source_target_pairs={{0,6},{2,4},{4,2},{6,0},{8,14},{10,12},{12,10},{14,8},{16,22},{18,... | collective-permute-start | bytes 196616 | tf_op jit(solution)/shard_map/ppermute | solution.py:500
  13.8 7.3 %collective-permute-start.5 = (bf16[288,128]{1,0:T(8,128)(2,1)S(1)}, bf16[288,128]{1,0:T(8,128)(2,1)S(1)}, u32[]{:S(2)}, u32[]{:S(2)}) collective-permute-start(bf16[288,128]{1,0:T(8,128)(2,1)S(1)} %shard_map.103.after_ref.refs_4_), channel_id=1, source_target_pairs={{0,24},{2,26},{4,28},{6,30},{8,16},{10,18},{12,20},{14,22},{16,8},... | collective-permute-start | bytes 221192 | tf_op jit(solution)/shard_map/ppermute | solution.py:500
  17.5 5.3 %collective-permute-start.4 = (bf16[288,128]{1,0:T(8,128)(2,1)S(1)}, bf16[288,128]{1,0:T(8,128)(2,1)S(1)}, u32[]{:S(2)}, u32[]{:S(2)}) collective-permute-start(bf16[288,128]{1,0:T(8,128)(2,1)S(1)} %shard_map.103.after_ref.refs_4_), channel_id=1, source_target_pairs={{0,16},{2,18},{4,20},{6,22},{8,24},{10,26},{12,28},{14,30},{16,0},... | collective-permute-start | bytes 221192 | tf_op jit(solution)/shard_map/ppermute | solution.py:500
  17.5 5.3 %collective-permute-start.3 = (bf16[288,128]{1,0:T(8,128)(2,1)S(1)}, bf16[288,128]{1,0:T(8,128)(2,1)S(1)}, u32[]{:S(2)}, u32[]{:S(2)}) collective-permute-start(bf16[288,128]{1,0:T(8,128)(2,1)S(1)} %shard_map.103.after_ref.refs_4_), channel_id=1, source_target_pairs={{0,8},{2,10},{4,12},{6,14},{8,0},{10,2},{12,4},{14,6},{16,24},{18,... | collective-permute-start | bytes 221192 | tf_op jit(solution)/shard_map/ppermute | solution.py:500
  18.3 8.8 %copy-start = (bf16[2048,128]{1,0:T(8,128)(2,1)S(1)}, bf16[2048,128]{1,0:T(8,128)(2,1)}, u32[]{:S(2)}) copy-start(bf16[2048,128]{1,0:T(8,128)(2,1)} %param.7) | copy-start | bytes 1572868
  18.3 8.8 %copy-start.1 = (bf16[2048,128]{1,0:T(8,128)(2,1)S(1)}, bf16[2048,128]{1,0:T(8,128)(2,1)}, u32[]{:S(2)}) copy-start(bf16[2048,128]{1,0:T(8,128)(2,1)} %param.8) | copy-start | bytes 1572868
  18.3 8.8 %copy-start.2 = (bf16[2048,128]{1,0:T(8,128)(2,1)S(1)}, bf16[2048,128]{1,0:T(8,128)(2,1)}, u32[]{:S(2)}) copy-start(bf16[2048,128]{1,0:T(8,128)(2,1)} %param.9) | copy-start | bytes 1572868
  23.5 5.0 %collective-permute-start.6 = (bf16[160,128]{1,0:T(8,128)(2,1)S(1)}, bf16[160,128]{1,0:T(8,128)(2,1)S(1)}, u32[]{:S(2)}, u32[]{:S(2)}) collective-permute-start(bf16[160,128]{1,0:T(8,128)(2,1)S(1)} %get-tuple-element.40), channel_id=1, source_target_pairs={{0,6},{2,4},{4,2},{6,0},{8,14},{10,12},{12,10},{14,8},{16,22},{18,... | collective-permute-start | bytes 122888 | tf_op jit(solution)/shard_map/ppermute | solution.py:500
  25.3 4.0 %collective-permute-start.7 = (bf16[160,128]{1,0:T(8,128)(2,1)S(1)}, bf16[160,128]{1,0:T(8,128)(2,1)S(1)}, u32[]{:S(2)}, u32[]{:S(2)}) collective-permute-start(bf16[160,128]{1,0:T(8,128)(2,1)S(1)} %get-tuple-element.41), channel_id=1, source_target_pairs={{0,2},{2,0},{4,6},{6,4},{8,10},{10,8},{12,14},{14,12},{16,18},{18,... | collective-permute-start | bytes 122888 | tf_op jit(solution)/shard_map/ppermute | solution.py:500
  26.0 4.0 %collective-permute-start.8 = (bf16[160,128]{1,0:T(8,128)(2,1)S(1)}, bf16[160,128]{1,0:T(8,128)(2,1)S(1)}, u32[]{:S(2)}, u32[]{:S(2)}) collective-permute-start(bf16[160,128]{1,0:T(8,128)(2,1)S(1)} %get-tuple-element.42), channel_id=1, source_target_pairs={{0,4},{2,6},{4,0},{6,2},{8,12},{10,14},{12,8},{14,10},{16,20},{18,... | collective-permute-start | bytes 122888 | tf_op jit(solution)/shard_map/ppermute | solution.py:500
  30.1 2.7 %collective-permute-start.9 = (f32[32,64]{1,0:T(8,128)S(1)}, f32[32,64]{1,0:T(8,128)S(1)}, u32[]{:S(2)}, u32[]{:S(2)}) collective-permute-start(f32[32,64]{1,0:T(8,128)S(1)} %add_add_fusion), channel_id=1, source_target_pairs={{0,1},{1,0},{2,3},{3,2},{4,5},{5,4},{6,7},{7,6},{8,9},{9,8},{10,11... | collective-permute-start | bytes 24584 | tf_op jit(solution)/shard_map/ppermute | solution.py:559

commit v9 on v8

--- a/solution.py
+++ b/solution.py
@@ -315,6 +315,7 @@
 
 
 def halves(blocks, rows):
+    blocks = [b.astype(F32) for b in blocks]
     return [b[:, :rows] for b in blocks], [b[:, rows:] for b in blocks]
 
 
@@ -324,7 +325,7 @@
     quads, rows, lanes = msgs[0].shape
     rows, flat = rows // 2, quads * rows
     modes = lanes // 8
-    heads, tails = halves(in_order([m[...].astype(F32) for m in msgs], place), rows)
+    heads, tails = halves(in_order([m[...] for m in msgs], place), rows)
     rate = own_rates(rate_ref, place, quads)
     nothing = jnp.zeros_like(heads[0])
     before, _, head, tail = scan_blocks(heads, tails, (nothing, nothing), rate, float(length))
@@ -346,7 +347,7 @@
     modes = lanes // 8
     rate = own_rates(rate_ref, place, quads)
     heads, tails = halves(
-        in_order([r[:flat].astype(F32).reshape(shape) for r in lines], level), rows
+        in_order([r[:flat].reshape(shape) for r in lines], level), rows
     )
     nothing = jnp.zeros_like(heads[0])
     before, after, _, _ = scan_blocks(
@@ -362,14 +363,20 @@
     for i in range(count):
         start[0] = jnp.where(level == i, before[i], start[0])
         start[1] = jnp.where(level == i, after[i], start[1])
-    heads, tails = halves(in_order([m[...].astype(F32) for m in msgs], place), rows)
-    before, after, _, _ = scan_blocks(heads, tails, start, rate, float(length))
-    found = [jnp.concatenate(pair, axis=1) for pair in zip(before, after, strict=True)]
-    found = in_order(found, place)
-    low = lane_iota((quads // 2,) + shape[1:]) < lanes // 2
-    for i in range(PLANE):
-        packed = jnp.where(low, found[i][: quads // 2], pltpu.roll(found[i][quads // 2 :], lanes // 2, 2))
-        outs[i][: flat // 2] = packed.astype(BF16).reshape(flat // 2, lanes)
+    heads, tails = halves(in_order([m[...] for m in msgs], place), rows)
+    decay = jnp.exp(-rate * float(length))
+    before, after = [start[0]], [start[1]]
+    for i in range(PLANE - 1):
+        before.append(decay * before[-1] + heads[i])
+        after.insert(0, decay * after[0] + tails[PLANE - 1 - i])
+    low = lane_iota((quads // 2, 2 * rows, lanes)) < lanes // 2
+    packed = []
+    for pair in zip(before, after, strict=True):
+        found = jnp.concatenate(pair, axis=1)
+        found = jnp.where(low, found[: quads // 2], pltpu.roll(found[quads // 2 :], lanes // 2, 2))
+        packed.append(found.astype(BF16).reshape(flat // 2, lanes))
+    for i, found in enumerate(in_order(packed, place)):
+        outs[i][: flat // 2] = found
         outs[i][flat // 2 :] = sums
 
 
@@ -412,19 +419,19 @@
                 gs[slot, local // 8, where, :] = both[rows:]
 
     def finish(slot):
-        conv, ig = (
-            jnp.concatenate(
-                [ref[slot, i].reshape(rows, 8, length) for i in range(part // 8)], axis=1
-            ).astype(BF16)
-            for ref in (cs, gs)
-        )
+        def natural(ref):
+            pieces = [ref[slot, i].reshape(rows, 8, length) for i in range(part // 8)]
+            return jnp.concatenate(pieces, axis=1).astype(BF16)
+
         own = spans[slot]
-        outs[0, slot] = product(g_ref[:, own, :], conv)
-        ig = dot(ig.reshape(rows * part, length), mirror, NN).reshape(conv.shape)
+        ig = dot(natural(gs).reshape(rows * part, length), mirror, NN)
+        outs[0, slot] = product(g_ref[:, own, :], natural(cs))
+        store(0, slot).start()
+        ig = ig.astype(BF16).reshape(rows, part, length)
         outs[1, slot] = product(ig, v_ref[:, own, :])
+        store(1, slot).start()
         outs[2, slot] = product(ig, k_ref[:, own, :])
-        for which in range(3):
-            store(which, slot).start()
+        store(2, slot).start()
 
     for slot in range(count + 1):
         if slot < count:

time: 33.6 us -> 33.4 us (level)
  no operation moved by 1% of the time
where the time goes in v9:
time: 33.4 us; the launch traced here: 33.2 us
  Pallas kernels  14.2 us (43%)
  starting transfers between devices  12.5 us (37%)
  waiting for transfers between devices  5.07 us (15%)
  between operations  0.76 us (2%)
  other arithmetic  0.69 us (2%)
    ppermute x9, starting transfers between devices, swap(): return lax.ppermute(x, 'ctx', [(i, i ^ bits) for i in range(count)])  12.5 us
    ppermute x9, waiting for transfers between devices, swap(): return lax.ppermute(x, 'ctx', [(i, i ^ bits) for i in range(count)])  5.06 us
    pallas_call x3, Pallas kernels, gradients(): call(functools.partial(outputs_kernel, indices), [vmem] * (5 + slots) + [...  3.83 us
    pallas_call x1, Pallas kernels, gradients(): call(sums_kernel, [anywhere] * 4 + [vmem] * 3, [vmem] * 3, [shaped(quarte...  3.41 us
    pallas_call x1, Pallas kernels, gradients(): call(states_kernel, [anywhere] * 5, [vmem] * (2 + PLANE), [shaped((PLANE...  2.86 us
    pallas_call x1, Pallas kernels, gradients(): call(local_kernel, [vmem] * 5, [vmem] * 2, [shaped((PLANE,) + quarter, F3...  2.8 us
  transfers between devices with their start and end apart: 10, of which 5 were waited for; matrix products, arithmetic and copies ran while one was open for 0% of the time, Pallas kernels for 30%

profile of v9, /device:TPU:0, one launch (start us, length us, event | category | flops | bytes accessed | tf_op | source)
XLA Modules:
  0.0 33.2 jit_solution(2868879664590904958)
XLA Ops:
  0.6 2.9 %shard_map.101 = (bf16[3,16,64,128]{3,2,1,0:T(8,128)(2,1)S(1)}, bf16[64,2,16,128]{3,2,1,0:T(8,128)(2,1)S(1)}, f32[16,128]{1,0:T(8,128)S(1)}, bf16[4,64,128]{2,1,...) custom-call(f32[16,64]{1,0:T(8,128)} %bitcast.30, bf16[32,64,128]{2,1,0:T(8,128)(2,1)} %bitcast.15, ...), custom_call_target="tpu_custom_call" | custom-call | flops 1000000000 | bytes 4000000 | tf_op jit(solution)/shard_map/pallas_call | solution.py:491
  3.5 3.0 %collective-permute-start = (bf16[4,64,128]{2,1,0:T(8,128)(2,1)S(1)}, bf16[4,64,128]{2,1,0:T(8,128)(2,1)S(1)}, u32[]{:S(2)}, u32[]{:S(2)}) collective-permute-start(bf16[4,64,128]{2,1,0:T(8,128)(2,1)S(1)} %get-tuple-element.34), channel_id=1, source_target_pairs={{0,2},{2,0},{4,6},{6,4},{8,10},{10,8},{12,14},{14,12},{16,18},{18,... | collective-permute-start | bytes 196616 | tf_op jit(solution)/shard_map/ppermute | solution.py:507
  6.5 1.5 %collective-permute-start.1 = (bf16[4,64,128]{2,1,0:T(8,128)(2,1)S(1)}, bf16[4,64,128]{2,1,0:T(8,128)(2,1)S(1)}, u32[]{:S(2)}, u32[]{:S(2)}) collective-permute-start(bf16[4,64,128]{2,1,0:T(8,128)(2,1)S(1)} %get-tuple-element.35), channel_id=1, source_target_pairs={{0,4},{2,6},{4,0},{6,2},{8,12},{10,14},{12,8},{14,10},{16,20},{18,... | collective-permute-start | bytes 196616 | tf_op jit(solution)/shard_map/ppermute | solution.py:507
  8.0 0.0 collective-permute-start.2
  8.1 3.4 %shard_map.102 = (bf16[16,64,128]{2,1,0:T(8,128)(2,1)S(1)}, bf16[4,64,128]{2,1,0:T(8,128)(2,1)S(1)}, f32[32,128]{1,0:T(8,128)S(1)}) custom-call(bf16[32,64,128]{2,1,0:T(8,128)(2,1)} %bitcast.16, bf16[32,64,128]{2,1,0:T(8,128)(2,1)} %bitcast.21, bf16[32,64,128]{2,1,0:T(8,128)(2,1)} %bitcast.26, bf16[32,64,128]{2,1,0:T(8,128)(2,1)} %bitcast.38, ...), custom_call_target="tpu_custom_call" | custom-call | flops 1000000000 | bytes 4000000 | tf_op jit(solution)/shard_map/pallas_call | solution.py:510
  11.5 1.7 %collective-permute-done.2.refs_3_ = bf16[4,64,128]{2,1,0:T(8,128)(2,1)S(1)} collective-permute-done((bf16[4,64,128]{2,1,0:T(8,128)(2,1)S(1)}, bf16[4,64,128]{2,1,0:T(8,128)(2,1)S(1)}, u32[]{:S(2)}, u32[]{:S(2)}) %collective-permute-start.2) | collective-permute-done | bytes 65568 | tf_op jit(solution)/shard_map/ppermute | solution.py:507
  13.2 0.6 %shard_map.103.after_ref.refs_4_ = bf16[288,128]{1,0:T(8,128)(2,1)S(1)} custom-call(f32[16,128]{1,0:T(8,128)S(1)} %get-tuple-element.32.rate_ref, bf16[4,64,128]{2,1,0:T(8,128)(2,1)S(1)} %get-tuple-element.33.refs_0_, bf16[4,64,128]{2,1,0:T(8,128)(2,1)S(1)} %collective-permute-done.refs_1_, bf16[4,64,128]{2,1,0:T(8,128)(2,1)S(1)} %collective-permute-done.1.refs_2_, ...), custom_call_target="tpu_custom_call" | custom-call | flops 10000000 | bytes 1000000 | tf_op jit(solution)/shard_map/pallas_call | solution.py:521
  13.8 3.6 %collective-permute-start.5 = (bf16[288,128]{1,0:T(8,128)(2,1)S(1)}, bf16[288,128]{1,0:T(8,128)(2,1)S(1)}, u32[]{:S(2)}, u32[]{:S(2)}) collective-permute-start(bf16[288,128]{1,0:T(8,128)(2,1)S(1)} %shard_map.103.after_ref.refs_4_), channel_id=1, source_target_pairs={{0,24},{2,26},{4,28},{6,30},{8,16},{10,18},{12,20},{14,22},{16,8},... | collective-permute-start | bytes 221192 | tf_op jit(solution)/shard_map/ppermute | solution.py:507
  17.5 0.8 %collective-permute-start.3 = (bf16[288,128]{1,0:T(8,128)(2,1)S(1)}, bf16[288,128]{1,0:T(8,128)(2,1)S(1)}, u32[]{:S(2)}, u32[]{:S(2)}) collective-permute-start(bf16[288,128]{1,0:T(8,128)(2,1)S(1)} %shard_map.103.after_ref.refs_4_), channel_id=1, source_target_pairs={{0,8},{2,10},{4,12},{6,14},{8,0},{10,2},{12,4},{14,6},{16,24},{18,... | collective-permute-start | bytes 221192 | tf_op jit(solution)/shard_map/ppermute | solution.py:507
  18.3 2.8 %shard_map.104 = (f32[4,16,64,128]{3,2,1,0:T(8,128)S(1)}, bf16[4,16,16,128]{3,2,1,0:T(8,128)(2,1)S(1)}) custom-call(bf16[16,64,128]{2,1,0:T(8,128)(2,1)S(1)} %get-tuple-element.31.own_ref, bf16[3,16,64,128]{3,2,1,0:T(8,128)(2,1)S(1)} %get-tuple-element.29.xc_ref, f32[16,64]{1,0:T(8,128)S(1)} %bitcast.32, f32[16,64]{1,0:T(8,128)S(1)} %bitcast.33, ...), custom_call_target="tpu_custom_call" | custom-call | flops 1000000000 | bytes 4000000 | tf_op jit(solution)/shard_map/pallas_call | solution.py:531
  21.1 1.6 %collective-permute-done.4.refs_6_ = bf16[288,128]{1,0:T(8,128)(2,1)S(1)} collective-permute-done((bf16[288,128]{1,0:T(8,128)(2,1)S(1)}, bf16[288,128]{1,0:T(8,128)(2,1)S(1)}, u32[]{:S(2)}, u32[]{:S(2)}) %collective-permute-start.4) | collective-permute-done | bytes 73760 | tf_op jit(solution)/shard_map/ppermute | solution.py:507
  22.7 0.6 %shard_map.105 = (bf16[160,128]{1,0:T(8,128)(2,1)S(1)}, bf16[160,128]{1,0:T(8,128)(2,1)S(1)}, bf16[160,128]{1,0:T(8,128)(2,1)S(1)}, bf16[160,128]{1,0:T(8,128)(2,1)S(1)}) custom-call(f32[16,128]{1,0:T(8,128)S(1)} %get-tuple-element.32.rate_ref, bf16[4,16,16,128]{3,2,1,0:T(8,128)(2,1)S(1)} %get-tuple-element.39.after_ref.taps_ref, ...), custom_call_target="tpu_custom_call" | custom-call | flops 10000000 | bytes 1000000 | tf_op jit(solution)/shard_map/pallas_call | solution.py:547
  23.4 1.7 %collective-permute-start.6 = (bf16[160,128]{1,0:T(8,128)(2,1)S(1)}, bf16[160,128]{1,0:T(8,128)(2,1)S(1)}, u32[]{:S(2)}, u32[]{:S(2)}) collective-permute-start(bf16[160,128]{1,0:T(8,128)(2,1)S(1)} %get-tuple-element.40), channel_id=1, source_target_pairs={{0,6},{2,4},{4,2},{6,0},{8,14},{10,12},{12,10},{14,8},{16,22},{18,... | collective-permute-start | bytes 122888 | tf_op jit(solution)/shard_map/ppermute | solution.py:507
  25.1 0.7 %collective-permute-start.7 = (bf16[160,128]{1,0:T(8,128)(2,1)S(1)}, bf16[160,128]{1,0:T(8,128)(2,1)S(1)}, u32[]{:S(2)}, u32[]{:S(2)}) collective-permute-start(bf16[160,128]{1,0:T(8,128)(2,1)S(1)} %get-tuple-element.41), channel_id=1, source_target_pairs={{0,2},{2,0},{4,6},{6,4},{8,10},{10,8},{12,14},{14,12},{16,18},{18,... | collective-permute-start | bytes 122888 | tf_op jit(solution)/shard_map/ppermute | solution.py:507
  25.9 1.1 %collective-permute-start.8 = (bf16[160,128]{1,0:T(8,128)(2,1)S(1)}, bf16[160,128]{1,0:T(8,128)(2,1)S(1)}, u32[]{:S(2)}, u32[]{:S(2)}) collective-permute-start(bf16[160,128]{1,0:T(8,128)(2,1)S(1)} %get-tuple-element.42), channel_id=1, source_target_pairs={{0,4},{2,6},{4,0},{6,2},{8,12},{10,14},{12,8},{14,10},{16,20},{18,... | collective-permute-start | bytes 122888 | tf_op jit(solution)/shard_map/ppermute | solution.py:507
  26.9 1.2 %shard_map.106 = (bf16[32,64,128]{2,1,0:T(8,128)(2,1)}, bf16[32,64,128]{2,1,0:T(8,128)(2,1)}, bf16[32,64,128]{2,1,0:T(8,128)(2,1)}) custom-call(bf16[32,64,128]{2,1,0:T(8,128)(2,1)S(1)} %bitcast.17, bf16[32,64,128]{2,1,0:T(8,128)(2,1)S(1)} %bitcast.22, bf16[32,64,128]{2,1,0:T(8,128)(2,1)S(1)} %bitcast.27, f32[4,16,64,128]{3,2,1,0:T(8,128)S(1)} %get-tuple-element.38.near_ref, ...), custom_call_target="tpu_custom_call" | custom-call | flops 200000000 | bytes 1000000 | tf_op jit(solution)/shard_map/pallas_call | solution.py:572
  28.1 0.2 collective-permute-done.6.refs_0_
  28.3 0.8 %collective-permute-done.7.refs_0_ = bf16[160,128]{1,0:T(8,128)(2,1)S(1)} collective-permute-done((bf16[160,128]{1,0:T(8,128)(2,1)S(1)}, bf16[160,128]{1,0:T(8,128)(2,1)S(1)}, u32[]{:S(2)}, u32[]{:S(2)}) %collective-permute-start.7) | collective-permute-done | bytes 40992 | tf_op jit(solution)/shard_map/ppermute | solution.py:507
  29.1 0.7 %collective-permute-done.8.refs_1_ = bf16[160,128]{1,0:T(8,128)(2,1)S(1)} collective-permute-done((bf16[160,128]{1,0:T(8,128)(2,1)S(1)}, bf16[160,128]{1,0:T(8,128)(2,1)S(1)}, u32[]{:S(2)}, u32[]{:S(2)}) %collective-permute-start.8) | collective-permute-done | bytes 40992 | tf_op jit(solution)/shard_map/ppermute | solution.py:507
  29.9 0.1 add_add_fusion
  29.9 0.0 collective-permute-start.9
  30.0 1.4 %shard_map.107 = (bf16[32,64,128]{2,1,0:T(8,128)(2,1)}, bf16[32,64,128]{2,1,0:T(8,128)(2,1)}, bf16[32,64,128]{2,1,0:T(8,128)(2,1)}) custom-call(bf16[32,64,128]{2,1,0:T(8,128)(2,1)S(1)} %bitcast.18, bf16[32,64,128]{2,1,0:T(8,128)(2,1)S(1)} %bitcast.23, bf16[32,64,128]{2,1,0:T(8,128)(2,1)S(1)} %bitcast.28, ...), custom_call_target="tpu_custom_call", output_to_operand_aliasing={{0}: (7, {}), {1}: (8, {}), {2}: (9, {})} | custom-call | flops 400000000 | bytes 2000000 | tf_op jit(solution)/shard_map/pallas_call | solution.py:572
  31.4 1.2 %shard_map.108 = (bf16[32,64,128]{2,1,0:T(8,128)(2,1)}, bf16[32,64,128]{2,1,0:T(8,128)(2,1)}, bf16[32,64,128]{2,1,0:T(8,128)(2,1)}) custom-call(bf16[32,64,128]{2,1,0:T(8,128)(2,1)S(1)} %bitcast.19, bf16[32,64,128]{2,1,0:T(8,128)(2,1)S(1)} %bitcast.24, bf16[32,64,128]{2,1,0:T(8,128)(2,1)S(1)} %bitcast.29, ...), custom_call_target="tpu_custom_call", output_to_operand_aliasing={{0}: (6, {}), {1}: (7, {}), {2}: (8, {})} | custom-call | flops 200000000 | bytes 1000000 | tf_op jit(solution)/shard_map/pallas_call | solution.py:572
  32.6 0.6 %fusion.1 = (f32[64,16]{0,1:T(8,128)}, f32[64,16]{0,1:T(8,128)}) fusion(f32[32,64]{1,0:T(8,128)S(1)} %add.31, f32[64,16]{0,1:T(8,128)S(1)} %copy-done.4, f32[64,16]{0,1:T(8,128)S(1)} %copy-done.3), kind=kLoop, calls=%fused_computation.3 | loop fusion | flops 5120 | bytes 24576 | tf_op jit(solution)/shard_map/transpose | solution.py:592
  (17 shorter events, 0.0 us)
Async XLA Ops:
  0.6 7.4 %copy-start.3 = (f32[64,16]{0,1:T(8,128)S(1)}, f32[64,16]{0,1:T(8,128)}, u32[]{:S(2)}) copy-start(f32[64,16]{0,1:T(8,128)} %param.11) | copy-start | bytes 12292
  3.5 14.8 %copy-start.4 = (f32[64,16]{0,1:T(8,128)S(1)}, f32[64,16]{0,1:T(8,128)}, u32[]{:S(2)}) copy-start(f32[64,16]{0,1:T(8,128)} %param.10) | copy-start | bytes 12292
  3.5 8.0 %collective-permute-start = (bf16[4,64,128]{2,1,0:T(8,128)(2,1)S(1)}, bf16[4,64,128]{2,1,0:T(8,128)(2,1)S(1)}, u32[]{:S(2)}, u32[]{:S(2)}) collective-permute-start(bf16[4,64,128]{2,1,0:T(8,128)(2,1)S(1)} %get-tuple-element.34), channel_id=1, source_target_pairs={{0,2},{2,0},{4,6},{6,4},{8,10},{10,8},{12,14},{14,12},{16,18},{18,... | collective-permute-start | bytes 196616 | tf_op jit(solution)/shard_map/ppermute | solution.py:507
  6.5 5.0 %collective-permute-start.1 = (bf16[4,64,128]{2,1,0:T(8,128)(2,1)S(1)}, bf16[4,64,128]{2,1,0:T(8,128)(2,1)S(1)}, u32[]{:S(2)}, u32[]{:S(2)}) collective-permute-start(bf16[4,64,128]{2,1,0:T(8,128)(2,1)S(1)} %get-tuple-element.35), channel_id=1, source_target_pairs={{0,4},{2,6},{4,0},{6,2},{8,12},{10,14},{12,8},{14,10},{16,20},{18,... | collective-permute-start | bytes 196616 | tf_op jit(solution)/shard_map/ppermute | solution.py:507
  8.0 5.2 %collective-permute-start.2 = (bf16[4,64,128]{2,1,0:T(8,128)(2,1)S(1)}, bf16[4,64,128]{2,1,0:T(8,128)(2,1)S(1)}, u32[]{:S(2)}, u32[]{:S(2)}) collective-permute-start(bf16[4,64,128]{2,1,0:T(8,128)(2,1)S(1)} %get-tuple-element.36), channel_id=1, source_target_pairs={{0,6},{2,4},{4,2},{6,0},{8,14},{10,12},{12,10},{14,8},{16,22},{18,... | collective-permute-start | bytes 196616 | tf_op jit(solution)/shard_map/ppermute | solution.py:507
  13.8 7.2 %collective-permute-start.5 = (bf16[288,128]{1,0:T(8,128)(2,1)S(1)}, bf16[288,128]{1,0:T(8,128)(2,1)S(1)}, u32[]{:S(2)}, u32[]{:S(2)}) collective-permute-start(bf16[288,128]{1,0:T(8,128)(2,1)S(1)} %shard_map.103.after_ref.refs_4_), channel_id=1, source_target_pairs={{0,24},{2,26},{4,28},{6,30},{8,16},{10,18},{12,20},{14,22},{16,8},... | collective-permute-start | bytes 221192 | tf_op jit(solution)/shard_map/ppermute | solution.py:507
  17.5 5.3 %collective-permute-start.4 = (bf16[288,128]{1,0:T(8,128)(2,1)S(1)}, bf16[288,128]{1,0:T(8,128)(2,1)S(1)}, u32[]{:S(2)}, u32[]{:S(2)}) collective-permute-start(bf16[288,128]{1,0:T(8,128)(2,1)S(1)} %shard_map.103.after_ref.refs_4_), channel_id=1, source_target_pairs={{0,16},{2,18},{4,20},{6,22},{8,24},{10,26},{12,28},{14,30},{16,0},... | collective-permute-start | bytes 221192 | tf_op jit(solution)/shard_map/ppermute | solution.py:507
  17.5 5.3 %collective-permute-start.3 = (bf16[288,128]{1,0:T(8,128)(2,1)S(1)}, bf16[288,128]{1,0:T(8,128)(2,1)S(1)}, u32[]{:S(2)}, u32[]{:S(2)}) collective-permute-start(bf16[288,128]{1,0:T(8,128)(2,1)S(1)} %shard_map.103.after_ref.refs_4_), channel_id=1, source_target_pairs={{0,8},{2,10},{4,12},{6,14},{8,0},{10,2},{12,4},{14,6},{16,24},{18,... | collective-permute-start | bytes 221192 | tf_op jit(solution)/shard_map/ppermute | solution.py:507
  18.3 8.7 %copy-start = (bf16[2048,128]{1,0:T(8,128)(2,1)S(1)}, bf16[2048,128]{1,0:T(8,128)(2,1)}, u32[]{:S(2)}) copy-start(bf16[2048,128]{1,0:T(8,128)(2,1)} %param.7) | copy-start | bytes 1572868
  18.3 8.7 %copy-start.1 = (bf16[2048,128]{1,0:T(8,128)(2,1)S(1)}, bf16[2048,128]{1,0:T(8,128)(2,1)}, u32[]{:S(2)}) copy-start(bf16[2048,128]{1,0:T(8,128)(2,1)} %param.8) | copy-start | bytes 1572868
  18.3 8.7 %copy-start.2 = (bf16[2048,128]{1,0:T(8,128)(2,1)S(1)}, bf16[2048,128]{1,0:T(8,128)(2,1)}, u32[]{:S(2)}) copy-start(bf16[2048,128]{1,0:T(8,128)(2,1)} %param.9) | copy-start | bytes 1572868
  23.4 5.0 %collective-permute-start.6 = (bf16[160,128]{1,0:T(8,128)(2,1)S(1)}, bf16[160,128]{1,0:T(8,128)(2,1)S(1)}, u32[]{:S(2)}, u32[]{:S(2)}) collective-permute-start(bf16[160,128]{1,0:T(8,128)(2,1)S(1)} %get-tuple-element.40), channel_id=1, source_target_pairs={{0,6},{2,4},{4,2},{6,0},{8,14},{10,12},{12,10},{14,8},{16,22},{18,... | collective-permute-start | bytes 122888 | tf_op jit(solution)/shard_map/ppermute | solution.py:507
  25.1 4.0 %collective-permute-start.7 = (bf16[160,128]{1,0:T(8,128)(2,1)S(1)}, bf16[160,128]{1,0:T(8,128)(2,1)S(1)}, u32[]{:S(2)}, u32[]{:S(2)}) collective-permute-start(bf16[160,128]{1,0:T(8,128)(2,1)S(1)} %get-tuple-element.41), channel_id=1, source_target_pairs={{0,2},{2,0},{4,6},{6,4},{8,10},{10,8},{12,14},{14,12},{16,18},{18,... | collective-permute-start | bytes 122888 | tf_op jit(solution)/shard_map/ppermute | solution.py:507
  25.9 4.0 %collective-permute-start.8 = (bf16[160,128]{1,0:T(8,128)(2,1)S(1)}, bf16[160,128]{1,0:T(8,128)(2,1)S(1)}, u32[]{:S(2)}, u32[]{:S(2)}) collective-permute-start(bf16[160,128]{1,0:T(8,128)(2,1)S(1)} %get-tuple-element.42), channel_id=1, source_target_pairs={{0,4},{2,6},{4,0},{6,2},{8,12},{10,14},{12,8},{14,10},{16,20},{18,... | collective-permute-start | bytes 122888 | tf_op jit(solution)/shard_map/ppermute | solution.py:507
  29.9 2.7 %collective-permute-start.9 = (f32[32,64]{1,0:T(8,128)S(1)}, f32[32,64]{1,0:T(8,128)S(1)}, u32[]{:S(2)}, u32[]{:S(2)}) collective-permute-start(f32[32,64]{1,0:T(8,128)S(1)} %add_add_fusion), channel_id=1, source_target_pairs={{0,1},{1,0},{2,3},{3,2},{4,5},{5,4},{6,7},{7,6},{8,9},{9,8},{10,11... | collective-permute-start | bytes 24584 | tf_op jit(solution)/shard_map/ppermute | solution.py:566

commit v10 on v9

--- a/solution.py
+++ b/solution.py
@@ -506,7 +506,9 @@
     def swap(x, bits):
         return lax.ppermute(x, "ctx", [(i, i ^ bits) for i in range(count)])
 
-    near = [swap(own[i - 1], i) for i in range(1, PLANE)]
+    near = []
+    for i in range(1, PLANE):
+        near.append(swap(own[i - 1], i))
     xo, mine, sums = call(
         sums_kernel,
         [anywhere] * 4 + [vmem] * 3,
@@ -567,7 +569,7 @@
         bit *= 2
 
     outs = ()
-    for indices in ((0,), tuple(range(1, PLANE - 1)), (PLANE - 1,)):
+    for indices in ((0,), (PLANE - 1, 1), (2,)):
         slots = len(indices)
         outs = call(
             functools.partial(outputs_kernel, indices),

time: 33.4 us -> 33.4 us (level)
  transfers between devices with their start and end apart: 10 -> 10, of which waited for: 5 -> 4; matrix products, arithmetic and copies ran while one was open for 0% -> 0% of each run, Pallas kernels for 30% -> 30%
where the time goes in v10:
time: 33.4 us; the launch traced here: 33.2 us
  Pallas kernels  14.2 us (43%)
  starting transfers between devices  12.5 us (37%)
  waiting for transfers between devices  5.03 us (15%)
  between operations  0.76 us (2%)
  other arithmetic  0.69 us (2%)
    ppermute x9, starting transfers between devices, swap(): return lax.ppermute(x, 'ctx', [(i, i ^ bits) for i in range(count)])  12.5 us
    ppermute x9, waiting for transfers between devices, swap(): return lax.ppermute(x, 'ctx', [(i, i ^ bits) for i in range(count)])  5.03 us
    pallas_call x3, Pallas kernels, gradients(): call(functools.partial(outputs_kernel, indices), [vmem] * (5 + slots) + [...  3.84 us
    pallas_call x1, Pallas kernels, gradients(): call(sums_kernel, [anywhere] * 4 + [vmem] * 3, [vmem] * 3, [shaped(quarte...  3.41 us
    pallas_call x1, Pallas kernels, gradients(): call(states_kernel, [anywhere] * 5, [vmem] * (2 + PLANE), [shaped((PLANE...  2.86 us
    pallas_call x1, Pallas kernels, gradients(): call(local_kernel, [vmem] * 5, [vmem] * 2, [shaped((PLANE,) + quarter, F3...  2.8 us
  transfers between devices with their start and end apart: 10, of which 4 were waited for; matrix products, arithmetic and copies ran while one was open for 0% of the time, Pallas kernels for 30%

profile of v10, /device:TPU:0, one launch (start us, length us, event | category | flops | bytes accessed | tf_op | source)
XLA Modules:
  0.0 33.2 jit_solution(15763253495346460867)
XLA Ops:
  0.6 2.9 %shard_map.101 = (bf16[3,16,64,128]{3,2,1,0:T(8,128)(2,1)S(1)}, bf16[64,2,16,128]{3,2,1,0:T(8,128)(2,1)S(1)}, f32[16,128]{1,0:T(8,128)S(1)}, bf16[4,64,128]{2,1,...) custom-call(f32[16,64]{1,0:T(8,128)} %bitcast.30, bf16[32,64,128]{2,1,0:T(8,128)(2,1)} %bitcast.15, ...), custom_call_target="tpu_custom_call" | custom-call | flops 1000000000 | bytes 4000000 | tf_op jit(solution)/shard_map/pallas_call | solution.py:491
  3.5 0.0 copy-start.4
  3.5 3.0 %collective-permute-start = (bf16[4,64,128]{2,1,0:T(8,128)(2,1)S(1)}, bf16[4,64,128]{2,1,0:T(8,128)(2,1)S(1)}, u32[]{:S(2)}, u32[]{:S(2)}) collective-permute-start(bf16[4,64,128]{2,1,0:T(8,128)(2,1)S(1)} %get-tuple-element.34), channel_id=1, source_target_pairs={{0,2},{2,0},{4,6},{6,4},{8,10},{10,8},{12,14},{14,12},{16,18},{18,... | collective-permute-start | bytes 196616 | tf_op jit(solution)/shard_map/ppermute | solution.py:507
  6.5 1.5 %collective-permute-start.1 = (bf16[4,64,128]{2,1,0:T(8,128)(2,1)S(1)}, bf16[4,64,128]{2,1,0:T(8,128)(2,1)S(1)}, u32[]{:S(2)}, u32[]{:S(2)}) collective-permute-start(bf16[4,64,128]{2,1,0:T(8,128)(2,1)S(1)} %get-tuple-element.35), channel_id=1, source_target_pairs={{0,4},{2,6},{4,0},{6,2},{8,12},{10,14},{12,8},{14,10},{16,20},{18,... | collective-permute-start | bytes 196616 | tf_op jit(solution)/shard_map/ppermute | solution.py:507
  8.0 0.0 collective-permute-start.2
  8.1 3.4 %shard_map.102 = (bf16[16,64,128]{2,1,0:T(8,128)(2,1)S(1)}, bf16[4,64,128]{2,1,0:T(8,128)(2,1)S(1)}, f32[32,128]{1,0:T(8,128)S(1)}) custom-call(bf16[32,64,128]{2,1,0:T(8,128)(2,1)} %bitcast.16, bf16[32,64,128]{2,1,0:T(8,128)(2,1)} %bitcast.21, bf16[32,64,128]{2,1,0:T(8,128)(2,1)} %bitcast.26, bf16[32,64,128]{2,1,0:T(8,128)(2,1)} %bitcast.38, ...), custom_call_target="tpu_custom_call" | custom-call | flops 1000000000 | bytes 4000000 | tf_op jit(solution)/shard_map/pallas_call | solution.py:512
  11.5 1.7 %collective-permute-done.2.refs_3_ = bf16[4,64,128]{2,1,0:T(8,128)(2,1)S(1)} collective-permute-done((bf16[4,64,128]{2,1,0:T(8,128)(2,1)S(1)}, bf16[4,64,128]{2,1,0:T(8,128)(2,1)S(1)}, u32[]{:S(2)}, u32[]{:S(2)}) %collective-permute-start.2) | collective-permute-done | bytes 65568 | tf_op jit(solution)/shard_map/ppermute | solution.py:507
  13.2 0.6 %shard_map.103.after_ref.refs_4_ = bf16[288,128]{1,0:T(8,128)(2,1)S(1)} custom-call(f32[16,128]{1,0:T(8,128)S(1)} %get-tuple-element.32.rate_ref, bf16[4,64,128]{2,1,0:T(8,128)(2,1)S(1)} %get-tuple-element.33.refs_0_, bf16[4,64,128]{2,1,0:T(8,128)(2,1)S(1)} %collective-permute-done.refs_1_, bf16[4,64,128]{2,1,0:T(8,128)(2,1)S(1)} %collective-permute-done.1.refs_2_, ...), custom_call_target="tpu_custom_call" | custom-call | flops 10000000 | bytes 1000000 | tf_op jit(solution)/shard_map/pallas_call | solution.py:523
  13.8 3.6 %collective-permute-start.5 = (bf16[288,128]{1,0:T(8,128)(2,1)S(1)}, bf16[288,128]{1,0:T(8,128)(2,1)S(1)}, u32[]{:S(2)}, u32[]{:S(2)}) collective-permute-start(bf16[288,128]{1,0:T(8,128)(2,1)S(1)} %shard_map.103.after_ref.refs_4_), channel_id=1, source_target_pairs={{0,24},{2,26},{4,28},{6,30},{8,16},{10,18},{12,20},{14,22},{16,8},... | collective-permute-start | bytes 221192 | tf_op jit(solution)/shard_map/ppermute | solution.py:507
  17.5 0.8 %collective-permute-start.3 = (bf16[288,128]{1,0:T(8,128)(2,1)S(1)}, bf16[288,128]{1,0:T(8,128)(2,1)S(1)}, u32[]{:S(2)}, u32[]{:S(2)}) collective-permute-start(bf16[288,128]{1,0:T(8,128)(2,1)S(1)} %shard_map.103.after_ref.refs_4_), channel_id=1, source_target_pairs={{0,8},{2,10},{4,12},{6,14},{8,0},{10,2},{12,4},{14,6},{16,24},{18,... | collective-permute-start | bytes 221192 | tf_op jit(solution)/shard_map/ppermute | solution.py:507
  18.3 2.8 %shard_map.104 = (f32[4,16,64,128]{3,2,1,0:T(8,128)S(1)}, bf16[4,16,16,128]{3,2,1,0:T(8,128)(2,1)S(1)}) custom-call(bf16[16,64,128]{2,1,0:T(8,128)(2,1)S(1)} %get-tuple-element.31.own_ref, bf16[3,16,64,128]{3,2,1,0:T(8,128)(2,1)S(1)} %get-tuple-element.29.xc_ref, f32[16,64]{1,0:T(8,128)S(1)} %bitcast.32, f32[16,64]{1,0:T(8,128)S(1)} %bitcast.33, ...), custom_call_target="tpu_custom_call" | custom-call | flops 1000000000 | bytes 4000000 | tf_op jit(solution)/shard_map/pallas_call | solution.py:533
  21.1 1.6 %collective-permute-done.4.refs_6_ = bf16[288,128]{1,0:T(8,128)(2,1)S(1)} collective-permute-done((bf16[288,128]{1,0:T(8,128)(2,1)S(1)}, bf16[288,128]{1,0:T(8,128)(2,1)S(1)}, u32[]{:S(2)}, u32[]{:S(2)}) %collective-permute-start.4) | collective-permute-done | bytes 73760 | tf_op jit(solution)/shard_map/ppermute | solution.py:507
  22.7 0.6 %shard_map.105 = (bf16[160,128]{1,0:T(8,128)(2,1)S(1)}, bf16[160,128]{1,0:T(8,128)(2,1)S(1)}, bf16[160,128]{1,0:T(8,128)(2,1)S(1)}, bf16[160,128]{1,0:T(8,128)(2,1)S(1)}) custom-call(f32[16,128]{1,0:T(8,128)S(1)} %get-tuple-element.32.rate_ref, bf16[4,16,16,128]{3,2,1,0:T(8,128)(2,1)S(1)} %get-tuple-element.39.after_ref.taps_ref, ...), custom_call_target="tpu_custom_call" | custom-call | flops 10000000 | bytes 1000000 | tf_op jit(solution)/shard_map/pallas_call | solution.py:549
  23.4 1.0 %collective-permute-start.6 = (bf16[160,128]{1,0:T(8,128)(2,1)S(1)}, bf16[160,128]{1,0:T(8,128)(2,1)S(1)}, u32[]{:S(2)}, u32[]{:S(2)}) collective-permute-start(bf16[160,128]{1,0:T(8,128)(2,1)S(1)} %get-tuple-element.40), channel_id=1, source_target_pairs={{0,4},{2,6},{4,0},{6,2},{8,12},{10,14},{12,8},{14,10},{16,20},{18,... | collective-permute-start | bytes 122888 | tf_op jit(solution)/shard_map/ppermute | solution.py:507
  24.4 1.4 %collective-permute-start.7 = (bf16[160,128]{1,0:T(8,128)(2,1)S(1)}, bf16[160,128]{1,0:T(8,128)(2,1)S(1)}, u32[]{:S(2)}, u32[]{:S(2)}) collective-permute-start(bf16[160,128]{1,0:T(8,128)(2,1)S(1)} %get-tuple-element.41), channel_id=1, source_target_pairs={{0,6},{2,4},{4,2},{6,0},{8,14},{10,12},{12,10},{14,8},{16,22},{18,... | collective-permute-start | bytes 122888 | tf_op jit(solution)/shard_map/ppermute | solution.py:507
  25.8 1.1 %collective-permute-start.8 = (bf16[160,128]{1,0:T(8,128)(2,1)S(1)}, bf16[160,128]{1,0:T(8,128)(2,1)S(1)}, u32[]{:S(2)}, u32[]{:S(2)}) collective-permute-start(bf16[160,128]{1,0:T(8,128)(2,1)S(1)} %get-tuple-element.42), channel_id=1, source_target_pairs={{0,2},{2,0},{4,6},{6,4},{8,10},{10,8},{12,14},{14,12},{16,18},{18,... | collective-permute-start | bytes 122888 | tf_op jit(solution)/shard_map/ppermute | solution.py:507
  26.9 1.2 %shard_map.106 = (bf16[32,64,128]{2,1,0:T(8,128)(2,1)}, bf16[32,64,128]{2,1,0:T(8,128)(2,1)}, bf16[32,64,128]{2,1,0:T(8,128)(2,1)}) custom-call(bf16[32,64,128]{2,1,0:T(8,128)(2,1)S(1)} %bitcast.17, bf16[32,64,128]{2,1,0:T(8,128)(2,1)S(1)} %bitcast.22, bf16[32,64,128]{2,1,0:T(8,128)(2,1)S(1)} %bitcast.27, f32[4,16,64,128]{3,2,1,0:T(8,128)S(1)} %get-tuple-element.38.near_ref, ...), custom_call_target="tpu_custom_call" | custom-call | flops 200000000 | bytes 1000000 | tf_op jit(solution)/shard_map/pallas_call | solution.py:574
  28.2 1.1 %collective-permute-done.7.refs_0_ = bf16[160,128]{1,0:T(8,128)(2,1)S(1)} collective-permute-done((bf16[160,128]{1,0:T(8,128)(2,1)S(1)}, bf16[160,128]{1,0:T(8,128)(2,1)S(1)}, u32[]{:S(2)}, u32[]{:S(2)}) %collective-permute-start.7) | collective-permute-done | bytes 40992 | tf_op jit(solution)/shard_map/ppermute | solution.py:507
  29.3 0.5 %collective-permute-done.8.refs_1_ = bf16[160,128]{1,0:T(8,128)(2,1)S(1)} collective-permute-done((bf16[160,128]{1,0:T(8,128)(2,1)S(1)}, bf16[160,128]{1,0:T(8,128)(2,1)S(1)}, u32[]{:S(2)}, u32[]{:S(2)}) %collective-permute-start.8) | collective-permute-done | bytes 40992 | tf_op jit(solution)/shard_map/ppermute | solution.py:507
  29.8 0.1 add_add_fusion
  29.9 0.0 collective-permute-start.9
  29.9 1.4 %shard_map.107 = (bf16[32,64,128]{2,1,0:T(8,128)(2,1)}, bf16[32,64,128]{2,1,0:T(8,128)(2,1)}, bf16[32,64,128]{2,1,0:T(8,128)(2,1)}) custom-call(bf16[32,64,128]{2,1,0:T(8,128)(2,1)S(1)} %bitcast.18, bf16[32,64,128]{2,1,0:T(8,128)(2,1)S(1)} %bitcast.23, bf16[32,64,128]{2,1,0:T(8,128)(2,1)S(1)} %bitcast.28, ...), custom_call_target="tpu_custom_call", output_to_operand_aliasing={{0}: (7, {}), {1}: (8, {}), {2}: (9, {})} | custom-call | flops 400000000 | bytes 2000000 | tf_op jit(solution)/shard_map/pallas_call | solution.py:574
  31.3 1.2 %shard_map.108 = (bf16[32,64,128]{2,1,0:T(8,128)(2,1)}, bf16[32,64,128]{2,1,0:T(8,128)(2,1)}, bf16[32,64,128]{2,1,0:T(8,128)(2,1)}) custom-call(bf16[32,64,128]{2,1,0:T(8,128)(2,1)S(1)} %bitcast.19, bf16[32,64,128]{2,1,0:T(8,128)(2,1)S(1)} %bitcast.24, bf16[32,64,128]{2,1,0:T(8,128)(2,1)S(1)} %bitcast.29, ...), custom_call_target="tpu_custom_call", output_to_operand_aliasing={{0}: (6, {}), {1}: (7, {}), {2}: (8, {})} | custom-call | flops 200000000 | bytes 1000000 | tf_op jit(solution)/shard_map/pallas_call | solution.py:574
  32.6 0.6 %fusion.1 = (f32[64,16]{0,1:T(8,128)}, f32[64,16]{0,1:T(8,128)}) fusion(f32[32,64]{1,0:T(8,128)S(1)} %add.31, f32[64,16]{0,1:T(8,128)S(1)} %copy-done.4, f32[64,16]{0,1:T(8,128)S(1)} %copy-done.3), kind=kLoop, calls=%fused_computation.3 | loop fusion | flops 5120 | bytes 24576 | tf_op jit(solution)/shard_map/transpose | solution.py:594
  (17 shorter events, 0.0 us)
Async XLA Ops:
  0.6 7.4 %copy-start.3 = (f32[64,16]{0,1:T(8,128)S(1)}, f32[64,16]{0,1:T(8,128)}, u32[]{:S(2)}) copy-start(f32[64,16]{0,1:T(8,128)} %param.11) | copy-start | bytes 12292
  3.5 14.8 %copy-start.4 = (f32[64,16]{0,1:T(8,128)S(1)}, f32[64,16]{0,1:T(8,128)}, u32[]{:S(2)}) copy-start(f32[64,16]{0,1:T(8,128)} %param.10) | copy-start | bytes 12292
  3.5 8.0 %collective-permute-start = (bf16[4,64,128]{2,1,0:T(8,128)(2,1)S(1)}, bf16[4,64,128]{2,1,0:T(8,128)(2,1)S(1)}, u32[]{:S(2)}, u32[]{:S(2)}) collective-permute-start(bf16[4,64,128]{2,1,0:T(8,128)(2,1)S(1)} %get-tuple-element.34), channel_id=1, source_target_pairs={{0,2},{2,0},{4,6},{6,4},{8,10},{10,8},{12,14},{14,12},{16,18},{18,... | collective-permute-start | bytes 196616 | tf_op jit(solution)/shard_map/ppermute | solution.py:507
  6.5 5.0 %collective-permute-start.1 = (bf16[4,64,128]{2,1,0:T(8,128)(2,1)S(1)}, bf16[4,64,128]{2,1,0:T(8,128)(2,1)S(1)}, u32[]{:S(2)}, u32[]{:S(2)}) collective-permute-start(bf16[4,64,128]{2,1,0:T(8,128)(2,1)S(1)} %get-tuple-element.35), channel_id=1, source_target_pairs={{0,4},{2,6},{4,0},{6,2},{8,12},{10,14},{12,8},{14,10},{16,20},{18,... | collective-permute-start | bytes 196616 | tf_op jit(solution)/shard_map/ppermute | solution.py:507
  8.0 5.2 %collective-permute-start.2 = (bf16[4,64,128]{2,1,0:T(8,128)(2,1)S(1)}, bf16[4,64,128]{2,1,0:T(8,128)(2,1)S(1)}, u32[]{:S(2)}, u32[]{:S(2)}) collective-permute-start(bf16[4,64,128]{2,1,0:T(8,128)(2,1)S(1)} %get-tuple-element.36), channel_id=1, source_target_pairs={{0,6},{2,4},{4,2},{6,0},{8,14},{10,12},{12,10},{14,8},{16,22},{18,... | collective-permute-start | bytes 196616 | tf_op jit(solution)/shard_map/ppermute | solution.py:507
  13.8 7.2 %collective-permute-start.5 = (bf16[288,128]{1,0:T(8,128)(2,1)S(1)}, bf16[288,128]{1,0:T(8,128)(2,1)S(1)}, u32[]{:S(2)}, u32[]{:S(2)}) collective-permute-start(bf16[288,128]{1,0:T(8,128)(2,1)S(1)} %shard_map.103.after_ref.refs_4_), channel_id=1, source_target_pairs={{0,24},{2,26},{4,28},{6,30},{8,16},{10,18},{12,20},{14,22},{16,8},... | collective-permute-start | bytes 221192 | tf_op jit(solution)/shard_map/ppermute | solution.py:507
  17.5 5.3 %collective-permute-start.4 = (bf16[288,128]{1,0:T(8,128)(2,1)S(1)}, bf16[288,128]{1,0:T(8,128)(2,1)S(1)}, u32[]{:S(2)}, u32[]{:S(2)}) collective-permute-start(bf16[288,128]{1,0:T(8,128)(2,1)S(1)} %shard_map.103.after_ref.refs_4_), channel_id=1, source_target_pairs={{0,16},{2,18},{4,20},{6,22},{8,24},{10,26},{12,28},{14,30},{16,0},... | collective-permute-start | bytes 221192 | tf_op jit(solution)/shard_map/ppermute | solution.py:507
  17.5 5.3 %collective-permute-start.3 = (bf16[288,128]{1,0:T(8,128)(2,1)S(1)}, bf16[288,128]{1,0:T(8,128)(2,1)S(1)}, u32[]{:S(2)}, u32[]{:S(2)}) collective-permute-start(bf16[288,128]{1,0:T(8,128)(2,1)S(1)} %shard_map.103.after_ref.refs_4_), channel_id=1, source_target_pairs={{0,8},{2,10},{4,12},{6,14},{8,0},{10,2},{12,4},{14,6},{16,24},{18,... | collective-permute-start | bytes 221192 | tf_op jit(solution)/shard_map/ppermute | solution.py:507
  18.3 8.7 %copy-start = (bf16[2048,128]{1,0:T(8,128)(2,1)S(1)}, bf16[2048,128]{1,0:T(8,128)(2,1)}, u32[]{:S(2)}) copy-start(bf16[2048,128]{1,0:T(8,128)(2,1)} %param.7) | copy-start | bytes 1572868
  18.3 8.7 %copy-start.1 = (bf16[2048,128]{1,0:T(8,128)(2,1)S(1)}, bf16[2048,128]{1,0:T(8,128)(2,1)}, u32[]{:S(2)}) copy-start(bf16[2048,128]{1,0:T(8,128)(2,1)} %param.8) | copy-start | bytes 1572868
  18.3 8.7 %copy-start.2 = (bf16[2048,128]{1,0:T(8,128)(2,1)S(1)}, bf16[2048,128]{1,0:T(8,128)(2,1)}, u32[]{:S(2)}) copy-start(bf16[2048,128]{1,0:T(8,128)(2,1)} %param.9) | copy-start | bytes 1572868
  23.4 4.8 %collective-permute-start.6 = (bf16[160,128]{1,0:T(8,128)(2,1)S(1)}, bf16[160,128]{1,0:T(8,128)(2,1)S(1)}, u32[]{:S(2)}, u32[]{:S(2)}) collective-permute-start(bf16[160,128]{1,0:T(8,128)(2,1)S(1)} %get-tuple-element.40), channel_id=1, source_target_pairs={{0,4},{2,6},{4,0},{6,2},{8,12},{10,14},{12,8},{14,10},{16,20},{18,... | collective-permute-start | bytes 122888 | tf_op jit(solution)/shard_map/ppermute | solution.py:507
  24.4 4.9 %collective-permute-start.7 = (bf16[160,128]{1,0:T(8,128)(2,1)S(1)}, bf16[160,128]{1,0:T(8,128)(2,1)S(1)}, u32[]{:S(2)}, u32[]{:S(2)}) collective-permute-start(bf16[160,128]{1,0:T(8,128)(2,1)S(1)} %get-tuple-element.41), channel_id=1, source_target_pairs={{0,6},{2,4},{4,2},{6,0},{8,14},{10,12},{12,10},{14,8},{16,22},{18,... | collective-permute-start | bytes 122888 | tf_op jit(solution)/shard_map/ppermute | solution.py:507
  25.8 4.0 %collective-permute-start.8 = (bf16[160,128]{1,0:T(8,128)(2,1)S(1)}, bf16[160,128]{1,0:T(8,128)(2,1)S(1)}, u32[]{:S(2)}, u32[]{:S(2)}) collective-permute-start(bf16[160,128]{1,0:T(8,128)(2,1)S(1)} %get-tuple-element.42), channel_id=1, source_target_pairs={{0,2},{2,0},{4,6},{6,4},{8,10},{10,8},{12,14},{14,12},{16,18},{18,... | collective-permute-start | bytes 122888 | tf_op jit(solution)/shard_map/ppermute | solution.py:507
  29.9 2.7 %collective-permute-start.9 = (f32[32,64]{1,0:T(8,128)S(1)}, f32[32,64]{1,0:T(8,128)S(1)}, u32[]{:S(2)}, u32[]{:S(2)}) collective-permute-start(f32[32,64]{1,0:T(8,128)S(1)} %add_add_fusion), channel_id=1, source_target_pairs={{0,1},{1,0},{2,3},{3,2},{4,5},{5,4},{6,7},{7,6},{8,9},{9,8},{10,11... | collective-permute-start | bytes 24584 | tf_op jit(solution)/shard_map/ppermute | solution.py:568

commit v11 on v10

--- a/solution.py
+++ b/solution.py
@@ -136,7 +136,7 @@
 
 
 def sums_kernel(k_hbm, v_hbm, g_hbm, q_hbm, xc_ref, w_ref, dec_ref, own_ref, out_ref, sums_ref, *rest):
-    bufs, sems, gs, cs, corr_ref = rest
+    bufs, sems, gs, cs, prods_ref = rest
     place, _ = places()
     work = Reducer((k_hbm, v_hbm, g_hbm, q_hbm), bufs, sems, w_ref, gs, cs)
     for copy in work.copies(0, place):
@@ -148,31 +148,36 @@
         lane_iota((length, length)) + lax.broadcasted_iota(jnp.int32, (length, length), 0) < length
     )
 
-    def correlate(ref, base):
+    def multiply(index, ref):
         for local in range(part):
-            prods = jnp.where(paired, dot(ref[local, :rows], ref[local, rows:], TN), 0.0)
-            prods = pltpu.roll(prods, 0, 1, stride=1, stride_axis=0)
-            corr_ref[pl.ds(base + local, 1), :] = jnp.sum(prods, axis=0, keepdims=True)
-
-    def others(slot, _):
-        correlate(xc_ref.at[slot], part * (place ^ (slot + 1)))
+            prods = dot(ref[local, :rows], ref[local, rows:], TN)
+            prods_ref[index, local] = jnp.where(paired, prods, 0.0).astype(BF16)
+
+    def others(index, _):
+        multiply(index, xc_ref.at[index - 1])
         return 0
 
-    lax.fori_loop(0, PLANE - 1, others, 0)
+    lax.fori_loop(1, PLANE, others, 0)
     work.load(0, place)
     work.reduce(0, place, own_ref, out_ref)
-    correlate(own_ref, part * place)
+    multiply(0, own_ref)
     dec = dec_ref[...]
-    lag = float(length - 1) - lane_iota((modes, length)).astype(F32)
+    middle = float(length // 2) - lane_iota((modes, length)).astype(F32)
     lane = lane_iota((modes, sums_ref.shape[1]))
 
-    def contract(quarter, carry):
+    def contract(index, carry):
         plain, moment = carry
         for local in range(part):
-            group = quarter * part + local
-            terms = jnp.exp(-column(dec, group) * lag) * corr_ref[pl.ds(group, 1), :]
-            plain = jnp.where(lane == group, jnp.sum(terms, axis=1, keepdims=True), plain)
-            moment = jnp.where(lane == group, jnp.sum(terms * lag, axis=1, keepdims=True), moment)
+            group = (place ^ index) * part + local
+            rate = column(dec, group)
+            basis = jnp.exp(-rate * middle)
+            left = jnp.concatenate([basis, middle * basis], axis=0).astype(BF16)
+            both = dot(left, prods_ref[index, local], NN)
+            basis = basis * jnp.exp(rate)
+            first = jnp.sum(basis * both[:modes], axis=1, keepdims=True)
+            second = basis * ((middle - 1.0) * both[:modes] + both[modes:])
+            plain = jnp.where(lane == group, first, plain)
+            moment = jnp.where(lane == group, jnp.sum(second, axis=1, keepdims=True), moment)
         return plain, moment
 
     zero = jnp.zeros(lane.shape, F32)
@@ -514,7 +519,7 @@
         [anywhere] * 4 + [vmem] * 3,
         [vmem] * 3,
         [shaped(quarter, BF16), block, shaped((2 * modes, lanes), F32)],
-        reducer(1) + [pltpu.VMEM((groups, length), F32)],
+        reducer(1) + [pltpu.VMEM((PLANE, part, length, length), BF16)],
         10**9,
         4 * 10**6,
     )(*in_hbm(key, value, grad, query), xc, weights, decay)
@@ -569,7 +574,7 @@
         bit *= 2
 
     outs = ()
-    for indices in ((0,), (PLANE - 1, 1), (2,)):
+    for indices in ((0,), (PLANE - 1,), tuple(range(1, PLANE - 1))):
         slots = len(indices)
         outs = call(
             functools.partial(outputs_kernel, indices),

time: 33.4 us -> 34 us (1.018)
  waiting for transfers between devices: 5.03 us -> 5.77 us
    ppermute x9, waiting for transfers between devices: 5.03 us -> 5.77 us  [swap(): return lax.ppermute(x, 'ctx', [(i, i ^ bits) for i in range(count)])]
  transfers between devices with their start and end apart: 10 -> 10, of which waited for: 4 -> 4; matrix products, arithmetic and copies ran while one was open for 0% -> 0% of each run, Pallas kernels for 30% -> 29%
where the time goes in v11:
time: 34 us; the launch traced here: 33.9 us
  Pallas kernels  14.1 us (41%)
  starting transfers between devices  12.5 us (37%)
  waiting for transfers between devices  5.77 us (17%)
  between operations  0.76 us (2%)
  other arithmetic  0.69 us (2%)
    ppermute x9, starting transfers between devices, swap(): return lax.ppermute(x, 'ctx', [(i, i ^ bits) for i in range(count)])  12.5 us
    ppermute x9, waiting for transfers between devices, swap(): return lax.ppermute(x, 'ctx', [(i, i ^ bits) for i in range(count)])  5.77 us
    pallas_call x3, Pallas kernels, gradients(): call(functools.partial(outputs_kernel, indices), [vmem] * (5 + slots) + [...  3.83 us
    pallas_call x1, Pallas kernels, gradients(): call(sums_kernel, [anywhere] * 4 + [vmem] * 3, [vmem] * 3, [shaped(quarte...  3.36 us
    pallas_call x1, Pallas kernels, gradients(): call(states_kernel, [anywhere] * 5, [vmem] * (2 + PLANE), [shaped((PLANE...  2.86 us
    pallas_call x1, Pallas kernels, gradients(): call(local_kernel, [vmem] * 5, [vmem] * 2, [shaped((PLANE,) + quarter, F3...  2.8 us
  transfers between devices with their start and end apart: 10, of which 4 were waited for; matrix products, arithmetic and copies ran while one was open for 0% of the time, Pallas kernels for 29%

profile of v11, /device:TPU:0, one launch (start us, length us, event | category | flops | bytes accessed | tf_op | source)
XLA Modules:
  0.0 33.9 jit_solution(12040508031860428281)
XLA Ops:
  0.6 2.9 %shard_map.101 = (bf16[3,16,64,128]{3,2,1,0:T(8,128)(2,1)S(1)}, bf16[64,2,16,128]{3,2,1,0:T(8,128)(2,1)S(1)}, f32[16,128]{1,0:T(8,128)S(1)}, bf16[4,64,128]{2,1,...) custom-call(f32[16,64]{1,0:T(8,128)} %bitcast.30, bf16[32,64,128]{2,1,0:T(8,128)(2,1)} %bitcast.15, ...), custom_call_target="tpu_custom_call" | custom-call | flops 1000000000 | bytes 4000000 | tf_op jit(solution)/shard_map/pallas_call | solution.py:496
  3.5 0.0 copy-start.4
  3.5 3.0 %collective-permute-start = (bf16[4,64,128]{2,1,0:T(8,128)(2,1)S(1)}, bf16[4,64,128]{2,1,0:T(8,128)(2,1)S(1)}, u32[]{:S(2)}, u32[]{:S(2)}) collective-permute-start(bf16[4,64,128]{2,1,0:T(8,128)(2,1)S(1)} %get-tuple-element.34), channel_id=1, source_target_pairs={{0,2},{2,0},{4,6},{6,4},{8,10},{10,8},{12,14},{14,12},{16,18},{18,... | collective-permute-start | bytes 196616 | tf_op jit(solution)/shard_map/ppermute | solution.py:512
  6.5 1.5 %collective-permute-start.1 = (bf16[4,64,128]{2,1,0:T(8,128)(2,1)S(1)}, bf16[4,64,128]{2,1,0:T(8,128)(2,1)S(1)}, u32[]{:S(2)}, u32[]{:S(2)}) collective-permute-start(bf16[4,64,128]{2,1,0:T(8,128)(2,1)S(1)} %get-tuple-element.35), channel_id=1, source_target_pairs={{0,4},{2,6},{4,0},{6,2},{8,12},{10,14},{12,8},{14,10},{16,20},{18,... | collective-permute-start | bytes 196616 | tf_op jit(solution)/shard_map/ppermute | solution.py:512
  8.0 0.0 collective-permute-start.2
  8.1 3.4 %shard_map.102 = (bf16[16,64,128]{2,1,0:T(8,128)(2,1)S(1)}, bf16[4,64,128]{2,1,0:T(8,128)(2,1)S(1)}, f32[32,128]{1,0:T(8,128)S(1)}) custom-call(bf16[32,64,128]{2,1,0:T(8,128)(2,1)} %bitcast.16, bf16[32,64,128]{2,1,0:T(8,128)(2,1)} %bitcast.21, bf16[32,64,128]{2,1,0:T(8,128)(2,1)} %bitcast.26, bf16[32,64,128]{2,1,0:T(8,128)(2,1)} %bitcast.38, ...), custom_call_target="tpu_custom_call" | custom-call | flops 1000000000 | bytes 4000000 | tf_op jit(solution)/shard_map/pallas_call | solution.py:517
  11.5 1.8 %collective-permute-done.2.refs_3_ = bf16[4,64,128]{2,1,0:T(8,128)(2,1)S(1)} collective-permute-done((bf16[4,64,128]{2,1,0:T(8,128)(2,1)S(1)}, bf16[4,64,128]{2,1,0:T(8,128)(2,1)S(1)}, u32[]{:S(2)}, u32[]{:S(2)}) %collective-permute-start.2) | collective-permute-done | bytes 65568 | tf_op jit(solution)/shard_map/ppermute | solution.py:512
  13.2 0.6 %shard_map.103.after_ref.refs_4_ = bf16[288,128]{1,0:T(8,128)(2,1)S(1)} custom-call(f32[16,128]{1,0:T(8,128)S(1)} %get-tuple-element.32.rate_ref, bf16[4,64,128]{2,1,0:T(8,128)(2,1)S(1)} %get-tuple-element.33.refs_0_, bf16[4,64,128]{2,1,0:T(8,128)(2,1)S(1)} %collective-permute-done.refs_1_, bf16[4,64,128]{2,1,0:T(8,128)(2,1)S(1)} %collective-permute-done.1.refs_2_, ...), custom_call_target="tpu_custom_call" | custom-call | flops 10000000 | bytes 1000000 | tf_op jit(solution)/shard_map/pallas_call | solution.py:528
  13.8 3.6 %collective-permute-start.5 = (bf16[288,128]{1,0:T(8,128)(2,1)S(1)}, bf16[288,128]{1,0:T(8,128)(2,1)S(1)}, u32[]{:S(2)}, u32[]{:S(2)}) collective-permute-start(bf16[288,128]{1,0:T(8,128)(2,1)S(1)} %shard_map.103.after_ref.refs_4_), channel_id=1, source_target_pairs={{0,24},{2,26},{4,28},{6,30},{8,16},{10,18},{12,20},{14,22},{16,8},... | collective-permute-start | bytes 221192 | tf_op jit(solution)/shard_map/ppermute | solution.py:512
  17.5 0.8 %collective-permute-start.3 = (bf16[288,128]{1,0:T(8,128)(2,1)S(1)}, bf16[288,128]{1,0:T(8,128)(2,1)S(1)}, u32[]{:S(2)}, u32[]{:S(2)}) collective-permute-start(bf16[288,128]{1,0:T(8,128)(2,1)S(1)} %shard_map.103.after_ref.refs_4_), channel_id=1, source_target_pairs={{0,8},{2,10},{4,12},{6,14},{8,0},{10,2},{12,4},{14,6},{16,24},{18,... | collective-permute-start | bytes 221192 | tf_op jit(solution)/shard_map/ppermute | solution.py:512
  18.3 2.8 %shard_map.104 = (f32[4,16,64,128]{3,2,1,0:T(8,128)S(1)}, bf16[4,16,16,128]{3,2,1,0:T(8,128)(2,1)S(1)}) custom-call(bf16[16,64,128]{2,1,0:T(8,128)(2,1)S(1)} %get-tuple-element.31.own_ref, bf16[3,16,64,128]{3,2,1,0:T(8,128)(2,1)S(1)} %get-tuple-element.29.xc_ref, f32[16,64]{1,0:T(8,128)S(1)} %bitcast.32, f32[16,64]{1,0:T(8,128)S(1)} %bitcast.33, ...), custom_call_target="tpu_custom_call" | custom-call | flops 1000000000 | bytes 4000000 | tf_op jit(solution)/shard_map/pallas_call | solution.py:538
  21.1 1.6 %collective-permute-done.4.refs_6_ = bf16[288,128]{1,0:T(8,128)(2,1)S(1)} collective-permute-done((bf16[288,128]{1,0:T(8,128)(2,1)S(1)}, bf16[288,128]{1,0:T(8,128)(2,1)S(1)}, u32[]{:S(2)}, u32[]{:S(2)}) %collective-permute-start.4) | collective-permute-done | bytes 73760 | tf_op jit(solution)/shard_map/ppermute | solution.py:512
  22.7 0.6 %shard_map.105 = (bf16[160,128]{1,0:T(8,128)(2,1)S(1)}, bf16[160,128]{1,0:T(8,128)(2,1)S(1)}, bf16[160,128]{1,0:T(8,128)(2,1)S(1)}, bf16[160,128]{1,0:T(8,128)(2,1)S(1)}) custom-call(f32[16,128]{1,0:T(8,128)S(1)} %get-tuple-element.32.rate_ref, bf16[4,16,16,128]{3,2,1,0:T(8,128)(2,1)S(1)} %get-tuple-element.39.after_ref.taps_ref, ...), custom_call_target="tpu_custom_call" | custom-call | flops 10000000 | bytes 1000000 | tf_op jit(solution)/shard_map/pallas_call | solution.py:554
  23.4 0.9 %collective-permute-start.6 = (bf16[160,128]{1,0:T(8,128)(2,1)S(1)}, bf16[160,128]{1,0:T(8,128)(2,1)S(1)}, u32[]{:S(2)}, u32[]{:S(2)}) collective-permute-start(bf16[160,128]{1,0:T(8,128)(2,1)S(1)} %get-tuple-element.40), channel_id=1, source_target_pairs={{0,2},{2,0},{4,6},{6,4},{8,10},{10,8},{12,14},{14,12},{16,18},{18,... | collective-permute-start | bytes 122888 | tf_op jit(solution)/shard_map/ppermute | solution.py:512
  24.3 1.3 %collective-permute-start.7 = (bf16[160,128]{1,0:T(8,128)(2,1)S(1)}, bf16[160,128]{1,0:T(8,128)(2,1)S(1)}, u32[]{:S(2)}, u32[]{:S(2)}) collective-permute-start(bf16[160,128]{1,0:T(8,128)(2,1)S(1)} %get-tuple-element.41), channel_id=1, source_target_pairs={{0,4},{2,6},{4,0},{6,2},{8,12},{10,14},{12,8},{14,10},{16,20},{18,... | collective-permute-start | bytes 122888 | tf_op jit(solution)/shard_map/ppermute | solution.py:512
  25.6 1.3 %collective-permute-start.8 = (bf16[160,128]{1,0:T(8,128)(2,1)S(1)}, bf16[160,128]{1,0:T(8,128)(2,1)S(1)}, u32[]{:S(2)}, u32[]{:S(2)}) collective-permute-start(bf16[160,128]{1,0:T(8,128)(2,1)S(1)} %get-tuple-element.42), channel_id=1, source_target_pairs={{0,6},{2,4},{4,2},{6,0},{8,14},{10,12},{12,10},{14,8},{16,22},{18,... | collective-permute-start | bytes 122888 | tf_op jit(solution)/shard_map/ppermute | solution.py:512
  26.9 1.2 %shard_map.106 = (bf16[32,64,128]{2,1,0:T(8,128)(2,1)}, bf16[32,64,128]{2,1,0:T(8,128)(2,1)}, bf16[32,64,128]{2,1,0:T(8,128)(2,1)}) custom-call(bf16[32,64,128]{2,1,0:T(8,128)(2,1)S(1)} %bitcast.17, bf16[32,64,128]{2,1,0:T(8,128)(2,1)S(1)} %bitcast.22, bf16[32,64,128]{2,1,0:T(8,128)(2,1)S(1)} %bitcast.27, f32[4,16,64,128]{3,2,1,0:T(8,128)S(1)} %get-tuple-element.38.near_ref, ...), custom_call_target="tpu_custom_call" | custom-call | flops 200000000 | bytes 1000000 | tf_op jit(solution)/shard_map/pallas_call | solution.py:579
  28.2 0.6 %collective-permute-done.7.refs_1_ = bf16[160,128]{1,0:T(8,128)(2,1)S(1)} collective-permute-done((bf16[160,128]{1,0:T(8,128)(2,1)S(1)}, bf16[160,128]{1,0:T(8,128)(2,1)S(1)}, u32[]{:S(2)}, u32[]{:S(2)}) %collective-permute-start.7) | collective-permute-done | bytes 40992 | tf_op jit(solution)/shard_map/ppermute | solution.py:512
  28.8 1.8 %collective-permute-done.8.refs_0_ = bf16[160,128]{1,0:T(8,128)(2,1)S(1)} collective-permute-done((bf16[160,128]{1,0:T(8,128)(2,1)S(1)}, bf16[160,128]{1,0:T(8,128)(2,1)S(1)}, u32[]{:S(2)}, u32[]{:S(2)}) %collective-permute-start.8) | collective-permute-done | bytes 40992 | tf_op jit(solution)/shard_map/ppermute | solution.py:512
  30.5 0.1 add_add_fusion
  30.6 0.0 collective-permute-start.9
  30.6 1.2 %shard_map.107 = (bf16[32,64,128]{2,1,0:T(8,128)(2,1)}, bf16[32,64,128]{2,1,0:T(8,128)(2,1)}, bf16[32,64,128]{2,1,0:T(8,128)(2,1)}) custom-call(bf16[32,64,128]{2,1,0:T(8,128)(2,1)S(1)} %bitcast.18, bf16[32,64,128]{2,1,0:T(8,128)(2,1)S(1)} %bitcast.23, bf16[32,64,128]{2,1,0:T(8,128)(2,1)S(1)} %bitcast.28, ...), custom_call_target="tpu_custom_call", output_to_operand_aliasing={{0}: (6, {}), {1}: (7, {}), {2}: (8, {})} | custom-call | flops 200000000 | bytes 1000000 | tf_op jit(solution)/shard_map/pallas_call | solution.py:579
  31.8 1.4 %shard_map.108 = (bf16[32,64,128]{2,1,0:T(8,128)(2,1)}, bf16[32,64,128]{2,1,0:T(8,128)(2,1)}, bf16[32,64,128]{2,1,0:T(8,128)(2,1)}) custom-call(bf16[32,64,128]{2,1,0:T(8,128)(2,1)S(1)} %bitcast.19, bf16[32,64,128]{2,1,0:T(8,128)(2,1)S(1)} %bitcast.24, bf16[32,64,128]{2,1,0:T(8,128)(2,1)S(1)} %bitcast.29, ...), custom_call_target="tpu_custom_call", output_to_operand_aliasing={{0}: (7, {}), {1}: (8, {}), {2}: (9, {})} | custom-call | flops 400000000 | bytes 2000000 | tf_op jit(solution)/shard_map/pallas_call | solution.py:579
  33.3 0.6 %fusion.1 = (f32[64,16]{0,1:T(8,128)}, f32[64,16]{0,1:T(8,128)}) fusion(f32[32,64]{1,0:T(8,128)S(1)} %add.31, f32[64,16]{0,1:T(8,128)S(1)} %copy-done.4, f32[64,16]{0,1:T(8,128)S(1)} %copy-done.3), kind=kLoop, calls=%fused_computation.3 | loop fusion | flops 5120 | bytes 24576 | tf_op jit(solution)/shard_map/transpose | solution.py:599
  (17 shorter events, 0.0 us)
Async XLA Ops:
  0.6 7.4 %copy-start.3 = (f32[64,16]{0,1:T(8,128)S(1)}, f32[64,16]{0,1:T(8,128)}, u32[]{:S(2)}) copy-start(f32[64,16]{0,1:T(8,128)} %param.11) | copy-start | bytes 12292
  3.5 14.8 %copy-start.4 = (f32[64,16]{0,1:T(8,128)S(1)}, f32[64,16]{0,1:T(8,128)}, u32[]{:S(2)}) copy-start(f32[64,16]{0,1:T(8,128)} %param.10) | copy-start | bytes 12292
  3.5 7.9 %collective-permute-start = (bf16[4,64,128]{2,1,0:T(8,128)(2,1)S(1)}, bf16[4,64,128]{2,1,0:T(8,128)(2,1)S(1)}, u32[]{:S(2)}, u32[]{:S(2)}) collective-permute-start(bf16[4,64,128]{2,1,0:T(8,128)(2,1)S(1)} %get-tuple-element.34), channel_id=1, source_target_pairs={{0,2},{2,0},{4,6},{6,4},{8,10},{10,8},{12,14},{14,12},{16,18},{18,... | collective-permute-start | bytes 196616 | tf_op jit(solution)/shard_map/ppermute | solution.py:512
  6.5 4.9 %collective-permute-start.1 = (bf16[4,64,128]{2,1,0:T(8,128)(2,1)S(1)}, bf16[4,64,128]{2,1,0:T(8,128)(2,1)S(1)}, u32[]{:S(2)}, u32[]{:S(2)}) collective-permute-start(bf16[4,64,128]{2,1,0:T(8,128)(2,1)S(1)} %get-tuple-element.35), channel_id=1, source_target_pairs={{0,4},{2,6},{4,0},{6,2},{8,12},{10,14},{12,8},{14,10},{16,20},{18,... | collective-permute-start | bytes 196616 | tf_op jit(solution)/shard_map/ppermute | solution.py:512
  8.0 5.2 %collective-permute-start.2 = (bf16[4,64,128]{2,1,0:T(8,128)(2,1)S(1)}, bf16[4,64,128]{2,1,0:T(8,128)(2,1)S(1)}, u32[]{:S(2)}, u32[]{:S(2)}) collective-permute-start(bf16[4,64,128]{2,1,0:T(8,128)(2,1)S(1)} %get-tuple-element.36), channel_id=1, source_target_pairs={{0,6},{2,4},{4,2},{6,0},{8,14},{10,12},{12,10},{14,8},{16,22},{18,... | collective-permute-start | bytes 196616 | tf_op jit(solution)/shard_map/ppermute | solution.py:512
  13.8 7.2 %collective-permute-start.5 = (bf16[288,128]{1,0:T(8,128)(2,1)S(1)}, bf16[288,128]{1,0:T(8,128)(2,1)S(1)}, u32[]{:S(2)}, u32[]{:S(2)}) collective-permute-start(bf16[288,128]{1,0:T(8,128)(2,1)S(1)} %shard_map.103.after_ref.refs_4_), channel_id=1, source_target_pairs={{0,24},{2,26},{4,28},{6,30},{8,16},{10,18},{12,20},{14,22},{16,8},... | collective-permute-start | bytes 221192 | tf_op jit(solution)/shard_map/ppermute | solution.py:512
  17.5 5.3 %collective-permute-start.4 = (bf16[288,128]{1,0:T(8,128)(2,1)S(1)}, bf16[288,128]{1,0:T(8,128)(2,1)S(1)}, u32[]{:S(2)}, u32[]{:S(2)}) collective-permute-start(bf16[288,128]{1,0:T(8,128)(2,1)S(1)} %shard_map.103.after_ref.refs_4_), channel_id=1, source_target_pairs={{0,16},{2,18},{4,20},{6,22},{8,24},{10,26},{12,28},{14,30},{16,0},... | collective-permute-start | bytes 221192 | tf_op jit(solution)/shard_map/ppermute | solution.py:512
  17.5 5.3 %collective-permute-start.3 = (bf16[288,128]{1,0:T(8,128)(2,1)S(1)}, bf16[288,128]{1,0:T(8,128)(2,1)S(1)}, u32[]{:S(2)}, u32[]{:S(2)}) collective-permute-start(bf16[288,128]{1,0:T(8,128)(2,1)S(1)} %shard_map.103.after_ref.refs_4_), channel_id=1, source_target_pairs={{0,8},{2,10},{4,12},{6,14},{8,0},{10,2},{12,4},{14,6},{16,24},{18,... | collective-permute-start | bytes 221192 | tf_op jit(solution)/shard_map/ppermute | solution.py:512
  18.3 8.7 %copy-start = (bf16[2048,128]{1,0:T(8,128)(2,1)S(1)}, bf16[2048,128]{1,0:T(8,128)(2,1)}, u32[]{:S(2)}) copy-start(bf16[2048,128]{1,0:T(8,128)(2,1)} %param.7) | copy-start | bytes 1572868
  18.3 8.7 %copy-start.1 = (bf16[2048,128]{1,0:T(8,128)(2,1)S(1)}, bf16[2048,128]{1,0:T(8,128)(2,1)}, u32[]{:S(2)}) copy-start(bf16[2048,128]{1,0:T(8,128)(2,1)} %param.8) | copy-start | bytes 1572868
  18.3 8.7 %copy-start.2 = (bf16[2048,128]{1,0:T(8,128)(2,1)S(1)}, bf16[2048,128]{1,0:T(8,128)(2,1)}, u32[]{:S(2)}) copy-start(bf16[2048,128]{1,0:T(8,128)(2,1)} %param.9) | copy-start | bytes 1572868
  23.4 4.8 %collective-permute-start.6 = (bf16[160,128]{1,0:T(8,128)(2,1)S(1)}, bf16[160,128]{1,0:T(8,128)(2,1)S(1)}, u32[]{:S(2)}, u32[]{:S(2)}) collective-permute-start(bf16[160,128]{1,0:T(8,128)(2,1)S(1)} %get-tuple-element.40), channel_id=1, source_target_pairs={{0,2},{2,0},{4,6},{6,4},{8,10},{10,8},{12,14},{14,12},{16,18},{18,... | collective-permute-start | bytes 122888 | tf_op jit(solution)/shard_map/ppermute | solution.py:512
  24.3 4.4 %collective-permute-start.7 = (bf16[160,128]{1,0:T(8,128)(2,1)S(1)}, bf16[160,128]{1,0:T(8,128)(2,1)S(1)}, u32[]{:S(2)}, u32[]{:S(2)}) collective-permute-start(bf16[160,128]{1,0:T(8,128)(2,1)S(1)} %get-tuple-element.41), channel_id=1, source_target_pairs={{0,4},{2,6},{4,0},{6,2},{8,12},{10,14},{12,8},{14,10},{16,20},{18,... | collective-permute-start | bytes 122888 | tf_op jit(solution)/shard_map/ppermute | solution.py:512
  25.6 4.9 %collective-permute-start.8 = (bf16[160,128]{1,0:T(8,128)(2,1)S(1)}, bf16[160,128]{1,0:T(8,128)(2,1)S(1)}, u32[]{:S(2)}, u32[]{:S(2)}) collective-permute-start(bf16[160,128]{1,0:T(8,128)(2,1)S(1)} %get-tuple-element.42), channel_id=1, source_target_pairs={{0,6},{2,4},{4,2},{6,0},{8,14},{10,12},{12,10},{14,8},{16,22},{18,... | collective-permute-start | bytes 122888 | tf_op jit(solution)/shard_map/ppermute | solution.py:512
  30.6 2.7 %collective-permute-start.9 = (f32[32,64]{1,0:T(8,128)S(1)}, f32[32,64]{1,0:T(8,128)S(1)}, u32[]{:S(2)}, u32[]{:S(2)}) collective-permute-start(f32[32,64]{1,0:T(8,128)S(1)} %add_add_fusion), channel_id=1, source_target_pairs={{0,1},{1,0},{2,3},{3,2},{4,5},{5,4},{6,7},{7,6},{8,9},{9,8},{10,11... | collective-permute-start | bytes 24584 | tf_op jit(solution)/shard_map/ppermute | solution.py:573

commit v12 on v11

--- a/solution.py
+++ b/solution.py
@@ -136,7 +136,7 @@
 
 
 def sums_kernel(k_hbm, v_hbm, g_hbm, q_hbm, xc_ref, w_ref, dec_ref, own_ref, out_ref, sums_ref, *rest):
-    bufs, sems, gs, cs, prods_ref = rest
+    bufs, sems, gs, cs, prods_ref, left_ref, basis_ref = rest
     place, _ = places()
     work = Reducer((k_hbm, v_hbm, g_hbm, q_hbm), bufs, sems, w_ref, gs, cs)
     for copy in work.copies(0, place):
@@ -153,27 +153,32 @@
             prods = dot(ref[local, :rows], ref[local, rows:], TN)
             prods_ref[index, local] = jnp.where(paired, prods, 0.0).astype(BF16)
 
-    def others(index, _):
-        multiply(index, xc_ref.at[index - 1])
-        return 0
-
-    lax.fori_loop(1, PLANE, others, 0)
+    multiply(1, xc_ref.at[0])
     work.load(0, place)
+    multiply(2, xc_ref.at[1])
     work.reduce(0, place, own_ref, out_ref)
+    multiply(3, xc_ref.at[2])
     multiply(0, own_ref)
     dec = dec_ref[...]
     middle = float(length // 2) - lane_iota((modes, length)).astype(F32)
     lane = lane_iota((modes, sums_ref.shape[1]))
 
+    def tables(index, _):
+        for local in range(part):
+            rate = column(dec, (place ^ index) * part + local)
+            basis = jnp.exp(-rate * middle)
+            left_ref[index, local] = jnp.concatenate([basis, middle * basis], axis=0).astype(BF16)
+            basis_ref[index, local] = basis * jnp.exp(rate)
+        return 0
+
+    lax.fori_loop(0, PLANE, tables, 0, unroll=2)
+
     def contract(index, carry):
         plain, moment = carry
         for local in range(part):
             group = (place ^ index) * part + local
-            rate = column(dec, group)
-            basis = jnp.exp(-rate * middle)
-            left = jnp.concatenate([basis, middle * basis], axis=0).astype(BF16)
-            both = dot(left, prods_ref[index, local], NN)
-            basis = basis * jnp.exp(rate)
+            both = dot(left_ref[index, local], prods_ref[index, local], NN)
+            basis = basis_ref[index, local]
             first = jnp.sum(basis * both[:modes], axis=1, keepdims=True)
             second = basis * ((middle - 1.0) * both[:modes] + both[modes:])
             plain = jnp.where(lane == group, first, plain)
@@ -181,7 +186,7 @@
         return plain, moment
 
     zero = jnp.zeros(lane.shape, F32)
-    plain, moment = lax.fori_loop(0, PLANE, contract, (zero, zero))
+    plain, moment = lax.fori_loop(0, PLANE, contract, (zero, zero), unroll=True)
     sums_ref[:modes] = plain
     sums_ref[modes:] = moment
 
@@ -519,7 +524,12 @@
         [anywhere] * 4 + [vmem] * 3,
         [vmem] * 3,
         [shaped(quarter, BF16), block, shaped((2 * modes, lanes), F32)],
-        reducer(1) + [pltpu.VMEM((PLANE, part, length, length), BF16)],
+        reducer(1)
+        + [
+            pltpu.VMEM((PLANE, part, length, length), BF16),
+            pltpu.VMEM((PLANE, part, 2 * modes, length), BF16),
+            pltpu.VMEM((PLANE, part, modes, length), F32),
+        ],
         10**9,
         4 * 10**6,
     )(*in_hbm(key, value, grad, query), xc, weights, decay)

time: 34 us -> 33.7 us (level)
  Pallas kernels: 14.1 us -> 13.7 us
    pallas_call x1, Pallas kernels: 3.36 us -> 2.97 us  [gradients(): call(sums_kernel, [anywhere] * 4 + [vmem] * 3, [vmem] * 3, [shaped(quarte...]
where the time goes in v12:
time: 33.7 us; the launch traced here: 33.5 us
  Pallas kernels  13.7 us (41%)
  starting transfers between devices  12.5 us (37%)
  waiting for transfers between devices  5.77 us (17%)
  between operations  0.76 us (2%)
  other arithmetic  0.69 us (2%)
    ppermute x9, starting transfers between devices, swap(): return lax.ppermute(x, 'ctx', [(i, i ^ bits) for i in range(count)])  12.5 us
    ppermute x9, waiting for transfers between devices, swap(): return lax.ppermute(x, 'ctx', [(i, i ^ bits) for i in range(count)])  5.77 us
    pallas_call x3, Pallas kernels, gradients(): call(functools.partial(outputs_kernel, indices), [vmem] * (5 + slots) + [...  3.83 us
    pallas_call x1, Pallas kernels, gradients(): call(sums_kernel, [anywhere] * 4 + [vmem] * 3, [vmem] * 3, [shaped(quarte...  2.97 us
    pallas_call x1, Pallas kernels, gradients(): call(states_kernel, [anywhere] * 5, [vmem] * (2 + PLANE), [shaped((PLANE...  2.86 us
    pallas_call x1, Pallas kernels, gradients(): call(local_kernel, [vmem] * 5, [vmem] * 2, [shaped((PLANE,) + quarter, F3...  2.8 us
  transfers between devices with their start and end apart: 10, of which 4 were waited for; matrix products, arithmetic and copies ran while one was open for 0% of the time, Pallas kernels for 29%

profile of v12, /device:TPU:0, one launch (start us, length us, event | category | flops | bytes accessed | tf_op | source)
XLA Modules:
  0.0 33.5 jit_solution(3148205689910433425)
XLA Ops:
  0.6 2.9 %shard_map.101 = (bf16[3,16,64,128]{3,2,1,0:T(8,128)(2,1)S(1)}, bf16[64,2,16,128]{3,2,1,0:T(8,128)(2,1)S(1)}, f32[16,128]{1,0:T(8,128)S(1)}, bf16[4,64,128]{2,1,...) custom-call(f32[16,64]{1,0:T(8,128)} %bitcast.30, bf16[32,64,128]{2,1,0:T(8,128)(2,1)} %bitcast.15, ...), custom_call_target="tpu_custom_call" | custom-call | flops 1000000000 | bytes 4000000 | tf_op jit(solution)/shard_map/pallas_call | solution.py:501
  3.5 0.0 copy-start.4
  3.5 3.0 %collective-permute-start = (bf16[4,64,128]{2,1,0:T(8,128)(2,1)S(1)}, bf16[4,64,128]{2,1,0:T(8,128)(2,1)S(1)}, u32[]{:S(2)}, u32[]{:S(2)}) collective-permute-start(bf16[4,64,128]{2,1,0:T(8,128)(2,1)S(1)} %get-tuple-element.34), channel_id=1, source_target_pairs={{0,2},{2,0},{4,6},{6,4},{8,10},{10,8},{12,14},{14,12},{16,18},{18,... | collective-permute-start | bytes 196616 | tf_op jit(solution)/shard_map/ppermute | solution.py:517
  6.5 1.5 %collective-permute-start.1 = (bf16[4,64,128]{2,1,0:T(8,128)(2,1)S(1)}, bf16[4,64,128]{2,1,0:T(8,128)(2,1)S(1)}, u32[]{:S(2)}, u32[]{:S(2)}) collective-permute-start(bf16[4,64,128]{2,1,0:T(8,128)(2,1)S(1)} %get-tuple-element.35), channel_id=1, source_target_pairs={{0,4},{2,6},{4,0},{6,2},{8,12},{10,14},{12,8},{14,10},{16,20},{18,... | collective-permute-start | bytes 196616 | tf_op jit(solution)/shard_map/ppermute | solution.py:517
  8.0 0.0 collective-permute-start.2
  8.1 3.0 %shard_map.102 = (bf16[16,64,128]{2,1,0:T(8,128)(2,1)S(1)}, bf16[4,64,128]{2,1,0:T(8,128)(2,1)S(1)}, f32[32,128]{1,0:T(8,128)S(1)}) custom-call(bf16[32,64,128]{2,1,0:T(8,128)(2,1)} %bitcast.16, bf16[32,64,128]{2,1,0:T(8,128)(2,1)} %bitcast.21, bf16[32,64,128]{2,1,0:T(8,128)(2,1)} %bitcast.26, bf16[32,64,128]{2,1,0:T(8,128)(2,1)} %bitcast.38, ...), custom_call_target="tpu_custom_call" | custom-call | flops 1000000000 | bytes 4000000 | tf_op jit(solution)/shard_map/pallas_call | solution.py:522
  11.1 2.1 %collective-permute-done.2.refs_3_ = bf16[4,64,128]{2,1,0:T(8,128)(2,1)S(1)} collective-permute-done((bf16[4,64,128]{2,1,0:T(8,128)(2,1)S(1)}, bf16[4,64,128]{2,1,0:T(8,128)(2,1)S(1)}, u32[]{:S(2)}, u32[]{:S(2)}) %collective-permute-start.2) | collective-permute-done | bytes 65568 | tf_op jit(solution)/shard_map/ppermute | solution.py:517
  13.2 0.6 %shard_map.103.after_ref.refs_4_ = bf16[288,128]{1,0:T(8,128)(2,1)S(1)} custom-call(f32[16,128]{1,0:T(8,128)S(1)} %get-tuple-element.32.rate_ref, bf16[4,64,128]{2,1,0:T(8,128)(2,1)S(1)} %get-tuple-element.33.refs_0_, bf16[4,64,128]{2,1,0:T(8,128)(2,1)S(1)} %collective-permute-done.refs_1_, bf16[4,64,128]{2,1,0:T(8,128)(2,1)S(1)} %collective-permute-done.1.refs_2_, ...), custom_call_target="tpu_custom_call" | custom-call | flops 10000000 | bytes 1000000 | tf_op jit(solution)/shard_map/pallas_call | solution.py:538
  13.8 3.6 %collective-permute-start.5 = (bf16[288,128]{1,0:T(8,128)(2,1)S(1)}, bf16[288,128]{1,0:T(8,128)(2,1)S(1)}, u32[]{:S(2)}, u32[]{:S(2)}) collective-permute-start(bf16[288,128]{1,0:T(8,128)(2,1)S(1)} %shard_map.103.after_ref.refs_4_), channel_id=1, source_target_pairs={{0,24},{2,26},{4,28},{6,30},{8,16},{10,18},{12,20},{14,22},{16,8},... | collective-permute-start | bytes 221192 | tf_op jit(solution)/shard_map/ppermute | solution.py:517
  17.5 0.8 %collective-permute-start.3 = (bf16[288,128]{1,0:T(8,128)(2,1)S(1)}, bf16[288,128]{1,0:T(8,128)(2,1)S(1)}, u32[]{:S(2)}, u32[]{:S(2)}) collective-permute-start(bf16[288,128]{1,0:T(8,128)(2,1)S(1)} %shard_map.103.after_ref.refs_4_), channel_id=1, source_target_pairs={{0,8},{2,10},{4,12},{6,14},{8,0},{10,2},{12,4},{14,6},{16,24},{18,... | collective-permute-start | bytes 221192 | tf_op jit(solution)/shard_map/ppermute | solution.py:517
  18.3 2.8 %shard_map.104 = (f32[4,16,64,128]{3,2,1,0:T(8,128)S(1)}, bf16[4,16,16,128]{3,2,1,0:T(8,128)(2,1)S(1)}) custom-call(bf16[16,64,128]{2,1,0:T(8,128)(2,1)S(1)} %get-tuple-element.31.own_ref, bf16[3,16,64,128]{3,2,1,0:T(8,128)(2,1)S(1)} %get-tuple-element.29.xc_ref, f32[16,64]{1,0:T(8,128)S(1)} %bitcast.32, f32[16,64]{1,0:T(8,128)S(1)} %bitcast.33, ...), custom_call_target="tpu_custom_call" | custom-call | flops 1000000000 | bytes 4000000 | tf_op jit(solution)/shard_map/pallas_call | solution.py:548
  21.1 1.6 %collective-permute-done.4.refs_6_ = bf16[288,128]{1,0:T(8,128)(2,1)S(1)} collective-permute-done((bf16[288,128]{1,0:T(8,128)(2,1)S(1)}, bf16[288,128]{1,0:T(8,128)(2,1)S(1)}, u32[]{:S(2)}, u32[]{:S(2)}) %collective-permute-start.4) | collective-permute-done | bytes 73760 | tf_op jit(solution)/shard_map/ppermute | solution.py:517
  22.7 0.6 %shard_map.105 = (bf16[160,128]{1,0:T(8,128)(2,1)S(1)}, bf16[160,128]{1,0:T(8,128)(2,1)S(1)}, bf16[160,128]{1,0:T(8,128)(2,1)S(1)}, bf16[160,128]{1,0:T(8,128)(2,1)S(1)}) custom-call(f32[16,128]{1,0:T(8,128)S(1)} %get-tuple-element.32.rate_ref, bf16[4,16,16,128]{3,2,1,0:T(8,128)(2,1)S(1)} %get-tuple-element.39.after_ref.taps_ref, ...), custom_call_target="tpu_custom_call" | custom-call | flops 10000000 | bytes 1000000 | tf_op jit(solution)/shard_map/pallas_call | solution.py:564
  23.4 0.8 %collective-permute-start.6 = (bf16[160,128]{1,0:T(8,128)(2,1)S(1)}, bf16[160,128]{1,0:T(8,128)(2,1)S(1)}, u32[]{:S(2)}, u32[]{:S(2)}) collective-permute-start(bf16[160,128]{1,0:T(8,128)(2,1)S(1)} %get-tuple-element.40), channel_id=1, source_target_pairs={{0,2},{2,0},{4,6},{6,4},{8,10},{10,8},{12,14},{14,12},{16,18},{18,... | collective-permute-start | bytes 122888 | tf_op jit(solution)/shard_map/ppermute | solution.py:517
  24.2 1.0 %collective-permute-start.7 = (bf16[160,128]{1,0:T(8,128)(2,1)S(1)}, bf16[160,128]{1,0:T(8,128)(2,1)S(1)}, u32[]{:S(2)}, u32[]{:S(2)}) collective-permute-start(bf16[160,128]{1,0:T(8,128)(2,1)S(1)} %get-tuple-element.41), channel_id=1, source_target_pairs={{0,4},{2,6},{4,0},{6,2},{8,12},{10,14},{12,8},{14,10},{16,20},{18,... | collective-permute-start | bytes 122888 | tf_op jit(solution)/shard_map/ppermute | solution.py:517
  25.2 1.7 %collective-permute-start.8 = (bf16[160,128]{1,0:T(8,128)(2,1)S(1)}, bf16[160,128]{1,0:T(8,128)(2,1)S(1)}, u32[]{:S(2)}, u32[]{:S(2)}) collective-permute-start(bf16[160,128]{1,0:T(8,128)(2,1)S(1)} %get-tuple-element.42), channel_id=1, source_target_pairs={{0,6},{2,4},{4,2},{6,0},{8,14},{10,12},{12,10},{14,8},{16,22},{18,... | collective-permute-start | bytes 122888 | tf_op jit(solution)/shard_map/ppermute | solution.py:517
  26.9 1.2 %shard_map.106 = (bf16[32,64,128]{2,1,0:T(8,128)(2,1)}, bf16[32,64,128]{2,1,0:T(8,128)(2,1)}, bf16[32,64,128]{2,1,0:T(8,128)(2,1)}) custom-call(bf16[32,64,128]{2,1,0:T(8,128)(2,1)S(1)} %bitcast.17, bf16[32,64,128]{2,1,0:T(8,128)(2,1)S(1)} %bitcast.22, bf16[32,64,128]{2,1,0:T(8,128)(2,1)S(1)} %bitcast.27, f32[4,16,64,128]{3,2,1,0:T(8,128)S(1)} %get-tuple-element.38.near_ref, ...), custom_call_target="tpu_custom_call" | custom-call | flops 200000000 | bytes 1000000 | tf_op jit(solution)/shard_map/pallas_call | solution.py:589
  28.2 0.4 %collective-permute-done.7.refs_1_ = bf16[160,128]{1,0:T(8,128)(2,1)S(1)} collective-permute-done((bf16[160,128]{1,0:T(8,128)(2,1)S(1)}, bf16[160,128]{1,0:T(8,128)(2,1)S(1)}, u32[]{:S(2)}, u32[]{:S(2)}) %collective-permute-start.7) | collective-permute-done | bytes 40992 | tf_op jit(solution)/shard_map/ppermute | solution.py:517
  28.5 1.6 %collective-permute-done.8.refs_0_ = bf16[160,128]{1,0:T(8,128)(2,1)S(1)} collective-permute-done((bf16[160,128]{1,0:T(8,128)(2,1)S(1)}, bf16[160,128]{1,0:T(8,128)(2,1)S(1)}, u32[]{:S(2)}, u32[]{:S(2)}) %collective-permute-start.8) | collective-permute-done | bytes 40992 | tf_op jit(solution)/shard_map/ppermute | solution.py:517
  30.1 0.1 add_add_fusion
  30.2 0.0 collective-permute-start.9
  30.2 1.2 %shard_map.107 = (bf16[32,64,128]{2,1,0:T(8,128)(2,1)}, bf16[32,64,128]{2,1,0:T(8,128)(2,1)}, bf16[32,64,128]{2,1,0:T(8,128)(2,1)}) custom-call(bf16[32,64,128]{2,1,0:T(8,128)(2,1)S(1)} %bitcast.18, bf16[32,64,128]{2,1,0:T(8,128)(2,1)S(1)} %bitcast.23, bf16[32,64,128]{2,1,0:T(8,128)(2,1)S(1)} %bitcast.28, ...), custom_call_target="tpu_custom_call", output_to_operand_aliasing={{0}: (6, {}), {1}: (7, {}), {2}: (8, {})} | custom-call | flops 200000000 | bytes 1000000 | tf_op jit(solution)/shard_map/pallas_call | solution.py:589
  31.5 1.4 %shard_map.108 = (bf16[32,64,128]{2,1,0:T(8,128)(2,1)}, bf16[32,64,128]{2,1,0:T(8,128)(2,1)}, bf16[32,64,128]{2,1,0:T(8,128)(2,1)}) custom-call(bf16[32,64,128]{2,1,0:T(8,128)(2,1)S(1)} %bitcast.19, bf16[32,64,128]{2,1,0:T(8,128)(2,1)S(1)} %bitcast.24, bf16[32,64,128]{2,1,0:T(8,128)(2,1)S(1)} %bitcast.29, ...), custom_call_target="tpu_custom_call", output_to_operand_aliasing={{0}: (7, {}), {1}: (8, {}), {2}: (9, {})} | custom-call | flops 400000000 | bytes 2000000 | tf_op jit(solution)/shard_map/pallas_call | solution.py:589
  32.9 0.6 %fusion.1 = (f32[64,16]{0,1:T(8,128)}, f32[64,16]{0,1:T(8,128)}) fusion(f32[32,64]{1,0:T(8,128)S(1)} %add.31, f32[64,16]{0,1:T(8,128)S(1)} %copy-done.4, f32[64,16]{0,1:T(8,128)S(1)} %copy-done.3), kind=kLoop, calls=%fused_computation.3 | loop fusion | flops 5120 | bytes 24576 | tf_op jit(solution)/shard_map/transpose | solution.py:609
  (17 shorter events, 0.0 us)
Async XLA Ops:
  0.6 7.4 %copy-start.3 = (f32[64,16]{0,1:T(8,128)S(1)}, f32[64,16]{0,1:T(8,128)}, u32[]{:S(2)}) copy-start(f32[64,16]{0,1:T(8,128)} %param.11) | copy-start | bytes 12292
  3.5 14.8 %copy-start.4 = (f32[64,16]{0,1:T(8,128)S(1)}, f32[64,16]{0,1:T(8,128)}, u32[]{:S(2)}) copy-start(f32[64,16]{0,1:T(8,128)} %param.10) | copy-start | bytes 12292
  3.5 7.5 %collective-permute-start = (bf16[4,64,128]{2,1,0:T(8,128)(2,1)S(1)}, bf16[4,64,128]{2,1,0:T(8,128)(2,1)S(1)}, u32[]{:S(2)}, u32[]{:S(2)}) collective-permute-start(bf16[4,64,128]{2,1,0:T(8,128)(2,1)S(1)} %get-tuple-element.34), channel_id=1, source_target_pairs={{0,2},{2,0},{4,6},{6,4},{8,10},{10,8},{12,14},{14,12},{16,18},{18,... | collective-permute-start | bytes 196616 | tf_op jit(solution)/shard_map/ppermute | solution.py:517
  6.5 4.5 %collective-permute-start.1 = (bf16[4,64,128]{2,1,0:T(8,128)(2,1)S(1)}, bf16[4,64,128]{2,1,0:T(8,128)(2,1)S(1)}, u32[]{:S(2)}, u32[]{:S(2)}) collective-permute-start(bf16[4,64,128]{2,1,0:T(8,128)(2,1)S(1)} %get-tuple-element.35), channel_id=1, source_target_pairs={{0,4},{2,6},{4,0},{6,2},{8,12},{10,14},{12,8},{14,10},{16,20},{18,... | collective-permute-start | bytes 196616 | tf_op jit(solution)/shard_map/ppermute | solution.py:517
  8.0 5.2 %collective-permute-start.2 = (bf16[4,64,128]{2,1,0:T(8,128)(2,1)S(1)}, bf16[4,64,128]{2,1,0:T(8,128)(2,1)S(1)}, u32[]{:S(2)}, u32[]{:S(2)}) collective-permute-start(bf16[4,64,128]{2,1,0:T(8,128)(2,1)S(1)} %get-tuple-element.36), channel_id=1, source_target_pairs={{0,6},{2,4},{4,2},{6,0},{8,14},{10,12},{12,10},{14,8},{16,22},{18,... | collective-permute-start | bytes 196616 | tf_op jit(solution)/shard_map/ppermute | solution.py:517
  13.8 7.2 %collective-permute-start.5 = (bf16[288,128]{1,0:T(8,128)(2,1)S(1)}, bf16[288,128]{1,0:T(8,128)(2,1)S(1)}, u32[]{:S(2)}, u32[]{:S(2)}) collective-permute-start(bf16[288,128]{1,0:T(8,128)(2,1)S(1)} %shard_map.103.after_ref.refs_4_), channel_id=1, source_target_pairs={{0,24},{2,26},{4,28},{6,30},{8,16},{10,18},{12,20},{14,22},{16,8},... | collective-permute-start | bytes 221192 | tf_op jit(solution)/shard_map/ppermute | solution.py:517
  17.5 5.3 %collective-permute-start.4 = (bf16[288,128]{1,0:T(8,128)(2,1)S(1)}, bf16[288,128]{1,0:T(8,128)(2,1)S(1)}, u32[]{:S(2)}, u32[]{:S(2)}) collective-permute-start(bf16[288,128]{1,0:T(8,128)(2,1)S(1)} %shard_map.103.after_ref.refs_4_), channel_id=1, source_target_pairs={{0,16},{2,18},{4,20},{6,22},{8,24},{10,26},{12,28},{14,30},{16,0},... | collective-permute-start | bytes 221192 | tf_op jit(solution)/shard_map/ppermute | solution.py:517
  17.5 5.3 %collective-permute-start.3 = (bf16[288,128]{1,0:T(8,128)(2,1)S(1)}, bf16[288,128]{1,0:T(8,128)(2,1)S(1)}, u32[]{:S(2)}, u32[]{:S(2)}) collective-permute-start(bf16[288,128]{1,0:T(8,128)(2,1)S(1)} %shard_map.103.after_ref.refs_4_), channel_id=1, source_target_pairs={{0,8},{2,10},{4,12},{6,14},{8,0},{10,2},{12,4},{14,6},{16,24},{18,... | collective-permute-start | bytes 221192 | tf_op jit(solution)/shard_map/ppermute | solution.py:517
  18.3 8.7 %copy-start = (bf16[2048,128]{1,0:T(8,128)(2,1)S(1)}, bf16[2048,128]{1,0:T(8,128)(2,1)}, u32[]{:S(2)}) copy-start(bf16[2048,128]{1,0:T(8,128)(2,1)} %param.7) | copy-start | bytes 1572868
  18.3 8.7 %copy-start.1 = (bf16[2048,128]{1,0:T(8,128)(2,1)S(1)}, bf16[2048,128]{1,0:T(8,128)(2,1)}, u32[]{:S(2)}) copy-start(bf16[2048,128]{1,0:T(8,128)(2,1)} %param.8) | copy-start | bytes 1572868
  18.3 8.7 %copy-start.2 = (bf16[2048,128]{1,0:T(8,128)(2,1)S(1)}, bf16[2048,128]{1,0:T(8,128)(2,1)}, u32[]{:S(2)}) copy-start(bf16[2048,128]{1,0:T(8,128)(2,1)} %param.9) | copy-start | bytes 1572868
  23.4 4.8 %collective-permute-start.6 = (bf16[160,128]{1,0:T(8,128)(2,1)S(1)}, bf16[160,128]{1,0:T(8,128)(2,1)S(1)}, u32[]{:S(2)}, u32[]{:S(2)}) collective-permute-start(bf16[160,128]{1,0:T(8,128)(2,1)S(1)} %get-tuple-element.40), channel_id=1, source_target_pairs={{0,2},{2,0},{4,6},{6,4},{8,10},{10,8},{12,14},{14,12},{16,18},{18,... | collective-permute-start | bytes 122888 | tf_op jit(solution)/shard_map/ppermute | solution.py:517
  24.2 4.4 %collective-permute-start.7 = (bf16[160,128]{1,0:T(8,128)(2,1)S(1)}, bf16[160,128]{1,0:T(8,128)(2,1)S(1)}, u32[]{:S(2)}, u32[]{:S(2)}) collective-permute-start(bf16[160,128]{1,0:T(8,128)(2,1)S(1)} %get-tuple-element.41), channel_id=1, source_target_pairs={{0,4},{2,6},{4,0},{6,2},{8,12},{10,14},{12,8},{14,10},{16,20},{18,... | collective-permute-start | bytes 122888 | tf_op jit(solution)/shard_map/ppermute | solution.py:517
  25.2 4.9 %collective-permute-start.8 = (bf16[160,128]{1,0:T(8,128)(2,1)S(1)}, bf16[160,128]{1,0:T(8,128)(2,1)S(1)}, u32[]{:S(2)}, u32[]{:S(2)}) collective-permute-start(bf16[160,128]{1,0:T(8,128)(2,1)S(1)} %get-tuple-element.42), channel_id=1, source_target_pairs={{0,6},{2,4},{4,2},{6,0},{8,14},{10,12},{12,10},{14,8},{16,22},{18,... | collective-permute-start | bytes 122888 | tf_op jit(solution)/shard_map/ppermute | solution.py:517
  30.2 2.7 %collective-permute-start.9 = (f32[32,64]{1,0:T(8,128)S(1)}, f32[32,64]{1,0:T(8,128)S(1)}, u32[]{:S(2)}, u32[]{:S(2)}) collective-permute-start(f32[32,64]{1,0:T(8,128)S(1)} %add_add_fusion), channel_id=1, source_target_pairs={{0,1},{1,0},{2,3},{3,2},{4,5},{5,4},{6,7},{7,6},{8,9},{9,8},{10,11... | collective-permute-start | bytes 24584 | tf_op jit(solution)/shard_map/ppermute | solution.py:583

commit v13 on v12

--- a/solution.py
+++ b/solution.py
@@ -270,34 +270,39 @@
     return arrays
 
 
-def advance(state, decay, gap):
-    half = state.shape[2] // 2
-    shifted = pltpu.roll(state, half, 2)
-    return decay * (state + jnp.where(lane_iota(state.shape) >= half, gap * shifted, 0.0))
-
-
-def scan_blocks(heads, tails, start, rate, gap):
+def scan_blocks(heads, tails, rate, gap):
+    half = rate.shape[2] // 2
     decay = jnp.exp(-rate * gap)
-    state, before = start[0], []
-    for head in heads:
-        before.append(state)
-        state = advance(state, decay, gap) + head
-    other, after = start[1], []
-    for tail in tails[::-1]:
-        after.insert(0, other)
-        other = advance(other, decay, gap) + tail
-    return before, after, state, other
-
-
-def pair_terms(before, tails, rate):
-    half = rate.shape[2] // 2
+    lift = jnp.where(lane_iota(rate.shape) >= half, gap * decay, 0.0)
+
+    def run(blocks):
+        state, reached = None, []
+        for block in blocks:
+            reached.append(state)
+            if state is not None:
+                block = decay * state + lift * pltpu.roll(state, half, 2) + block
+            state = block
+        return reached, state
+
+    before, head = run(heads)
+    after, tail = run(tails[::-1])
+    return before, after[::-1], head, tail
+
+
+def pair_sums(before, tails):
+    half = tails[0].shape[2] // 2
     plain, moment = 0.0, 0.0
-    for state, tail in zip(before, tails, strict=True):
+    for state, tail in zip(before[1:], tails[1:], strict=True):
         plain = plain + state * tail
         moment = moment + state * pltpu.roll(tail, half, 2)
-    plain, moment = jnp.sum(plain, axis=1), jnp.sum(moment, axis=1)
+    return jnp.sum(plain, axis=1), jnp.sum(moment, axis=1)
+
+
+def pair_terms(sums, rate):
+    half = rate.shape[1] // 2
+    plain, moment = (jnp.concatenate(x, axis=0) for x in zip(*sums, strict=True))
     moment = moment + pltpu.roll(moment, half, 1) - pltpu.roll(plain, half, 1)
-    return jnp.where(lane_iota(plain.shape) < half, plain, moment) * jnp.exp(rate[:, 0])
+    return jnp.where(lane_iota(plain.shape) < half, plain, moment) * jnp.exp(rate)
 
 
 def spread(terms, place, acc, modes):
@@ -320,8 +325,7 @@
 
 
 def own_rates(rate_ref, place, quads):
-    rate = rate_ref[pl.ds(place * quads, quads), :]
-    return rate.reshape(quads, 1, rate.shape[1])
+    return rate_ref[pl.ds(place * quads, quads), :]
 
 
 def halves(blocks, rows):
@@ -333,16 +337,19 @@
     *msgs, sums_ref, out_ref, acc = refs
     place, _ = places()
     quads, rows, lanes = msgs[0].shape
-    rows, flat = rows // 2, quads * rows
+    flat = quads * rows
     modes = lanes // 8
-    heads, tails = halves(in_order([m[...] for m in msgs], place), rows)
     rate = own_rates(rate_ref, place, quads)
-    nothing = jnp.zeros_like(heads[0])
-    before, _, head, tail = scan_blocks(heads, tails, (nothing, nothing), rate, float(length))
-    both = jnp.concatenate([head, tail], axis=1)
-    out_ref[:flat] = both.astype(BF16).reshape(flat, lanes)
+    sums = []
+    for quad in range(quads):
+        one = slice(quad, quad + 1)
+        heads, tails = halves(in_order([m[one] for m in msgs], place), rows // 2)
+        before, _, head, tail = scan_blocks(heads, tails, rate[one, None], float(length))
+        both = jnp.concatenate([head, tail], axis=1).astype(BF16)
+        out_ref[quad * rows : (quad + 1) * rows] = both[0]
+        sums.append(pair_sums(before, tails))
     acc[...] = sums_ref[...]
-    spread(pair_terms(before, tails, rate), place, acc, modes)
+    spread(pair_terms(sums, rate), place, acc, modes)
     out_ref[flat:] = split_pair(acc[...], lanes // 2)
 
 
@@ -352,42 +359,45 @@
     outs, acc = refs[PLANE + count : -1], refs[-1]
     place, level = places()
     quads, rows, lanes = msgs[0].shape
-    shape = (quads, rows, lanes)
-    rows, flat = rows // 2, quads * rows
+    flat = quads * rows
     modes = lanes // 8
     rate = own_rates(rate_ref, place, quads)
-    heads, tails = halves(
-        in_order([r[:flat].reshape(shape) for r in lines], level), rows
-    )
-    nothing = jnp.zeros_like(heads[0])
-    before, after, _, _ = scan_blocks(
-        heads, tails, (nothing, nothing), rate, float(PLANE * length)
-    )
+    sums, found = [], []
+    for quad in range(quads):
+        one = slice(quad, quad + 1)
+        part = slice(quad * rows, (quad + 1) * rows)
+        heads, tails = halves(in_order([r[part][None] for r in lines], level), rows // 2)
+        before, after, _, _ = scan_blocks(heads, tails, rate[one, None], float(PLANE * length))
+        sums.append(pair_sums(before, tails))
+        start = [jnp.zeros_like(heads[0]), jnp.zeros_like(heads[0])]
+        for i in range(1, count):
+            start[0] = jnp.where(level == i, before[i], start[0])
+            start[1] = jnp.where(level == i - 1, after[i - 1], start[1])
+        heads, tails = halves(in_order([m[one] for m in msgs], place), rows // 2)
+        decay = jnp.exp(-rate[one, None] * float(length))
+        before, after = [start[0]], [start[1]]
+        for i in range(PLANE - 1):
+            before.append(decay * before[-1] + heads[i])
+            after.insert(0, decay * after[0] + tails[PLANE - 1 - i])
+        found.append(
+            [jnp.concatenate(pair, axis=1)[0] for pair in zip(before, after, strict=True)]
+        )
+    low = lane_iota((rows, lanes)) < lanes // 2
+    for quad in range(quads // 2):
+        packed = [
+            jnp.where(low, x, pltpu.roll(y, lanes // 2, 1)).astype(BF16)
+            for x, y in zip(found[quad], found[quad + quads // 2], strict=True)
+        ]
+        for i, x in enumerate(in_order(packed, place)):
+            outs[i][quad * rows : (quad + 1) * rows] = x
     total = join_pair(lines[0][flat:], lanes // 2)
     for r in lines[1:]:
         total = total + join_pair(r[flat:], lanes // 2)
     acc[...] = total
-    spread(pair_terms(before, tails, rate), place, acc, modes)
-    sums = split_pair(acc[...], lanes // 2)
-    start = [nothing, nothing]
-    for i in range(count):
-        start[0] = jnp.where(level == i, before[i], start[0])
-        start[1] = jnp.where(level == i, after[i], start[1])
-    heads, tails = halves(in_order([m[...] for m in msgs], place), rows)
-    decay = jnp.exp(-rate * float(length))
-    before, after = [start[0]], [start[1]]
-    for i in range(PLANE - 1):
-        before.append(decay * before[-1] + heads[i])
-        after.insert(0, decay * after[0] + tails[PLANE - 1 - i])
-    low = lane_iota((quads // 2, 2 * rows, lanes)) < lanes // 2
-    packed = []
-    for pair in zip(before, after, strict=True):
-        found = jnp.concatenate(pair, axis=1)
-        found = jnp.where(low, found[: quads // 2], pltpu.roll(found[quads // 2 :], lanes // 2, 2))
-        packed.append(found.astype(BF16).reshape(flat // 2, lanes))
-    for i, found in enumerate(in_order(packed, place)):
-        outs[i][: flat // 2] = found
-        outs[i][flat // 2 :] = sums
+    spread(pair_terms(sums, rate), place, acc, modes)
+    total = split_pair(acc[...], lanes // 2)
+    for i in range(PLANE):
+        outs[i][flat // 2 :] = total
 
 
 def outputs_kernel(indices, k_ref, v_ref, g_ref, near_ref, taps_ref, *refs):

time: 33.7 us -> 33.4 us (level)
  no operation moved by 1% of the time
where the time goes in v13:
time: 33.4 us; the launch traced here: 33.3 us
  Pallas kernels  13.6 us (41%)
  starting transfers between devices  12.4 us (37%)
  waiting for transfers between devices  5.77 us (17%)
  between operations  0.76 us (2%)
  other arithmetic  0.69 us (2%)
    ppermute x9, starting transfers between devices, swap(): return lax.ppermute(x, 'ctx', [(i, i ^ bits) for i in range(count)])  12.4 us
    ppermute x9, waiting for transfers between devices, swap(): return lax.ppermute(x, 'ctx', [(i, i ^ bits) for i in range(count)])  5.77 us
    pallas_call x3, Pallas kernels, gradients(): call(functools.partial(outputs_kernel, indices), [vmem] * (5 + slots) + [...  3.84 us
    pallas_call x1, Pallas kernels, gradients(): call(sums_kernel, [anywhere] * 4 + [vmem] * 3, [vmem] * 3, [shaped(quarte...  2.97 us
    pallas_call x1, Pallas kernels, gradients(): call(states_kernel, [anywhere] * 5, [vmem] * (2 + PLANE), [shaped((PLANE...  2.86 us
    pallas_call x1, Pallas kernels, gradients(): call(local_kernel, [vmem] * 5, [vmem] * 2, [shaped((PLANE,) + quarter, F3...  2.8 us
  transfers between devices with their start and end apart: 10, of which 4 were waited for; matrix products, arithmetic and copies ran while one was open for 0% of the time, Pallas kernels for 29%

profile of v13, /device:TPU:0, one launch (start us, length us, event | category | flops | bytes accessed | tf_op | source)
XLA Modules:
  0.0 33.3 jit_solution(10672269949544378901)
XLA Ops:
  0.6 2.9 %shard_map.101 = (bf16[3,16,64,128]{3,2,1,0:T(8,128)(2,1)S(1)}, bf16[64,2,16,128]{3,2,1,0:T(8,128)(2,1)S(1)}, f32[16,128]{1,0:T(8,128)S(1)}, bf16[4,64,128]{2,1,...) custom-call(f32[16,64]{1,0:T(8,128)} %bitcast.30, bf16[32,64,128]{2,1,0:T(8,128)(2,1)} %bitcast.15, ...), custom_call_target="tpu_custom_call" | custom-call | flops 1000000000 | bytes 4000000 | tf_op jit(solution)/shard_map/pallas_call | solution.py:511
  3.5 0.0 copy-start.4
  3.5 3.0 %collective-permute-start = (bf16[4,64,128]{2,1,0:T(8,128)(2,1)S(1)}, bf16[4,64,128]{2,1,0:T(8,128)(2,1)S(1)}, u32[]{:S(2)}, u32[]{:S(2)}) collective-permute-start(bf16[4,64,128]{2,1,0:T(8,128)(2,1)S(1)} %get-tuple-element.34), channel_id=1, source_target_pairs={{0,2},{2,0},{4,6},{6,4},{8,10},{10,8},{12,14},{14,12},{16,18},{18,... | collective-permute-start | bytes 196616 | tf_op jit(solution)/shard_map/ppermute | solution.py:527
  6.5 1.5 %collective-permute-start.1 = (bf16[4,64,128]{2,1,0:T(8,128)(2,1)S(1)}, bf16[4,64,128]{2,1,0:T(8,128)(2,1)S(1)}, u32[]{:S(2)}, u32[]{:S(2)}) collective-permute-start(bf16[4,64,128]{2,1,0:T(8,128)(2,1)S(1)} %get-tuple-element.35), channel_id=1, source_target_pairs={{0,4},{2,6},{4,0},{6,2},{8,12},{10,14},{12,8},{14,10},{16,20},{18,... | collective-permute-start | bytes 196616 | tf_op jit(solution)/shard_map/ppermute | solution.py:527
  8.0 0.0 collective-permute-start.2
  8.1 3.0 %shard_map.102 = (bf16[16,64,128]{2,1,0:T(8,128)(2,1)S(1)}, bf16[4,64,128]{2,1,0:T(8,128)(2,1)S(1)}, f32[32,128]{1,0:T(8,128)S(1)}) custom-call(bf16[32,64,128]{2,1,0:T(8,128)(2,1)} %bitcast.16, bf16[32,64,128]{2,1,0:T(8,128)(2,1)} %bitcast.21, bf16[32,64,128]{2,1,0:T(8,128)(2,1)} %bitcast.26, bf16[32,64,128]{2,1,0:T(8,128)(2,1)} %bitcast.38, ...), custom_call_target="tpu_custom_call" | custom-call | flops 1000000000 | bytes 4000000 | tf_op jit(solution)/shard_map/pallas_call | solution.py:532
  11.1 2.1 %collective-permute-done.2.refs_3_ = bf16[4,64,128]{2,1,0:T(8,128)(2,1)S(1)} collective-permute-done((bf16[4,64,128]{2,1,0:T(8,128)(2,1)S(1)}, bf16[4,64,128]{2,1,0:T(8,128)(2,1)S(1)}, u32[]{:S(2)}, u32[]{:S(2)}) %collective-permute-start.2) | collective-permute-done | bytes 65568 | tf_op jit(solution)/shard_map/ppermute | solution.py:527
  13.2 0.6 %shard_map.103.after_ref.refs_4_ = bf16[288,128]{1,0:T(8,128)(2,1)S(1)} custom-call(f32[16,128]{1,0:T(8,128)S(1)} %get-tuple-element.32.rate_ref, bf16[4,64,128]{2,1,0:T(8,128)(2,1)S(1)} %get-tuple-element.33.refs_0_, bf16[4,64,128]{2,1,0:T(8,128)(2,1)S(1)} %collective-permute-done.refs_1_, bf16[4,64,128]{2,1,0:T(8,128)(2,1)S(1)} %collective-permute-done.1.refs_2_, ...), custom_call_target="tpu_custom_call" | custom-call | flops 10000000 | bytes 1000000 | tf_op jit(solution)/shard_map/pallas_call | solution.py:548
  13.8 3.6 %collective-permute-start.5 = (bf16[288,128]{1,0:T(8,128)(2,1)S(1)}, bf16[288,128]{1,0:T(8,128)(2,1)S(1)}, u32[]{:S(2)}, u32[]{:S(2)}) collective-permute-start(bf16[288,128]{1,0:T(8,128)(2,1)S(1)} %shard_map.103.after_ref.refs_4_), channel_id=1, source_target_pairs={{0,24},{2,26},{4,28},{6,30},{8,16},{10,18},{12,20},{14,22},{16,8},... | collective-permute-start | bytes 221192 | tf_op jit(solution)/shard_map/ppermute | solution.py:527
  17.4 0.8 %collective-permute-start.3 = (bf16[288,128]{1,0:T(8,128)(2,1)S(1)}, bf16[288,128]{1,0:T(8,128)(2,1)S(1)}, u32[]{:S(2)}, u32[]{:S(2)}) collective-permute-start(bf16[288,128]{1,0:T(8,128)(2,1)S(1)} %shard_map.103.after_ref.refs_4_), channel_id=1, source_target_pairs={{0,8},{2,10},{4,12},{6,14},{8,0},{10,2},{12,4},{14,6},{16,24},{18,... | collective-permute-start | bytes 221192 | tf_op jit(solution)/shard_map/ppermute | solution.py:527
  18.2 2.8 %shard_map.104 = (f32[4,16,64,128]{3,2,1,0:T(8,128)S(1)}, bf16[4,16,16,128]{3,2,1,0:T(8,128)(2,1)S(1)}) custom-call(bf16[16,64,128]{2,1,0:T(8,128)(2,1)S(1)} %get-tuple-element.31.own_ref, bf16[3,16,64,128]{3,2,1,0:T(8,128)(2,1)S(1)} %get-tuple-element.29.xc_ref, f32[16,64]{1,0:T(8,128)S(1)} %bitcast.32, f32[16,64]{1,0:T(8,128)S(1)} %bitcast.33, ...), custom_call_target="tpu_custom_call" | custom-call | flops 1000000000 | bytes 4000000 | tf_op jit(solution)/shard_map/pallas_call | solution.py:558
  21.0 1.6 %collective-permute-done.4.refs_6_ = bf16[288,128]{1,0:T(8,128)(2,1)S(1)} collective-permute-done((bf16[288,128]{1,0:T(8,128)(2,1)S(1)}, bf16[288,128]{1,0:T(8,128)(2,1)S(1)}, u32[]{:S(2)}, u32[]{:S(2)}) %collective-permute-start.4) | collective-permute-done | bytes 73760 | tf_op jit(solution)/shard_map/ppermute | solution.py:527
  22.6 0.6 %shard_map.105 = (bf16[160,128]{1,0:T(8,128)(2,1)S(1)}, bf16[160,128]{1,0:T(8,128)(2,1)S(1)}, bf16[160,128]{1,0:T(8,128)(2,1)S(1)}, bf16[160,128]{1,0:T(8,128)(2,1)S(1)}) custom-call(f32[16,128]{1,0:T(8,128)S(1)} %get-tuple-element.32.rate_ref, bf16[4,16,16,128]{3,2,1,0:T(8,128)(2,1)S(1)} %get-tuple-element.39.after_ref.taps_ref, ...), custom_call_target="tpu_custom_call" | custom-call | flops 10000000 | bytes 1000000 | tf_op jit(solution)/shard_map/pallas_call | solution.py:574
  23.2 0.8 %collective-permute-start.6 = (bf16[160,128]{1,0:T(8,128)(2,1)S(1)}, bf16[160,128]{1,0:T(8,128)(2,1)S(1)}, u32[]{:S(2)}, u32[]{:S(2)}) collective-permute-start(bf16[160,128]{1,0:T(8,128)(2,1)S(1)} %get-tuple-element.40), channel_id=1, source_target_pairs={{0,2},{2,0},{4,6},{6,4},{8,10},{10,8},{12,14},{14,12},{16,18},{18,... | collective-permute-start | bytes 122888 | tf_op jit(solution)/shard_map/ppermute | solution.py:527
  24.0 1.1 %collective-permute-start.7 = (bf16[160,128]{1,0:T(8,128)(2,1)S(1)}, bf16[160,128]{1,0:T(8,128)(2,1)S(1)}, u32[]{:S(2)}, u32[]{:S(2)}) collective-permute-start(bf16[160,128]{1,0:T(8,128)(2,1)S(1)} %get-tuple-element.41), channel_id=1, source_target_pairs={{0,4},{2,6},{4,0},{6,2},{8,12},{10,14},{12,8},{14,10},{16,20},{18,... | collective-permute-start | bytes 122888 | tf_op jit(solution)/shard_map/ppermute | solution.py:527
  25.0 1.7 %collective-permute-start.8 = (bf16[160,128]{1,0:T(8,128)(2,1)S(1)}, bf16[160,128]{1,0:T(8,128)(2,1)S(1)}, u32[]{:S(2)}, u32[]{:S(2)}) collective-permute-start(bf16[160,128]{1,0:T(8,128)(2,1)S(1)} %get-tuple-element.42), channel_id=1, source_target_pairs={{0,6},{2,4},{4,2},{6,0},{8,14},{10,12},{12,10},{14,8},{16,22},{18,... | collective-permute-start | bytes 122888 | tf_op jit(solution)/shard_map/ppermute | solution.py:527
  26.7 1.2 %shard_map.106 = (bf16[32,64,128]{2,1,0:T(8,128)(2,1)}, bf16[32,64,128]{2,1,0:T(8,128)(2,1)}, bf16[32,64,128]{2,1,0:T(8,128)(2,1)}) custom-call(bf16[32,64,128]{2,1,0:T(8,128)(2,1)S(1)} %bitcast.17, bf16[32,64,128]{2,1,0:T(8,128)(2,1)S(1)} %bitcast.22, bf16[32,64,128]{2,1,0:T(8,128)(2,1)S(1)} %bitcast.27, f32[4,16,64,128]{3,2,1,0:T(8,128)S(1)} %get-tuple-element.38.near_ref, ...), custom_call_target="tpu_custom_call" | custom-call | flops 200000000 | bytes 1000000 | tf_op jit(solution)/shard_map/pallas_call | solution.py:599
  27.9 0.4 %collective-permute-done.7.refs_1_ = bf16[160,128]{1,0:T(8,128)(2,1)S(1)} collective-permute-done((bf16[160,128]{1,0:T(8,128)(2,1)S(1)}, bf16[160,128]{1,0:T(8,128)(2,1)S(1)}, u32[]{:S(2)}, u32[]{:S(2)}) %collective-permute-start.7) | collective-permute-done | bytes 40992 | tf_op jit(solution)/shard_map/ppermute | solution.py:527
  28.3 1.6 %collective-permute-done.8.refs_0_ = bf16[160,128]{1,0:T(8,128)(2,1)S(1)} collective-permute-done((bf16[160,128]{1,0:T(8,128)(2,1)S(1)}, bf16[160,128]{1,0:T(8,128)(2,1)S(1)}, u32[]{:S(2)}, u32[]{:S(2)}) %collective-permute-start.8) | collective-permute-done | bytes 40992 | tf_op jit(solution)/shard_map/ppermute | solution.py:527
  29.9 0.1 add_add_fusion
  30.0 0.0 collective-permute-start.9
  30.0 1.2 %shard_map.107 = (bf16[32,64,128]{2,1,0:T(8,128)(2,1)}, bf16[32,64,128]{2,1,0:T(8,128)(2,1)}, bf16[32,64,128]{2,1,0:T(8,128)(2,1)}) custom-call(bf16[32,64,128]{2,1,0:T(8,128)(2,1)S(1)} %bitcast.18, bf16[32,64,128]{2,1,0:T(8,128)(2,1)S(1)} %bitcast.23, bf16[32,64,128]{2,1,0:T(8,128)(2,1)S(1)} %bitcast.28, ...), custom_call_target="tpu_custom_call", output_to_operand_aliasing={{0}: (6, {}), {1}: (7, {}), {2}: (8, {})} | custom-call | flops 200000000 | bytes 1000000 | tf_op jit(solution)/shard_map/pallas_call | solution.py:599
  31.2 1.4 %shard_map.108 = (bf16[32,64,128]{2,1,0:T(8,128)(2,1)}, bf16[32,64,128]{2,1,0:T(8,128)(2,1)}, bf16[32,64,128]{2,1,0:T(8,128)(2,1)}) custom-call(bf16[32,64,128]{2,1,0:T(8,128)(2,1)S(1)} %bitcast.19, bf16[32,64,128]{2,1,0:T(8,128)(2,1)S(1)} %bitcast.24, bf16[32,64,128]{2,1,0:T(8,128)(2,1)S(1)} %bitcast.29, ...), custom_call_target="tpu_custom_call", output_to_operand_aliasing={{0}: (7, {}), {1}: (8, {}), {2}: (9, {})} | custom-call | flops 400000000 | bytes 2000000 | tf_op jit(solution)/shard_map/pallas_call | solution.py:599
  32.7 0.6 %fusion.1 = (f32[64,16]{0,1:T(8,128)}, f32[64,16]{0,1:T(8,128)}) fusion(f32[32,64]{1,0:T(8,128)S(1)} %add.31, f32[64,16]{0,1:T(8,128)S(1)} %copy-done.4, f32[64,16]{0,1:T(8,128)S(1)} %copy-done.3), kind=kLoop, calls=%fused_computation.3 | loop fusion | flops 5120 | bytes 24576 | tf_op jit(solution)/shard_map/transpose | solution.py:619
  (17 shorter events, 0.0 us)
Async XLA Ops:
  0.6 7.4 %copy-start.3 = (f32[64,16]{0,1:T(8,128)S(1)}, f32[64,16]{0,1:T(8,128)}, u32[]{:S(2)}) copy-start(f32[64,16]{0,1:T(8,128)} %param.11) | copy-start | bytes 12292
  3.5 14.7 %copy-start.4 = (f32[64,16]{0,1:T(8,128)S(1)}, f32[64,16]{0,1:T(8,128)}, u32[]{:S(2)}) copy-start(f32[64,16]{0,1:T(8,128)} %param.10) | copy-start | bytes 12292
  3.5 7.5 %collective-permute-start = (bf16[4,64,128]{2,1,0:T(8,128)(2,1)S(1)}, bf16[4,64,128]{2,1,0:T(8,128)(2,1)S(1)}, u32[]{:S(2)}, u32[]{:S(2)}) collective-permute-start(bf16[4,64,128]{2,1,0:T(8,128)(2,1)S(1)} %get-tuple-element.34), channel_id=1, source_target_pairs={{0,2},{2,0},{4,6},{6,4},{8,10},{10,8},{12,14},{14,12},{16,18},{18,... | collective-permute-start | bytes 196616 | tf_op jit(solution)/shard_map/ppermute | solution.py:527
  6.5 4.5 %collective-permute-start.1 = (bf16[4,64,128]{2,1,0:T(8,128)(2,1)S(1)}, bf16[4,64,128]{2,1,0:T(8,128)(2,1)S(1)}, u32[]{:S(2)}, u32[]{:S(2)}) collective-permute-start(bf16[4,64,128]{2,1,0:T(8,128)(2,1)S(1)} %get-tuple-element.35), channel_id=1, source_target_pairs={{0,4},{2,6},{4,0},{6,2},{8,12},{10,14},{12,8},{14,10},{16,20},{18,... | collective-permute-start | bytes 196616 | tf_op jit(solution)/shard_map/ppermute | solution.py:527
  8.0 5.2 %collective-permute-start.2 = (bf16[4,64,128]{2,1,0:T(8,128)(2,1)S(1)}, bf16[4,64,128]{2,1,0:T(8,128)(2,1)S(1)}, u32[]{:S(2)}, u32[]{:S(2)}) collective-permute-start(bf16[4,64,128]{2,1,0:T(8,128)(2,1)S(1)} %get-tuple-element.36), channel_id=1, source_target_pairs={{0,6},{2,4},{4,2},{6,0},{8,14},{10,12},{12,10},{14,8},{16,22},{18,... | collective-permute-start | bytes 196616 | tf_op jit(solution)/shard_map/ppermute | solution.py:527
  13.8 7.2 %collective-permute-start.5 = (bf16[288,128]{1,0:T(8,128)(2,1)S(1)}, bf16[288,128]{1,0:T(8,128)(2,1)S(1)}, u32[]{:S(2)}, u32[]{:S(2)}) collective-permute-start(bf16[288,128]{1,0:T(8,128)(2,1)S(1)} %shard_map.103.after_ref.refs_4_), channel_id=1, source_target_pairs={{0,24},{2,26},{4,28},{6,30},{8,16},{10,18},{12,20},{14,22},{16,8},... | collective-permute-start | bytes 221192 | tf_op jit(solution)/shard_map/ppermute | solution.py:527
  17.4 5.3 %collective-permute-start.4 = (bf16[288,128]{1,0:T(8,128)(2,1)S(1)}, bf16[288,128]{1,0:T(8,128)(2,1)S(1)}, u32[]{:S(2)}, u32[]{:S(2)}) collective-permute-start(bf16[288,128]{1,0:T(8,128)(2,1)S(1)} %shard_map.103.after_ref.refs_4_), channel_id=1, source_target_pairs={{0,16},{2,18},{4,20},{6,22},{8,24},{10,26},{12,28},{14,30},{16,0},... | collective-permute-start | bytes 221192 | tf_op jit(solution)/shard_map/ppermute | solution.py:527
  17.4 5.3 %collective-permute-start.3 = (bf16[288,128]{1,0:T(8,128)(2,1)S(1)}, bf16[288,128]{1,0:T(8,128)(2,1)S(1)}, u32[]{:S(2)}, u32[]{:S(2)}) collective-permute-start(bf16[288,128]{1,0:T(8,128)(2,1)S(1)} %shard_map.103.after_ref.refs_4_), channel_id=1, source_target_pairs={{0,8},{2,10},{4,12},{6,14},{8,0},{10,2},{12,4},{14,6},{16,24},{18,... | collective-permute-start | bytes 221192 | tf_op jit(solution)/shard_map/ppermute | solution.py:527
  18.2 8.5 %copy-start = (bf16[2048,128]{1,0:T(8,128)(2,1)S(1)}, bf16[2048,128]{1,0:T(8,128)(2,1)}, u32[]{:S(2)}) copy-start(bf16[2048,128]{1,0:T(8,128)(2,1)} %param.7) | copy-start | bytes 1572868
  18.2 8.5 %copy-start.1 = (bf16[2048,128]{1,0:T(8,128)(2,1)S(1)}, bf16[2048,128]{1,0:T(8,128)(2,1)}, u32[]{:S(2)}) copy-start(bf16[2048,128]{1,0:T(8,128)(2,1)} %param.8) | copy-start | bytes 1572868
  18.2 8.5 %copy-start.2 = (bf16[2048,128]{1,0:T(8,128)(2,1)S(1)}, bf16[2048,128]{1,0:T(8,128)(2,1)}, u32[]{:S(2)}) copy-start(bf16[2048,128]{1,0:T(8,128)(2,1)} %param.9) | copy-start | bytes 1572868
  23.2 4.7 %collective-permute-start.6 = (bf16[160,128]{1,0:T(8,128)(2,1)S(1)}, bf16[160,128]{1,0:T(8,128)(2,1)S(1)}, u32[]{:S(2)}, u32[]{:S(2)}) collective-permute-start(bf16[160,128]{1,0:T(8,128)(2,1)S(1)} %get-tuple-element.40), channel_id=1, source_target_pairs={{0,2},{2,0},{4,6},{6,4},{8,10},{10,8},{12,14},{14,12},{16,18},{18,... | collective-permute-start | bytes 122888 | tf_op jit(solution)/shard_map/ppermute | solution.py:527
  24.0 4.4 %collective-permute-start.7 = (bf16[160,128]{1,0:T(8,128)(2,1)S(1)}, bf16[160,128]{1,0:T(8,128)(2,1)S(1)}, u32[]{:S(2)}, u32[]{:S(2)}) collective-permute-start(bf16[160,128]{1,0:T(8,128)(2,1)S(1)} %get-tuple-element.41), channel_id=1, source_target_pairs={{0,4},{2,6},{4,0},{6,2},{8,12},{10,14},{12,8},{14,10},{16,20},{18,... | collective-permute-start | bytes 122888 | tf_op jit(solution)/shard_map/ppermute | solution.py:527
  25.0 4.9 %collective-permute-start.8 = (bf16[160,128]{1,0:T(8,128)(2,1)S(1)}, bf16[160,128]{1,0:T(8,128)(2,1)S(1)}, u32[]{:S(2)}, u32[]{:S(2)}) collective-permute-start(bf16[160,128]{1,0:T(8,128)(2,1)S(1)} %get-tuple-element.42), channel_id=1, source_target_pairs={{0,6},{2,4},{4,2},{6,0},{8,14},{10,12},{12,10},{14,8},{16,22},{18,... | collective-permute-start | bytes 122888 | tf_op jit(solution)/shard_map/ppermute | solution.py:527
  30.0 2.7 %collective-permute-start.9 = (f32[32,64]{1,0:T(8,128)S(1)}, f32[32,64]{1,0:T(8,128)S(1)}, u32[]{:S(2)}, u32[]{:S(2)}) collective-permute-start(f32[32,64]{1,0:T(8,128)S(1)} %add_add_fusion), channel_id=1, source_target_pairs={{0,1},{1,0},{2,3},{3,2},{4,5},{5,4},{6,7},{7,6},{8,9},{9,8},{10,11... | collective-permute-start | bytes 24584 | tf_op jit(solution)/shard_map/ppermute | solution.py:593

commit v14 on v13

--- a/solution.py
+++ b/solution.py
@@ -246,17 +246,17 @@
     lax.fori_loop(1, PLANE, others, 0)
 
 
-def split_pair(x, half):
-    head = x.astype(BF16).astype(F32)
-    tail = (x - head).astype(BF16).astype(F32)
-    low = lane_iota(x.shape) < half
-    return jnp.where(low, head, pltpu.roll(jnp.where(low, tail, 0.0), half, x.ndim - 1)).astype(BF16)
-
-
-def join_pair(x, half):
+def pack_sums(x, half):
+    rows = x.shape[0] // 2
+    low = lane_iota((rows, x.shape[1])) < half
+    return jnp.where(low, x[:rows], pltpu.roll(x[rows:], half, 1)).astype(BF16)
+
+
+def unpack_sums(x, half):
     x = x.astype(F32)
     low = lane_iota(x.shape) < half
-    return jnp.where(low, x + pltpu.roll(x, half, x.ndim - 1), 0.0)
+    both = jnp.concatenate([x, pltpu.roll(x, half, 1)], axis=0)
+    return jnp.where(jnp.concatenate([low, low], axis=0), both, 0.0)
 
 
 def in_order(arrays, place):
@@ -350,7 +350,7 @@
         sums.append(pair_sums(before, tails))
     acc[...] = sums_ref[...]
     spread(pair_terms(sums, rate), place, acc, modes)
-    out_ref[flat:] = split_pair(acc[...], lanes // 2)
+    out_ref[flat:] = pack_sums(acc[...], lanes // 2)
 
 
 def line_kernel(length, rate_ref, after_ref, *refs):
@@ -390,12 +390,12 @@
         ]
         for i, x in enumerate(in_order(packed, place)):
             outs[i][quad * rows : (quad + 1) * rows] = x
-    total = join_pair(lines[0][flat:], lanes // 2)
+    total = unpack_sums(lines[0][flat:], lanes // 2)
     for r in lines[1:]:
-        total = total + join_pair(r[flat:], lanes // 2)
+        total = total + unpack_sums(r[flat:], lanes // 2)
     acc[...] = total
     spread(pair_terms(sums, rate), place, acc, modes)
-    total = split_pair(acc[...], lanes // 2)
+    total = pack_sums(acc[...], lanes // 2)
     for i in range(PLANE):
         outs[i][flat // 2 :] = total
 
@@ -549,12 +549,14 @@
         functools.partial(plane_kernel, length),
         [vmem] * (2 + PLANE),
         vmem,
-        shaped((flat + 2 * modes, lanes), BF16),
+        shaped((flat + modes, lanes), BF16),
         [pltpu.VMEM((2 * modes, lanes), F32)],
         10**7,
         10**6,
     )(rates, *near, sums)
-    line = [plane] + [swap(plane, PLANE * i) for i in range(1, depth)]
+    line = [plane]
+    for i in range(1, depth):
+        line.append(swap(plane, PLANE * i))
     near_part, taps = call(
         local_kernel,
         [vmem] * 5,
@@ -575,7 +577,7 @@
         functools.partial(line_kernel, length),
         [vmem] * (2 + PLANE + depth),
         [vmem] * PLANE,
-        [shaped((flat // 2 + 2 * modes, lanes), BF16)] * PLANE,
+        [shaped((flat // 2 + modes, lanes), BF16)] * PLANE,
         [pltpu.VMEM((2 * modes, lanes), F32)],
         10**7,
         10**6,
@@ -584,10 +586,7 @@
     for i in range(1, PLANE):
         back.append(swap(sent[i], i))
 
-    total = sum(
-        b[flat // 2 :, : lanes // 2].astype(F32) + b[flat // 2 :, lanes // 2 :].astype(F32)
-        for b in back
-    )
+    total = sum(b[flat // 2 :].astype(F32) for b in back)
     bit = 1
     while bit < tp:
         total = total + lax.ppermute(total, "tp", [(i, i ^ bit) for i in range(tp)])
@@ -612,7 +611,7 @@
             {5 + slots + i: i for i in range(len(outs))},
         )(key, value, grad, near_part, taps, *(back[i] for i in indices), *outs)
     tokens = count * length
-    plain, moment = total[:modes, :groups], total[modes:, :groups]
+    plain, moment = total[:, :groups], total[:, lanes // 2 : lanes // 2 + groups]
     return (
         *(x.reshape(chans, length) for x in outs),
         (plain / tokens).T,

time: 33.4 us -> 33.1 us (level)
    ppermute x9, waiting for transfers between devices: 5.77 us -> 5.43 us  [swap(): return lax.ppermute(x, 'ctx', [(i, i ^ bits) for i in range(count)])]
  transfers between devices with their start and end apart: 10 -> 10, of which waited for: 4 -> 3; matrix products, arithmetic and copies ran while one was open for 0% -> 0% of each run, Pallas kernels for 29% -> 29%
where the time goes in v14:
time: 33.1 us; the launch traced here: 33 us
  Pallas kernels  13.6 us (41%)
  starting transfers between devices  12.4 us (37%)
  waiting for transfers between devices  5.44 us (16%)
  between operations  0.76 us (2%)
  other arithmetic  0.69 us (2%)
    ppermute x9, starting transfers between devices, swap(): return lax.ppermute(x, 'ctx', [(i, i ^ bits) for i in range(count)])  12.4 us
    ppermute x9, waiting for transfers between devices, swap(): return lax.ppermute(x, 'ctx', [(i, i ^ bits) for i in range(count)])  5.43 us
    pallas_call x3, Pallas kernels, gradients(): call(functools.partial(outputs_kernel, indices), [vmem] * (5 + slots) + [...  3.85 us
    pallas_call x1, Pallas kernels, gradients(): call(sums_kernel, [anywhere] * 4 + [vmem] * 3, [vmem] * 3, [shaped(quarte...  2.97 us
    pallas_call x1, Pallas kernels, gradients(): call(states_kernel, [anywhere] * 5, [vmem] * (2 + PLANE), [shaped((PLANE...  2.86 us
    pallas_call x1, Pallas kernels, gradients(): call(local_kernel, [vmem] * 5, [vmem] * 2, [shaped((PLANE,) + quarter, F3...  2.82 us
    transpose x1, other arithmetic, gradients(): return (*(x.reshape(chans, length) for x in outs), (plain / tokens).T, (-...  0.68 us
  transfers between devices with their start and end apart: 10, of which 3 were waited for; matrix products, arithmetic and copies ran while one was open for 0% of the time, Pallas kernels for 29%

profile of v14, /device:TPU:0, one launch (start us, length us, event | category | flops | bytes accessed | tf_op | source)
XLA Modules:
  0.0 33.0 jit_solution(15048170515453466290)
XLA Ops:
  0.6 2.9 %shard_map.101 = (bf16[3,16,64,128]{3,2,1,0:T(8,128)(2,1)S(1)}, bf16[64,2,16,128]{3,2,1,0:T(8,128)(2,1)S(1)}, f32[16,128]{1,0:T(8,128)S(1)}, bf16[4,64,128]{2,1,...) custom-call(f32[16,64]{1,0:T(8,128)} %bitcast.30, bf16[32,64,128]{2,1,0:T(8,128)(2,1)} %bitcast.15, ...), custom_call_target="tpu_custom_call" | custom-call | flops 1000000000 | bytes 4000000 | tf_op jit(solution)/shard_map/pallas_call | solution.py:511
  3.5 0.0 copy-start.4
  3.5 3.0 %collective-permute-start = (bf16[4,64,128]{2,1,0:T(8,128)(2,1)S(1)}, bf16[4,64,128]{2,1,0:T(8,128)(2,1)S(1)}, u32[]{:S(2)}, u32[]{:S(2)}) collective-permute-start(bf16[4,64,128]{2,1,0:T(8,128)(2,1)S(1)} %get-tuple-element.34), channel_id=1, source_target_pairs={{0,2},{2,0},{4,6},{6,4},{8,10},{10,8},{12,14},{14,12},{16,18},{18,... | collective-permute-start | bytes 196616 | tf_op jit(solution)/shard_map/ppermute | solution.py:527
  6.5 1.5 %collective-permute-start.1 = (bf16[4,64,128]{2,1,0:T(8,128)(2,1)S(1)}, bf16[4,64,128]{2,1,0:T(8,128)(2,1)S(1)}, u32[]{:S(2)}, u32[]{:S(2)}) collective-permute-start(bf16[4,64,128]{2,1,0:T(8,128)(2,1)S(1)} %get-tuple-element.35), channel_id=1, source_target_pairs={{0,4},{2,6},{4,0},{6,2},{8,12},{10,14},{12,8},{14,10},{16,20},{18,... | collective-permute-start | bytes 196616 | tf_op jit(solution)/shard_map/ppermute | solution.py:527
  8.0 0.0 collective-permute-start.2
  8.1 3.0 %shard_map.102 = (bf16[16,64,128]{2,1,0:T(8,128)(2,1)S(1)}, bf16[4,64,128]{2,1,0:T(8,128)(2,1)S(1)}, f32[32,128]{1,0:T(8,128)S(1)}) custom-call(bf16[32,64,128]{2,1,0:T(8,128)(2,1)} %bitcast.16, bf16[32,64,128]{2,1,0:T(8,128)(2,1)} %bitcast.21, bf16[32,64,128]{2,1,0:T(8,128)(2,1)} %bitcast.26, bf16[32,64,128]{2,1,0:T(8,128)(2,1)} %bitcast.38, ...), custom_call_target="tpu_custom_call" | custom-call | flops 1000000000 | bytes 4000000 | tf_op jit(solution)/shard_map/pallas_call | solution.py:532
  11.1 0.0 collective-permute-done.refs_1_
  11.1 0.0 collective-permute-done.1.refs_2_
  11.1 2.1 %collective-permute-done.2.refs_3_ = bf16[4,64,128]{2,1,0:T(8,128)(2,1)S(1)} collective-permute-done((bf16[4,64,128]{2,1,0:T(8,128)(2,1)S(1)}, bf16[4,64,128]{2,1,0:T(8,128)(2,1)S(1)}, u32[]{:S(2)}, u32[]{:S(2)}) %collective-permute-start.2) | collective-permute-done | bytes 65568 | tf_op jit(solution)/shard_map/ppermute | solution.py:527
  13.2 0.5 %shard_map.103.after_ref.refs_4_ = bf16[272,128]{1,0:T(8,128)(2,1)S(1)} custom-call(f32[16,128]{1,0:T(8,128)S(1)} %get-tuple-element.32.rate_ref, bf16[4,64,128]{2,1,0:T(8,128)(2,1)S(1)} %get-tuple-element.33.refs_0_, bf16[4,64,128]{2,1,0:T(8,128)(2,1)S(1)} %collective-permute-done.refs_1_, bf16[4,64,128]{2,1,0:T(8,128)(2,1)S(1)} %collective-permute-done.1.refs_2_, ...), custom_call_target="tpu_custom_call" | custom-call | flops 10000000 | bytes 1000000 | tf_op jit(solution)/shard_map/pallas_call | solution.py:548
  13.8 3.6 %collective-permute-start.5 = (bf16[272,128]{1,0:T(8,128)(2,1)S(1)}, bf16[272,128]{1,0:T(8,128)(2,1)S(1)}, u32[]{:S(2)}, u32[]{:S(2)}) collective-permute-start(bf16[272,128]{1,0:T(8,128)(2,1)S(1)} %shard_map.103.after_ref.refs_4_), channel_id=1, source_target_pairs={{0,24},{2,26},{4,28},{6,30},{8,16},{10,18},{12,20},{14,22},{16,8},... | collective-permute-start | bytes 208904 | tf_op jit(solution)/shard_map/ppermute | solution.py:527
  17.4 0.0 collective-permute-start.4
  17.4 0.8 %collective-permute-start.3 = (bf16[272,128]{1,0:T(8,128)(2,1)S(1)}, bf16[272,128]{1,0:T(8,128)(2,1)S(1)}, u32[]{:S(2)}, u32[]{:S(2)}) collective-permute-start(bf16[272,128]{1,0:T(8,128)(2,1)S(1)} %shard_map.103.after_ref.refs_4_), channel_id=1, source_target_pairs={{0,8},{2,10},{4,12},{6,14},{8,0},{10,2},{12,4},{14,6},{16,24},{18,... | collective-permute-start | bytes 208904 | tf_op jit(solution)/shard_map/ppermute | solution.py:527
  18.2 2.8 %shard_map.104 = (f32[4,16,64,128]{3,2,1,0:T(8,128)S(1)}, bf16[4,16,16,128]{3,2,1,0:T(8,128)(2,1)S(1)}) custom-call(bf16[16,64,128]{2,1,0:T(8,128)(2,1)S(1)} %get-tuple-element.31.own_ref, bf16[3,16,64,128]{3,2,1,0:T(8,128)(2,1)S(1)} %get-tuple-element.29.xc_ref, f32[16,64]{1,0:T(8,128)S(1)} %bitcast.32, f32[16,64]{1,0:T(8,128)S(1)} %bitcast.33, ...), custom_call_target="tpu_custom_call" | custom-call | flops 1000000000 | bytes 4000000 | tf_op jit(solution)/shard_map/pallas_call | solution.py:560
  21.0 1.6 %collective-permute-done.4.refs_6_ = bf16[272,128]{1,0:T(8,128)(2,1)S(1)} collective-permute-done((bf16[272,128]{1,0:T(8,128)(2,1)S(1)}, bf16[272,128]{1,0:T(8,128)(2,1)S(1)}, u32[]{:S(2)}, u32[]{:S(2)}) %collective-permute-start.4) | collective-permute-done | bytes 69664 | tf_op jit(solution)/shard_map/ppermute | solution.py:527
  22.6 0.6 %shard_map.105 = (bf16[144,128]{1,0:T(8,128)(2,1)S(1)}, bf16[144,128]{1,0:T(8,128)(2,1)S(1)}, bf16[144,128]{1,0:T(8,128)(2,1)S(1)}, bf16[144,128]{1,0:T(8,128)(2,1)S(1)}) custom-call(f32[16,128]{1,0:T(8,128)S(1)} %get-tuple-element.32.rate_ref, bf16[4,16,16,128]{3,2,1,0:T(8,128)(2,1)S(1)} %get-tuple-element.39.after_ref.taps_ref, ...), custom_call_target="tpu_custom_call" | custom-call | flops 10000000 | bytes 1000000 | tf_op jit(solution)/shard_map/pallas_call | solution.py:576
  23.1 0.6 %collective-permute-start.6 = (bf16[144,128]{1,0:T(8,128)(2,1)S(1)}, bf16[144,128]{1,0:T(8,128)(2,1)S(1)}, u32[]{:S(2)}, u32[]{:S(2)}) collective-permute-start(bf16[144,128]{1,0:T(8,128)(2,1)S(1)} %get-tuple-element.40), channel_id=1, source_target_pairs={{0,2},{2,0},{4,6},{6,4},{8,10},{10,8},{12,14},{14,12},{16,18},{18,... | collective-permute-start | bytes 110600 | tf_op jit(solution)/shard_map/ppermute | solution.py:527
  23.7 1.0 %collective-permute-start.7 = (bf16[144,128]{1,0:T(8,128)(2,1)S(1)}, bf16[144,128]{1,0:T(8,128)(2,1)S(1)}, u32[]{:S(2)}, u32[]{:S(2)}) collective-permute-start(bf16[144,128]{1,0:T(8,128)(2,1)S(1)} %get-tuple-element.41), channel_id=1, source_target_pairs={{0,4},{2,6},{4,0},{6,2},{8,12},{10,14},{12,8},{14,10},{16,20},{18,... | collective-permute-start | bytes 110600 | tf_op jit(solution)/shard_map/ppermute | solution.py:527
  24.7 1.9 %collective-permute-start.8 = (bf16[144,128]{1,0:T(8,128)(2,1)S(1)}, bf16[144,128]{1,0:T(8,128)(2,1)S(1)}, u32[]{:S(2)}, u32[]{:S(2)}) collective-permute-start(bf16[144,128]{1,0:T(8,128)(2,1)S(1)} %get-tuple-element.42), channel_id=1, source_target_pairs={{0,6},{2,4},{4,2},{6,0},{8,14},{10,12},{12,10},{14,8},{16,22},{18,... | collective-permute-start | bytes 110600 | tf_op jit(solution)/shard_map/ppermute | solution.py:527
  26.7 1.2 %shard_map.106 = (bf16[32,64,128]{2,1,0:T(8,128)(2,1)}, bf16[32,64,128]{2,1,0:T(8,128)(2,1)}, bf16[32,64,128]{2,1,0:T(8,128)(2,1)}) custom-call(bf16[32,64,128]{2,1,0:T(8,128)(2,1)S(1)} %bitcast.17, bf16[32,64,128]{2,1,0:T(8,128)(2,1)S(1)} %bitcast.22, bf16[32,64,128]{2,1,0:T(8,128)(2,1)S(1)} %bitcast.27, f32[4,16,64,128]{3,2,1,0:T(8,128)S(1)} %get-tuple-element.38.near_ref, ...), custom_call_target="tpu_custom_call" | custom-call | flops 200000000 | bytes 1000000 | tf_op jit(solution)/shard_map/pallas_call | solution.py:598
  27.9 1.7 %collective-permute-done.8.refs_0_ = bf16[144,128]{1,0:T(8,128)(2,1)S(1)} collective-permute-done((bf16[144,128]{1,0:T(8,128)(2,1)S(1)}, bf16[144,128]{1,0:T(8,128)(2,1)S(1)}, u32[]{:S(2)}, u32[]{:S(2)}) %collective-permute-start.8) | collective-permute-done | bytes 36896 | tf_op jit(solution)/shard_map/ppermute | solution.py:527
  29.6 1.2 %shard_map.107 = (bf16[32,64,128]{2,1,0:T(8,128)(2,1)}, bf16[32,64,128]{2,1,0:T(8,128)(2,1)}, bf16[32,64,128]{2,1,0:T(8,128)(2,1)}) custom-call(bf16[32,64,128]{2,1,0:T(8,128)(2,1)S(1)} %bitcast.18, bf16[32,64,128]{2,1,0:T(8,128)(2,1)S(1)} %bitcast.23, bf16[32,64,128]{2,1,0:T(8,128)(2,1)S(1)} %bitcast.28, ...), custom_call_target="tpu_custom_call", output_to_operand_aliasing={{0}: (6, {}), {1}: (7, {}), {2}: (8, {})} | custom-call | flops 200000000 | bytes 1000000 | tf_op jit(solution)/shard_map/pallas_call | solution.py:598
  30.8 1.4 %shard_map.108 = (bf16[32,64,128]{2,1,0:T(8,128)(2,1)}, bf16[32,64,128]{2,1,0:T(8,128)(2,1)}, bf16[32,64,128]{2,1,0:T(8,128)(2,1)}) custom-call(bf16[32,64,128]{2,1,0:T(8,128)(2,1)S(1)} %bitcast.19, bf16[32,64,128]{2,1,0:T(8,128)(2,1)S(1)} %bitcast.24, bf16[32,64,128]{2,1,0:T(8,128)(2,1)S(1)} %bitcast.29, ...), custom_call_target="tpu_custom_call", output_to_operand_aliasing={{0}: (7, {}), {1}: (8, {}), {2}: (9, {})} | custom-call | flops 400000000 | bytes 2000000 | tf_op jit(solution)/shard_map/pallas_call | solution.py:598
  32.3 0.7 %fusion.1 = (f32[64,16]{0,1:T(8,128)}, f32[64,16]{0,1:T(8,128)}) fusion(f32[16,128]{1,0:T(8,128)S(1)} %add.15, f32[64,16]{0,1:T(8,128)S(1)} %copy-done.4, f32[64,16]{0,1:T(8,128)S(1)} %copy-done.3), kind=kLoop, calls=%fused_computation.2 | loop fusion | flops 5120 | bytes 24576 | tf_op jit(solution)/shard_map/transpose | solution.py:618
  (17 shorter events, 0.0 us)
Async XLA Ops:
  0.6 7.4 %copy-start.3 = (f32[64,16]{0,1:T(8,128)S(1)}, f32[64,16]{0,1:T(8,128)}, u32[]{:S(2)}) copy-start(f32[64,16]{0,1:T(8,128)} %param.11) | copy-start | bytes 12292
  3.5 14.6 %copy-start.4 = (f32[64,16]{0,1:T(8,128)S(1)}, f32[64,16]{0,1:T(8,128)}, u32[]{:S(2)}) copy-start(f32[64,16]{0,1:T(8,128)} %param.10) | copy-start | bytes 12292
  3.5 7.5 %collective-permute-start = (bf16[4,64,128]{2,1,0:T(8,128)(2,1)S(1)}, bf16[4,64,128]{2,1,0:T(8,128)(2,1)S(1)}, u32[]{:S(2)}, u32[]{:S(2)}) collective-permute-start(bf16[4,64,128]{2,1,0:T(8,128)(2,1)S(1)} %get-tuple-element.34), channel_id=1, source_target_pairs={{0,2},{2,0},{4,6},{6,4},{8,10},{10,8},{12,14},{14,12},{16,18},{18,... | collective-permute-start | bytes 196616 | tf_op jit(solution)/shard_map/ppermute | solution.py:527
  6.5 4.5 %collective-permute-start.1 = (bf16[4,64,128]{2,1,0:T(8,128)(2,1)S(1)}, bf16[4,64,128]{2,1,0:T(8,128)(2,1)S(1)}, u32[]{:S(2)}, u32[]{:S(2)}) collective-permute-start(bf16[4,64,128]{2,1,0:T(8,128)(2,1)S(1)} %get-tuple-element.35), channel_id=1, source_target_pairs={{0,4},{2,6},{4,0},{6,2},{8,12},{10,14},{12,8},{14,10},{16,20},{18,... | collective-permute-start | bytes 196616 | tf_op jit(solution)/shard_map/ppermute | solution.py:527
  8.0 5.2 %collective-permute-start.2 = (bf16[4,64,128]{2,1,0:T(8,128)(2,1)S(1)}, bf16[4,64,128]{2,1,0:T(8,128)(2,1)S(1)}, u32[]{:S(2)}, u32[]{:S(2)}) collective-permute-start(bf16[4,64,128]{2,1,0:T(8,128)(2,1)S(1)} %get-tuple-element.36), channel_id=1, source_target_pairs={{0,6},{2,4},{4,2},{6,0},{8,14},{10,12},{12,10},{14,8},{16,22},{18,... | collective-permute-start | bytes 196616 | tf_op jit(solution)/shard_map/ppermute | solution.py:527
  13.8 7.2 %collective-permute-start.5 = (bf16[272,128]{1,0:T(8,128)(2,1)S(1)}, bf16[272,128]{1,0:T(8,128)(2,1)S(1)}, u32[]{:S(2)}, u32[]{:S(2)}) collective-permute-start(bf16[272,128]{1,0:T(8,128)(2,1)S(1)} %shard_map.103.after_ref.refs_4_), channel_id=1, source_target_pairs={{0,24},{2,26},{4,28},{6,30},{8,16},{10,18},{12,20},{14,22},{16,8},... | collective-permute-start | bytes 208904 | tf_op jit(solution)/shard_map/ppermute | solution.py:527
  17.4 5.2 %collective-permute-start.4 = (bf16[272,128]{1,0:T(8,128)(2,1)S(1)}, bf16[272,128]{1,0:T(8,128)(2,1)S(1)}, u32[]{:S(2)}, u32[]{:S(2)}) collective-permute-start(bf16[272,128]{1,0:T(8,128)(2,1)S(1)} %shard_map.103.after_ref.refs_4_), channel_id=1, source_target_pairs={{0,16},{2,18},{4,20},{6,22},{8,24},{10,26},{12,28},{14,30},{16,0},... | collective-permute-start | bytes 208904 | tf_op jit(solution)/shard_map/ppermute | solution.py:527
  17.4 5.2 %collective-permute-start.3 = (bf16[272,128]{1,0:T(8,128)(2,1)S(1)}, bf16[272,128]{1,0:T(8,128)(2,1)S(1)}, u32[]{:S(2)}, u32[]{:S(2)}) collective-permute-start(bf16[272,128]{1,0:T(8,128)(2,1)S(1)} %shard_map.103.after_ref.refs_4_), channel_id=1, source_target_pairs={{0,8},{2,10},{4,12},{6,14},{8,0},{10,2},{12,4},{14,6},{16,24},{18,... | collective-permute-start | bytes 208904 | tf_op jit(solution)/shard_map/ppermute | solution.py:527
  18.2 8.5 %copy-start = (bf16[2048,128]{1,0:T(8,128)(2,1)S(1)}, bf16[2048,128]{1,0:T(8,128)(2,1)}, u32[]{:S(2)}) copy-start(bf16[2048,128]{1,0:T(8,128)(2,1)} %param.7) | copy-start | bytes 1572868
  18.2 8.5 %copy-start.1 = (bf16[2048,128]{1,0:T(8,128)(2,1)S(1)}, bf16[2048,128]{1,0:T(8,128)(2,1)}, u32[]{:S(2)}) copy-start(bf16[2048,128]{1,0:T(8,128)(2,1)} %param.8) | copy-start | bytes 1572868
  18.2 8.5 %copy-start.2 = (bf16[2048,128]{1,0:T(8,128)(2,1)S(1)}, bf16[2048,128]{1,0:T(8,128)(2,1)}, u32[]{:S(2)}) copy-start(bf16[2048,128]{1,0:T(8,128)(2,1)} %param.9) | copy-start | bytes 1572868
  23.1 4.7 %collective-permute-start.6 = (bf16[144,128]{1,0:T(8,128)(2,1)S(1)}, bf16[144,128]{1,0:T(8,128)(2,1)S(1)}, u32[]{:S(2)}, u32[]{:S(2)}) collective-permute-start(bf16[144,128]{1,0:T(8,128)(2,1)S(1)} %get-tuple-element.40), channel_id=1, source_target_pairs={{0,2},{2,0},{4,6},{6,4},{8,10},{10,8},{12,14},{14,12},{16,18},{18,... | collective-permute-start | bytes 110600 | tf_op jit(solution)/shard_map/ppermute | solution.py:527
  23.7 4.2 %collective-permute-start.7 = (bf16[144,128]{1,0:T(8,128)(2,1)S(1)}, bf16[144,128]{1,0:T(8,128)(2,1)S(1)}, u32[]{:S(2)}, u32[]{:S(2)}) collective-permute-start(bf16[144,128]{1,0:T(8,128)(2,1)S(1)} %get-tuple-element.41), channel_id=1, source_target_pairs={{0,4},{2,6},{4,0},{6,2},{8,12},{10,14},{12,8},{14,10},{16,20},{18,... | collective-permute-start | bytes 110600 | tf_op jit(solution)/shard_map/ppermute | solution.py:527
  24.7 4.9 %collective-permute-start.8 = (bf16[144,128]{1,0:T(8,128)(2,1)S(1)}, bf16[144,128]{1,0:T(8,128)(2,1)S(1)}, u32[]{:S(2)}, u32[]{:S(2)}) collective-permute-start(bf16[144,128]{1,0:T(8,128)(2,1)S(1)} %get-tuple-element.42), channel_id=1, source_target_pairs={{0,6},{2,4},{4,2},{6,0},{8,14},{10,12},{12,10},{14,8},{16,22},{18,... | collective-permute-start | bytes 110600 | tf_op jit(solution)/shard_map/ppermute | solution.py:527
  29.6 2.7 %collective-permute-start.9 = (f32[16,128]{1,0:T(8,128)S(1)}, f32[16,128]{1,0:T(8,128)S(1)}, u32[]{:S(2)}, u32[]{:S(2)}) collective-permute-start(f32[16,128]{1,0:T(8,128)S(1)} %convert_add_fusion), channel_id=1, source_target_pairs={{0,1},{1,0},{2,3},{3,2},{4,5},{5,4},{6,7},{7,6},{8,9},{9,8},{10,11... | collective-permute-start | bytes 24584 | tf_op jit(solution)/shard_map/ppermute | solution.py:592
